TPU v7x, 32 devices: a whole 2x2x4 slice. The times are simulated.
32 devices in a mesh: groups: 2 (over x), blk: 16 (over z, y, core).
Axes of the slice: x: 2, y: 2, z: 4, core: 2. Of those that a mesh axis runs over, the one named last changes fastest.
Arguments:
- embeddings: bfloat16 [6144, 256], P(('groups', 'blk')), parts along dimension 0, may hold values from -12 to 12
- codebook: bfloat16 [16384, 256], P(('groups', 'blk')), parts along dimension 0, may hold values from -5 to 5
Outputs:
- codebook_shift: bfloat16 [16384, 256], P(('groups', 'blk')), parts along dimension 0
- occupancy: float32 [16384], P(('groups', 'blk')), parts along dimension 0
- soft_quantized: bfloat16 [6144, 256], P(('groups', 'blk')), parts along dimension 0
- row_lse: float32 [6144], P(('groups', 'blk')), parts along dimension 0
There are 2 independent parts, one for each index of `groups`. A program takes and returns all parts, laid end to end along the dimension named above; each array names one. Nothing has to cross between parts.
All inputs are finite; a program needn't handle non-finite values.
Results may differ from a plain program's by a relative error of at most 0.005.
Values may be sent and summed in bfloat16 or wider, within the bound.
No kernel may reach another device: no remote copies, remote signals or barrier semaphores. Data moves between devices by JAX's collectives and lax.ppermute only.
A program may use at most 64 MiB of HBM per device.

v0:
```python
import math

import jax
import jax.numpy as jnp
from jax import lax
from jax.sharding import PartitionSpec as P


def row_block():
    return 1024


def block_scores(rows_data, code_block, norm_term, sharpness):
    return (
        sharpness
        * jnp.einsum("rd,kd->rk", rows_data, code_block, preferred_element_type=jnp.float32)
        - norm_term[None, :]
    )


def stats_block(rows_data, code_blocks, norm_terms, sharpness):

    def stat_step(running, scanned):
        running_max, running_sum = running
        code_block, norm_term = scanned
        scores = block_scores(rows_data, code_block, norm_term, sharpness)
        new_max = jnp.maximum(running_max, jnp.max(scores, axis=1))
        running_sum = running_sum * jnp.exp(running_max - new_max) + jnp.sum(
            jnp.exp(scores - new_max[:, None]), axis=1
        )
        return ((new_max, running_sum), None)

    row_count = rows_data.shape[0]
    initial = (
        jnp.full((row_count,), -jnp.inf, dtype=jnp.float32),
        jnp.zeros((row_count,), jnp.float32),
    )
    final, ignored = lax.scan(stat_step, initial, (code_blocks, norm_terms))
    return final


def row_stats(rows_data, code_blocks, norm_terms, sharpness):
    count = rows_data.shape[0]
    size = row_block()
    blocks = rows_data.reshape(count // size, size, rows_data.shape[1])
    result = lax.map(lambda rows: stats_block(rows, code_blocks, norm_terms, sharpness), blocks)
    return (result[0].reshape(count), result[1].reshape(count))


def share_pass(rows_data, lse_rows, code_blocks, norm_terms, sharpness):
    count = rows_data.shape[0]
    width = rows_data.shape[1]
    size = row_block()
    row_blocks = rows_data.reshape(count // size, size, width)
    lse_blocks = lse_rows.reshape(count // size, size)
    block_count = code_blocks.shape[0]
    block_size = code_blocks.shape[1]
    k_dev = block_count * block_size

    def outer_step(totals, scanned):
        rows_here, lse_here = scanned

        def inner_step(rebuilt, inner):
            code_block, norm_term = inner
            scores = block_scores(rows_here, code_block, norm_term, sharpness)
            shares = jnp.exp(scores - lse_here[:, None]).astype(jnp.bfloat16)
            weighted = jnp.einsum(
                "rk,rd->kd", shares, rows_here, preferred_element_type=jnp.float32
            )
            masses = jnp.sum(shares, axis=0, dtype=jnp.float32)
            rebuilt = rebuilt + jnp.dot(shares, code_block, preferred_element_type=jnp.float32)
            return (rebuilt, (weighted, masses))

        start = jnp.zeros((size, width), jnp.float32)
        rebuilt, stacked = lax.scan(inner_step, start, (code_blocks, norm_terms))
        new_totals = (
            totals[0] + stacked[0].reshape(k_dev, width),
            totals[1] + stacked[1].reshape(k_dev),
        )
        return (new_totals, rebuilt)

    initial = (jnp.zeros((k_dev, width), jnp.float32), jnp.zeros((k_dev,), jnp.float32))
    totals, per_rows = lax.scan(outer_step, initial, (row_blocks, lse_blocks))
    return (per_rows.reshape(count, per_rows.shape[2]), totals[0], totals[1])


def on_device(embeddings, codebook):
    rows_dev = embeddings.shape[0]
    feature_width = embeddings.shape[1]
    k_dev = codebook.shape[0]
    sharpness = 3.0 / math.sqrt(feature_width)
    block_size = min(k_dev, 1024)
    block_count = k_dev // block_size
    code_blocks = codebook.reshape(block_count, block_size, feature_width)
    norm_terms = (
        0.5 * sharpness * jnp.sum(jnp.square(codebook.astype(jnp.float32)), axis=1)
    ).reshape(block_count, block_size)
    gathered = lax.all_gather(embeddings, "blk", axis=0, tiled=True)
    local_max, local_sum = row_stats(gathered, code_blocks, norm_terms, sharpness)
    global_max = lax.pmax(local_max.astype(jnp.bfloat16), "blk").astype(local_max.dtype)
    global_total = lax.psum(local_sum * jnp.exp(local_max - global_max), "blk")
    lse_all = global_max + jnp.log(global_total)
    rebuilt, weighted, masses = share_pass(gathered, lse_all, code_blocks, norm_terms, sharpness)
    own_rebuilt = lax.psum_scatter(rebuilt, "blk", scatter_dimension=0, tiled=True)
    soft_quantized = own_rebuilt.astype(jnp.bfloat16)
    prior_mass = rows_dev / k_dev
    codebook_shift = (
        (weighted - masses[:, None] * codebook.astype(jnp.float32)) / (masses[:, None] + prior_mass)
    ).astype(jnp.bfloat16)
    occupancy = masses * (k_dev / rows_dev)
    own_lse = lax.dynamic_slice_in_dim(lse_all, lax.axis_index("blk") * rows_dev, rows_dev, 0)
    return (codebook_shift, occupancy, soft_quantized, own_lse)


def solution(mesh):
    in_specs = (P(("groups", "blk"), None), P(("groups", "blk"), None))
    out_specs = (
        P(("groups", "blk"), None),
        P(("groups", "blk")),
        P(("groups", "blk"), None),
        P(("groups", "blk")),
    )
    return jax.shard_map(
        on_device, mesh=mesh, in_specs=in_specs, out_specs=out_specs, check_vma=False
    )
```

profile of v0, /device:TPU:0, one launch (start us, length us, event | category | flops | bytes accessed | tf_op | source)
XLA Modules:
  0.0 236.2 jit_solution(4751557155126825032)
XLA Ops:
  7.2 0.7 all-gather.2.cloned.1.call-update
  8.0 1.1 fusion.15
  9.1 43.6 %all-gather.2.cloned.1.call-done = bf16[3072,256]{1,0:T(8,128)(2,1)} async-done(((bf16[192,256]{1,0:T(8,128)(2,1)}), bf16[3072,256]{1,0:T(8,128)(2,1)}) %all-gather.2.cloned.1.call-update) | async-done | bytes 1572880 | tf_op jit(solution)/shard_map/all_gather | solution.py:98
  52.7 6.9 %while.27 = (s32[]{:T(128)}, f32[3,1024]{1,0:T(4,128)S(1)}, f32[3,1024]{1,0:T(4,128)S(1)}, bf16[3,1024,256]{2,1,0:T(8,128)(2,1)}, bf16[1,512,256]{2,1,0:T(8,128)...) while((s32[]{:T(128)}, f32[3,1024]{1,0:T(4,128)S(1)}, f32[3,1024]{1,0:T(4,128)S(1)}, ...), condition=%wide.region_4.5_spmd, body=%wide.region_1.4_spmd.sunk | while | flops 272106496 | bytes 5025897 | solution.py:46
  52.7 1.6 fusion.29
  55.0 1.6 fusion.29
  57.3 1.6 fusion.29
  59.6 32.1 %pmax.7 = bf16[3072]{0:T(1024)(128)(2,1)S(1)} all-reduce(bf16[3072]{0:T(1024)(128)(2,1)S(1)} %convert_element_type.25), channel_id=1, replica_groups=mesh['groups'=2,'blk'=16] {'blk'}, use_global_device_ids=true, to_apply=%region_5.6 | all-reduce | flops 3072 | bytes 12288 | tf_op jit(solution)/shard_map/pmax | solution.py:100
  91.7 57.6 %psum.7 = f32[3072]{0:T(1024)S(1)} all-reduce(f32[3072]{0:T(1024)S(1)} %fusion.20), channel_id=1, replica_groups=mesh['groups'=2,'blk'=16] {'blk'}, use_global_device_ids=true, to_apply=%region_6.7 | all-reduce | flops 3072 | bytes 24576 | tf_op jit(solution)/shard_map/psum | solution.py:101
  149.4 14.8 %while.28 = (s32[]{:T(128)}, f32[512,256]{1,0:T(8,128)S(1)}, f32[512]{0:T(512)S(1)}, f32[3,1024,256]{2,1,0:T(8,128)}, bf16[3,1024,256]{2,1,0:T(8,128)(2,1)}, /*i...) while((s32[]{:T(128)}, f32[512,256]{1,0:T(8,128)S(1)}, ...), condition=%wide.region_9.10_spmd.clone, body=%wide.region_7.9_spmd.clone.sunk | while | flops 808714752 | bytes 7887012 | solution.py:83
  149.4 1.8 convert_reduce_fusion.2
  151.2 1.7 convolution_add_fusion.2
  152.9 1.4 fusion.34
  154.3 1.8 convert_reduce_fusion.2
  156.1 1.7 convolution_add_fusion.2
  157.8 1.5 fusion.34
  159.3 1.8 convert_reduce_fusion.2
  161.1 1.7 convolution_add_fusion.2
  162.8 1.4 fusion.34
  164.2 0.6 dynamic_slice.24
  164.9 0.6 broadcast_multiply_fusion
  165.4 0.9 fusion.18
  166.4 61.4 %reduce-scatter.2.cloned.1.call-done = f32[192,256]{1,0:T(8,128)} async-done(((f32[3072,256]{1,0:T(8,128)}), f32[192,256]{1,0:T(8,128)}) %reduce-scatter.2.cloned.1.call-update) | async-done | bytes 196624 | tf_op jit(solution)/shard_map/reduce_scatter | solution.py:104
  227.8 1.6 convert_element_type.28
  (41 shorter events, 2.2 us)
Async XLA Ops:
  7.2 45.5 %all-gather.2.cloned.1.call-start = ((), (), s32[]{:S(2)}) async-start(), calls=%async_computation.1 | async-start | bytes 1671168 | tf_op jit(solution)/shard_map/all_gather | solution.py:98
  7.9 219.9 %reduce-scatter.2.cloned.1.call-start = ((), (), s32[]{:S(2)}) async-start(), calls=%async_computation.2 | async-start | bytes 3342336 | tf_op jit(solution)/shard_map/reduce_scatter | solution.py:104
  151.2 1.7 copy-start
  156.1 1.7 copy-start
  161.1 1.7 copy-start
  164.2 1.3 copy-start.1
Sparse Core Ops, SparseCore 0:
  10.3 42.3 all-gather.1
  164.3 63.4 reduce-scatter.1
where the time goes:
time: 237 us; the launch traced here: 236 us
  waiting for transfers between devices  106 us (45%)
  blocking collectives  89.7 us (38%)
  matrix products  19.4 us (8%)
  between operations  14.1 us (6%)
  other arithmetic  5.73 us (2%)
    reduce_scatter x1, waiting for transfers between devices, on_device(): lax.psum_scatter(rebuilt, 'blk', scatter_dimension=0, tiled=True)  61.4 us
    psum x1, blocking collectives, on_device(): global_total = lax.psum(local_sum * jnp.exp(local_max - global_max), 'blk')  57.6 us
    all_gather x1, waiting for transfers between devices, on_device(): gathered = lax.all_gather(embeddings, 'blk', axis=0, tiled=True)  43.6 us
    pmax x1, blocking collectives, on_device(): lax.pmax(local_max.astype(jnp.bfloat16), 'blk').astype(local_max.dtype)  32.1 us
    dot_general x6, matrix products, block_scores(): jnp.einsum('rd,kd->rk', rows_data, code_block, preferred_element_type=jnp...  10.1 us
    dot_general x3, matrix products, inner_step(): jnp.einsum('rk,rd->kd', shares, rows_here, preferred_element_type=jnp.flo...  4.99 us
  transfers between devices with their start and end apart: 2, of which 2 were waited for; matrix products, arithmetic and copies ran while one was open for 1% of the time, Pallas kernels for 0%

commit v1 on v0

v1 whole, which is shorter than its diff:
```python
import functools
import math

import jax
import jax.numpy as jnp
from jax import lax
from jax.experimental import pallas as pl
from jax.experimental.pallas import tpu as pltpu
from jax.sharding import PartitionSpec as P

AXIS = "blk"
LOG2E = math.log2(math.e)
LN2 = math.log(2.0)
VMEM_LIMIT = 48 * 1024 * 1024


def nt_dot(a, b):
    return lax.dot_general(a, b, (((1,), (1,)), ((), ())), preferred_element_type=jnp.float32)


def norm_column(code, scale):
    c = code.astype(jnp.float32)
    return (0.5 * scale) * jnp.sum(c * c, axis=1, keepdims=True)


def rows_kernel(outer, inner, tile, scale, place_ref, *refs):
    emb = refs[:outer]
    code = refs[outer : outer + inner]
    lam_ref, stacked_ref = refs[outer + inner : outer + inner + 2]
    parts = refs[outer + inner + 2 : 2 * outer + inner + 2]
    code_t, scores, total = refs[2 * outer + inner + 2 :]
    rows_dev = emb[0].shape[0]
    k_dev = code[0].shape[0]
    place = place_ref[0]
    for j in range(outer):
        spot = pl.multiple_of((place ^ j) * rows_dev, rows_dev)
        stacked_ref[pl.ds(spot, rows_dev), :] = emb[j][...]
    norms = []
    for k in range(inner):
        block = code[k][...]
        code_t[:, k * k_dev : (k + 1) * k_dev] = block.T
        norms.append(norm_column(block, scale))

    def one_tile(start):
        rows = stacked_ref[pl.ds(start, tile), :]
        top = None
        for k in range(inner):
            s = scale * nt_dot(code[k][...], rows) - norms[k]
            scores[k * k_dev : (k + 1) * k_dev, :] = s
            m = jnp.max(s, axis=0, keepdims=True)
            top = m if top is None else jnp.maximum(top, m)
        mass = jnp.zeros((1, tile), jnp.float32)
        acc = jnp.zeros((code_t.shape[0], tile), jnp.float32)
        for k in range(inner):
            p = jnp.exp2(scores[k * k_dev : (k + 1) * k_dev, :] - top)
            mass = mass + jnp.sum(p, axis=0, keepdims=True)
            acc = acc + jnp.dot(
                code_t[:, k * k_dev : (k + 1) * k_dev],
                p.astype(jnp.bfloat16),
                preferred_element_type=jnp.float32,
            )
        lam_ref[:, pl.ds(start, tile)] = LN2 * (top + jnp.log2(mass))
        total[pl.ds(start, tile), :] = (acc * (1.0 / mass)).T.astype(jnp.bfloat16)

    count = outer * rows_dev // tile
    if count <= 4:
        for t in range(count):
            one_tile(t * tile)
    else:
        pl.loop(0, count)(lambda t: one_tile(pl.multiple_of(t * tile, tile)))
    for j in range(outer):
        spot = pl.multiple_of((place ^ j) * rows_dev, rows_dev)
        parts[j][...] = total[pl.ds(spot, rows_dev), :]


def rows_calc(place, emb, code):
    outer, inner = len(emb), len(code)
    rows_dev, width = emb[0].shape
    k_dev = code[0].shape[0]
    rows = outer * rows_dev
    entries = inner * k_dev
    tile = math.gcd(rows, 256)
    vmem = pl.BlockSpec(memory_space=pltpu.VMEM)
    out = pl.pallas_call(
        functools.partial(rows_kernel, outer, inner, tile, LOG2E * 3.0 / math.sqrt(width)),
        out_shape=[
            jax.ShapeDtypeStruct((1, rows), jnp.float32),
            jax.ShapeDtypeStruct((rows, width), jnp.bfloat16),
        ]
        + [jax.ShapeDtypeStruct((rows_dev, width), jnp.bfloat16)] * outer,
        in_specs=[pl.BlockSpec(memory_space=pltpu.SMEM)] + [vmem] * (outer + inner),
        out_specs=[vmem] * (outer + 2),
        scratch_shapes=[
            pltpu.VMEM((width, entries), jnp.bfloat16),
            pltpu.VMEM((entries, tile), jnp.float32),
            pltpu.VMEM((rows, width), jnp.bfloat16),
        ],
        compiler_params=pltpu.CompilerParams(vmem_limit_bytes=VMEM_LIMIT),
        cost_estimate=pl.CostEstimate(
            flops=4 * rows * entries * width,
            bytes_accessed=2 * (rows + entries) * width,
            transcendentals=rows * entries,
        ),
        name="rows_calc",
    )(place, *emb, *code)
    return out[0], out[1], out[2:]


def combine_kernel(outer, place_ref, lse_ref, *refs):
    lams = refs[:outer]
    parts = refs[outer : 2 * outer]
    soft_ref, own_ref, columns = refs[2 * outer :]
    rows_dev, width = parts[0].shape
    rows = lse_ref.shape[1]
    lanes = columns.shape[1]
    place = place_ref[0]
    spot = pl.multiple_of(place * rows_dev, rows_dev)
    total = jnp.zeros((rows_dev, width), jnp.float32)
    for j in range(outer):
        w = jnp.exp(lams[j][...] - lse_ref[...])
        columns[...] = jnp.broadcast_to(w, (lanes, rows)).T
        mine = columns[pl.ds(spot, rows_dev), :]
        mine = jnp.concatenate([mine] * (width // lanes), axis=1)
        total = total + mine * parts[j][...].astype(jnp.float32)
    soft_ref[...] = total.astype(jnp.bfloat16)
    columns[...] = jnp.broadcast_to(lse_ref[...], (lanes, rows)).T
    own_ref[...] = columns[pl.ds(spot, rows_dev), :].T[:1, :]


def combine(place, lse, lams, parts):
    outer = len(parts)
    rows_dev, width = parts[0].shape
    lanes = math.gcd(width, 128)
    vmem = pl.BlockSpec(memory_space=pltpu.VMEM)
    return pl.pallas_call(
        functools.partial(combine_kernel, outer),
        out_shape=[
            jax.ShapeDtypeStruct((rows_dev, width), jnp.bfloat16),
            jax.ShapeDtypeStruct((1, rows_dev), jnp.float32),
        ],
        in_specs=[pl.BlockSpec(memory_space=pltpu.SMEM)] + [vmem] * (2 * outer + 1),
        out_specs=[vmem] * 2,
        scratch_shapes=[pltpu.VMEM((outer * rows_dev, lanes), jnp.float32)],
        compiler_params=pltpu.CompilerParams(vmem_limit_bytes=VMEM_LIMIT),
        cost_estimate=pl.CostEstimate(
            flops=2 * outer * rows_dev * width,
            bytes_accessed=2 * outer * rows_dev * width,
            transcendentals=0,
        ),
        name="combine",
    )(place, lse, *lams, *parts)


def columns_kernel(inner, tile, scale, rows_dev, *refs):
    code_ref = refs[0]
    emb = refs[1 : 1 + inner]
    lse = refs[1 + inner : 1 + 2 * inner]
    shift_ref, occ_ref, weighted, folded = refs[1 + 2 * inner :]
    k_dev, width = code_ref.shape
    code = code_ref[...]
    norm = norm_column(code, scale)
    lanes = folded.shape[1]
    weighted[...] = jnp.zeros_like(weighted)
    folded[...] = jnp.zeros_like(folded)

    def one_tile(g, start):
        rows = emb[g][pl.ds(start, tile), :]
        level = LOG2E * lse[g][:, pl.ds(start, tile)]
        s = scale * nt_dot(code, rows) - norm
        shares = jnp.exp2(s - level).astype(jnp.bfloat16)
        wide = shares.astype(jnp.float32)
        part = folded[...]
        for i in range(tile // lanes):
            part = part + wide[:, i * lanes : (i + 1) * lanes]
        folded[...] = part
        weighted[...] += jnp.dot(shares, rows, preferred_element_type=jnp.float32)

    count = emb[0].shape[0] // tile
    for g in range(inner):
        if count <= 4:
            for t in range(count):
                one_tile(g, t * tile)
        else:
            pl.loop(0, count)(lambda t: one_tile(g, pl.multiple_of(t * tile, tile)))
    masses = jnp.sum(folded[...], axis=1, keepdims=True)
    prior = rows_dev / k_dev
    shift_ref[...] = (
        (weighted[...] - masses * code.astype(jnp.float32)) / (masses + prior)
    ).astype(jnp.bfloat16)
    spread = jnp.broadcast_to(masses * (k_dev / rows_dev), (k_dev, lanes)).T
    occ_ref[...] = spread[:1, :]


def columns_calc(code, emb, lse, rows_dev):
    inner = len(emb)
    k_dev, width = code.shape
    rows = emb[0].shape[0]
    tile = math.gcd(rows, 256)
    lanes = math.gcd(tile, 128)
    vmem = pl.BlockSpec(memory_space=pltpu.VMEM)
    return pl.pallas_call(
        functools.partial(
            columns_kernel, inner, tile, LOG2E * 3.0 / math.sqrt(width), rows_dev
        ),
        out_shape=[
            jax.ShapeDtypeStruct((k_dev, width), jnp.bfloat16),
            jax.ShapeDtypeStruct((1, k_dev), jnp.float32),
        ],
        in_specs=[vmem] * (2 * inner + 1),
        out_specs=[vmem] * 2,
        scratch_shapes=[
            pltpu.VMEM((k_dev, width), jnp.float32),
            pltpu.VMEM((k_dev, lanes), jnp.float32),
        ],
        compiler_params=pltpu.CompilerParams(vmem_limit_bytes=VMEM_LIMIT),
        cost_estimate=pl.CostEstimate(
            flops=4 * inner * rows * k_dev * width,
            bytes_accessed=2 * (inner * rows + 2 * k_dev) * width,
            transcendentals=inner * rows * k_dev,
        ),
        name="columns_calc",
    )(code, *emb, *lse)


def on_device(size, embeddings, codebook):
    inner = 4
    outer = size // inner
    rows_dev = embeddings.shape[0]
    place = (lax.axis_index(AXIS) // inner).astype(jnp.int32).reshape(1)

    def swap(x, step):
        return lax.ppermute(x, AXIS, [(i, i ^ step) for i in range(size)])

    code_y = swap(codebook, 2)
    emb = [embeddings] + [swap(embeddings, inner * j) for j in range(1, outer)]
    code = [codebook, swap(codebook, 1), code_y, swap(code_y, 1)]
    lam, stacked, parts = rows_calc(place, emb, code)

    lams = [lam] + [swap(lam, inner * j) for j in range(1, outer)]
    parts = [parts[0]] + [swap(parts[j], inner * j) for j in range(1, outer)]
    top = functools.reduce(jnp.maximum, lams)
    lse = top + jnp.log(sum(jnp.exp(x - top) for x in lams))

    stacked_y = swap(stacked, 2)
    lse_y = swap(lse, 2)
    every_emb = [stacked, swap(stacked, 1), stacked_y, swap(stacked_y, 1)]
    every_lse = [lse, swap(lse, 1), lse_y, swap(lse_y, 1)]
    soft, own_lse = combine(place, lse, lams, parts)
    shift, occupancy = columns_calc(codebook, every_emb, every_lse, rows_dev)
    return shift, occupancy.reshape(-1), soft, own_lse.reshape(-1)


def solution(mesh):
    specs = P(("groups", AXIS), None)
    flat = P(("groups", AXIS))
    return jax.shard_map(
        functools.partial(on_device, mesh.shape[AXIS]),
        mesh=mesh,
        in_specs=(specs, specs),
        out_specs=(specs, flat, specs, flat),
        check_vma=False,
    )
```

time: 237 us -> 63.2 us (0.27)
  blocking collectives: 89.7 us -> 0 us
  waiting for transfers between devices: 106 us -> 32.1 us
  starting transfers between devices: 0.08 us -> 20.1 us
  matrix products: 19.4 us -> 0 us
  between operations: 14.1 us -> 0.69 us
  Pallas kernels: 0 us -> 8.15 us
  other arithmetic: 5.73 us -> 0.04 us
    reduce_scatter x1 -> x0, waiting for transfers between devices: 61.4 us -> none  [on_device(): lax.psum_scatter(rebuilt, 'blk', scatter_dimension=0, tiled=True)]
    psum x1 -> x0, blocking collectives: 57.6 us -> none  [on_device(): global_total = lax.psum(local_sum * jnp.exp(local_max - global_max), 'blk')]
    all_gather x1 -> x0, waiting for transfers between devices: 43.6 us -> none  [on_device(): gathered = lax.all_gather(embeddings, 'blk', axis=0, tiled=True)]
    pmax x1 -> x0, blocking collectives: 32.1 us -> none  [on_device(): lax.pmax(local_max.astype(jnp.bfloat16), 'blk').astype(local_max.dtype)]
    ppermute x0 -> x18, waiting for transfers between devices: none -> 32.1 us  [swap(): return lax.ppermute(x, AXIS, [(i, i ^ step) for i in range(size)])]
    ppermute x0 -> x18, starting transfers between devices: none -> 20.1 us  [swap(): return lax.ppermute(x, AXIS, [(i, i ^ step) for i in range(size)])]
    dot_general x12 -> x0, matrix products: 19.4 us -> none  [the longest x6 10.1 us: block_scores(): jnp.einsum('rd,kd->rk', rows_data, code_block, preferred_element_type=jnp...]
    pallas_call x0 -> x3, Pallas kernels: none -> 8.15 us  [the longest x1 3.77 us: rows_calc(): pl.pallas_call(functools.partial(rows_kernel, outer, inner, tile, LOG2E *...]
  transfers between devices with their start and end apart: 2 -> 18, of which waited for: 2 -> 9; matrix products, arithmetic and copies ran while one was open for 1% -> 0% of each run, Pallas kernels for 0% -> 2%
where the time goes in v1:
time: 63.2 us; the launch traced here: 62.9 us
  waiting for transfers between devices  32.1 us (51%)
  starting transfers between devices  20.1 us (32%)
  Pallas kernels  8.15 us (13%)
  local copies, waits for them, and re-layouts  1.85 us (3%)
  between operations  0.69 us (1%)
    ppermute x18, waiting for transfers between devices, swap(): return lax.ppermute(x, AXIS, [(i, i ^ step) for i in range(size)])  32.1 us
    ppermute x18, starting transfers between devices, swap(): return lax.ppermute(x, AXIS, [(i, i ^ step) for i in range(size)])  20.1 us
    pallas_call x1, Pallas kernels, rows_calc(): pl.pallas_call(functools.partial(rows_kernel, outer, inner, tile, LOG2E *...  3.77 us
    pallas_call x1, Pallas kernels, columns_calc(): pl.pallas_call(functools.partial(columns_kernel, inner, tile, LOG2E * 3.0...  3.13 us
    unnamed x6, local copies, waits for them, and re-layouts  1.85 us
  transfers between devices with their start and end apart: 18, of which 9 were waited for; matrix products, arithmetic and copies ran while one was open for 0% of the time, Pallas kernels for 2%

profile of v1, /device:TPU:0, one launch (start us, length us, event | category | flops | bytes accessed | tf_op | source)
XLA Modules:
  0.0 62.9 jit_solution(15713045466132714757)
XLA Ops:
  0.6 3.0 %collective-permute-start.4 = (bf16[512,256]{1,0:T(8,128)(2,1)}, bf16[512,256]{1,0:T(8,128)(2,1)S(1)}, u32[]{:S(2)}, u32[]{:S(2)}) collective-permute-start(bf16[512,256]{1,0:T(8,128)(2,1)} %refs_0_.3), channel_id=1, source_target_pairs={{0,2},{1,3},{2,0},{3,1},{4,6},{5,7},{6,4},{7,5},{8,10},{9,11},{10,... | collective-permute-start | bytes 786440 | tf_op jit(solution)/shard_map/ppermute | solution.py:232
  3.7 6.5 %collective-permute-done.4.refs_6_ = bf16[512,256]{1,0:T(8,128)(2,1)S(1)} collective-permute-done((bf16[512,256]{1,0:T(8,128)(2,1)}, bf16[512,256]{1,0:T(8,128)(2,1)S(1)}, u32[]{:S(2)}, u32[]{:S(2)}) %collective-permute-start.4) | collective-permute-done | bytes 262176 | tf_op jit(solution)/shard_map/ppermute | solution.py:232
  10.2 2.8 %collective-permute-start.1 = (bf16[192,256]{1,0:T(8,128)(2,1)}, bf16[192,256]{1,0:T(8,128)(2,1)S(1)}, u32[]{:S(2)}, u32[]{:S(2)}) collective-permute-start(bf16[192,256]{1,0:T(8,128)(2,1)} %refs_0_.2), channel_id=1, source_target_pairs={{0,8},{1,9},{2,10},{3,11},{4,12},{5,13},{6,14},{7,15},{8,0},{9,1},... | collective-permute-start | bytes 294920 | tf_op jit(solution)/shard_map/ppermute | solution.py:232
  13.0 1.6 %collective-permute-start = (bf16[192,256]{1,0:T(8,128)(2,1)}, bf16[192,256]{1,0:T(8,128)(2,1)S(1)}, u32[]{:S(2)}, u32[]{:S(2)}) collective-permute-start(bf16[192,256]{1,0:T(8,128)(2,1)} %refs_0_.2), channel_id=1, source_target_pairs={{0,4},{1,5},{2,6},{3,7},{4,0},{5,1},{6,2},{7,3},{8,12},{9,13},{10,... | collective-permute-start | bytes 294920 | tf_op jit(solution)/shard_map/ppermute | solution.py:232
  14.6 4.5 %collective-permute-done.1.refs_2_ = bf16[192,256]{1,0:T(8,128)(2,1)S(1)} collective-permute-done((bf16[192,256]{1,0:T(8,128)(2,1)}, bf16[192,256]{1,0:T(8,128)(2,1)S(1)}, u32[]{:S(2)}, u32[]{:S(2)}) %collective-permute-start.1) | collective-permute-done | bytes 98336 | tf_op jit(solution)/shard_map/ppermute | solution.py:232
  19.1 3.0 %collective-permute-done.2.refs_3_ = bf16[192,256]{1,0:T(8,128)(2,1)S(1)} collective-permute-done((bf16[192,256]{1,0:T(8,128)(2,1)}, bf16[192,256]{1,0:T(8,128)(2,1)S(1)}, u32[]{:S(2)}, u32[]{:S(2)}) %collective-permute-start.2) | collective-permute-done | bytes 98336 | tf_op jit(solution)/shard_map/ppermute | solution.py:232
  22.1 0.9 %copy-done = bf16[512,256]{1,0:T(8,128)(2,1)S(1)} copy-done((bf16[512,256]{1,0:T(8,128)(2,1)S(1)}, bf16[512,256]{1,0:T(8,128)(2,1)}, u32[]{:S(2)}) %copy-start) | copy-done | bytes 262168
  23.1 0.9 %copy-done.2 = bf16[192,256]{1,0:T(8,128)(2,1)S(1)} copy-done((bf16[192,256]{1,0:T(8,128)(2,1)S(1)}, bf16[192,256]{1,0:T(8,128)(2,1)}, u32[]{:S(2)}) %copy-start.2) | copy-done | bytes 98328
  23.9 3.8 %rows_calc.1 = (f32[1,768]{1,0:T(1,128)S(1)}, bf16[768,256]{1,0:T(8,128)(2,1)S(1)}, bf16[192,256]{1,0:T(8,128)(2,1)S(1)}, bf16[192,256]{1,0:T(8,128)(2,1)S(1)}, ...) custom-call(s32[1]{0:T(128)} %bitcast.place_ref, bf16[192,256]{1,0:T(8,128)(2,1)S(1)} %copy-done.2, ...), custom_call_target="tpu_custom_call" | custom-call | flops 1610612736 | bytes 1441792 | tf_op jit(solution)/shard_map/rows_calc/pallas_call | solution.py:84
  27.7 1.6 %collective-permute-start.7 = (bf16[768,256]{1,0:T(8,128)(2,1)S(1)}, bf16[768,256]{1,0:T(8,128)(2,1)S(1)}, u32[]{:S(2)}, u32[]{:S(2)}) collective-permute-start(bf16[768,256]{1,0:T(8,128)(2,1)S(1)} %get-tuple-element.14.refs_1_), channel_id=1, source_target_pairs={{0,2},{1,3},{2,0},{3,1},{4,6},{5,7},{6,4},{7,5},{8,10},{9,11},{10,... | collective-permute-start | bytes 1179656 | tf_op jit(solution)/shard_map/ppermute | solution.py:232
  29.3 9.2 %collective-permute-done.7.refs_3_ = bf16[768,256]{1,0:T(8,128)(2,1)S(1)} collective-permute-done((bf16[768,256]{1,0:T(8,128)(2,1)S(1)}, bf16[768,256]{1,0:T(8,128)(2,1)S(1)}, u32[]{:S(2)}, u32[]{:S(2)}) %collective-permute-start.7) | collective-permute-done | bytes 393248 | tf_op jit(solution)/shard_map/ppermute | solution.py:232
  38.5 2.4 %collective-permute-start.11 = (f32[1,768]{1,0:T(1,128)S(1)}, f32[1,768]{1,0:T(1,128)S(1)}, u32[]{:S(2)}, u32[]{:S(2)}) collective-permute-start(f32[1,768]{1,0:T(1,128)S(1)} %get-tuple-element.15.refs_0_), channel_id=1, source_target_pairs={{0,12},{1,13},{2,14},{3,15},{4,8},{5,9},{6,10},{7,11},{8,4},{9,5},... | collective-permute-start | bytes 9224 | tf_op jit(solution)/shard_map/ppermute | solution.py:232
  40.9 1.5 %collective-permute-start.10 = (f32[1,768]{1,0:T(1,128)S(1)}, f32[1,768]{1,0:T(1,128)S(1)}, u32[]{:S(2)}, u32[]{:S(2)}) collective-permute-start(f32[1,768]{1,0:T(1,128)S(1)} %get-tuple-element.15.refs_0_), channel_id=1, source_target_pairs={{0,8},{1,9},{2,10},{3,11},{4,12},{5,13},{6,14},{7,15},{8,0},{9,1},... | collective-permute-start | bytes 9224 | tf_op jit(solution)/shard_map/ppermute | solution.py:232
  42.4 0.6 collective-permute-start.9
  43.0 0.9 %collective-permute-done.11.refs_3_ = f32[1,768]{1,0:T(1,128)S(1)} collective-permute-done((f32[1,768]{1,0:T(1,128)S(1)}, f32[1,768]{1,0:T(1,128)S(1)}, u32[]{:S(2)}, u32[]{:S(2)}) %collective-permute-start.11) | collective-permute-done | bytes 3104 | tf_op jit(solution)/shard_map/ppermute | solution.py:232
  43.9 1.5 %collective-permute-done.10.refs_2_ = f32[1,768]{1,0:T(1,128)S(1)} collective-permute-done((f32[1,768]{1,0:T(1,128)S(1)}, f32[1,768]{1,0:T(1,128)S(1)}, u32[]{:S(2)}, u32[]{:S(2)}) %collective-permute-start.10) | collective-permute-done | bytes 3104 | tf_op jit(solution)/shard_map/ppermute | solution.py:232
  45.4 0.6 collective-permute-done.9.refs_1_
  46.1 1.6 %collective-permute-start.13 = (f32[1,768]{1,0:T(1,128)S(1)}, f32[1,768]{1,0:T(1,128)S(1)}, u32[]{:S(2)}, u32[]{:S(2)}) collective-permute-start(f32[1,768]{1,0:T(1,128)S(1)} %log_add_fusion.refs_5_.lse_ref), channel_id=1, source_target_pairs={{0,2},{1,3},{2,0},{3,1},{4,6},{5,7},{6,4},{7,5},{8,10},{9,11},{10,... | collective-permute-start | bytes 9224 | tf_op jit(solution)/shard_map/ppermute | solution.py:232
  47.7 1.5 %collective-permute-start.15 = (bf16[192,256]{1,0:T(8,128)(2,1)S(1)}, bf16[192,256]{1,0:T(8,128)(2,1)S(1)}, u32[]{:S(2)}, u32[]{:S(2)}) collective-permute-start(bf16[192,256]{1,0:T(8,128)(2,1)S(1)} %get-tuple-element.19), channel_id=1, source_target_pairs={{0,4},{1,5},{2,6},{3,7},{4,0},{5,1},{6,2},{7,3},{8,12},{9,13},{10,... | collective-permute-start | bytes 294920 | tf_op jit(solution)/shard_map/ppermute | solution.py:232
  49.1 2.0 %collective-permute-start.16 = (bf16[192,256]{1,0:T(8,128)(2,1)S(1)}, bf16[192,256]{1,0:T(8,128)(2,1)S(1)}, u32[]{:S(2)}, u32[]{:S(2)}) collective-permute-start(bf16[192,256]{1,0:T(8,128)(2,1)S(1)} %get-tuple-element.20), channel_id=1, source_target_pairs={{0,8},{1,9},{2,10},{3,11},{4,12},{5,13},{6,14},{7,15},{8,0},{9,1},... | collective-permute-start | bytes 294920 | tf_op jit(solution)/shard_map/ppermute | solution.py:232
  51.1 1.5 %collective-permute-start.17 = (bf16[192,256]{1,0:T(8,128)(2,1)S(1)}, bf16[192,256]{1,0:T(8,128)(2,1)S(1)}, u32[]{:S(2)}, u32[]{:S(2)}) collective-permute-start(bf16[192,256]{1,0:T(8,128)(2,1)S(1)} %get-tuple-element.21), channel_id=1, source_target_pairs={{0,12},{1,13},{2,14},{3,15},{4,8},{5,9},{6,10},{7,11},{8,4},{9,5},... | collective-permute-start | bytes 294920 | tf_op jit(solution)/shard_map/ppermute | solution.py:232
  52.8 5.7 %collective-permute-done.16.refs_6_ = bf16[192,256]{1,0:T(8,128)(2,1)S(1)} collective-permute-done((bf16[192,256]{1,0:T(8,128)(2,1)S(1)}, bf16[192,256]{1,0:T(8,128)(2,1)S(1)}, u32[]{:S(2)}, u32[]{:S(2)}) %collective-permute-start.16) | collective-permute-done | bytes 98336 | tf_op jit(solution)/shard_map/ppermute | solution.py:232
  58.5 1.3 %combine.1 = (bf16[192,256]{1,0:T(8,128)(2,1)}, f32[1,192]{1,0:T(1,128)}) custom-call(s32[1]{0:T(128)} %bitcast.place_ref, f32[1,768]{1,0:T(1,128)S(1)} %log_add_fusion.refs_5_.lse_ref, f32[1,768]{1,0:T(1,128)S(1)} %get-tuple-element.15.refs_0_, f32[1,768]{1,0:T(1,128)S(1)} %collective-permute-done.9.refs_1_, f32[1,768]{1,0:T(1,128)S(1)} %collective-permute-done.10.refs_2_, ...), custom_call_target="tpu_custom_call" | custom-call | flops 393216 | bytes 393216 | tf_op jit(solution)/shard_map/combine/pallas_call | solution.py:135
  59.8 3.1 %columns_calc.1 = (bf16[512,256]{1,0:T(8,128)(2,1)}, f32[1,512]{1,0:T(1,128)}) custom-call(bf16[512,256]{1,0:T(8,128)(2,1)S(1)} %copy-done.1, bf16[768,256]{1,0:T(8,128)(2,1)S(1)} %get-tuple-element.14.refs_1_, bf16[768,256]{1,0:T(8,128)(2,1)S(1)} %collective-permute-done.6.refs_2_, bf16[768,256]{1,0:T(8,128)(2,1)S(1)} %collective-permute-done.7.refs_3_, ...), custom_call_target="tpu_custom_call" | custom-call | flops 1610612736 | bytes 2097152 | tf_op jit(solution)/shard_map/columns_calc/pallas_call | solution.py:201
  (22 shorter events, 0.3 us)
Async XLA Ops:
  0.6 9.6 %collective-permute-start.4 = (bf16[512,256]{1,0:T(8,128)(2,1)}, bf16[512,256]{1,0:T(8,128)(2,1)S(1)}, u32[]{:S(2)}, u32[]{:S(2)}) collective-permute-start(bf16[512,256]{1,0:T(8,128)(2,1)} %refs_0_.3), channel_id=1, source_target_pairs={{0,2},{1,3},{2,0},{3,1},{4,6},{5,7},{6,4},{7,5},{8,10},{9,11},{10,... | collective-permute-start | bytes 786440 | tf_op jit(solution)/shard_map/ppermute | solution.py:232
  3.7 18.4 %collective-permute-start.3 = (bf16[512,256]{1,0:T(8,128)(2,1)}, bf16[512,256]{1,0:T(8,128)(2,1)S(1)}, u32[]{:S(2)}, u32[]{:S(2)}) collective-permute-start(bf16[512,256]{1,0:T(8,128)(2,1)} %refs_0_.3), channel_id=1, source_target_pairs={{0,1},{1,0},{2,3},{3,2},{4,5},{5,4},{6,7},{7,6},{8,9},{9,8},{10,11... | collective-permute-start | bytes 786440 | tf_op jit(solution)/shard_map/ppermute | solution.py:232
  10.2 11.9 %collective-permute-start.5 = (bf16[512,256]{1,0:T(8,128)(2,1)S(1)}, bf16[512,256]{1,0:T(8,128)(2,1)S(1)}, u32[]{:S(2)}, u32[]{:S(2)}) collective-permute-start(bf16[512,256]{1,0:T(8,128)(2,1)S(1)} %collective-permute-done.4.refs_6_), channel_id=1, source_target_pairs={{0,1},{1,0},{2,3},{3,2},{4,5},{5,4},{6,7},{7,6},{8,9},{9,8},{10,11... | collective-permute-start | bytes 786440 | tf_op jit(solution)/shard_map/ppermute | solution.py:232
  10.2 8.9 %collective-permute-start.1 = (bf16[192,256]{1,0:T(8,128)(2,1)}, bf16[192,256]{1,0:T(8,128)(2,1)S(1)}, u32[]{:S(2)}, u32[]{:S(2)}) collective-permute-start(bf16[192,256]{1,0:T(8,128)(2,1)} %refs_0_.2), channel_id=1, source_target_pairs={{0,8},{1,9},{2,10},{3,11},{4,12},{5,13},{6,14},{7,15},{8,0},{9,1},... | collective-permute-start | bytes 294920 | tf_op jit(solution)/shard_map/ppermute | solution.py:232
  13.0 6.1 %collective-permute-start = (bf16[192,256]{1,0:T(8,128)(2,1)}, bf16[192,256]{1,0:T(8,128)(2,1)S(1)}, u32[]{:S(2)}, u32[]{:S(2)}) collective-permute-start(bf16[192,256]{1,0:T(8,128)(2,1)} %refs_0_.2), channel_id=1, source_target_pairs={{0,4},{1,5},{2,6},{3,7},{4,0},{5,1},{6,2},{7,3},{8,12},{9,13},{10,... | collective-permute-start | bytes 294920 | tf_op jit(solution)/shard_map/ppermute | solution.py:232
  14.6 7.5 %collective-permute-start.2 = (bf16[192,256]{1,0:T(8,128)(2,1)}, bf16[192,256]{1,0:T(8,128)(2,1)S(1)}, u32[]{:S(2)}, u32[]{:S(2)}) collective-permute-start(bf16[192,256]{1,0:T(8,128)(2,1)} %refs_0_.2), channel_id=1, source_target_pairs={{0,12},{1,13},{2,14},{3,15},{4,8},{5,9},{6,10},{7,11},{8,4},{9,5},... | collective-permute-start | bytes 294920 | tf_op jit(solution)/shard_map/ppermute | solution.py:232
  22.1 1.0 %copy-start = (bf16[512,256]{1,0:T(8,128)(2,1)S(1)}, bf16[512,256]{1,0:T(8,128)(2,1)}, u32[]{:S(2)}) copy-start(bf16[512,256]{1,0:T(8,128)(2,1)} %refs_0_.3) | copy-start | bytes 786436
  23.1 0.9 %copy-start.2 = (bf16[192,256]{1,0:T(8,128)(2,1)S(1)}, bf16[192,256]{1,0:T(8,128)(2,1)}, u32[]{:S(2)}) copy-start(bf16[192,256]{1,0:T(8,128)(2,1)} %refs_0_.2) | copy-start | bytes 294916
  27.7 32.1 %copy-start.1 = (bf16[512,256]{1,0:T(8,128)(2,1)S(1)}, bf16[512,256]{1,0:T(8,128)(2,1)}, u32[]{:S(2)}) copy-start(bf16[512,256]{1,0:T(8,128)(2,1)} %refs_0_.3) | copy-start | bytes 786436
  27.7 10.7 %collective-permute-start.7 = (bf16[768,256]{1,0:T(8,128)(2,1)S(1)}, bf16[768,256]{1,0:T(8,128)(2,1)S(1)}, u32[]{:S(2)}, u32[]{:S(2)}) collective-permute-start(bf16[768,256]{1,0:T(8,128)(2,1)S(1)} %get-tuple-element.14.refs_1_), channel_id=1, source_target_pairs={{0,2},{1,3},{2,0},{3,1},{4,6},{5,7},{6,4},{7,5},{8,10},{9,11},{10,... | collective-permute-start | bytes 1179656 | tf_op jit(solution)/shard_map/ppermute | solution.py:232
  29.3 30.4 %collective-permute-start.6 = (bf16[768,256]{1,0:T(8,128)(2,1)S(1)}, bf16[768,256]{1,0:T(8,128)(2,1)S(1)}, u32[]{:S(2)}, u32[]{:S(2)}) collective-permute-start(bf16[768,256]{1,0:T(8,128)(2,1)S(1)} %get-tuple-element.14.refs_1_), channel_id=1, source_target_pairs={{0,1},{1,0},{2,3},{3,2},{4,5},{5,4},{6,7},{7,6},{8,9},{9,8},{10,11... | collective-permute-start | bytes 1179656 | tf_op jit(solution)/shard_map/ppermute | solution.py:232
  38.5 21.3 %collective-permute-start.8 = (bf16[768,256]{1,0:T(8,128)(2,1)S(1)}, bf16[768,256]{1,0:T(8,128)(2,1)S(1)}, u32[]{:S(2)}, u32[]{:S(2)}) collective-permute-start(bf16[768,256]{1,0:T(8,128)(2,1)S(1)} %collective-permute-done.7.refs_3_), channel_id=1, source_target_pairs={{0,1},{1,0},{2,3},{3,2},{4,5},{5,4},{6,7},{7,6},{8,9},{9,8},{10,11... | collective-permute-start | bytes 1179656 | tf_op jit(solution)/shard_map/ppermute | solution.py:232
  38.5 5.4 %collective-permute-start.11 = (f32[1,768]{1,0:T(1,128)S(1)}, f32[1,768]{1,0:T(1,128)S(1)}, u32[]{:S(2)}, u32[]{:S(2)}) collective-permute-start(f32[1,768]{1,0:T(1,128)S(1)} %get-tuple-element.15.refs_0_), channel_id=1, source_target_pairs={{0,12},{1,13},{2,14},{3,15},{4,8},{5,9},{6,10},{7,11},{8,4},{9,5},... | collective-permute-start | bytes 9224 | tf_op jit(solution)/shard_map/ppermute | solution.py:232
  40.9 4.5 %collective-permute-start.10 = (f32[1,768]{1,0:T(1,128)S(1)}, f32[1,768]{1,0:T(1,128)S(1)}, u32[]{:S(2)}, u32[]{:S(2)}) collective-permute-start(f32[1,768]{1,0:T(1,128)S(1)} %get-tuple-element.15.refs_0_), channel_id=1, source_target_pairs={{0,8},{1,9},{2,10},{3,11},{4,12},{5,13},{6,14},{7,15},{8,0},{9,1},... | collective-permute-start | bytes 9224 | tf_op jit(solution)/shard_map/ppermute | solution.py:232
  42.4 3.6 %collective-permute-start.9 = (f32[1,768]{1,0:T(1,128)S(1)}, f32[1,768]{1,0:T(1,128)S(1)}, u32[]{:S(2)}, u32[]{:S(2)}) collective-permute-start(f32[1,768]{1,0:T(1,128)S(1)} %get-tuple-element.15.refs_0_), channel_id=1, source_target_pairs={{0,4},{1,5},{2,6},{3,7},{4,0},{5,1},{6,2},{7,3},{8,12},{9,13},{10,... | collective-permute-start | bytes 9224 | tf_op jit(solution)/shard_map/ppermute | solution.py:232
  46.1 5.1 %collective-permute-start.13 = (f32[1,768]{1,0:T(1,128)S(1)}, f32[1,768]{1,0:T(1,128)S(1)}, u32[]{:S(2)}, u32[]{:S(2)}) collective-permute-start(f32[1,768]{1,0:T(1,128)S(1)} %log_add_fusion.refs_5_.lse_ref), channel_id=1, source_target_pairs={{0,2},{1,3},{2,0},{3,1},{4,6},{5,7},{6,4},{7,5},{8,10},{9,11},{10,... | collective-permute-start | bytes 9224 | tf_op jit(solution)/shard_map/ppermute | solution.py:232
  47.7 5.2 %collective-permute-start.15 = (bf16[192,256]{1,0:T(8,128)(2,1)S(1)}, bf16[192,256]{1,0:T(8,128)(2,1)S(1)}, u32[]{:S(2)}, u32[]{:S(2)}) collective-permute-start(bf16[192,256]{1,0:T(8,128)(2,1)S(1)} %get-tuple-element.19), channel_id=1, source_target_pairs={{0,4},{1,5},{2,6},{3,7},{4,0},{5,1},{6,2},{7,3},{8,12},{9,13},{10,... | collective-permute-start | bytes 294920 | tf_op jit(solution)/shard_map/ppermute | solution.py:232
  49.1 9.4 %collective-permute-start.16 = (bf16[192,256]{1,0:T(8,128)(2,1)S(1)}, bf16[192,256]{1,0:T(8,128)(2,1)S(1)}, u32[]{:S(2)}, u32[]{:S(2)}) collective-permute-start(bf16[192,256]{1,0:T(8,128)(2,1)S(1)} %get-tuple-element.20), channel_id=1, source_target_pairs={{0,8},{1,9},{2,10},{3,11},{4,12},{5,13},{6,14},{7,15},{8,0},{9,1},... | collective-permute-start | bytes 294920 | tf_op jit(solution)/shard_map/ppermute | solution.py:232
  51.1 7.4 %collective-permute-start.17 = (bf16[192,256]{1,0:T(8,128)(2,1)S(1)}, bf16[192,256]{1,0:T(8,128)(2,1)S(1)}, u32[]{:S(2)}, u32[]{:S(2)}) collective-permute-start(bf16[192,256]{1,0:T(8,128)(2,1)S(1)} %get-tuple-element.21), channel_id=1, source_target_pairs={{0,12},{1,13},{2,14},{3,15},{4,8},{5,9},{6,10},{7,11},{8,4},{9,5},... | collective-permute-start | bytes 294920 | tf_op jit(solution)/shard_map/ppermute | solution.py:232
  52.8 6.9 %collective-permute-start.12 = (f32[1,768]{1,0:T(1,128)S(1)}, f32[1,768]{1,0:T(1,128)S(1)}, u32[]{:S(2)}, u32[]{:S(2)}) collective-permute-start(f32[1,768]{1,0:T(1,128)S(1)} %log_add_fusion.refs_5_.lse_ref), channel_id=1, source_target_pairs={{0,1},{1,0},{2,3},{3,2},{4,5},{5,4},{6,7},{7,6},{8,9},{9,8},{10,11... | collective-permute-start | bytes 9224 | tf_op jit(solution)/shard_map/ppermute | solution.py:232
  58.5 1.3 %collective-permute-start.14 = (f32[1,768]{1,0:T(1,128)S(1)}, f32[1,768]{1,0:T(1,128)S(1)}, u32[]{:S(2)}, u32[]{:S(2)}) collective-permute-start(f32[1,768]{1,0:T(1,128)S(1)} %collective-permute-done.13.refs_7_), channel_id=1, source_target_pairs={{0,1},{1,0},{2,3},{3,2},{4,5},{5,4},{6,7},{7,6},{8,9},{9,8},{10,11... | collective-permute-start | bytes 9224 | tf_op jit(solution)/shard_map/ppermute | solution.py:232

commit v2 on v1

v2 whole, which is shorter than its diff:
```python
import functools
import math

import jax
import jax.numpy as jnp
from jax import lax
from jax.experimental import pallas as pl
from jax.experimental.pallas import tpu as pltpu
from jax.sharding import PartitionSpec as P

AXIS = "blk"
LOG2E = math.log2(math.e)
LN2 = math.log(2.0)
VMEM_LIMIT = 48 * 1024 * 1024


def nt_dot(a, b):
    return lax.dot_general(a, b, (((1,), (1,)), ((), ())), preferred_element_type=jnp.float32)


def norm_column(code, scale):
    c = code.astype(jnp.float32)
    return (0.5 * scale) * jnp.sum(c * c, axis=1, keepdims=True)


def stack_kernel(inner, place_ref, *refs):
    blocks, out_ref = refs[:-1], refs[-1]
    rows_dev = blocks[0].shape[0]
    place = place_ref[0] // inner
    for j, block in enumerate(blocks):
        spot = pl.multiple_of((place ^ j) * rows_dev, rows_dev)
        out_ref[pl.ds(spot, rows_dev), :] = block[...]


def stack(place, blocks, inner):
    rows_dev, width = blocks[0].shape
    vmem = pl.BlockSpec(memory_space=pltpu.VMEM)
    return pl.pallas_call(
        functools.partial(stack_kernel, inner),
        out_shape=jax.ShapeDtypeStruct((len(blocks) * rows_dev, width), blocks[0].dtype),
        in_specs=[pl.BlockSpec(memory_space=pltpu.SMEM)] + [vmem] * len(blocks),
        out_specs=vmem,
        compiler_params=pltpu.CompilerParams(vmem_limit_bytes=VMEM_LIMIT),
        cost_estimate=pl.CostEstimate(
            flops=0, bytes_accessed=4 * len(blocks) * rows_dev * width, transcendentals=0
        ),
        name="stack",
    )(place, *blocks)


def rows_kernel(outer, inner, tile, scale, place_ref, stacked_ref, *refs):
    code = refs[:inner]
    lam_ref = refs[inner]
    parts = refs[inner + 1 : inner + 1 + outer]
    code_t, scores, total = refs[inner + 1 + outer :]
    rows = stacked_ref.shape[0]
    rows_dev = rows // outer
    k_dev = code[0].shape[0]
    place = place_ref[0] // inner
    norms = []
    for k in range(inner):
        block = code[k][...]
        code_t[:, k * k_dev : (k + 1) * k_dev] = block.T
        norms.append(norm_column(block, scale))

    def one_tile(start):
        rows_here = stacked_ref[pl.ds(start, tile), :]
        top = None
        for k in range(inner):
            s = scale * nt_dot(code[k][...], rows_here) - norms[k]
            scores[k * k_dev : (k + 1) * k_dev, :] = s
            m = jnp.max(s, axis=0, keepdims=True)
            top = m if top is None else jnp.maximum(top, m)
        mass = jnp.zeros((1, tile), jnp.float32)
        acc = jnp.zeros((code_t.shape[0], tile), jnp.float32)
        for k in range(inner):
            p = jnp.exp2(scores[k * k_dev : (k + 1) * k_dev, :] - top)
            mass = mass + jnp.sum(p, axis=0, keepdims=True)
            acc = acc + jnp.dot(
                code_t[:, k * k_dev : (k + 1) * k_dev],
                p.astype(jnp.bfloat16),
                preferred_element_type=jnp.float32,
            )
        lam = LN2 * (top + jnp.log2(mass))
        lam_ref[:, :, pl.ds(start, tile)] = jnp.broadcast_to(
            lam.reshape(1, 1, tile), (lam_ref.shape[0], 1, tile)
        )
        total[pl.ds(start, tile), :] = (acc * (1.0 / mass)).T.astype(jnp.bfloat16)

    count = rows // tile
    if count <= 4:
        for t in range(count):
            one_tile(t * tile)
    else:
        pl.loop(0, count)(lambda t: one_tile(pl.multiple_of(t * tile, tile)))
    for j in range(outer):
        spot = pl.multiple_of((place ^ j) * rows_dev, rows_dev)
        parts[j][...] = total[pl.ds(spot, rows_dev), :]


def rows_calc(place, stacked, code, outer):
    inner = len(code)
    rows, width = stacked.shape
    rows_dev = rows // outer
    k_dev = code[0].shape[0]
    entries = inner * k_dev
    tile = math.gcd(rows, 256)
    vmem = pl.BlockSpec(memory_space=pltpu.VMEM)
    out = pl.pallas_call(
        functools.partial(rows_kernel, outer, inner, tile, LOG2E * 3.0 / math.sqrt(width)),
        out_shape=[jax.ShapeDtypeStruct((outer * inner, 1, rows), jnp.float32)]
        + [jax.ShapeDtypeStruct((rows_dev, width), jnp.bfloat16)] * outer,
        in_specs=[pl.BlockSpec(memory_space=pltpu.SMEM)] + [vmem] * (1 + inner),
        out_specs=[vmem] * (outer + 1),
        scratch_shapes=[
            pltpu.VMEM((width, entries), jnp.bfloat16),
            pltpu.VMEM((entries, tile), jnp.float32),
            pltpu.VMEM((rows, width), jnp.bfloat16),
        ],
        compiler_params=pltpu.CompilerParams(vmem_limit_bytes=VMEM_LIMIT),
        cost_estimate=pl.CostEstimate(
            flops=4 * rows * entries * width,
            bytes_accessed=2 * (rows + entries) * width,
            transcendentals=rows * entries,
        ),
        name="rows_calc",
    )(place, stacked, *code)
    return out[0], out[1:]


def final_kernel(outer, inner, tile, scale, place_ref, lam_ref, code_ref, *refs):
    emb = refs[:inner]
    parts = refs[inner : inner + outer]
    shift_ref, occ_ref, soft_ref, own_ref = refs[inner + outer : inner + outer + 4]
    lse, columns, weighted, folded = refs[inner + outer + 4 :]
    k_dev, width = code_ref.shape
    rows_dev = parts[0].shape[0]
    rows = emb[0].shape[0]
    lanes = folded.shape[1]
    place, spoke = place_ref[0] // inner, place_ref[0] % inner

    def lam(z, q):
        return lam_ref[z * inner + q]

    for g in range(inner):
        each = [lam(z, spoke ^ g) for z in range(outer)]
        top = functools.reduce(jnp.maximum, each)
        lse[g : g + 1, :] = top + jnp.log(sum(jnp.exp(x - top) for x in each))

    code = code_ref[...]
    norm = norm_column(code, scale)
    weighted[...] = jnp.zeros_like(weighted)
    folded[...] = jnp.zeros_like(folded)

    def one_tile(g, start):
        rows_here = emb[g][pl.ds(start, tile), :]
        level = LOG2E * lse[g : g + 1, pl.ds(start, tile)]
        s = scale * nt_dot(code, rows_here) - norm
        shares = jnp.exp2(s - level).astype(jnp.bfloat16)
        wide = shares.astype(jnp.float32)
        part = folded[...]
        for i in range(tile // lanes):
            part = part + wide[:, i * lanes : (i + 1) * lanes]
        folded[...] = part
        weighted[...] += jnp.dot(shares, rows_here, preferred_element_type=jnp.float32)

    count = rows // tile
    for g in range(inner):
        if count <= 4:
            for t in range(count):
                one_tile(g, t * tile)
        else:
            pl.loop(0, count)(lambda t: one_tile(g, pl.multiple_of(t * tile, tile)))
    masses = jnp.sum(folded[...], axis=1, keepdims=True)
    prior = rows_dev / k_dev
    shift_ref[...] = (
        (weighted[...] - masses * code.astype(jnp.float32)) / (masses + prior)
    ).astype(jnp.bfloat16)
    spread = jnp.broadcast_to(masses * (k_dev / rows_dev), (k_dev, lanes)).T
    occ_ref[...] = spread[:1, :]

    spot = pl.multiple_of(place * rows_dev, rows_dev)

    def own_rows(line):
        columns[...] = jnp.broadcast_to(line, (lanes, rows)).T
        return columns[pl.ds(spot, rows_dev), :]

    mine = lse[0:1, :]
    total = jnp.zeros((rows_dev, width), jnp.float32)
    for j in range(outer):
        w = own_rows(jnp.exp(lam(place ^ j, spoke) - mine))
        w = jnp.concatenate([w] * (width // lanes), axis=1)
        total = total + w * parts[j][...].astype(jnp.float32)
    soft_ref[...] = total.astype(jnp.bfloat16)
    own_ref[...] = own_rows(mine).T[:1, :]


def final_calc(place, lam, code, emb, parts):
    inner, outer = len(emb), len(parts)
    k_dev, width = code.shape
    rows = emb[0].shape[0]
    rows_dev = rows // outer
    tile = math.gcd(rows, 256)
    lanes = math.gcd(tile, 128)
    vmem = pl.BlockSpec(memory_space=pltpu.VMEM)
    return pl.pallas_call(
        functools.partial(
            final_kernel, outer, inner, tile, LOG2E * 3.0 / math.sqrt(width)
        ),
        out_shape=[
            jax.ShapeDtypeStruct((k_dev, width), jnp.bfloat16),
            jax.ShapeDtypeStruct((1, k_dev), jnp.float32),
            jax.ShapeDtypeStruct((rows_dev, width), jnp.bfloat16),
            jax.ShapeDtypeStruct((1, rows_dev), jnp.float32),
        ],
        in_specs=[pl.BlockSpec(memory_space=pltpu.SMEM)] + [vmem] * (2 + inner + outer),
        out_specs=[vmem] * 4,
        scratch_shapes=[
            pltpu.VMEM((inner, rows), jnp.float32),
            pltpu.VMEM((rows, lanes), jnp.float32),
            pltpu.VMEM((k_dev, width), jnp.float32),
            pltpu.VMEM((k_dev, lanes), jnp.float32),
        ],
        compiler_params=pltpu.CompilerParams(vmem_limit_bytes=VMEM_LIMIT),
        cost_estimate=pl.CostEstimate(
            flops=4 * inner * rows * k_dev * width,
            bytes_accessed=2 * (inner * rows + 2 * k_dev) * width,
            transcendentals=inner * rows * k_dev,
        ),
        name="final_calc",
    )(place, lam, code, *emb, *parts)


def on_device(size, embeddings, codebook):
    inner = 4
    outer = size // inner
    place = lax.axis_index(AXIS).astype(jnp.int32).reshape(1)

    def swap(x, step):
        return lax.ppermute(x, AXIS, [(i, i ^ step) for i in range(size)])

    code_y = swap(codebook, 2)
    code_c = swap(codebook, 1)
    emb = [swap(embeddings, inner * j) for j in range(1, outer)]
    code_y, *emb = lax.optimization_barrier((code_y, *emb))
    stacked = stack(place, [embeddings] + emb, inner)
    code = [codebook, code_c, code_y, swap(code_y, 1)]
    stacked_y = swap(stacked, 2)
    lam, parts = rows_calc(place, stacked, code, outer)

    stacked_y, lam = lax.optimization_barrier((stacked_y, lam))
    parts = [parts[0]] + [swap(parts[j], inner * j) for j in range(1, outer)]
    lam = lax.all_to_all(lam, AXIS, 0, 0)
    every_emb = [stacked, swap(stacked, 1), stacked_y, swap(stacked_y, 1)]
    shift, occupancy, soft, own_lse = final_calc(place, lam, codebook, every_emb, parts)
    return shift, occupancy.reshape(-1), soft, own_lse.reshape(-1)


def solution(mesh):
    specs = P(("groups", AXIS), None)
    flat = P(("groups", AXIS))
    return jax.shard_map(
        functools.partial(on_device, mesh.shape[AXIS]),
        mesh=mesh,
        in_specs=(specs, specs),
        out_specs=(specs, flat, specs, flat),
        check_vma=False,
    )
```

time: 63.2 us -> 45.9 us (0.73)
  waiting for transfers between devices: 32.1 us -> 20.2 us
  starting transfers between devices: 20.1 us -> 16.9 us
  Pallas kernels: 8.15 us -> 6.87 us
  local copies, waits for them, and re-layouts: 1.85 us -> 1 us
    ppermute x18 -> x12, waiting for transfers between devices: 32.1 us -> 17.3 us  [swap(): return lax.ppermute(x, AXIS, [(i, i ^ step) for i in range(size)])]
    ppermute x18 -> x12, starting transfers between devices: 20.1 us -> 13.1 us  [swap(): return lax.ppermute(x, AXIS, [(i, i ^ step) for i in range(size)])]
    all_to_all x0 -> x1, starting transfers between devices: none -> 3.74 us  [on_device(): lam = lax.all_to_all(lam, AXIS, 0, 0)]
    all_to_all x0 -> x1, waiting for transfers between devices: none -> 2.96 us  [on_device(): lam = lax.all_to_all(lam, AXIS, 0, 0)]
    pallas_call x2, Pallas kernels: 4.38 us -> 3.2 us  [the longest x1 3.17 us: final_calc(): pl.pallas_call(functools.partial(final_kernel, outer, inner, tile, LOG2E...]
    unnamed x6 -> x4, local copies, waits for them, and re-layouts: 1.85 us -> 1 us
  transfers between devices with their start and end apart: 18 -> 13, of which waited for: 9 -> 5; matrix products, arithmetic and copies ran while one was open for 0% -> 0% of each run, Pallas kernels for 2% -> 8%
where the time goes in v2:
time: 45.9 us; the launch traced here: 45.6 us
  waiting for transfers between devices  20.2 us (44%)
  starting transfers between devices  16.9 us (37%)
  Pallas kernels  6.87 us (15%)
  local copies, waits for them, and re-layouts  1 us (2%)
  between operations  0.68 us (1%)
    ppermute x12, waiting for transfers between devices, swap(): return lax.ppermute(x, AXIS, [(i, i ^ step) for i in range(size)])  17.3 us
    ppermute x12, starting transfers between devices, swap(): return lax.ppermute(x, AXIS, [(i, i ^ step) for i in range(size)])  13.1 us
    all_to_all x1, starting transfers between devices, on_device(): lam = lax.all_to_all(lam, AXIS, 0, 0)  3.74 us
    pallas_call x1, Pallas kernels, rows_calc(): pl.pallas_call(functools.partial(rows_kernel, outer, inner, tile, LOG2E *...  3.67 us
    pallas_call x1, Pallas kernels, final_calc(): pl.pallas_call(functools.partial(final_kernel, outer, inner, tile, LOG2E...  3.17 us
    all_to_all x1, waiting for transfers between devices, on_device(): lam = lax.all_to_all(lam, AXIS, 0, 0)  2.96 us
    unnamed x4, local copies, waits for them, and re-layouts  1 us
  transfers between devices with their start and end apart: 13, of which 5 were waited for; matrix products, arithmetic and copies ran while one was open for 0% of the time, Pallas kernels for 8%

profile of v2, /device:TPU:0, one launch (start us, length us, event | category | flops | bytes accessed | tf_op | source)
XLA Modules:
  0.0 45.6 jit_solution(7534536132497852023)
XLA Ops:
  0.6 3.0 %collective-permute-start = (bf16[512,256]{1,0:T(8,128)(2,1)}, bf16[512,256]{1,0:T(8,128)(2,1)S(1)}, u32[]{:S(2)}, u32[]{:S(2)}) collective-permute-start(bf16[512,256]{1,0:T(8,128)(2,1)} %code_ref.1), channel_id=1, source_target_pairs={{0,2},{1,3},{2,0},{3,1},{4,6},{5,7},{6,4},{7,5},{8,10},{9,11},{10,... | collective-permute-start | bytes 786440 | tf_op jit(solution)/shard_map/ppermute | solution.py:240
  3.7 2.6 %collective-permute-start.2 = (bf16[192,256]{1,0:T(8,128)(2,1)}, bf16[192,256]{1,0:T(8,128)(2,1)S(1)}, u32[]{:S(2)}, u32[]{:S(2)}) collective-permute-start(bf16[192,256]{1,0:T(8,128)(2,1)} %refs_0_.2), channel_id=1, source_target_pairs={{0,8},{1,9},{2,10},{3,11},{4,12},{5,13},{6,14},{7,15},{8,0},{9,1},... | collective-permute-start | bytes 294920 | tf_op jit(solution)/shard_map/ppermute | solution.py:240
  6.3 1.6 %collective-permute-start.1 = (bf16[192,256]{1,0:T(8,128)(2,1)}, bf16[192,256]{1,0:T(8,128)(2,1)S(1)}, u32[]{:S(2)}, u32[]{:S(2)}) collective-permute-start(bf16[192,256]{1,0:T(8,128)(2,1)} %refs_0_.2), channel_id=1, source_target_pairs={{0,4},{1,5},{2,6},{3,7},{4,0},{5,1},{6,2},{7,3},{8,12},{9,13},{10,... | collective-permute-start | bytes 294920 | tf_op jit(solution)/shard_map/ppermute | solution.py:240
  7.8 0.2 collective-permute-start.3
  8.1 3.9 %collective-permute-done.2.refs_2_ = bf16[192,256]{1,0:T(8,128)(2,1)S(1)} collective-permute-done((bf16[192,256]{1,0:T(8,128)(2,1)}, bf16[192,256]{1,0:T(8,128)(2,1)S(1)}, u32[]{:S(2)}, u32[]{:S(2)}) %collective-permute-start.2) | collective-permute-done | bytes 98336 | tf_op jit(solution)/shard_map/ppermute | solution.py:240
  12.0 0.0 collective-permute-done.1.refs_1_
  12.0 2.5 %collective-permute-done.3.refs_3_ = bf16[192,256]{1,0:T(8,128)(2,1)S(1)} collective-permute-done((bf16[192,256]{1,0:T(8,128)(2,1)}, bf16[192,256]{1,0:T(8,128)(2,1)S(1)}, u32[]{:S(2)}, u32[]{:S(2)}) %collective-permute-start.3) | collective-permute-done | bytes 98336 | tf_op jit(solution)/shard_map/ppermute | solution.py:240
  14.5 0.0 collective-permute-done.refs_2_
  14.5 0.0 collective-permute-start.6
  14.5 0.9 %copy-done = bf16[192,256]{1,0:T(8,128)(2,1)S(1)} copy-done((bf16[192,256]{1,0:T(8,128)(2,1)S(1)}, bf16[192,256]{1,0:T(8,128)(2,1)}, u32[]{:S(2)}) %copy-start) | copy-done | bytes 98328
  15.5 0.6 %collective-permute-start.4 = (bf16[768,256]{1,0:T(8,128)(2,1)S(1)}, bf16[768,256]{1,0:T(8,128)(2,1)S(1)}, u32[]{:S(2)}, u32[]{:S(2)}) collective-permute-start(bf16[768,256]{1,0:T(8,128)(2,1)S(1)} %stack.1.stacked_ref.refs_0_), channel_id=1, source_target_pairs={{0,2},{1,3},{2,0},{3,1},{4,6},{5,7},{6,4},{7,5},{8,10},{9,11},{10,... | collective-permute-start | bytes 1179656 | tf_op jit(solution)/shard_map/ppermute | solution.py:240
  16.0 0.2 collective-permute-start.7
  16.3 0.0 collective-permute-done.6.refs_3_
  16.3 0.1 copy-done.1
  16.4 3.7 %rows_calc.1 = (f32[16,1,768]{2,1,0:T(1,128)}, bf16[192,256]{1,0:T(8,128)(2,1)S(1)}, bf16[192,256]{1,0:T(8,128)(2,1)S(1)}, bf16[192,256]{1,0:T(8,128)(2,1)S(1)}, bf16[192,256]{1,0:T(8,128)(2,1)S(1)}) custom-call(s32[1]{0:T(128)} %bitcast.place_ref, bf16[768,256]{1,0:T(8,128)(2,1)S(1)} %stack.1.stacked_ref.refs_0_, bf16[512,256]{1,0:T(8,128)(2,1)S(1)} %copy-done.1, ...), custom_call_target="tpu_custom_call" | custom-call | flops 1610612736 | bytes 1441792 | tf_op jit(solution)/shard_map/rows_calc/pallas_call | solution.py:109
  20.0 7.0 %collective-permute-done.4.refs_2_ = bf16[768,256]{1,0:T(8,128)(2,1)S(1)} collective-permute-done((bf16[768,256]{1,0:T(8,128)(2,1)S(1)}, bf16[768,256]{1,0:T(8,128)(2,1)S(1)}, u32[]{:S(2)}, u32[]{:S(2)}) %collective-permute-start.4) | collective-permute-done | bytes 393248 | tf_op jit(solution)/shard_map/ppermute | solution.py:240
  27.0 0.0 collective-permute-start.8
  27.1 1.6 %collective-permute-start.9 = (bf16[192,256]{1,0:T(8,128)(2,1)S(1)}, bf16[192,256]{1,0:T(8,128)(2,1)S(1)}, u32[]{:S(2)}, u32[]{:S(2)}) collective-permute-start(bf16[192,256]{1,0:T(8,128)(2,1)S(1)} %get-tuple-element.27), channel_id=1, source_target_pairs={{0,4},{1,5},{2,6},{3,7},{4,0},{5,1},{6,2},{7,3},{8,12},{9,13},{10,... | collective-permute-start | bytes 294920 | tf_op jit(solution)/shard_map/ppermute | solution.py:240
  28.7 1.8 %collective-permute-start.10 = (bf16[192,256]{1,0:T(8,128)(2,1)S(1)}, bf16[192,256]{1,0:T(8,128)(2,1)S(1)}, u32[]{:S(2)}, u32[]{:S(2)}) collective-permute-start(bf16[192,256]{1,0:T(8,128)(2,1)S(1)} %get-tuple-element.28), channel_id=1, source_target_pairs={{0,8},{1,9},{2,10},{3,11},{4,12},{5,13},{6,14},{7,15},{8,0},{9,1},... | collective-permute-start | bytes 294920 | tf_op jit(solution)/shard_map/ppermute | solution.py:240
  30.5 1.5 %collective-permute-start.11 = (bf16[192,256]{1,0:T(8,128)(2,1)S(1)}, bf16[192,256]{1,0:T(8,128)(2,1)S(1)}, u32[]{:S(2)}, u32[]{:S(2)}) collective-permute-start(bf16[192,256]{1,0:T(8,128)(2,1)S(1)} %get-tuple-element.29), channel_id=1, source_target_pairs={{0,12},{1,13},{2,14},{3,15},{4,8},{5,9},{6,10},{7,11},{8,4},{9,5},... | collective-permute-start | bytes 294920 | tf_op jit(solution)/shard_map/ppermute | solution.py:240
  31.9 3.7 %all-to-all-start = ((f32[16,1,768]{2,1,0:T(1,128)}), f32[16,1,768]{2,1,0:T(1,128)S(1)}, u32[]{:S(2)}, u32[]{:S(2)}) async-start(f32[16,1,768]{2,1,0:T(1,128)} %get-tuple-element.24), calls=%async_computation | async-start | bytes 98304 | tf_op jit(solution)/shard_map/all_to_all | solution.py:253
  35.7 3.8 %collective-permute-done.11.refs_7_ = bf16[192,256]{1,0:T(8,128)(2,1)S(1)} collective-permute-done((bf16[192,256]{1,0:T(8,128)(2,1)S(1)}, bf16[192,256]{1,0:T(8,128)(2,1)S(1)}, u32[]{:S(2)}, u32[]{:S(2)}) %collective-permute-start.11) | collective-permute-done | bytes 98336 | tf_op jit(solution)/shard_map/ppermute | solution.py:240
  39.5 3.0 %all-to-all-done.lam_ref = f32[16,1,768]{2,1,0:T(1,128)S(1)} async-done(((f32[16,1,768]{2,1,0:T(1,128)}), f32[16,1,768]{2,1,0:T(1,128)S(1)}, u32[]{:S(2)}, u32[]{:S(2)}) %all-to-all-start) | async-done | bytes 49184 | tf_op jit(solution)/shard_map/all_to_all | solution.py:253
  42.5 3.2 %final_calc.1 = (bf16[512,256]{1,0:T(8,128)(2,1)}, f32[1,512]{1,0:T(1,128)}, bf16[192,256]{1,0:T(8,128)(2,1)}, f32[1,192]{1,0:T(1,128)}) custom-call(s32[1]{0:T(128)} %bitcast.place_ref, f32[16,1,768]{2,1,0:T(1,128)S(1)} %all-to-all-done.lam_ref, bf16[512,256]{1,0:T(8,128)(2,1)S(1)} %copy-done.1, bf16[768,256]{1,0:T(8,128)(2,1)S(1)} %stack.1.stacked_ref.refs_0_, ...), custom_call_target="tpu_custom_call" | custom-call | flops 1610612736 | bytes 2097152 | tf_op jit(solution)/shard_map/final_calc/pallas_call | solution.py:206
  (9 shorter events, 0.1 us)
Async XLA Ops:
  0.6 13.9 %collective-permute-start = (bf16[512,256]{1,0:T(8,128)(2,1)}, bf16[512,256]{1,0:T(8,128)(2,1)S(1)}, u32[]{:S(2)}, u32[]{:S(2)}) collective-permute-start(bf16[512,256]{1,0:T(8,128)(2,1)} %code_ref.1), channel_id=1, source_target_pairs={{0,2},{1,3},{2,0},{3,1},{4,6},{5,7},{6,4},{7,5},{8,10},{9,11},{10,... | collective-permute-start | bytes 786440 | tf_op jit(solution)/shard_map/ppermute | solution.py:240
  3.7 8.3 %collective-permute-start.2 = (bf16[192,256]{1,0:T(8,128)(2,1)}, bf16[192,256]{1,0:T(8,128)(2,1)S(1)}, u32[]{:S(2)}, u32[]{:S(2)}) collective-permute-start(bf16[192,256]{1,0:T(8,128)(2,1)} %refs_0_.2), channel_id=1, source_target_pairs={{0,8},{1,9},{2,10},{3,11},{4,12},{5,13},{6,14},{7,15},{8,0},{9,1},... | collective-permute-start | bytes 294920 | tf_op jit(solution)/shard_map/ppermute | solution.py:240
  6.3 5.7 %collective-permute-start.1 = (bf16[192,256]{1,0:T(8,128)(2,1)}, bf16[192,256]{1,0:T(8,128)(2,1)S(1)}, u32[]{:S(2)}, u32[]{:S(2)}) collective-permute-start(bf16[192,256]{1,0:T(8,128)(2,1)} %refs_0_.2), channel_id=1, source_target_pairs={{0,4},{1,5},{2,6},{3,7},{4,0},{5,1},{6,2},{7,3},{8,12},{9,13},{10,... | collective-permute-start | bytes 294920 | tf_op jit(solution)/shard_map/ppermute | solution.py:240
  7.8 6.7 %collective-permute-start.3 = (bf16[192,256]{1,0:T(8,128)(2,1)}, bf16[192,256]{1,0:T(8,128)(2,1)S(1)}, u32[]{:S(2)}, u32[]{:S(2)}) collective-permute-start(bf16[192,256]{1,0:T(8,128)(2,1)} %refs_0_.2), channel_id=1, source_target_pairs={{0,12},{1,13},{2,14},{3,15},{4,8},{5,9},{6,10},{7,11},{8,4},{9,5},... | collective-permute-start | bytes 294920 | tf_op jit(solution)/shard_map/ppermute | solution.py:240
  8.1 8.2 %collective-permute-start.5 = (bf16[512,256]{1,0:T(8,128)(2,1)}, bf16[512,256]{1,0:T(8,128)(2,1)S(1)}, u32[]{:S(2)}, u32[]{:S(2)}) collective-permute-start(bf16[512,256]{1,0:T(8,128)(2,1)} %code_ref.1), channel_id=1, source_target_pairs={{0,1},{1,0},{2,3},{3,2},{4,5},{5,4},{6,7},{7,6},{8,9},{9,8},{10,11... | collective-permute-start | bytes 786440 | tf_op jit(solution)/shard_map/ppermute | solution.py:240
  14.5 1.7 %collective-permute-start.6 = (bf16[512,256]{1,0:T(8,128)(2,1)S(1)}, bf16[512,256]{1,0:T(8,128)(2,1)S(1)}, u32[]{:S(2)}, u32[]{:S(2)}) collective-permute-start(bf16[512,256]{1,0:T(8,128)(2,1)S(1)} %collective-permute-done.refs_2_), channel_id=1, source_target_pairs={{0,1},{1,0},{2,3},{3,2},{4,5},{5,4},{6,7},{7,6},{8,9},{9,8},{10,11... | collective-permute-start | bytes 786440 | tf_op jit(solution)/shard_map/ppermute | solution.py:240
  14.5 0.9 %copy-start = (bf16[192,256]{1,0:T(8,128)(2,1)S(1)}, bf16[192,256]{1,0:T(8,128)(2,1)}, u32[]{:S(2)}) copy-start(bf16[192,256]{1,0:T(8,128)(2,1)} %refs_0_.2) | copy-start | bytes 294916
  15.4 0.9 %copy-start.1 = (bf16[512,256]{1,0:T(8,128)(2,1)S(1)}, bf16[512,256]{1,0:T(8,128)(2,1)}, u32[]{:S(2)}) copy-start(bf16[512,256]{1,0:T(8,128)(2,1)} %code_ref.1) | copy-start | bytes 786436
  15.5 11.6 %collective-permute-start.4 = (bf16[768,256]{1,0:T(8,128)(2,1)S(1)}, bf16[768,256]{1,0:T(8,128)(2,1)S(1)}, u32[]{:S(2)}, u32[]{:S(2)}) collective-permute-start(bf16[768,256]{1,0:T(8,128)(2,1)S(1)} %stack.1.stacked_ref.refs_0_), channel_id=1, source_target_pairs={{0,2},{1,3},{2,0},{3,1},{4,6},{5,7},{6,4},{7,5},{8,10},{9,11},{10,... | collective-permute-start | bytes 1179656 | tf_op jit(solution)/shard_map/ppermute | solution.py:240
  16.0 23.5 %collective-permute-start.7 = (bf16[768,256]{1,0:T(8,128)(2,1)S(1)}, bf16[768,256]{1,0:T(8,128)(2,1)S(1)}, u32[]{:S(2)}, u32[]{:S(2)}) collective-permute-start(bf16[768,256]{1,0:T(8,128)(2,1)S(1)} %stack.1.stacked_ref.refs_0_), channel_id=1, source_target_pairs={{0,1},{1,0},{2,3},{3,2},{4,5},{5,4},{6,7},{7,6},{8,9},{9,8},{10,11... | collective-permute-start | bytes 1179656 | tf_op jit(solution)/shard_map/ppermute | solution.py:240
  27.0 15.4 %collective-permute-start.8 = (bf16[768,256]{1,0:T(8,128)(2,1)S(1)}, bf16[768,256]{1,0:T(8,128)(2,1)S(1)}, u32[]{:S(2)}, u32[]{:S(2)}) collective-permute-start(bf16[768,256]{1,0:T(8,128)(2,1)S(1)} %collective-permute-done.4.refs_2_), channel_id=1, source_target_pairs={{0,1},{1,0},{2,3},{3,2},{4,5},{5,4},{6,7},{7,6},{8,9},{9,8},{10,11... | collective-permute-start | bytes 1179656 | tf_op jit(solution)/shard_map/ppermute | solution.py:240
  27.1 8.6 %collective-permute-start.9 = (bf16[192,256]{1,0:T(8,128)(2,1)S(1)}, bf16[192,256]{1,0:T(8,128)(2,1)S(1)}, u32[]{:S(2)}, u32[]{:S(2)}) collective-permute-start(bf16[192,256]{1,0:T(8,128)(2,1)S(1)} %get-tuple-element.27), channel_id=1, source_target_pairs={{0,4},{1,5},{2,6},{3,7},{4,0},{5,1},{6,2},{7,3},{8,12},{9,13},{10,... | collective-permute-start | bytes 294920 | tf_op jit(solution)/shard_map/ppermute | solution.py:240
  28.7 7.0 %collective-permute-start.10 = (bf16[192,256]{1,0:T(8,128)(2,1)S(1)}, bf16[192,256]{1,0:T(8,128)(2,1)S(1)}, u32[]{:S(2)}, u32[]{:S(2)}) collective-permute-start(bf16[192,256]{1,0:T(8,128)(2,1)S(1)} %get-tuple-element.28), channel_id=1, source_target_pairs={{0,8},{1,9},{2,10},{3,11},{4,12},{5,13},{6,14},{7,15},{8,0},{9,1},... | collective-permute-start | bytes 294920 | tf_op jit(solution)/shard_map/ppermute | solution.py:240
  30.5 9.0 %collective-permute-start.11 = (bf16[192,256]{1,0:T(8,128)(2,1)S(1)}, bf16[192,256]{1,0:T(8,128)(2,1)S(1)}, u32[]{:S(2)}, u32[]{:S(2)}) collective-permute-start(bf16[192,256]{1,0:T(8,128)(2,1)S(1)} %get-tuple-element.29), channel_id=1, source_target_pairs={{0,12},{1,13},{2,14},{3,15},{4,8},{5,9},{6,10},{7,11},{8,4},{9,5},... | collective-permute-start | bytes 294920 | tf_op jit(solution)/shard_map/ppermute | solution.py:240
  31.9 10.5 %all-to-all-start = ((f32[16,1,768]{2,1,0:T(1,128)}), f32[16,1,768]{2,1,0:T(1,128)S(1)}, u32[]{:S(2)}, u32[]{:S(2)}) async-start(f32[16,1,768]{2,1,0:T(1,128)} %get-tuple-element.24), calls=%async_computation | async-start | bytes 98304 | tf_op jit(solution)/shard_map/all_to_all | solution.py:253

commit v3 on v2

v3 whole, which is shorter than its diff:
```python
import functools
import math

import jax
import jax.numpy as jnp
from jax import lax
from jax.experimental import pallas as pl
from jax.experimental.pallas import tpu as pltpu
from jax.sharding import PartitionSpec as P

AXIS = "blk"
LOG2E = math.log2(math.e)
LN2 = math.log(2.0)
VMEM_LIMIT = 16 * 1024 * 1024


def nt_dot(a, b):
    return lax.dot_general(a, b, (((1,), (1,)), ((), ())), preferred_element_type=jnp.float32)


def norm_column(code, scale):
    c = code.astype(jnp.float32)
    return (0.5 * scale) * jnp.sum(c * c, axis=1, keepdims=True)


def tiles(rows, tile, body):
    count = rows // tile
    if count <= 4:
        for t in range(count):
            body(t * tile)
    else:
        pl.loop(0, count)(lambda t: body(pl.multiple_of(t * tile, tile)))


def stack_kernel(inner, place_ref, own_ref, *refs):
    blocks, out_ref, sem = refs[:-2], refs[-2], refs[-1]
    rows_dev = own_ref.shape[0]
    place = place_ref[0] // inner

    def spot(j):
        return pl.ds(pl.multiple_of((place ^ j) * rows_dev, rows_dev), rows_dev)

    own = pltpu.make_async_copy(own_ref, out_ref.at[spot(0)], sem)
    own.start()
    for j, block in enumerate(blocks):
        out_ref[spot(j + 1), :] = block[...]
    own.wait()


def stack(place, own, blocks, inner):
    rows_dev, width = own.shape
    count = 1 + len(blocks)
    vmem = pl.BlockSpec(memory_space=pltpu.VMEM)
    return pl.pallas_call(
        functools.partial(stack_kernel, inner),
        out_shape=jax.ShapeDtypeStruct((count * rows_dev, width), own.dtype),
        in_specs=[pl.BlockSpec(memory_space=pltpu.SMEM), pl.BlockSpec(memory_space=pltpu.HBM)]
        + [vmem] * len(blocks),
        out_specs=vmem,
        scratch_shapes=[pltpu.SemaphoreType.DMA(())],
        compiler_params=pltpu.CompilerParams(vmem_limit_bytes=VMEM_LIMIT),
        cost_estimate=pl.CostEstimate(
            flops=0, bytes_accessed=4 * count * rows_dev * width, transcendentals=0
        ),
        name="stack",
    )(place, own, *blocks)


def rows_kernel(outer, inner, tile, scale, place_ref, stacked_ref, *refs):
    code = refs[:inner]
    lam_ref = refs[inner]
    parts = refs[inner + 1 : inner + 1 + outer]
    code_t, scores, total = refs[inner + 1 + outer :]
    rows = stacked_ref.shape[0]
    rows_dev = rows // outer
    k_dev = code[0].shape[0]
    place = place_ref[0] // inner
    norms = []
    for k in range(inner):
        block = code[k][...]
        code_t[:, k * k_dev : (k + 1) * k_dev] = block.T
        norms.append(norm_column(block, scale))

    def one_tile(start):
        rows_here = stacked_ref[pl.ds(start, tile), :]
        top = None
        for k in range(inner):
            s = scale * nt_dot(code[k][...], rows_here) - norms[k]
            scores[k * k_dev : (k + 1) * k_dev, :] = s
            m = jnp.max(s, axis=0, keepdims=True)
            top = m if top is None else jnp.maximum(top, m)
        mass = jnp.zeros((1, tile), jnp.float32)
        acc = jnp.zeros((code_t.shape[0], tile), jnp.float32)
        for k in range(inner):
            p = jnp.exp2(scores[k * k_dev : (k + 1) * k_dev, :] - top)
            mass = mass + jnp.sum(p, axis=0, keepdims=True)
            acc = acc + jnp.dot(
                code_t[:, k * k_dev : (k + 1) * k_dev],
                p.astype(jnp.bfloat16),
                preferred_element_type=jnp.float32,
            )
        lam = LN2 * (top + jnp.log2(mass))
        lam_ref[:, :, pl.ds(start, tile)] = jnp.broadcast_to(
            lam.reshape(1, 1, tile), (lam_ref.shape[0], 1, tile)
        )
        total[pl.ds(start, tile), :] = (acc * (1.0 / mass)).T.astype(jnp.bfloat16)

    tiles(rows, tile, one_tile)
    for j in range(outer):
        spot = pl.multiple_of((place ^ j) * rows_dev, rows_dev)
        parts[j][...] = total[pl.ds(spot, rows_dev), :]


def rows_calc(place, stacked, code, outer):
    inner = len(code)
    rows, width = stacked.shape
    rows_dev = rows // outer
    k_dev = code[0].shape[0]
    entries = inner * k_dev
    tile = math.gcd(rows, 256)
    vmem = pl.BlockSpec(memory_space=pltpu.VMEM)
    out = pl.pallas_call(
        functools.partial(rows_kernel, outer, inner, tile, LOG2E * 3.0 / math.sqrt(width)),
        out_shape=[jax.ShapeDtypeStruct((outer * inner, 1, rows), jnp.float32)]
        + [jax.ShapeDtypeStruct((rows_dev, width), jnp.bfloat16)] * outer,
        in_specs=[pl.BlockSpec(memory_space=pltpu.SMEM)] + [vmem] * (1 + inner),
        out_specs=[vmem] * (outer + 1),
        scratch_shapes=[
            pltpu.VMEM((width, entries), jnp.bfloat16),
            pltpu.VMEM((entries, tile), jnp.float32),
            pltpu.VMEM((rows, width), jnp.bfloat16),
        ],
        compiler_params=pltpu.CompilerParams(vmem_limit_bytes=VMEM_LIMIT),
        cost_estimate=pl.CostEstimate(
            flops=4 * rows * entries * width,
            bytes_accessed=2 * (rows + entries) * width,
            transcendentals=rows * entries,
        ),
        name="rows_calc",
    )(place, stacked, *code)
    return out[0], out[1:]


def norm_kernel(scale, code_ref, out_ref):
    out_ref[...] = jnp.broadcast_to(norm_column(code_ref[...], scale), out_ref.shape)


def norm_calc(code, scale):
    k_dev, width = code.shape
    lanes = math.gcd(width, 128)
    vmem = pl.BlockSpec(memory_space=pltpu.VMEM)
    return pl.pallas_call(
        functools.partial(norm_kernel, scale),
        out_shape=jax.ShapeDtypeStruct((k_dev, lanes), jnp.float32),
        in_specs=[vmem],
        out_specs=vmem,
        compiler_params=pltpu.CompilerParams(vmem_limit_bytes=VMEM_LIMIT),
        cost_estimate=pl.CostEstimate(
            flops=2 * k_dev * width, bytes_accessed=2 * k_dev * width, transcendentals=0
        ),
        name="norm_calc",
    )(code)


def read_lse(lam_ref, outer, inner, spoke):
    each = [lam_ref[z * inner + spoke] for z in range(outer)]
    top = functools.reduce(jnp.maximum, each)
    return top + jnp.log(sum(jnp.exp(x - top) for x in each))


def add_groups(groups, tile, scale, levels, code_ref, norm_ref, emb, weighted, folded):
    lanes = folded.shape[1]
    code = code_ref[...]
    norm = jnp.concatenate([norm_ref[...]] * (tile // lanes), axis=1)
    for g, emb_ref in zip(groups, emb):
        level = LOG2E * levels(g)
        for start in range(0, emb_ref.shape[0], tile):
            rows_here = emb_ref[start : start + tile, :]
            s = scale * nt_dot(code, rows_here) - norm
            shares = jnp.exp2(s - level[:, start : start + tile]).astype(jnp.bfloat16)
            wide = shares.astype(jnp.float32)
            part = folded[...]
            for i in range(tile // lanes):
                part = part + wide[:, i * lanes : (i + 1) * lanes]
            folded[...] = part
            weighted[...] += jnp.dot(shares, rows_here, preferred_element_type=jnp.float32)


def early_kernel(outer, inner, groups, tile, scale, place_ref, lam_ref, code_ref, norm_ref, *refs):
    emb = refs[: len(groups)]
    parts = refs[len(groups) : len(groups) + outer]
    weighted, folded, soft_ref, own_ref, columns = refs[len(groups) + outer :]
    rows_dev, width = parts[0].shape
    rows, lanes = columns.shape
    place, spoke = place_ref[0] // inner, place_ref[0] % inner
    weighted[...] = jnp.zeros_like(weighted)
    folded[...] = jnp.zeros_like(folded)
    levels = lambda g: read_lse(lam_ref, outer, inner, spoke ^ g)
    add_groups(groups, tile, scale, levels, code_ref, norm_ref, emb, weighted, folded)

    spot = pl.multiple_of(place * rows_dev, rows_dev)
    mine = levels(0)

    def own_rows(line):
        columns[...] = jnp.broadcast_to(line, (lanes, rows)).T
        return columns[pl.ds(spot, rows_dev), :]

    total = jnp.zeros((rows_dev, width), jnp.float32)
    for j in range(outer):
        w = own_rows(jnp.exp(lam_ref[(place ^ j) * inner + spoke] - mine))
        w = jnp.concatenate([w] * (width // lanes), axis=1)
        total = total + w * parts[j][...].astype(jnp.float32)
    soft_ref[...] = total.astype(jnp.bfloat16)
    own_ref[...] = own_rows(mine).T[:1, :]


def late_kernel(outer, inner, groups, tile, scale, place_ref, lam_ref, code_ref, norm_ref, *refs):
    emb = refs[: len(groups)]
    weighted_in, folded_in, shift_ref, occ_ref, weighted, folded = refs[len(groups) :]
    k_dev = code_ref.shape[0]
    rows_dev = emb[0].shape[0] // outer
    spoke = place_ref[0] % inner
    weighted[...] = weighted_in[...]
    folded[...] = folded_in[...]
    levels = lambda g: read_lse(lam_ref, outer, inner, spoke ^ g)
    add_groups(groups, tile, scale, levels, code_ref, norm_ref, emb, weighted, folded)
    masses = jnp.sum(folded[...], axis=1, keepdims=True)
    prior = rows_dev / k_dev
    shift_ref[...] = (
        (weighted[...] - masses * code_ref[...].astype(jnp.float32)) / (masses + prior)
    ).astype(jnp.bfloat16)
    spread = jnp.broadcast_to(masses * (k_dev / rows_dev), folded.shape).T
    occ_ref[...] = spread[:1, :]


def columns_calc(place, lam, code, norm, groups, emb, inner, parts=(), sums=()):
    k_dev, width = code.shape
    rows = emb[0].shape[0]
    outer = lam.shape[0] // inner
    rows_dev = rows // outer
    tile = math.gcd(rows, 256)
    lanes = norm.shape[1]
    totals = [((k_dev, width), jnp.float32), ((k_dev, lanes), jnp.float32)]
    if parts:
        body, out = early_kernel, totals + [((rows_dev, width), jnp.bfloat16), ((1, rows_dev), jnp.float32)]
        scratch = [pltpu.VMEM((rows, lanes), jnp.float32)]
    else:
        body, out = late_kernel, [((k_dev, width), jnp.bfloat16), ((1, k_dev), jnp.float32)]
        scratch = [pltpu.VMEM(*x) for x in totals]
    extra = [*parts, *sums]
    vmem = pl.BlockSpec(memory_space=pltpu.VMEM)
    return pl.pallas_call(
        functools.partial(body, outer, inner, groups, tile, LOG2E * 3.0 / math.sqrt(width)),
        out_shape=[jax.ShapeDtypeStruct(*x) for x in out],
        in_specs=[pl.BlockSpec(memory_space=pltpu.SMEM)] + [vmem] * (3 + len(emb) + len(extra)),
        out_specs=[vmem] * len(out),
        scratch_shapes=scratch,
        compiler_params=pltpu.CompilerParams(vmem_limit_bytes=VMEM_LIMIT),
        cost_estimate=pl.CostEstimate(
            flops=(64 if parts else 4) * len(emb) * rows * k_dev * width,
            bytes_accessed=2 * (len(emb) * rows + 2 * k_dev) * width,
            transcendentals=len(emb) * rows * k_dev,
        ),
        name="columns_calc",
    )(place, lam, code, norm, *emb, *extra)


def after(x, y):
    return lax.optimization_barrier((x, y))[0]


def on_device(size, embeddings, codebook):
    inner = 4
    outer = size // inner
    place = lax.axis_index(AXIS).astype(jnp.int32).reshape(1)

    def swap(x, step):
        return lax.ppermute(x, AXIS, [(i, i ^ step) for i in range(size)])

    code_y = swap(codebook, 2)
    code_c = swap(codebook, 1)
    emb = [swap(embeddings, inner * j) for j in range(1, outer)]
    code_y, *emb = lax.optimization_barrier((code_y, *emb))
    stacked = stack(place, embeddings, emb, inner)
    stacked_y = swap(stacked, 2)
    stacked_c = swap(stacked, 1)
    code = [codebook, code_c, code_y, swap(code_y, 1)]
    lam, parts = rows_calc(place, stacked, code, outer)

    parts = [parts[0]] + [swap(parts[j], inner * j) for j in range(1, outer)]
    lam = lax.all_to_all(lam, AXIS, 0, 0)
    norm = norm_calc(codebook, LOG2E * 3.0 / math.sqrt(codebook.shape[1]))
    stacked_yc = swap(stacked_y, 1)
    weighted, folded, soft, own_lse = columns_calc(
        place, lam, codebook, norm, (0, 1, 2), [stacked, stacked_c, stacked_y], inner, parts=parts
    )
    shift, occupancy = columns_calc(
        place, lam, codebook, norm, (3,), [stacked_yc], inner, sums=(weighted, folded)
    )
    return shift, occupancy.reshape(-1), soft, own_lse.reshape(-1)


def solution(mesh):
    specs = P(("groups", AXIS), None)
    flat = P(("groups", AXIS))
    return jax.shard_map(
        functools.partial(on_device, mesh.shape[AXIS]),
        mesh=mesh,
        in_specs=(specs, specs),
        out_specs=(specs, flat, specs, flat),
        check_vma=False,
    )
```

time: 45.9 us -> 40.6 us (0.88)
  waiting for transfers between devices: 20.2 us -> 12.6 us
  starting transfers between devices: 16.9 us -> 18.4 us
  Pallas kernels: 6.87 us -> 7.74 us
    ppermute x12, waiting for transfers between devices: 17.3 us -> 6.48 us  [swap(): return lax.ppermute(x, AXIS, [(i, i ^ step) for i in range(size)])]
    all_to_all x1, waiting for transfers between devices: 2.96 us -> 6.13 us  [on_device(): lam = lax.all_to_all(lam, AXIS, 0, 0)]
    all_to_all x1, starting transfers between devices: 3.74 us -> 4.77 us  [on_device(): lam = lax.all_to_all(lam, AXIS, 0, 0)]
    pallas_call x1 -> x3, Pallas kernels: 3.17 us -> 3.94 us  [the longest x2 3.8 us: columns_calc(): pl.pallas_call(functools.partial(body, outer, inner, groups, tile, LOG2E...]
    ppermute x12, starting transfers between devices: 13.1 us -> 13.7 us  [swap(): return lax.ppermute(x, AXIS, [(i, i ^ step) for i in range(size)])]
  transfers between devices with their start and end apart: 13 -> 13, of which waited for: 5 -> 3; matrix products, arithmetic and copies ran while one was open for 0% -> 0% of each run, Pallas kernels for 8% -> 15%
where the time goes in v3:
time: 40.6 us; the launch traced here: 40.4 us
  starting transfers between devices  18.4 us (45%)
  waiting for transfers between devices  12.6 us (31%)
  Pallas kernels  7.74 us (19%)
  local copies, waits for them, and re-layouts  0.9 us (2%)
  between operations  0.7 us (2%)
    ppermute x12, starting transfers between devices, swap(): return lax.ppermute(x, AXIS, [(i, i ^ step) for i in range(size)])  13.7 us
    ppermute x12, waiting for transfers between devices, swap(): return lax.ppermute(x, AXIS, [(i, i ^ step) for i in range(size)])  6.48 us
    all_to_all x1, waiting for transfers between devices, on_device(): lam = lax.all_to_all(lam, AXIS, 0, 0)  6.13 us
    all_to_all x1, starting transfers between devices, on_device(): lam = lax.all_to_all(lam, AXIS, 0, 0)  4.77 us
    pallas_call x2, Pallas kernels, columns_calc(): pl.pallas_call(functools.partial(body, outer, inner, groups, tile, LOG2E...  3.8 us
    pallas_call x1, Pallas kernels, rows_calc(): pl.pallas_call(functools.partial(rows_kernel, outer, inner, tile, LOG2E *...  3.67 us
    unnamed x4, local copies, waits for them, and re-layouts  0.9 us
  transfers between devices with their start and end apart: 13, of which 3 were waited for; matrix products, arithmetic and copies ran while one was open for 0% of the time, Pallas kernels for 15%

profile of v3, /device:TPU:0, one launch (start us, length us, event | category | flops | bytes accessed | tf_op | source)
XLA Modules:
  0.0 40.4 jit_solution(14483843937924160950)
XLA Ops:
  0.6 3.0 %collective-permute-start = (bf16[512,256]{1,0:T(8,128)(2,1)}, bf16[512,256]{1,0:T(8,128)(2,1)S(1)}, u32[]{:S(2)}, u32[]{:S(2)}) collective-permute-start(bf16[512,256]{1,0:T(8,128)(2,1)} %code_ref.5), channel_id=1, source_target_pairs={{0,2},{1,3},{2,0},{3,1},{4,6},{5,7},{6,4},{7,5},{8,10},{9,11},{10,... | collective-permute-start | bytes 786440 | tf_op jit(solution)/shard_map/ppermute | solution.py:278
  3.7 2.6 %collective-permute-start.2 = (bf16[192,256]{1,0:T(8,128)(2,1)}, bf16[192,256]{1,0:T(8,128)(2,1)S(1)}, u32[]{:S(2)}, u32[]{:S(2)}) collective-permute-start(bf16[192,256]{1,0:T(8,128)(2,1)} %own_ref.1), channel_id=1, source_target_pairs={{0,8},{1,9},{2,10},{3,11},{4,12},{5,13},{6,14},{7,15},{8,0},{9,1},... | collective-permute-start | bytes 294920 | tf_op jit(solution)/shard_map/ppermute | solution.py:278
  6.3 1.6 %collective-permute-start.1 = (bf16[192,256]{1,0:T(8,128)(2,1)}, bf16[192,256]{1,0:T(8,128)(2,1)S(1)}, u32[]{:S(2)}, u32[]{:S(2)}) collective-permute-start(bf16[192,256]{1,0:T(8,128)(2,1)} %own_ref.1), channel_id=1, source_target_pairs={{0,4},{1,5},{2,6},{3,7},{4,0},{5,1},{6,2},{7,3},{8,12},{9,13},{10,... | collective-permute-start | bytes 294920 | tf_op jit(solution)/shard_map/ppermute | solution.py:278
  7.8 0.2 collective-permute-start.3
  8.1 0.0 collective-permute-start.4
  8.1 3.9 %collective-permute-done.2.refs_1_ = bf16[192,256]{1,0:T(8,128)(2,1)S(1)} collective-permute-done((bf16[192,256]{1,0:T(8,128)(2,1)}, bf16[192,256]{1,0:T(8,128)(2,1)S(1)}, u32[]{:S(2)}, u32[]{:S(2)}) %collective-permute-start.2) | collective-permute-done | bytes 98336 | tf_op jit(solution)/shard_map/ppermute | solution.py:278
  12.0 0.0 collective-permute-done.1.refs_0_
  12.0 2.5 %collective-permute-done.3.refs_2_ = bf16[192,256]{1,0:T(8,128)(2,1)S(1)} collective-permute-done((bf16[192,256]{1,0:T(8,128)(2,1)}, bf16[192,256]{1,0:T(8,128)(2,1)S(1)}, u32[]{:S(2)}, u32[]{:S(2)}) %collective-permute-start.3) | collective-permute-done | bytes 98336 | tf_op jit(solution)/shard_map/ppermute | solution.py:278
  14.5 0.9 %copy-done.1 = bf16[192,256]{1,0:T(8,128)(2,1)S(1)} copy-done((bf16[192,256]{1,0:T(8,128)(2,1)S(1)}, bf16[192,256]{1,0:T(8,128)(2,1)}, u32[]{:S(2)}) %copy-start.1) | copy-done | bytes 98328
  15.4 0.1 stack.1.stacked_ref.refs_0_
  15.6 0.6 %collective-permute-start.6 = (bf16[768,256]{1,0:T(8,128)(2,1)S(1)}, bf16[768,256]{1,0:T(8,128)(2,1)S(1)}, u32[]{:S(2)}, u32[]{:S(2)}) collective-permute-start(bf16[768,256]{1,0:T(8,128)(2,1)S(1)} %stack.1.stacked_ref.refs_0_), channel_id=1, source_target_pairs={{0,2},{1,3},{2,0},{3,1},{4,6},{5,7},{6,4},{7,5},{8,10},{9,11},{10,... | collective-permute-start | bytes 1179656 | tf_op jit(solution)/shard_map/ppermute | solution.py:278
  16.1 0.2 collective-permute-start.8
  16.4 0.0 copy-done
  16.4 3.7 %rows_calc.1 = (f32[16,1,768]{2,1,0:T(1,128)}, bf16[192,256]{1,0:T(8,128)(2,1)S(1)}, bf16[192,256]{1,0:T(8,128)(2,1)S(1)}, bf16[192,256]{1,0:T(8,128)(2,1)S(1)}, bf16[192,256]{1,0:T(8,128)(2,1)S(1)}) custom-call(s32[1]{0:T(128)} %bitcast.place_ref, bf16[768,256]{1,0:T(8,128)(2,1)S(1)} %stack.1.stacked_ref.refs_0_, bf16[512,256]{1,0:T(8,128)(2,1)S(1)} %copy-done, ...), custom_call_target="tpu_custom_call" | custom-call | flops 1610612736 | bytes 1441792 | tf_op jit(solution)/shard_map/rows_calc/pallas_call | solution.py:122
  20.0 1.7 %collective-permute-start.9 = (bf16[192,256]{1,0:T(8,128)(2,1)S(1)}, bf16[192,256]{1,0:T(8,128)(2,1)S(1)}, u32[]{:S(2)}, u32[]{:S(2)}) collective-permute-start(bf16[192,256]{1,0:T(8,128)(2,1)S(1)} %get-tuple-element.25), channel_id=1, source_target_pairs={{0,4},{1,5},{2,6},{3,7},{4,0},{5,1},{6,2},{7,3},{8,12},{9,13},{10,... | collective-permute-start | bytes 294920 | tf_op jit(solution)/shard_map/ppermute | solution.py:278
  21.7 1.9 %collective-permute-start.10 = (bf16[192,256]{1,0:T(8,128)(2,1)S(1)}, bf16[192,256]{1,0:T(8,128)(2,1)S(1)}, u32[]{:S(2)}, u32[]{:S(2)}) collective-permute-start(bf16[192,256]{1,0:T(8,128)(2,1)S(1)} %get-tuple-element.26), channel_id=1, source_target_pairs={{0,8},{1,9},{2,10},{3,11},{4,12},{5,13},{6,14},{7,15},{8,0},{9,1},... | collective-permute-start | bytes 294920 | tf_op jit(solution)/shard_map/ppermute | solution.py:278
  23.6 1.4 %collective-permute-start.11 = (bf16[192,256]{1,0:T(8,128)(2,1)S(1)}, bf16[192,256]{1,0:T(8,128)(2,1)S(1)}, u32[]{:S(2)}, u32[]{:S(2)}) collective-permute-start(bf16[192,256]{1,0:T(8,128)(2,1)S(1)} %get-tuple-element.27), channel_id=1, source_target_pairs={{0,12},{1,13},{2,14},{3,15},{4,8},{5,9},{6,10},{7,11},{8,4},{9,5},... | collective-permute-start | bytes 294920 | tf_op jit(solution)/shard_map/ppermute | solution.py:278
  25.0 4.8 %all-to-all-start = ((f32[16,1,768]{2,1,0:T(1,128)}), f32[16,1,768]{2,1,0:T(1,128)S(1)}, u32[]{:S(2)}, u32[]{:S(2)}) async-start(f32[16,1,768]{2,1,0:T(1,128)} %get-tuple-element.23), calls=%async_computation | async-start | bytes 98304 | tf_op jit(solution)/shard_map/all_to_all | solution.py:291
  29.8 0.1 norm_calc.1.norm_ref
  29.9 0.0 collective-permute-done.6.refs_2_
  29.9 0.5 %collective-permute-start.7 = (bf16[768,256]{1,0:T(8,128)(2,1)S(1)}, bf16[768,256]{1,0:T(8,128)(2,1)S(1)}, u32[]{:S(2)}, u32[]{:S(2)}) collective-permute-start(bf16[768,256]{1,0:T(8,128)(2,1)S(1)} %collective-permute-done.6.refs_2_), channel_id=1, source_target_pairs={{0,1},{1,0},{2,3},{3,2},{4,5},{5,4},{6,7},{7,6},{8,9},{9,8},{10,11... | collective-permute-start | bytes 1179656 | tf_op jit(solution)/shard_map/ppermute | solution.py:278
  30.4 6.1 %all-to-all-done.lam_ref = f32[16,1,768]{2,1,0:T(1,128)S(1)} async-done(((f32[16,1,768]{2,1,0:T(1,128)}), f32[16,1,768]{2,1,0:T(1,128)S(1)}, u32[]{:S(2)}, u32[]{:S(2)}) %all-to-all-start) | async-done | bytes 49184 | tf_op jit(solution)/shard_map/all_to_all | solution.py:291
  36.6 2.3 %columns_calc.2 = (f32[512,256]{1,0:T(8,128)S(1)}, f32[512,128]{1,0:T(8,128)S(1)}, bf16[192,256]{1,0:T(8,128)(2,1)}, f32[1,192]{1,0:T(1,128)}) custom-call(s32[1]{0:T(128)} %bitcast.place_ref, f32[16,1,768]{2,1,0:T(1,128)S(1)} %all-to-all-done.lam_ref, bf16[512,256]{1,0:T(8,128)(2,1)S(1)} %copy-done, f32[512,128]{1,0:T(8,128)S(1)} %norm_calc.1.norm_ref, ...), custom_call_target="tpu_custom_call" | custom-call | flops 19327352832 | bytes 1703936 | tf_op jit(solution)/shard_map/columns_calc/pallas_call | solution.py:252
  38.8 1.5 %columns_calc.3 = (bf16[512,256]{1,0:T(8,128)(2,1)}, f32[1,512]{1,0:T(1,128)}) custom-call(s32[1]{0:T(128)} %bitcast.place_ref, f32[16,1,768]{2,1,0:T(1,128)S(1)} %all-to-all-done.lam_ref, bf16[512,256]{1,0:T(8,128)(2,1)S(1)} %copy-done, f32[512,128]{1,0:T(8,128)S(1)} %norm_calc.1.norm_ref, bf16[768,256]{1,0:T(8,128)(2,1)S(1)} %collective-permute-done.7.refs_0_, ...), custom_call_target="tpu_custom_call" | custom-call | flops 402653184 | bytes 917504 | tf_op jit(solution)/shard_map/columns_calc/pallas_call | solution.py:252
  (11 shorter events, 0.0 us)
Async XLA Ops:
  0.6 13.9 %collective-permute-start = (bf16[512,256]{1,0:T(8,128)(2,1)}, bf16[512,256]{1,0:T(8,128)(2,1)S(1)}, u32[]{:S(2)}, u32[]{:S(2)}) collective-permute-start(bf16[512,256]{1,0:T(8,128)(2,1)} %code_ref.5), channel_id=1, source_target_pairs={{0,2},{1,3},{2,0},{3,1},{4,6},{5,7},{6,4},{7,5},{8,10},{9,11},{10,... | collective-permute-start | bytes 786440 | tf_op jit(solution)/shard_map/ppermute | solution.py:278
  3.7 8.3 %collective-permute-start.2 = (bf16[192,256]{1,0:T(8,128)(2,1)}, bf16[192,256]{1,0:T(8,128)(2,1)S(1)}, u32[]{:S(2)}, u32[]{:S(2)}) collective-permute-start(bf16[192,256]{1,0:T(8,128)(2,1)} %own_ref.1), channel_id=1, source_target_pairs={{0,8},{1,9},{2,10},{3,11},{4,12},{5,13},{6,14},{7,15},{8,0},{9,1},... | collective-permute-start | bytes 294920 | tf_op jit(solution)/shard_map/ppermute | solution.py:278
  6.3 5.7 %collective-permute-start.1 = (bf16[192,256]{1,0:T(8,128)(2,1)}, bf16[192,256]{1,0:T(8,128)(2,1)S(1)}, u32[]{:S(2)}, u32[]{:S(2)}) collective-permute-start(bf16[192,256]{1,0:T(8,128)(2,1)} %own_ref.1), channel_id=1, source_target_pairs={{0,4},{1,5},{2,6},{3,7},{4,0},{5,1},{6,2},{7,3},{8,12},{9,13},{10,... | collective-permute-start | bytes 294920 | tf_op jit(solution)/shard_map/ppermute | solution.py:278
  7.8 6.7 %collective-permute-start.3 = (bf16[192,256]{1,0:T(8,128)(2,1)}, bf16[192,256]{1,0:T(8,128)(2,1)S(1)}, u32[]{:S(2)}, u32[]{:S(2)}) collective-permute-start(bf16[192,256]{1,0:T(8,128)(2,1)} %own_ref.1), channel_id=1, source_target_pairs={{0,12},{1,13},{2,14},{3,15},{4,8},{5,9},{6,10},{7,11},{8,4},{9,5},... | collective-permute-start | bytes 294920 | tf_op jit(solution)/shard_map/ppermute | solution.py:278
  8.1 8.3 %collective-permute-start.4 = (bf16[512,256]{1,0:T(8,128)(2,1)}, bf16[512,256]{1,0:T(8,128)(2,1)S(1)}, u32[]{:S(2)}, u32[]{:S(2)}) collective-permute-start(bf16[512,256]{1,0:T(8,128)(2,1)} %code_ref.5), channel_id=1, source_target_pairs={{0,1},{1,0},{2,3},{3,2},{4,5},{5,4},{6,7},{7,6},{8,9},{9,8},{10,11... | collective-permute-start | bytes 786440 | tf_op jit(solution)/shard_map/ppermute | solution.py:278
  14.5 1.8 %collective-permute-start.5 = (bf16[512,256]{1,0:T(8,128)(2,1)S(1)}, bf16[512,256]{1,0:T(8,128)(2,1)S(1)}, u32[]{:S(2)}, u32[]{:S(2)}) collective-permute-start(bf16[512,256]{1,0:T(8,128)(2,1)S(1)} %collective-permute-done.refs_2_), channel_id=1, source_target_pairs={{0,1},{1,0},{2,3},{3,2},{4,5},{5,4},{6,7},{7,6},{8,9},{9,8},{10,11... | collective-permute-start | bytes 786440 | tf_op jit(solution)/shard_map/ppermute | solution.py:278
  14.5 0.9 %copy-start.1 = (bf16[192,256]{1,0:T(8,128)(2,1)S(1)}, bf16[192,256]{1,0:T(8,128)(2,1)}, u32[]{:S(2)}) copy-start(bf16[192,256]{1,0:T(8,128)(2,1)} %own_ref.1) | copy-start | bytes 294916
  15.4 1.0 %copy-start = (bf16[512,256]{1,0:T(8,128)(2,1)S(1)}, bf16[512,256]{1,0:T(8,128)(2,1)}, u32[]{:S(2)}) copy-start(bf16[512,256]{1,0:T(8,128)(2,1)} %code_ref.5) | copy-start | bytes 786436
  15.6 14.4 %collective-permute-start.6 = (bf16[768,256]{1,0:T(8,128)(2,1)S(1)}, bf16[768,256]{1,0:T(8,128)(2,1)S(1)}, u32[]{:S(2)}, u32[]{:S(2)}) collective-permute-start(bf16[768,256]{1,0:T(8,128)(2,1)S(1)} %stack.1.stacked_ref.refs_0_), channel_id=1, source_target_pairs={{0,2},{1,3},{2,0},{3,1},{4,6},{5,7},{6,4},{7,5},{8,10},{9,11},{10,... | collective-permute-start | bytes 1179656 | tf_op jit(solution)/shard_map/ppermute | solution.py:278
  16.1 20.4 %collective-permute-start.8 = (bf16[768,256]{1,0:T(8,128)(2,1)S(1)}, bf16[768,256]{1,0:T(8,128)(2,1)S(1)}, u32[]{:S(2)}, u32[]{:S(2)}) collective-permute-start(bf16[768,256]{1,0:T(8,128)(2,1)S(1)} %stack.1.stacked_ref.refs_0_), channel_id=1, source_target_pairs={{0,1},{1,0},{2,3},{3,2},{4,5},{5,4},{6,7},{7,6},{8,9},{9,8},{10,11... | collective-permute-start | bytes 1179656 | tf_op jit(solution)/shard_map/ppermute | solution.py:278
  20.0 16.5 %collective-permute-start.9 = (bf16[192,256]{1,0:T(8,128)(2,1)S(1)}, bf16[192,256]{1,0:T(8,128)(2,1)S(1)}, u32[]{:S(2)}, u32[]{:S(2)}) collective-permute-start(bf16[192,256]{1,0:T(8,128)(2,1)S(1)} %get-tuple-element.25), channel_id=1, source_target_pairs={{0,4},{1,5},{2,6},{3,7},{4,0},{5,1},{6,2},{7,3},{8,12},{9,13},{10,... | collective-permute-start | bytes 294920 | tf_op jit(solution)/shard_map/ppermute | solution.py:278
  21.7 14.8 %collective-permute-start.10 = (bf16[192,256]{1,0:T(8,128)(2,1)S(1)}, bf16[192,256]{1,0:T(8,128)(2,1)S(1)}, u32[]{:S(2)}, u32[]{:S(2)}) collective-permute-start(bf16[192,256]{1,0:T(8,128)(2,1)S(1)} %get-tuple-element.26), channel_id=1, source_target_pairs={{0,8},{1,9},{2,10},{3,11},{4,12},{5,13},{6,14},{7,15},{8,0},{9,1},... | collective-permute-start | bytes 294920 | tf_op jit(solution)/shard_map/ppermute | solution.py:278
  23.6 12.9 %collective-permute-start.11 = (bf16[192,256]{1,0:T(8,128)(2,1)S(1)}, bf16[192,256]{1,0:T(8,128)(2,1)S(1)}, u32[]{:S(2)}, u32[]{:S(2)}) collective-permute-start(bf16[192,256]{1,0:T(8,128)(2,1)S(1)} %get-tuple-element.27), channel_id=1, source_target_pairs={{0,12},{1,13},{2,14},{3,15},{4,8},{5,9},{6,10},{7,11},{8,4},{9,5},... | collective-permute-start | bytes 294920 | tf_op jit(solution)/shard_map/ppermute | solution.py:278
  25.0 11.5 %all-to-all-start = ((f32[16,1,768]{2,1,0:T(1,128)}), f32[16,1,768]{2,1,0:T(1,128)S(1)}, u32[]{:S(2)}, u32[]{:S(2)}) async-start(f32[16,1,768]{2,1,0:T(1,128)} %get-tuple-element.23), calls=%async_computation | async-start | bytes 98304 | tf_op jit(solution)/shard_map/all_to_all | solution.py:291
  29.9 8.9 %collective-permute-start.7 = (bf16[768,256]{1,0:T(8,128)(2,1)S(1)}, bf16[768,256]{1,0:T(8,128)(2,1)S(1)}, u32[]{:S(2)}, u32[]{:S(2)}) collective-permute-start(bf16[768,256]{1,0:T(8,128)(2,1)S(1)} %collective-permute-done.6.refs_2_), channel_id=1, source_target_pairs={{0,1},{1,0},{2,3},{3,2},{4,5},{5,4},{6,7},{7,6},{8,9},{9,8},{10,11... | collective-permute-start | bytes 1179656 | tf_op jit(solution)/shard_map/ppermute | solution.py:278

commit v4 on v3

v4 whole, which is shorter than its diff:
```python
import functools
import math

import jax
import jax.numpy as jnp
from jax import lax
from jax.experimental import pallas as pl
from jax.experimental.pallas import tpu as pltpu
from jax.sharding import PartitionSpec as P

AXIS = "blk"
LOG2E = math.log2(math.e)
LN2 = math.log(2.0)
VMEM_LIMIT = 20 * 1024 * 1024
EARLY = 64


def nt_dot(a, b):
    return lax.dot_general(a, b, (((1,), (1,)), ((), ())), preferred_element_type=jnp.float32)


def norm_column(code, scale):
    c = code.astype(jnp.float32)
    return (0.5 * scale) * jnp.sum(c * c, axis=1, keepdims=True)


def tiles(rows, tile, body):
    count = rows // tile
    if count <= 4:
        for t in range(count):
            body(t * tile, t * tile)
    else:
        pl.loop(0, count)(lambda t: body(pl.multiple_of(t * tile, tile), 0))


def keep_kernel(x_ref, out_ref):
    out_ref[...] = x_ref[...]


def keep(x):
    vmem = pl.BlockSpec(memory_space=pltpu.VMEM)
    return pl.pallas_call(
        keep_kernel,
        out_shape=jax.ShapeDtypeStruct(x.shape, x.dtype),
        in_specs=[vmem],
        out_specs=vmem,
        compiler_params=pltpu.CompilerParams(vmem_limit_bytes=VMEM_LIMIT),
        cost_estimate=pl.CostEstimate(flops=0, bytes_accessed=4 * x.size, transcendentals=0),
        name="keep",
    )(x)


def stack_kernel(inner, place_ref, *refs):
    blocks, out_ref = refs[:-1], refs[-1]
    rows_dev = blocks[0].shape[0]
    place = place_ref[0] // inner
    for j, block in enumerate(blocks):
        spot = pl.multiple_of((place ^ j) * rows_dev, rows_dev)
        out_ref[pl.ds(spot, rows_dev), :] = block[...]


def stack(place, blocks, inner):
    rows_dev, width = blocks[0].shape
    vmem = pl.BlockSpec(memory_space=pltpu.VMEM)
    return pl.pallas_call(
        functools.partial(stack_kernel, inner),
        out_shape=jax.ShapeDtypeStruct((len(blocks) * rows_dev, width), blocks[0].dtype),
        in_specs=[pl.BlockSpec(memory_space=pltpu.SMEM)] + [vmem] * len(blocks),
        out_specs=vmem,
        compiler_params=pltpu.CompilerParams(vmem_limit_bytes=VMEM_LIMIT),
        cost_estimate=pl.CostEstimate(
            flops=0, bytes_accessed=4 * len(blocks) * rows_dev * width, transcendentals=0
        ),
        name="stack",
    )(place, *blocks)


def fold_lanes(op, x, lanes):
    parts = [x[:, i : i + lanes] for i in range(0, x.shape[1], lanes)]
    return functools.reduce(op, parts)


def rows_kernel(outer, inner, tile, scale, place_ref, stacked_ref, *refs):
    code = refs[:inner]
    lam_ref = refs[inner]
    parts = refs[inner + 1 : inner + 1 + outer]
    scores, total = refs[inner + 1 + outer :]
    rows, width = stacked_ref.shape
    rows_dev = rows // outer
    k_dev = code[0].shape[0]
    lanes = math.gcd(k_dev, 128)
    place = place_ref[0] // inner
    norms = [
        jnp.broadcast_to(norm_column(code[k][...], scale), (k_dev, lanes)).T[:1, :]
        for k in range(inner)
    ]

    def one_tile(start, slot):
        rows_here = stacked_ref[pl.ds(start, tile), :]
        top = None
        for k in range(inner):
            s = scale * nt_dot(rows_here, code[k][...]) - norms[k]
            scores[slot : slot + tile, k * k_dev : (k + 1) * k_dev] = s
            m = fold_lanes(jnp.maximum, s, lanes)
            top = m if top is None else jnp.maximum(top, m)
        top = jnp.max(top, axis=1, keepdims=True)
        mass = jnp.zeros((tile, lanes), jnp.float32)
        acc = jnp.zeros((tile, width), jnp.float32)
        for k in range(inner):
            p = jnp.exp2(scores[slot : slot + tile, k * k_dev : (k + 1) * k_dev] - top)
            mass = mass + fold_lanes(jnp.add, p, lanes)
            acc = acc + jnp.dot(
                p.astype(jnp.bfloat16), code[k][...], preferred_element_type=jnp.float32
            )
        mass = jnp.sum(mass, axis=1, keepdims=True)
        lam = jnp.broadcast_to(LN2 * (top + jnp.log2(mass)), (tile, lanes)).T[:1, :]
        lam_ref[:, :, pl.ds(start, tile)] = jnp.broadcast_to(
            lam.reshape(1, 1, tile), (lam_ref.shape[0], 1, tile)
        )
        total[pl.ds(start, tile), :] = (acc * (1.0 / mass)).astype(jnp.bfloat16)

    tiles(rows, tile, one_tile)
    for j in range(outer):
        spot = pl.multiple_of((place ^ j) * rows_dev, rows_dev)
        parts[j][...] = total[pl.ds(spot, rows_dev), :]


def rows_calc(place, stacked, code, outer):
    inner = len(code)
    rows, width = stacked.shape
    rows_dev = rows // outer
    entries = inner * code[0].shape[0]
    tile = math.gcd(rows, 256)
    vmem = pl.BlockSpec(memory_space=pltpu.VMEM)
    out = pl.pallas_call(
        functools.partial(rows_kernel, outer, inner, tile, LOG2E * 3.0 / math.sqrt(width)),
        out_shape=[jax.ShapeDtypeStruct((outer * inner, 1, rows), jnp.float32)]
        + [jax.ShapeDtypeStruct((rows_dev, width), jnp.bfloat16)] * outer,
        in_specs=[pl.BlockSpec(memory_space=pltpu.SMEM)] + [vmem] * (1 + inner),
        out_specs=[vmem] * (outer + 1),
        scratch_shapes=[
            pltpu.VMEM((min(rows, 4 * tile), entries), jnp.float32),
            pltpu.VMEM((rows, width), jnp.bfloat16),
        ],
        compiler_params=pltpu.CompilerParams(vmem_limit_bytes=VMEM_LIMIT),
        cost_estimate=pl.CostEstimate(
            flops=4 * rows * entries * width,
            bytes_accessed=2 * (rows + entries) * width,
            transcendentals=rows * entries,
        ),
        name="rows_calc",
    )(place, stacked, *code)
    return out[0], out[1:]


def norm_kernel(scale, code_ref, out_ref):
    out_ref[...] = jnp.broadcast_to(norm_column(code_ref[...], scale), out_ref.shape)


def norm_calc(code, scale):
    k_dev, width = code.shape
    lanes = math.gcd(width, 128)
    vmem = pl.BlockSpec(memory_space=pltpu.VMEM)
    return pl.pallas_call(
        functools.partial(norm_kernel, scale),
        out_shape=jax.ShapeDtypeStruct((k_dev, lanes), jnp.float32),
        in_specs=[vmem],
        out_specs=vmem,
        compiler_params=pltpu.CompilerParams(vmem_limit_bytes=VMEM_LIMIT),
        cost_estimate=pl.CostEstimate(
            flops=2 * k_dev * width, bytes_accessed=2 * k_dev * width, transcendentals=0
        ),
        name="norm_calc",
    )(code)


def read_lse(lam_ref, outer, inner, spoke):
    each = [lam_ref[z * inner + spoke] for z in range(outer)]
    top = functools.reduce(jnp.maximum, each)
    return top + jnp.log(sum(jnp.exp(x - top) for x in each))


def add_groups(groups, tile, scale, levels, code_ref, norm_ref, emb, weighted, folded):
    lanes = folded.shape[1]
    code = code_ref[...]
    norm = jnp.concatenate([norm_ref[...]] * (tile // lanes), axis=1)
    for g, emb_ref in zip(groups, emb):
        level = LOG2E * levels(g)
        for start in range(0, emb_ref.shape[0], tile):
            rows_here = emb_ref[start : start + tile, :]
            s = scale * nt_dot(code, rows_here) - norm
            shares = jnp.exp2(s - level[:, start : start + tile]).astype(jnp.bfloat16)
            wide = shares.astype(jnp.float32)
            part = folded[...]
            for i in range(tile // lanes):
                part = part + wide[:, i * lanes : (i + 1) * lanes]
            folded[...] = part
            weighted[...] += jnp.dot(shares, rows_here, preferred_element_type=jnp.float32)


def early_kernel(outer, inner, groups, tile, scale, place_ref, lam_ref, code_ref, norm_ref, *refs):
    emb = refs[: len(groups)]
    weighted, folded = refs[len(groups) :]
    spoke = place_ref[0] % inner
    weighted[...] = jnp.zeros_like(weighted)
    folded[...] = jnp.zeros_like(folded)
    levels = lambda g: read_lse(lam_ref, outer, inner, spoke ^ g)
    add_groups(groups, tile, scale, levels, code_ref, norm_ref, emb, weighted, folded)


def late_kernel(outer, inner, groups, tile, scale, place_ref, lam_ref, code_ref, norm_ref, *refs):
    emb = refs[: len(groups)]
    weighted_in, folded_in, shift_ref, occ_ref, weighted, folded = refs[len(groups) :]
    k_dev = code_ref.shape[0]
    rows_dev = emb[0].shape[0] // outer
    spoke = place_ref[0] % inner
    weighted[...] = weighted_in[...]
    folded[...] = folded_in[...]
    levels = lambda g: read_lse(lam_ref, outer, inner, spoke ^ g)
    add_groups(groups, tile, scale, levels, code_ref, norm_ref, emb, weighted, folded)
    masses = jnp.sum(folded[...], axis=1, keepdims=True)
    prior = rows_dev / k_dev
    shift_ref[...] = (
        (weighted[...] - masses * code_ref[...].astype(jnp.float32)) / (masses + prior)
    ).astype(jnp.bfloat16)
    spread = jnp.broadcast_to(masses * (k_dev / rows_dev), folded.shape).T
    occ_ref[...] = spread[:1, :]


def columns_calc(place, lam, code, norm, groups, emb, inner, sums=()):
    k_dev, width = code.shape
    rows = emb[0].shape[0]
    outer = lam.shape[0] // inner
    tile = math.gcd(rows, 768)
    lanes = norm.shape[1]
    totals = [((k_dev, width), jnp.float32), ((k_dev, lanes), jnp.float32)]
    if sums:
        body, out = late_kernel, [((k_dev, width), jnp.bfloat16), ((1, k_dev), jnp.float32)]
        scratch = [pltpu.VMEM(*x) for x in totals]
    else:
        body, out, scratch = early_kernel, totals, []
    vmem = pl.BlockSpec(memory_space=pltpu.VMEM)
    return pl.pallas_call(
        functools.partial(body, outer, inner, groups, tile, LOG2E * 3.0 / math.sqrt(width)),
        out_shape=[jax.ShapeDtypeStruct(*x) for x in out],
        in_specs=[pl.BlockSpec(memory_space=pltpu.SMEM)] + [vmem] * (3 + len(emb) + len(sums)),
        out_specs=[vmem] * len(out),
        scratch_shapes=scratch,
        compiler_params=pltpu.CompilerParams(vmem_limit_bytes=VMEM_LIMIT),
        cost_estimate=pl.CostEstimate(
            flops=(4 if sums else EARLY) * len(emb) * rows * k_dev * width,
            bytes_accessed=2 * (len(emb) * rows + 2 * k_dev) * width,
            transcendentals=len(emb) * rows * k_dev,
        ),
        name="columns_calc",
    )(place, lam, code, norm, *emb, *sums)


def combine_kernel(outer, inner, place_ref, lam_ref, *refs):
    parts, (soft_ref, own_ref, columns) = refs[:outer], refs[outer:]
    rows_dev, width = parts[0].shape
    rows, lanes = columns.shape
    place, spoke = place_ref[0] // inner, place_ref[0] % inner
    spot = pl.multiple_of(place * rows_dev, rows_dev)
    mine = read_lse(lam_ref, outer, inner, spoke)

    def own_rows(line):
        columns[...] = jnp.broadcast_to(line, (lanes, rows)).T
        return columns[pl.ds(spot, rows_dev), :]

    total = jnp.zeros((rows_dev, width), jnp.float32)
    for j in range(outer):
        w = own_rows(jnp.exp(lam_ref[(place ^ j) * inner + spoke] - mine))
        w = jnp.concatenate([w] * (width // lanes), axis=1)
        total = total + w * parts[j][...].astype(jnp.float32)
    soft_ref[...] = total.astype(jnp.bfloat16)
    own_ref[...] = own_rows(mine).T[:1, :]


def combine(place, lam, parts):
    outer = len(parts)
    inner = lam.shape[0] // outer
    rows_dev, width = parts[0].shape
    lanes = math.gcd(width, 128)
    vmem = pl.BlockSpec(memory_space=pltpu.VMEM)
    return pl.pallas_call(
        functools.partial(combine_kernel, outer, inner),
        out_shape=[
            jax.ShapeDtypeStruct((rows_dev, width), jnp.bfloat16),
            jax.ShapeDtypeStruct((1, rows_dev), jnp.float32),
        ],
        in_specs=[pl.BlockSpec(memory_space=pltpu.SMEM)] + [vmem] * (outer + 1),
        out_specs=[vmem] * 2,
        scratch_shapes=[pltpu.VMEM((outer * rows_dev, lanes), jnp.float32)],
        compiler_params=pltpu.CompilerParams(vmem_limit_bytes=VMEM_LIMIT),
        cost_estimate=pl.CostEstimate(
            flops=2 * outer * rows_dev * width,
            bytes_accessed=2 * outer * rows_dev * width,
            transcendentals=0,
        ),
        name="combine",
    )(place, lam, *parts)


def after(x, y):
    return lax.optimization_barrier((x, y))[0]


def on_device(size, embeddings, codebook):
    inner = 4
    outer = size // inner
    place = lax.axis_index(AXIS).astype(jnp.int32).reshape(1)

    def swap(x, step):
        return lax.ppermute(x, AXIS, [(i, i ^ step) for i in range(size)])

    code_y = swap(codebook, 2)
    code_c = swap(codebook, 1)
    emb = [swap(embeddings, inner * j) for j in range(1, outer)]
    code_y, *emb = lax.optimization_barrier((code_y, keep(embeddings), *emb))
    stacked = stack(place, emb, inner)
    stacked_y = swap(stacked, 2)
    stacked_c = swap(stacked, 1)
    code = [codebook, code_c, code_y, swap(code_y, 1)]
    lam, parts = rows_calc(place, stacked, code, outer)

    order = sorted(range(1, outer), key=lambda j: j < 2)
    sent = {j: swap(parts[j], inner * j) for j in order}
    lam = lax.all_to_all(lam, AXIS, 0, 0)
    norm = norm_calc(codebook, LOG2E * 3.0 / math.sqrt(codebook.shape[1]))
    stacked_yc = swap(stacked_y, 1)
    sums = columns_calc(
        place, lam, codebook, norm, (0, 1, 2), [stacked, stacked_c, stacked_y], inner
    )
    shift, occupancy = columns_calc(
        place, lam, codebook, norm, (3,), [stacked_yc], inner, sums
    )
    parts = [after(parts[0], occupancy)] + [sent[j] for j in range(1, outer)]
    soft, own_lse = combine(place, lam, parts)
    return shift, occupancy.reshape(-1), soft, own_lse.reshape(-1)


def solution(mesh):
    specs = P(("groups", AXIS), None)
    flat = P(("groups", AXIS))
    return jax.shard_map(
        functools.partial(on_device, mesh.shape[AXIS]),
        mesh=mesh,
        in_specs=(specs, specs),
        out_specs=(specs, flat, specs, flat),
        check_vma=False,
    )
```

time: 40.6 us -> 40.4 us (level)
  starting transfers between devices: 18.4 us -> 16.7 us
  waiting for transfers between devices: 12.6 us -> 13.9 us
    ppermute x12, waiting for transfers between devices: 6.48 us -> 11.3 us  [swap(): return lax.ppermute(x, AXIS, [(i, i ^ step) for i in range(size)])]
    all_to_all x1, waiting for transfers between devices: 6.13 us -> 2.5 us  [on_device(): lam = lax.all_to_all(lam, AXIS, 0, 0)]
    pallas_call x0 -> x2, Pallas kernels: none -> 1.28 us  [the longest x1 1.27 us: combine(): pl.pallas_call(functools.partial(combine_kernel, outer, inner), out_shape...]
    ppermute x12, starting transfers between devices: 13.7 us -> 12.4 us  [swap(): return lax.ppermute(x, AXIS, [(i, i ^ step) for i in range(size)])]
    pallas_call x2, Pallas kernels: 3.8 us -> 3.01 us  [columns_calc(): pl.pallas_call(functools.partial(body, outer, inner, groups, tile, LOG2E...]
    all_to_all x1, starting transfers between devices: 4.77 us -> 4.27 us  [on_device(): lam = lax.all_to_all(lam, AXIS, 0, 0)]
  transfers between devices with their start and end apart: 13 -> 13, of which waited for: 3 -> 5; matrix products, arithmetic and copies ran while one was open for 0% -> 0% of each run, Pallas kernels for 15% -> 17%
where the time goes in v4:
time: 40.4 us; the launch traced here: 40.2 us
  starting transfers between devices  16.7 us (41%)
  waiting for transfers between devices  13.9 us (34%)
  Pallas kernels  8.03 us (20%)
  local copies, waits for them, and re-layouts  0.93 us (2%)
  between operations  0.68 us (2%)
    ppermute x12, starting transfers between devices, swap(): return lax.ppermute(x, AXIS, [(i, i ^ step) for i in range(size)])  12.4 us
    ppermute x12, waiting for transfers between devices, swap(): return lax.ppermute(x, AXIS, [(i, i ^ step) for i in range(size)])  11.3 us
    all_to_all x1, starting transfers between devices, on_device(): lam = lax.all_to_all(lam, AXIS, 0, 0)  4.27 us
    pallas_call x1, Pallas kernels, rows_calc(): pl.pallas_call(functools.partial(rows_kernel, outer, inner, tile, LOG2E *...  3.56 us
    pallas_call x2, Pallas kernels, columns_calc(): pl.pallas_call(functools.partial(body, outer, inner, groups, tile, LOG2E...  3.01 us
    all_to_all x1, waiting for transfers between devices, on_device(): lam = lax.all_to_all(lam, AXIS, 0, 0)  2.5 us
    pallas_call x1, Pallas kernels, combine(): pl.pallas_call(functools.partial(combine_kernel, outer, inner), out_shape...  1.27 us
    unnamed x4, local copies, waits for them, and re-layouts  0.93 us
  transfers between devices with their start and end apart: 13, of which 5 were waited for; matrix products, arithmetic and copies ran while one was open for 0% of the time, Pallas kernels for 17%

profile of v4, /device:TPU:0, one launch (start us, length us, event | category | flops | bytes accessed | tf_op | source)
XLA Modules:
  0.0 40.2 jit_solution(3325473510586990243)
XLA Ops:
  0.6 3.0 %collective-permute-start = (bf16[512,256]{1,0:T(8,128)(2,1)}, bf16[512,256]{1,0:T(8,128)(2,1)S(1)}, u32[]{:S(2)}, u32[]{:S(2)}) collective-permute-start(bf16[512,256]{1,0:T(8,128)(2,1)} %code_ref.5), channel_id=1, source_target_pairs={{0,2},{1,3},{2,0},{3,1},{4,6},{5,7},{6,4},{7,5},{8,10},{9,11},{10,... | collective-permute-start | bytes 786440 | tf_op jit(solution)/shard_map/ppermute | solution.py:315
  3.7 1.6 %collective-permute-start.1 = (bf16[192,256]{1,0:T(8,128)(2,1)}, bf16[192,256]{1,0:T(8,128)(2,1)S(1)}, u32[]{:S(2)}, u32[]{:S(2)}) collective-permute-start(bf16[192,256]{1,0:T(8,128)(2,1)} %x_ref.1), channel_id=1, source_target_pairs={{0,4},{1,5},{2,6},{3,7},{4,0},{5,1},{6,2},{7,3},{8,12},{9,13},{10,... | collective-permute-start | bytes 294920 | tf_op jit(solution)/shard_map/ppermute | solution.py:315
  5.2 2.5 %collective-permute-start.3 = (bf16[192,256]{1,0:T(8,128)(2,1)}, bf16[192,256]{1,0:T(8,128)(2,1)S(1)}, u32[]{:S(2)}, u32[]{:S(2)}) collective-permute-start(bf16[192,256]{1,0:T(8,128)(2,1)} %x_ref.1), channel_id=1, source_target_pairs={{0,12},{1,13},{2,14},{3,15},{4,8},{5,9},{6,10},{7,11},{8,4},{9,5},... | collective-permute-start | bytes 294920 | tf_op jit(solution)/shard_map/ppermute | solution.py:315
  7.7 0.1 collective-permute-start.2
  7.8 0.9 %copy-done.1 = bf16[192,256]{1,0:T(8,128)(2,1)S(1)} copy-done((bf16[192,256]{1,0:T(8,128)(2,1)S(1)}, bf16[192,256]{1,0:T(8,128)(2,1)}, u32[]{:S(2)}) %copy-start.1) | copy-done | bytes 98328
  8.8 0.0 collective-permute-done.1.refs_1_
  8.8 4.6 %collective-permute-done.3.refs_3_ = bf16[192,256]{1,0:T(8,128)(2,1)S(1)} collective-permute-done((bf16[192,256]{1,0:T(8,128)(2,1)}, bf16[192,256]{1,0:T(8,128)(2,1)S(1)}, u32[]{:S(2)}, u32[]{:S(2)}) %collective-permute-start.3) | collective-permute-done | bytes 98336 | tf_op jit(solution)/shard_map/ppermute | solution.py:315
  13.3 3.3 %collective-permute-done.2.refs_2_ = bf16[192,256]{1,0:T(8,128)(2,1)S(1)} collective-permute-done((bf16[192,256]{1,0:T(8,128)(2,1)}, bf16[192,256]{1,0:T(8,128)(2,1)S(1)}, u32[]{:S(2)}, u32[]{:S(2)}) %collective-permute-start.2) | collective-permute-done | bytes 98336 | tf_op jit(solution)/shard_map/ppermute | solution.py:315
  16.6 0.0 collective-permute-start.5
  16.7 0.6 %collective-permute-start.6 = (bf16[768,256]{1,0:T(8,128)(2,1)S(1)}, bf16[768,256]{1,0:T(8,128)(2,1)S(1)}, u32[]{:S(2)}, u32[]{:S(2)}) collective-permute-start(bf16[768,256]{1,0:T(8,128)(2,1)S(1)} %stack.1.stacked_ref.refs_0_), channel_id=1, source_target_pairs={{0,2},{1,3},{2,0},{3,1},{4,6},{5,7},{6,4},{7,5},{8,10},{9,11},{10,... | collective-permute-start | bytes 1179656 | tf_op jit(solution)/shard_map/ppermute | solution.py:315
  17.3 0.2 collective-permute-start.8
  17.5 0.0 collective-permute-done.4.refs_1_
  17.5 0.7 %collective-permute-done.5.refs_3_ = bf16[512,256]{1,0:T(8,128)(2,1)S(1)} collective-permute-done((bf16[512,256]{1,0:T(8,128)(2,1)S(1)}, bf16[512,256]{1,0:T(8,128)(2,1)S(1)}, u32[]{:S(2)}, u32[]{:S(2)}) %collective-permute-start.5) | collective-permute-done | bytes 262176 | tf_op jit(solution)/shard_map/ppermute | solution.py:315
  18.2 3.6 %rows_calc.1 = (f32[16,1,768]{2,1,0:T(1,128)}, bf16[192,256]{1,0:T(8,128)(2,1)S(1)}, bf16[192,256]{1,0:T(8,128)(2,1)S(1)}, bf16[192,256]{1,0:T(8,128)(2,1)S(1)}, bf16[192,256]{1,0:T(8,128)(2,1)S(1)}) custom-call(s32[1]{0:T(128)} %bitcast.place_ref, bf16[768,256]{1,0:T(8,128)(2,1)S(1)} %stack.1.stacked_ref.refs_0_, bf16[512,256]{1,0:T(8,128)(2,1)S(1)} %copy-done, ...), custom_call_target="tpu_custom_call" | custom-call | flops 1610612736 | bytes 1441792 | tf_op jit(solution)/shard_map/rows_calc/pallas_call | solution.py:135
  21.7 4.3 %all-to-all-start = ((f32[16,1,768]{2,1,0:T(1,128)}), f32[16,1,768]{2,1,0:T(1,128)S(1)}, u32[]{:S(2)}, u32[]{:S(2)}) async-start(f32[16,1,768]{2,1,0:T(1,128)} %get-tuple-element.26), calls=%async_computation | async-start | bytes 98304 | tf_op jit(solution)/shard_map/all_to_all | solution.py:329
  26.0 0.1 norm_calc.1.norm_ref
  26.2 2.0 %collective-permute-start.9 = (bf16[192,256]{1,0:T(8,128)(2,1)S(1)}, bf16[192,256]{1,0:T(8,128)(2,1)S(1)}, u32[]{:S(2)}, u32[]{:S(2)}) collective-permute-start(bf16[192,256]{1,0:T(8,128)(2,1)S(1)} %get-tuple-element.33), channel_id=1, source_target_pairs={{0,4},{1,5},{2,6},{3,7},{4,0},{5,1},{6,2},{7,3},{8,12},{9,13},{10,... | collective-permute-start | bytes 294920 | tf_op jit(solution)/shard_map/ppermute | solution.py:315
  28.1 2.4 %collective-permute-start.10 = (bf16[192,256]{1,0:T(8,128)(2,1)S(1)}, bf16[192,256]{1,0:T(8,128)(2,1)S(1)}, u32[]{:S(2)}, u32[]{:S(2)}) collective-permute-start(bf16[192,256]{1,0:T(8,128)(2,1)S(1)} %get-tuple-element.34), channel_id=1, source_target_pairs={{0,8},{1,9},{2,10},{3,11},{4,12},{5,13},{6,14},{7,15},{8,0},{9,1},... | collective-permute-start | bytes 294920 | tf_op jit(solution)/shard_map/ppermute | solution.py:315
  30.5 0.1 collective-permute-start.11
  30.6 2.5 %all-to-all-done.lam_ref = f32[16,1,768]{2,1,0:T(1,128)S(1)} async-done(((f32[16,1,768]{2,1,0:T(1,128)}), f32[16,1,768]{2,1,0:T(1,128)S(1)}, u32[]{:S(2)}, u32[]{:S(2)}) %all-to-all-start) | async-done | bytes 49184 | tf_op jit(solution)/shard_map/all_to_all | solution.py:329
  33.1 1.5 %columns_calc.2 = (f32[512,256]{1,0:T(8,128)S(1)}, f32[512,128]{1,0:T(8,128)S(1)}) custom-call(s32[1]{0:T(128)} %bitcast.place_ref, f32[16,1,768]{2,1,0:T(1,128)S(1)} %all-to-all-done.lam_ref, bf16[512,256]{1,0:T(8,128)(2,1)S(1)} %copy-done, f32[512,128]{1,0:T(8,128)S(1)} %norm_calc.1.norm_ref, bf16[768,256]{1,0:T(8,128)(2,1)S(1)} %stack.1.stacked_ref.refs_0_, ...), custom_call_target="tpu_custom_call" | custom-call | flops 19327352832 | bytes 1703936 | tf_op jit(solution)/shard_map/columns_calc/pallas_call | solution.py:243
  34.7 1.5 %columns_calc.3 = (bf16[512,256]{1,0:T(8,128)(2,1)}, f32[1,512]{1,0:T(1,128)}) custom-call(s32[1]{0:T(128)} %bitcast.place_ref, f32[16,1,768]{2,1,0:T(1,128)S(1)} %all-to-all-done.lam_ref, bf16[512,256]{1,0:T(8,128)(2,1)S(1)} %copy-done, f32[512,128]{1,0:T(8,128)S(1)} %norm_calc.1.norm_ref, bf16[768,256]{1,0:T(8,128)(2,1)S(1)} %collective-permute-done.7.refs_0_, ...), custom_call_target="tpu_custom_call" | custom-call | flops 402653184 | bytes 917504 | tf_op jit(solution)/shard_map/columns_calc/pallas_call | solution.py:243
  36.1 2.8 %collective-permute-done.10.refs_2_ = bf16[192,256]{1,0:T(8,128)(2,1)S(1)} collective-permute-done((bf16[192,256]{1,0:T(8,128)(2,1)S(1)}, bf16[192,256]{1,0:T(8,128)(2,1)S(1)}, u32[]{:S(2)}, u32[]{:S(2)}) %collective-permute-start.10) | collective-permute-done | bytes 98336 | tf_op jit(solution)/shard_map/ppermute | solution.py:315
  38.9 1.3 %combine.1 = (bf16[192,256]{1,0:T(8,128)(2,1)}, f32[1,192]{1,0:T(1,128)}) custom-call(s32[1]{0:T(128)} %bitcast.place_ref, f32[16,1,768]{2,1,0:T(1,128)S(1)} %all-to-all-done.lam_ref, bf16[192,256]{1,0:T(8,128)(2,1)S(1)} %get-tuple-element.32.refs_0_, bf16[192,256]{1,0:T(8,128)(2,1)S(1)} %collective-permute-done.9.refs_1_, ...), custom_call_target="tpu_custom_call" | custom-call | flops 393216 | bytes 393216 | tf_op jit(solution)/shard_map/combine/pallas_call | solution.py:286
  (13 shorter events, 0.1 us)
Async XLA Ops:
  0.6 16.0 %collective-permute-start = (bf16[512,256]{1,0:T(8,128)(2,1)}, bf16[512,256]{1,0:T(8,128)(2,1)S(1)}, u32[]{:S(2)}, u32[]{:S(2)}) collective-permute-start(bf16[512,256]{1,0:T(8,128)(2,1)} %code_ref.5), channel_id=1, source_target_pairs={{0,2},{1,3},{2,0},{3,1},{4,6},{5,7},{6,4},{7,5},{8,10},{9,11},{10,... | collective-permute-start | bytes 786440 | tf_op jit(solution)/shard_map/ppermute | solution.py:315
  3.7 5.1 %collective-permute-start.1 = (bf16[192,256]{1,0:T(8,128)(2,1)}, bf16[192,256]{1,0:T(8,128)(2,1)S(1)}, u32[]{:S(2)}, u32[]{:S(2)}) collective-permute-start(bf16[192,256]{1,0:T(8,128)(2,1)} %x_ref.1), channel_id=1, source_target_pairs={{0,4},{1,5},{2,6},{3,7},{4,0},{5,1},{6,2},{7,3},{8,12},{9,13},{10,... | collective-permute-start | bytes 294920 | tf_op jit(solution)/shard_map/ppermute | solution.py:315
  5.2 8.1 %collective-permute-start.3 = (bf16[192,256]{1,0:T(8,128)(2,1)}, bf16[192,256]{1,0:T(8,128)(2,1)S(1)}, u32[]{:S(2)}, u32[]{:S(2)}) collective-permute-start(bf16[192,256]{1,0:T(8,128)(2,1)} %x_ref.1), channel_id=1, source_target_pairs={{0,12},{1,13},{2,14},{3,15},{4,8},{5,9},{6,10},{7,11},{8,4},{9,5},... | collective-permute-start | bytes 294920 | tf_op jit(solution)/shard_map/ppermute | solution.py:315
  7.7 8.9 %collective-permute-start.2 = (bf16[192,256]{1,0:T(8,128)(2,1)}, bf16[192,256]{1,0:T(8,128)(2,1)S(1)}, u32[]{:S(2)}, u32[]{:S(2)}) collective-permute-start(bf16[192,256]{1,0:T(8,128)(2,1)} %x_ref.1), channel_id=1, source_target_pairs={{0,8},{1,9},{2,10},{3,11},{4,12},{5,13},{6,14},{7,15},{8,0},{9,1},... | collective-permute-start | bytes 294920 | tf_op jit(solution)/shard_map/ppermute | solution.py:315
  7.8 9.6 %collective-permute-start.4 = (bf16[512,256]{1,0:T(8,128)(2,1)}, bf16[512,256]{1,0:T(8,128)(2,1)S(1)}, u32[]{:S(2)}, u32[]{:S(2)}) collective-permute-start(bf16[512,256]{1,0:T(8,128)(2,1)} %code_ref.5), channel_id=1, source_target_pairs={{0,1},{1,0},{2,3},{3,2},{4,5},{5,4},{6,7},{7,6},{8,9},{9,8},{10,11... | collective-permute-start | bytes 786440 | tf_op jit(solution)/shard_map/ppermute | solution.py:315
  7.8 0.9 %copy-start.1 = (bf16[192,256]{1,0:T(8,128)(2,1)S(1)}, bf16[192,256]{1,0:T(8,128)(2,1)}, u32[]{:S(2)}) copy-start(bf16[192,256]{1,0:T(8,128)(2,1)} %x_ref.1) | copy-start | bytes 294916
  16.6 1.5 %collective-permute-start.5 = (bf16[512,256]{1,0:T(8,128)(2,1)S(1)}, bf16[512,256]{1,0:T(8,128)(2,1)S(1)}, u32[]{:S(2)}, u32[]{:S(2)}) collective-permute-start(bf16[512,256]{1,0:T(8,128)(2,1)S(1)} %collective-permute-done.refs_2_), channel_id=1, source_target_pairs={{0,1},{1,0},{2,3},{3,2},{4,5},{5,4},{6,7},{7,6},{8,9},{9,8},{10,11... | collective-permute-start | bytes 786440 | tf_op jit(solution)/shard_map/ppermute | solution.py:315
  16.6 1.5 %copy-start = (bf16[512,256]{1,0:T(8,128)(2,1)S(1)}, bf16[512,256]{1,0:T(8,128)(2,1)}, u32[]{:S(2)}) copy-start(bf16[512,256]{1,0:T(8,128)(2,1)} %code_ref.5) | copy-start | bytes 786436
  16.7 13.9 %collective-permute-start.6 = (bf16[768,256]{1,0:T(8,128)(2,1)S(1)}, bf16[768,256]{1,0:T(8,128)(2,1)S(1)}, u32[]{:S(2)}, u32[]{:S(2)}) collective-permute-start(bf16[768,256]{1,0:T(8,128)(2,1)S(1)} %stack.1.stacked_ref.refs_0_), channel_id=1, source_target_pairs={{0,2},{1,3},{2,0},{3,1},{4,6},{5,7},{6,4},{7,5},{8,10},{9,11},{10,... | collective-permute-start | bytes 1179656 | tf_op jit(solution)/shard_map/ppermute | solution.py:315
  17.3 15.9 %collective-permute-start.8 = (bf16[768,256]{1,0:T(8,128)(2,1)S(1)}, bf16[768,256]{1,0:T(8,128)(2,1)S(1)}, u32[]{:S(2)}, u32[]{:S(2)}) collective-permute-start(bf16[768,256]{1,0:T(8,128)(2,1)S(1)} %stack.1.stacked_ref.refs_0_), channel_id=1, source_target_pairs={{0,1},{1,0},{2,3},{3,2},{4,5},{5,4},{6,7},{7,6},{8,9},{9,8},{10,11... | collective-permute-start | bytes 1179656 | tf_op jit(solution)/shard_map/ppermute | solution.py:315
  21.7 11.4 %all-to-all-start = ((f32[16,1,768]{2,1,0:T(1,128)}), f32[16,1,768]{2,1,0:T(1,128)S(1)}, u32[]{:S(2)}, u32[]{:S(2)}) async-start(f32[16,1,768]{2,1,0:T(1,128)} %get-tuple-element.26), calls=%async_computation | async-start | bytes 98304 | tf_op jit(solution)/shard_map/all_to_all | solution.py:329
  26.2 10.0 %collective-permute-start.9 = (bf16[192,256]{1,0:T(8,128)(2,1)S(1)}, bf16[192,256]{1,0:T(8,128)(2,1)S(1)}, u32[]{:S(2)}, u32[]{:S(2)}) collective-permute-start(bf16[192,256]{1,0:T(8,128)(2,1)S(1)} %get-tuple-element.33), channel_id=1, source_target_pairs={{0,4},{1,5},{2,6},{3,7},{4,0},{5,1},{6,2},{7,3},{8,12},{9,13},{10,... | collective-permute-start | bytes 294920 | tf_op jit(solution)/shard_map/ppermute | solution.py:315
  28.1 10.8 %collective-permute-start.10 = (bf16[192,256]{1,0:T(8,128)(2,1)S(1)}, bf16[192,256]{1,0:T(8,128)(2,1)S(1)}, u32[]{:S(2)}, u32[]{:S(2)}) collective-permute-start(bf16[192,256]{1,0:T(8,128)(2,1)S(1)} %get-tuple-element.34), channel_id=1, source_target_pairs={{0,8},{1,9},{2,10},{3,11},{4,12},{5,13},{6,14},{7,15},{8,0},{9,1},... | collective-permute-start | bytes 294920 | tf_op jit(solution)/shard_map/ppermute | solution.py:315
  30.5 8.4 %collective-permute-start.11 = (bf16[192,256]{1,0:T(8,128)(2,1)S(1)}, bf16[192,256]{1,0:T(8,128)(2,1)S(1)}, u32[]{:S(2)}, u32[]{:S(2)}) collective-permute-start(bf16[192,256]{1,0:T(8,128)(2,1)S(1)} %get-tuple-element.35), channel_id=1, source_target_pairs={{0,12},{1,13},{2,14},{3,15},{4,8},{5,9},{6,10},{7,11},{8,4},{9,5},... | collective-permute-start | bytes 294920 | tf_op jit(solution)/shard_map/ppermute | solution.py:315
  30.6 4.1 %collective-permute-start.7 = (bf16[768,256]{1,0:T(8,128)(2,1)S(1)}, bf16[768,256]{1,0:T(8,128)(2,1)S(1)}, u32[]{:S(2)}, u32[]{:S(2)}) collective-permute-start(bf16[768,256]{1,0:T(8,128)(2,1)S(1)} %collective-permute-done.6.refs_2_), channel_id=1, source_target_pairs={{0,1},{1,0},{2,3},{3,2},{4,5},{5,4},{6,7},{7,6},{8,9},{9,8},{10,11... | collective-permute-start | bytes 1179656 | tf_op jit(solution)/shard_map/ppermute | solution.py:315

commit v5 on v4

--- a/solution.py
+++ b/solution.py
@@ -13,6 +13,7 @@
 LN2 = math.log(2.0)
 VMEM_LIMIT = 20 * 1024 * 1024
 EARLY = 64
+STACK = 1 << 32
 
 
 def nt_dot(a, b):
@@ -50,29 +51,29 @@
     )(x)
 
 
-def stack_kernel(inner, place_ref, *refs):
-    blocks, out_ref = refs[:-1], refs[-1]
+def stack_kernel(inner, steps, place_ref, *refs):
+    blocks, out_ref = refs[: len(steps)], refs[-1]
     rows_dev = blocks[0].shape[0]
     place = place_ref[0] // inner
-    for j, block in enumerate(blocks):
+    for j, block in zip(steps, blocks):
         spot = pl.multiple_of((place ^ j) * rows_dev, rows_dev)
         out_ref[pl.ds(spot, rows_dev), :] = block[...]
 
 
-def stack(place, blocks, inner):
-    rows_dev, width = blocks[0].shape
-    vmem = pl.BlockSpec(memory_space=pltpu.VMEM)
-    return pl.pallas_call(
-        functools.partial(stack_kernel, inner),
-        out_shape=jax.ShapeDtypeStruct((len(blocks) * rows_dev, width), blocks[0].dtype),
-        in_specs=[pl.BlockSpec(memory_space=pltpu.SMEM)] + [vmem] * len(blocks),
+def stack(place, blocks, steps, inner, shape, into=()):
+    vmem = pl.BlockSpec(memory_space=pltpu.VMEM)
+    return pl.pallas_call(
+        functools.partial(stack_kernel, inner, steps),
+        out_shape=jax.ShapeDtypeStruct(shape, blocks[0].dtype),
+        in_specs=[pl.BlockSpec(memory_space=pltpu.SMEM)] + [vmem] * (len(blocks) + len(into)),
         out_specs=vmem,
-        compiler_params=pltpu.CompilerParams(vmem_limit_bytes=VMEM_LIMIT),
-        cost_estimate=pl.CostEstimate(
-            flops=0, bytes_accessed=4 * len(blocks) * rows_dev * width, transcendentals=0
+        input_output_aliases={1 + len(blocks): 0} if into else {},
+        compiler_params=pltpu.CompilerParams(vmem_limit_bytes=VMEM_LIMIT),
+        cost_estimate=pl.CostEstimate(
+            flops=0 if into else STACK, bytes_accessed=4 * shape[0] * shape[1], transcendentals=0
         ),
         name="stack",
-    )(place, *blocks)
+    )(place, *blocks, *into)
 
 
 def fold_lanes(op, x, lanes):
@@ -256,7 +257,7 @@
     )(place, lam, code, norm, *emb, *sums)
 
 
-def combine_kernel(outer, inner, place_ref, lam_ref, *refs):
+def combine_kernel(outer, inner, order, place_ref, lam_ref, *refs):
     parts, (soft_ref, own_ref, columns) = refs[:outer], refs[outer:]
     rows_dev, width = parts[0].shape
     rows, lanes = columns.shape
@@ -269,22 +270,22 @@
         return columns[pl.ds(spot, rows_dev), :]
 
     total = jnp.zeros((rows_dev, width), jnp.float32)
-    for j in range(outer):
+    for j, part in zip(order, parts):
         w = own_rows(jnp.exp(lam_ref[(place ^ j) * inner + spoke] - mine))
         w = jnp.concatenate([w] * (width // lanes), axis=1)
-        total = total + w * parts[j][...].astype(jnp.float32)
+        total = total + w * part[...].astype(jnp.float32)
     soft_ref[...] = total.astype(jnp.bfloat16)
     own_ref[...] = own_rows(mine).T[:1, :]
 
 
-def combine(place, lam, parts):
+def combine(place, lam, parts, order):
     outer = len(parts)
     inner = lam.shape[0] // outer
     rows_dev, width = parts[0].shape
     lanes = math.gcd(width, 128)
     vmem = pl.BlockSpec(memory_space=pltpu.VMEM)
     return pl.pallas_call(
-        functools.partial(combine_kernel, outer, inner),
+        functools.partial(combine_kernel, outer, inner, order),
         out_shape=[
             jax.ShapeDtypeStruct((rows_dev, width), jnp.bfloat16),
             jax.ShapeDtypeStruct((1, rows_dev), jnp.float32),
@@ -317,15 +318,18 @@
     code_y = swap(codebook, 2)
     code_c = swap(codebook, 1)
     emb = [swap(embeddings, inner * j) for j in range(1, outer)]
-    code_y, *emb = lax.optimization_barrier((code_y, keep(embeddings), *emb))
-    stacked = stack(place, emb, inner)
+    shape = (outer * embeddings.shape[0], embeddings.shape[1])
+    steps = (0,) + tuple(range(2, outer))
+    far = stack(place, [keep(embeddings)] + emb[1:], steps, inner, shape)
+    code_y, near, far = lax.optimization_barrier((code_y, emb[0], far))
+    stacked = stack(place, [near], (1,), inner, shape, (far,))
     stacked_y = swap(stacked, 2)
     stacked_c = swap(stacked, 1)
     code = [codebook, code_c, code_y, swap(code_y, 1)]
     lam, parts = rows_calc(place, stacked, code, outer)
 
-    order = sorted(range(1, outer), key=lambda j: j < 2)
-    sent = {j: swap(parts[j], inner * j) for j in order}
+    order = (*range(2, outer), 1, 0)
+    sent = [swap(parts[j], inner * j) for j in order[:-1]]
     lam = lax.all_to_all(lam, AXIS, 0, 0)
     norm = norm_calc(codebook, LOG2E * 3.0 / math.sqrt(codebook.shape[1]))
     stacked_yc = swap(stacked_y, 1)
@@ -335,8 +339,7 @@
     shift, occupancy = columns_calc(
         place, lam, codebook, norm, (3,), [stacked_yc], inner, sums
     )
-    parts = [after(parts[0], occupancy)] + [sent[j] for j in range(1, outer)]
-    soft, own_lse = combine(place, lam, parts)
+    soft, own_lse = combine(place, lam, sent + [after(parts[0], occupancy)], order)
     return shift, occupancy.reshape(-1), soft, own_lse.reshape(-1)
 
 

time: 40.4 us -> 40.4 us (level)
  waiting for transfers between devices: 13.9 us -> 11.1 us
  starting transfers between devices: 16.7 us -> 19.4 us
    ppermute x12, waiting for transfers between devices: 11.3 us -> 8.57 us  [swap(): return lax.ppermute(x, AXIS, [(i, i ^ step) for i in range(size)])]
    all_to_all x1, starting transfers between devices: 4.27 us -> 5.63 us  [on_device(): lam = lax.all_to_all(lam, AXIS, 0, 0)]
    ppermute x12, starting transfers between devices: 12.4 us -> 13.7 us  [swap(): return lax.ppermute(x, AXIS, [(i, i ^ step) for i in range(size)])]
    pallas_call x2 -> x3, Pallas kernels: 1.31 us -> 1.31 us  [the longest x1 1.27 us: combine(): pl.pallas_call(functools.partial(combine_kernel, outer, inner, order), ou...]
  transfers between devices with their start and end apart: 13 -> 13, of which waited for: 5 -> 6; matrix products, arithmetic and copies ran while one was open for 0% -> 0% of each run, Pallas kernels for 17% -> 17%
where the time goes in v5:
time: 40.4 us; the launch traced here: 40.2 us
  starting transfers between devices  19.4 us (48%)
  waiting for transfers between devices  11.1 us (27%)
  Pallas kernels  8.09 us (20%)
  local copies, waits for them, and re-layouts  0.9 us (2%)
  between operations  0.7 us (2%)
    ppermute x12, starting transfers between devices, swap(): return lax.ppermute(x, AXIS, [(i, i ^ step) for i in range(size)])  13.7 us
    ppermute x12, waiting for transfers between devices, swap(): return lax.ppermute(x, AXIS, [(i, i ^ step) for i in range(size)])  8.57 us
    all_to_all x1, starting transfers between devices, on_device(): lam = lax.all_to_all(lam, AXIS, 0, 0)  5.63 us
    pallas_call x1, Pallas kernels, rows_calc(): pl.pallas_call(functools.partial(rows_kernel, outer, inner, tile, LOG2E *...  3.62 us
    pallas_call x2, Pallas kernels, columns_calc(): pl.pallas_call(functools.partial(body, outer, inner, groups, tile, LOG2E...  3.01 us
    all_to_all x1, waiting for transfers between devices, on_device(): lam = lax.all_to_all(lam, AXIS, 0, 0)  2.58 us
    pallas_call x1, Pallas kernels, combine(): pl.pallas_call(functools.partial(combine_kernel, outer, inner, order), ou...  1.27 us
    unnamed x4, local copies, waits for them, and re-layouts  0.9 us
  transfers between devices with their start and end apart: 13, of which 6 were waited for; matrix products, arithmetic and copies ran while one was open for 0% of the time, Pallas kernels for 17%

profile of v5, /device:TPU:0, one launch (start us, length us, event | category | flops | bytes accessed | tf_op | source)
XLA Modules:
  0.0 40.2 jit_solution(15649072817491184376)
XLA Ops:
  0.6 5.1 %collective-permute-start.3 = (bf16[192,256]{1,0:T(8,128)(2,1)}, bf16[192,256]{1,0:T(8,128)(2,1)S(1)}, u32[]{:S(2)}, u32[]{:S(2)}) collective-permute-start(bf16[192,256]{1,0:T(8,128)(2,1)} %x_ref.1), channel_id=1, source_target_pairs={{0,12},{1,13},{2,14},{3,15},{4,8},{5,9},{6,10},{7,11},{8,4},{9,5},... | collective-permute-start | bytes 294920 | tf_op jit(solution)/shard_map/ppermute | solution.py:316
  5.7 0.0 collective-permute-start.2
  5.7 0.6 %collective-permute-start.1 = (bf16[192,256]{1,0:T(8,128)(2,1)}, bf16[192,256]{1,0:T(8,128)(2,1)S(1)}, u32[]{:S(2)}, u32[]{:S(2)}) collective-permute-start(bf16[192,256]{1,0:T(8,128)(2,1)} %x_ref.1), channel_id=1, source_target_pairs={{0,4},{1,5},{2,6},{3,7},{4,0},{5,1},{6,2},{7,3},{8,12},{9,13},{10,... | collective-permute-start | bytes 294920 | tf_op jit(solution)/shard_map/ppermute | solution.py:316
  6.4 1.7 %collective-permute-start = (bf16[512,256]{1,0:T(8,128)(2,1)}, bf16[512,256]{1,0:T(8,128)(2,1)S(1)}, u32[]{:S(2)}, u32[]{:S(2)}) collective-permute-start(bf16[512,256]{1,0:T(8,128)(2,1)} %code_ref.5), channel_id=1, source_target_pairs={{0,2},{1,3},{2,0},{3,1},{4,6},{5,7},{6,4},{7,5},{8,10},{9,11},{10,... | collective-permute-start | bytes 786440 | tf_op jit(solution)/shard_map/ppermute | solution.py:316
  8.1 0.9 %copy-done.1 = bf16[192,256]{1,0:T(8,128)(2,1)S(1)} copy-done((bf16[192,256]{1,0:T(8,128)(2,1)S(1)}, bf16[192,256]{1,0:T(8,128)(2,1)}, u32[]{:S(2)}) %copy-start.1) | copy-done | bytes 98328
  9.0 0.7 %collective-permute-done.3.refs_2_ = bf16[192,256]{1,0:T(8,128)(2,1)S(1)} collective-permute-done((bf16[192,256]{1,0:T(8,128)(2,1)}, bf16[192,256]{1,0:T(8,128)(2,1)S(1)}, u32[]{:S(2)}, u32[]{:S(2)}) %collective-permute-start.3) | collective-permute-done | bytes 98336 | tf_op jit(solution)/shard_map/ppermute | solution.py:316
  9.7 4.6 %collective-permute-done.2.refs_1_ = bf16[192,256]{1,0:T(8,128)(2,1)S(1)} collective-permute-done((bf16[192,256]{1,0:T(8,128)(2,1)}, bf16[192,256]{1,0:T(8,128)(2,1)S(1)}, u32[]{:S(2)}, u32[]{:S(2)}) %collective-permute-start.2) | collective-permute-done | bytes 98336 | tf_op jit(solution)/shard_map/ppermute | solution.py:316
  14.3 0.0 copy-start
  14.3 1.0 %collective-permute-done.refs_2_ = bf16[512,256]{1,0:T(8,128)(2,1)S(1)} collective-permute-done((bf16[512,256]{1,0:T(8,128)(2,1)}, bf16[512,256]{1,0:T(8,128)(2,1)S(1)}, u32[]{:S(2)}, u32[]{:S(2)}) %collective-permute-start) | collective-permute-done | bytes 262176 | tf_op jit(solution)/shard_map/ppermute | solution.py:316
  15.3 0.0 collective-permute-start.5
  15.3 1.7 %collective-permute-start.6 = (bf16[768,256]{1,0:T(8,128)(2,1)S(1)}, bf16[768,256]{1,0:T(8,128)(2,1)S(1)}, u32[]{:S(2)}, u32[]{:S(2)}) collective-permute-start(bf16[768,256]{1,0:T(8,128)(2,1)S(1)} %stack.3.stacked_ref.refs_0_), channel_id=1, source_target_pairs={{0,2},{1,3},{2,0},{3,1},{4,6},{5,7},{6,4},{7,5},{8,10},{9,11},{10,... | collective-permute-start | bytes 1179656 | tf_op jit(solution)/shard_map/ppermute | solution.py:316
  17.1 0.2 collective-permute-start.8
  17.3 3.6 %rows_calc.1 = (f32[16,1,768]{2,1,0:T(1,128)}, bf16[192,256]{1,0:T(8,128)(2,1)S(1)}, bf16[192,256]{1,0:T(8,128)(2,1)S(1)}, bf16[192,256]{1,0:T(8,128)(2,1)S(1)}, bf16[192,256]{1,0:T(8,128)(2,1)S(1)}) custom-call(s32[1]{0:T(128)} %bitcast.place_ref, bf16[768,256]{1,0:T(8,128)(2,1)S(1)} %stack.3.stacked_ref.refs_0_, bf16[512,256]{1,0:T(8,128)(2,1)S(1)} %copy-done, ...), custom_call_target="tpu_custom_call" | custom-call | flops 1610612736 | bytes 1441792 | tf_op jit(solution)/shard_map/rows_calc/pallas_call | solution.py:136
  20.9 5.6 %all-to-all-start = ((f32[16,1,768]{2,1,0:T(1,128)}), f32[16,1,768]{2,1,0:T(1,128)S(1)}, u32[]{:S(2)}, u32[]{:S(2)}) async-start(f32[16,1,768]{2,1,0:T(1,128)} %get-tuple-element.22), calls=%async_computation | async-start | bytes 98304 | tf_op jit(solution)/shard_map/all_to_all | solution.py:333
  26.6 0.1 norm_calc.1.norm_ref
  26.7 2.9 %collective-permute-start.9 = (bf16[192,256]{1,0:T(8,128)(2,1)S(1)}, bf16[192,256]{1,0:T(8,128)(2,1)S(1)}, u32[]{:S(2)}, u32[]{:S(2)}) collective-permute-start(bf16[192,256]{1,0:T(8,128)(2,1)S(1)} %get-tuple-element.27), channel_id=1, source_target_pairs={{0,8},{1,9},{2,10},{3,11},{4,12},{5,13},{6,14},{7,15},{8,0},{9,1},... | collective-permute-start | bytes 294920 | tf_op jit(solution)/shard_map/ppermute | solution.py:316
  29.6 1.5 %collective-permute-start.10 = (bf16[192,256]{1,0:T(8,128)(2,1)S(1)}, bf16[192,256]{1,0:T(8,128)(2,1)S(1)}, u32[]{:S(2)}, u32[]{:S(2)}) collective-permute-start(bf16[192,256]{1,0:T(8,128)(2,1)S(1)} %get-tuple-element.28), channel_id=1, source_target_pairs={{0,12},{1,13},{2,14},{3,15},{4,8},{5,9},{6,10},{7,11},{8,4},{9,5},... | collective-permute-start | bytes 294920 | tf_op jit(solution)/shard_map/ppermute | solution.py:316
  31.1 0.0 collective-permute-start.11
  31.1 2.6 %all-to-all-done.lam_ref = f32[16,1,768]{2,1,0:T(1,128)S(1)} async-done(((f32[16,1,768]{2,1,0:T(1,128)}), f32[16,1,768]{2,1,0:T(1,128)S(1)}, u32[]{:S(2)}, u32[]{:S(2)}) %all-to-all-start) | async-done | bytes 49184 | tf_op jit(solution)/shard_map/all_to_all | solution.py:333
  33.7 1.5 %columns_calc.2 = (f32[512,256]{1,0:T(8,128)S(1)}, f32[512,128]{1,0:T(8,128)S(1)}) custom-call(s32[1]{0:T(128)} %bitcast.place_ref, f32[16,1,768]{2,1,0:T(1,128)S(1)} %all-to-all-done.lam_ref, bf16[512,256]{1,0:T(8,128)(2,1)S(1)} %copy-done, f32[512,128]{1,0:T(8,128)S(1)} %norm_calc.1.norm_ref, bf16[768,256]{1,0:T(8,128)(2,1)S(1)} %stack.3.stacked_ref.refs_0_, ...), custom_call_target="tpu_custom_call" | custom-call | flops 19327352832 | bytes 1703936 | tf_op jit(solution)/shard_map/columns_calc/pallas_call | solution.py:244
  35.2 1.5 %columns_calc.3 = (bf16[512,256]{1,0:T(8,128)(2,1)}, f32[1,512]{1,0:T(1,128)}) custom-call(s32[1]{0:T(128)} %bitcast.place_ref, f32[16,1,768]{2,1,0:T(1,128)S(1)} %all-to-all-done.lam_ref, bf16[512,256]{1,0:T(8,128)(2,1)S(1)} %copy-done, f32[512,128]{1,0:T(8,128)S(1)} %norm_calc.1.norm_ref, bf16[768,256]{1,0:T(8,128)(2,1)S(1)} %collective-permute-done.7.refs_0_, ...), custom_call_target="tpu_custom_call" | custom-call | flops 402653184 | bytes 917504 | tf_op jit(solution)/shard_map/columns_calc/pallas_call | solution.py:244
  36.7 1.8 %collective-permute-done.9.refs_0_ = bf16[192,256]{1,0:T(8,128)(2,1)S(1)} collective-permute-done((bf16[192,256]{1,0:T(8,128)(2,1)S(1)}, bf16[192,256]{1,0:T(8,128)(2,1)S(1)}, u32[]{:S(2)}, u32[]{:S(2)}) %collective-permute-start.9) | collective-permute-done | bytes 98336 | tf_op jit(solution)/shard_map/ppermute | solution.py:316
  38.5 0.4 %collective-permute-done.11.refs_2_ = bf16[192,256]{1,0:T(8,128)(2,1)S(1)} collective-permute-done((bf16[192,256]{1,0:T(8,128)(2,1)S(1)}, bf16[192,256]{1,0:T(8,128)(2,1)S(1)}, u32[]{:S(2)}, u32[]{:S(2)}) %collective-permute-start.11) | collective-permute-done | bytes 98336 | tf_op jit(solution)/shard_map/ppermute | solution.py:316
  38.9 1.3 %combine.1 = (bf16[192,256]{1,0:T(8,128)(2,1)}, f32[1,192]{1,0:T(1,128)}) custom-call(s32[1]{0:T(128)} %bitcast.place_ref, f32[16,1,768]{2,1,0:T(1,128)S(1)} %all-to-all-done.lam_ref, bf16[192,256]{1,0:T(8,128)(2,1)S(1)} %collective-permute-done.9.refs_0_, bf16[192,256]{1,0:T(8,128)(2,1)S(1)} %collective-permute-done.10.refs_1_, ...), custom_call_target="tpu_custom_call" | custom-call | flops 393216 | bytes 393216 | tf_op jit(solution)/shard_map/combine/pallas_call | solution.py:287
  (14 shorter events, 0.1 us)
Async XLA Ops:
  0.6 9.0 %collective-permute-start.3 = (bf16[192,256]{1,0:T(8,128)(2,1)}, bf16[192,256]{1,0:T(8,128)(2,1)S(1)}, u32[]{:S(2)}, u32[]{:S(2)}) collective-permute-start(bf16[192,256]{1,0:T(8,128)(2,1)} %x_ref.1), channel_id=1, source_target_pairs={{0,12},{1,13},{2,14},{3,15},{4,8},{5,9},{6,10},{7,11},{8,4},{9,5},... | collective-permute-start | bytes 294920 | tf_op jit(solution)/shard_map/ppermute | solution.py:316
  5.7 8.5 %collective-permute-start.2 = (bf16[192,256]{1,0:T(8,128)(2,1)}, bf16[192,256]{1,0:T(8,128)(2,1)S(1)}, u32[]{:S(2)}, u32[]{:S(2)}) collective-permute-start(bf16[192,256]{1,0:T(8,128)(2,1)} %x_ref.1), channel_id=1, source_target_pairs={{0,8},{1,9},{2,10},{3,11},{4,12},{5,13},{6,14},{7,15},{8,0},{9,1},... | collective-permute-start | bytes 294920 | tf_op jit(solution)/shard_map/ppermute | solution.py:316
  5.7 8.5 %collective-permute-start.1 = (bf16[192,256]{1,0:T(8,128)(2,1)}, bf16[192,256]{1,0:T(8,128)(2,1)S(1)}, u32[]{:S(2)}, u32[]{:S(2)}) collective-permute-start(bf16[192,256]{1,0:T(8,128)(2,1)} %x_ref.1), channel_id=1, source_target_pairs={{0,4},{1,5},{2,6},{3,7},{4,0},{5,1},{6,2},{7,3},{8,12},{9,13},{10,... | collective-permute-start | bytes 294920 | tf_op jit(solution)/shard_map/ppermute | solution.py:316
  6.4 10.9 %collective-permute-start.4 = (bf16[512,256]{1,0:T(8,128)(2,1)}, bf16[512,256]{1,0:T(8,128)(2,1)S(1)}, u32[]{:S(2)}, u32[]{:S(2)}) collective-permute-start(bf16[512,256]{1,0:T(8,128)(2,1)} %code_ref.5), channel_id=1, source_target_pairs={{0,1},{1,0},{2,3},{3,2},{4,5},{5,4},{6,7},{7,6},{8,9},{9,8},{10,11... | collective-permute-start | bytes 786440 | tf_op jit(solution)/shard_map/ppermute | solution.py:316
  6.4 8.9 %collective-permute-start = (bf16[512,256]{1,0:T(8,128)(2,1)}, bf16[512,256]{1,0:T(8,128)(2,1)S(1)}, u32[]{:S(2)}, u32[]{:S(2)}) collective-permute-start(bf16[512,256]{1,0:T(8,128)(2,1)} %code_ref.5), channel_id=1, source_target_pairs={{0,2},{1,3},{2,0},{3,1},{4,6},{5,7},{6,4},{7,5},{8,10},{9,11},{10,... | collective-permute-start | bytes 786440 | tf_op jit(solution)/shard_map/ppermute | solution.py:316
  8.1 0.9 %copy-start.1 = (bf16[192,256]{1,0:T(8,128)(2,1)S(1)}, bf16[192,256]{1,0:T(8,128)(2,1)}, u32[]{:S(2)}) copy-start(bf16[192,256]{1,0:T(8,128)(2,1)} %x_ref.1) | copy-start | bytes 294916
  14.3 3.0 %copy-start = (bf16[512,256]{1,0:T(8,128)(2,1)S(1)}, bf16[512,256]{1,0:T(8,128)(2,1)}, u32[]{:S(2)}) copy-start(bf16[512,256]{1,0:T(8,128)(2,1)} %code_ref.5) | copy-start | bytes 786436
  15.3 2.0 %collective-permute-start.5 = (bf16[512,256]{1,0:T(8,128)(2,1)S(1)}, bf16[512,256]{1,0:T(8,128)(2,1)S(1)}, u32[]{:S(2)}, u32[]{:S(2)}) collective-permute-start(bf16[512,256]{1,0:T(8,128)(2,1)S(1)} %collective-permute-done.refs_2_), channel_id=1, source_target_pairs={{0,1},{1,0},{2,3},{3,2},{4,5},{5,4},{6,7},{7,6},{8,9},{9,8},{10,11... | collective-permute-start | bytes 786440 | tf_op jit(solution)/shard_map/ppermute | solution.py:316
  15.3 15.7 %collective-permute-start.6 = (bf16[768,256]{1,0:T(8,128)(2,1)S(1)}, bf16[768,256]{1,0:T(8,128)(2,1)S(1)}, u32[]{:S(2)}, u32[]{:S(2)}) collective-permute-start(bf16[768,256]{1,0:T(8,128)(2,1)S(1)} %stack.3.stacked_ref.refs_0_), channel_id=1, source_target_pairs={{0,2},{1,3},{2,0},{3,1},{4,6},{5,7},{6,4},{7,5},{8,10},{9,11},{10,... | collective-permute-start | bytes 1179656 | tf_op jit(solution)/shard_map/ppermute | solution.py:316
  17.1 16.6 %collective-permute-start.8 = (bf16[768,256]{1,0:T(8,128)(2,1)S(1)}, bf16[768,256]{1,0:T(8,128)(2,1)S(1)}, u32[]{:S(2)}, u32[]{:S(2)}) collective-permute-start(bf16[768,256]{1,0:T(8,128)(2,1)S(1)} %stack.3.stacked_ref.refs_0_), channel_id=1, source_target_pairs={{0,1},{1,0},{2,3},{3,2},{4,5},{5,4},{6,7},{7,6},{8,9},{9,8},{10,11... | collective-permute-start | bytes 1179656 | tf_op jit(solution)/shard_map/ppermute | solution.py:316
  20.9 12.7 %all-to-all-start = ((f32[16,1,768]{2,1,0:T(1,128)}), f32[16,1,768]{2,1,0:T(1,128)S(1)}, u32[]{:S(2)}, u32[]{:S(2)}) async-start(f32[16,1,768]{2,1,0:T(1,128)} %get-tuple-element.22), calls=%async_computation | async-start | bytes 98304 | tf_op jit(solution)/shard_map/all_to_all | solution.py:333
  26.7 11.8 %collective-permute-start.9 = (bf16[192,256]{1,0:T(8,128)(2,1)S(1)}, bf16[192,256]{1,0:T(8,128)(2,1)S(1)}, u32[]{:S(2)}, u32[]{:S(2)}) collective-permute-start(bf16[192,256]{1,0:T(8,128)(2,1)S(1)} %get-tuple-element.27), channel_id=1, source_target_pairs={{0,8},{1,9},{2,10},{3,11},{4,12},{5,13},{6,14},{7,15},{8,0},{9,1},... | collective-permute-start | bytes 294920 | tf_op jit(solution)/shard_map/ppermute | solution.py:316
  29.6 8.9 %collective-permute-start.10 = (bf16[192,256]{1,0:T(8,128)(2,1)S(1)}, bf16[192,256]{1,0:T(8,128)(2,1)S(1)}, u32[]{:S(2)}, u32[]{:S(2)}) collective-permute-start(bf16[192,256]{1,0:T(8,128)(2,1)S(1)} %get-tuple-element.28), channel_id=1, source_target_pairs={{0,12},{1,13},{2,14},{3,15},{4,8},{5,9},{6,10},{7,11},{8,4},{9,5},... | collective-permute-start | bytes 294920 | tf_op jit(solution)/shard_map/ppermute | solution.py:316
  31.1 7.9 %collective-permute-start.11 = (bf16[192,256]{1,0:T(8,128)(2,1)S(1)}, bf16[192,256]{1,0:T(8,128)(2,1)S(1)}, u32[]{:S(2)}, u32[]{:S(2)}) collective-permute-start(bf16[192,256]{1,0:T(8,128)(2,1)S(1)} %get-tuple-element.29), channel_id=1, source_target_pairs={{0,4},{1,5},{2,6},{3,7},{4,0},{5,1},{6,2},{7,3},{8,12},{9,13},{10,... | collective-permute-start | bytes 294920 | tf_op jit(solution)/shard_map/ppermute | solution.py:316
  31.1 4.1 %collective-permute-start.7 = (bf16[768,256]{1,0:T(8,128)(2,1)S(1)}, bf16[768,256]{1,0:T(8,128)(2,1)S(1)}, u32[]{:S(2)}, u32[]{:S(2)}) collective-permute-start(bf16[768,256]{1,0:T(8,128)(2,1)S(1)} %collective-permute-done.6.refs_2_), channel_id=1, source_target_pairs={{0,1},{1,0},{2,3},{3,2},{4,5},{5,4},{6,7},{7,6},{8,9},{9,8},{10,11... | collective-permute-start | bytes 1179656 | tf_op jit(solution)/shard_map/ppermute | solution.py:316

commit v6 on v5

--- a/solution.py
+++ b/solution.py
@@ -13,7 +13,7 @@
 LN2 = math.log(2.0)
 VMEM_LIMIT = 20 * 1024 * 1024
 EARLY = 64
-STACK = 1 << 32
+STACK = 3 << 29
 
 
 def nt_dot(a, b):
@@ -258,31 +258,27 @@
 
 
 def combine_kernel(outer, inner, order, place_ref, lam_ref, *refs):
-    parts, (soft_ref, own_ref, columns) = refs[:outer], refs[outer:]
+    parts, (soft_ref, own_ref) = refs[:outer], refs[outer:]
     rows_dev, width = parts[0].shape
-    rows, lanes = columns.shape
+    rows = lam_ref.shape[2]
     place, spoke = place_ref[0] // inner, place_ref[0] % inner
-    spot = pl.multiple_of(place * rows_dev, rows_dev)
     mine = read_lse(lam_ref, outer, inner, spoke)
-
-    def own_rows(line):
-        columns[...] = jnp.broadcast_to(line, (lanes, rows)).T
-        return columns[pl.ds(spot, rows_dev), :]
-
+    lines = [jnp.exp(lam_ref[(place ^ j) * inner + spoke] - mine) for j in order] + [mine]
+    lines += [mine] * (-len(lines) % 8)
+    near = pltpu.roll(jnp.concatenate(lines, axis=0), rows - place * rows_dev, 1)
+    near = near[:, : min(rows, -(-rows_dev // 128) * 128)]
+    columns = near.T
     total = jnp.zeros((rows_dev, width), jnp.float32)
-    for j, part in zip(order, parts):
-        w = own_rows(jnp.exp(lam_ref[(place ^ j) * inner + spoke] - mine))
-        w = jnp.concatenate([w] * (width // lanes), axis=1)
-        total = total + w * part[...].astype(jnp.float32)
+    for i, part in enumerate(parts):
+        total = total + columns[:rows_dev, i : i + 1] * part[...].astype(jnp.float32)
     soft_ref[...] = total.astype(jnp.bfloat16)
-    own_ref[...] = own_rows(mine).T[:1, :]
+    own_ref[...] = near[outer : outer + 1, :rows_dev]
 
 
 def combine(place, lam, parts, order):
     outer = len(parts)
     inner = lam.shape[0] // outer
     rows_dev, width = parts[0].shape
-    lanes = math.gcd(width, 128)
     vmem = pl.BlockSpec(memory_space=pltpu.VMEM)
     return pl.pallas_call(
         functools.partial(combine_kernel, outer, inner, order),
@@ -292,7 +288,6 @@
         ],
         in_specs=[pl.BlockSpec(memory_space=pltpu.SMEM)] + [vmem] * (outer + 1),
         out_specs=[vmem] * 2,
-        scratch_shapes=[pltpu.VMEM((outer * rows_dev, lanes), jnp.float32)],
         compiler_params=pltpu.CompilerParams(vmem_limit_bytes=VMEM_LIMIT),
         cost_estimate=pl.CostEstimate(
             flops=2 * outer * rows_dev * width,
@@ -317,12 +312,9 @@
 
     code_y = swap(codebook, 2)
     code_c = swap(codebook, 1)
-    emb = [swap(embeddings, inner * j) for j in range(1, outer)]
     shape = (outer * embeddings.shape[0], embeddings.shape[1])
-    steps = (0,) + tuple(range(2, outer))
-    far = stack(place, [keep(embeddings)] + emb[1:], steps, inner, shape)
-    code_y, near, far = lax.optimization_barrier((code_y, emb[0], far))
-    stacked = stack(place, [near], (1,), inner, shape, (far,))
+    steps = (*range(2, outer), 1, 0)
+    stacked = stack(place, [keep(embeddings) if i == 0 else swap(embeddings, inner * i) for i in steps], steps, inner, shape)
     stacked_y = swap(stacked, 2)
     stacked_c = swap(stacked, 1)
     code = [codebook, code_c, code_y, swap(code_y, 1)]

time: 40.4 us -> 38.9 us (0.963)
  starting transfers between devices: 19.4 us -> 16.1 us
  waiting for transfers between devices: 11.1 us -> 12.8 us
    ppermute x12, starting transfers between devices: 13.7 us -> 11.5 us  [swap(): return lax.ppermute(x, AXIS, [(i, i ^ step) for i in range(size)])]
    ppermute x12, waiting for transfers between devices: 8.57 us -> 10.5 us  [swap(): return lax.ppermute(x, AXIS, [(i, i ^ step) for i in range(size)])]
    all_to_all x1, starting transfers between devices: 5.63 us -> 4.61 us  [on_device(): lam = lax.all_to_all(lam, AXIS, 0, 0)]
  transfers between devices with their start and end apart: 13 -> 13, of which waited for: 6 -> 7; matrix products, arithmetic and copies ran while one was open for 0% -> 0% of each run, Pallas kernels for 17% -> 17%
where the time goes in v6:
time: 38.9 us; the launch traced here: 38.6 us
  starting transfers between devices  16.1 us (41%)
  waiting for transfers between devices  12.8 us (33%)
  Pallas kernels  7.78 us (20%)
  local copies, waits for them, and re-layouts  1.25 us (3%)
  between operations  0.68 us (2%)
    ppermute x12, starting transfers between devices, swap(): return lax.ppermute(x, AXIS, [(i, i ^ step) for i in range(size)])  11.5 us
    ppermute x12, waiting for transfers between devices, swap(): return lax.ppermute(x, AXIS, [(i, i ^ step) for i in range(size)])  10.5 us
    all_to_all x1, starting transfers between devices, on_device(): lam = lax.all_to_all(lam, AXIS, 0, 0)  4.61 us
    pallas_call x1, Pallas kernels, rows_calc(): pl.pallas_call(functools.partial(rows_kernel, outer, inner, tile, LOG2E *...  3.56 us
    pallas_call x2, Pallas kernels, columns_calc(): pl.pallas_call(functools.partial(body, outer, inner, groups, tile, LOG2E...  3.01 us
    all_to_all x1, waiting for transfers between devices, on_device(): lam = lax.all_to_all(lam, AXIS, 0, 0)  2.35 us
    unnamed x4, local copies, waits for them, and re-layouts  1.25 us
    pallas_call x1, Pallas kernels, combine(): pl.pallas_call(functools.partial(combine_kernel, outer, inner, order), ou...  1.02 us
  transfers between devices with their start and end apart: 13, of which 7 were waited for; matrix products, arithmetic and copies ran while one was open for 0% of the time, Pallas kernels for 17%

profile of v6, /device:TPU:0, one launch (start us, length us, event | category | flops | bytes accessed | tf_op | source)
XLA Modules:
  0.0 38.6 jit_solution(18424437138571701605)
XLA Ops:
  0.6 3.0 %collective-permute-start.4 = (bf16[512,256]{1,0:T(8,128)(2,1)}, bf16[512,256]{1,0:T(8,128)(2,1)S(1)}, u32[]{:S(2)}, u32[]{:S(2)}) collective-permute-start(bf16[512,256]{1,0:T(8,128)(2,1)} %code_ref.5), channel_id=1, source_target_pairs={{0,2},{1,3},{2,0},{3,1},{4,6},{5,7},{6,4},{7,5},{8,10},{9,11},{10,... | collective-permute-start | bytes 786440 | tf_op jit(solution)/shard_map/ppermute | solution.py:311
  3.7 3.6 %collective-permute-start.1 = (bf16[192,256]{1,0:T(8,128)(2,1)}, bf16[192,256]{1,0:T(8,128)(2,1)S(1)}, u32[]{:S(2)}, u32[]{:S(2)}) collective-permute-start(bf16[192,256]{1,0:T(8,128)(2,1)} %x_ref.1), channel_id=1, source_target_pairs={{0,12},{1,13},{2,14},{3,15},{4,8},{5,9},{6,10},{7,11},{8,4},{9,5},... | collective-permute-start | bytes 294920 | tf_op jit(solution)/shard_map/ppermute | solution.py:311
  7.3 0.0 collective-permute-start
  7.3 0.8 %collective-permute-start.2 = (bf16[192,256]{1,0:T(8,128)(2,1)}, bf16[192,256]{1,0:T(8,128)(2,1)S(1)}, u32[]{:S(2)}, u32[]{:S(2)}) collective-permute-start(bf16[192,256]{1,0:T(8,128)(2,1)} %x_ref.1), channel_id=1, source_target_pairs={{0,4},{1,5},{2,6},{3,7},{4,0},{5,1},{6,2},{7,3},{8,12},{9,13},{10,... | collective-permute-start | bytes 294920 | tf_op jit(solution)/shard_map/ppermute | solution.py:311
  8.1 0.0 collective-permute-start.3
  8.1 0.9 %copy-done.1 = bf16[192,256]{1,0:T(8,128)(2,1)S(1)} copy-done((bf16[192,256]{1,0:T(8,128)(2,1)S(1)}, bf16[192,256]{1,0:T(8,128)(2,1)}, u32[]{:S(2)}) %copy-start.1) | copy-done | bytes 98328
  9.0 1.2 %collective-permute-done.4.refs_2_ = bf16[512,256]{1,0:T(8,128)(2,1)S(1)} collective-permute-done((bf16[512,256]{1,0:T(8,128)(2,1)}, bf16[512,256]{1,0:T(8,128)(2,1)S(1)}, u32[]{:S(2)}, u32[]{:S(2)}) %collective-permute-start.4) | collective-permute-done | bytes 262176 | tf_op jit(solution)/shard_map/ppermute | solution.py:311
  10.2 1.2 %collective-permute-done.1.refs_1_ = bf16[192,256]{1,0:T(8,128)(2,1)S(1)} collective-permute-done((bf16[192,256]{1,0:T(8,128)(2,1)}, bf16[192,256]{1,0:T(8,128)(2,1)S(1)}, u32[]{:S(2)}, u32[]{:S(2)}) %collective-permute-start.1) | collective-permute-done | bytes 98336 | tf_op jit(solution)/shard_map/ppermute | solution.py:311
  11.4 4.1 %collective-permute-done.refs_0_ = bf16[192,256]{1,0:T(8,128)(2,1)S(1)} collective-permute-done((bf16[192,256]{1,0:T(8,128)(2,1)}, bf16[192,256]{1,0:T(8,128)(2,1)S(1)}, u32[]{:S(2)}, u32[]{:S(2)}) %collective-permute-start) | collective-permute-done | bytes 98336 | tf_op jit(solution)/shard_map/ppermute | solution.py:311
  15.5 0.6 %collective-permute-start.6 = (bf16[768,256]{1,0:T(8,128)(2,1)S(1)}, bf16[768,256]{1,0:T(8,128)(2,1)S(1)}, u32[]{:S(2)}, u32[]{:S(2)}) collective-permute-start(bf16[768,256]{1,0:T(8,128)(2,1)S(1)} %stack.1.stacked_ref.refs_0_), channel_id=1, source_target_pairs={{0,2},{1,3},{2,0},{3,1},{4,6},{5,7},{6,4},{7,5},{8,10},{9,11},{10,... | collective-permute-start | bytes 1179656 | tf_op jit(solution)/shard_map/ppermute | solution.py:311
  16.1 0.3 copy-done
  16.4 3.6 %rows_calc.1 = (f32[16,1,768]{2,1,0:T(1,128)}, bf16[192,256]{1,0:T(8,128)(2,1)S(1)}, bf16[192,256]{1,0:T(8,128)(2,1)S(1)}, bf16[192,256]{1,0:T(8,128)(2,1)S(1)}, bf16[192,256]{1,0:T(8,128)(2,1)S(1)}) custom-call(s32[1]{0:T(128)} %bitcast.place_ref, bf16[768,256]{1,0:T(8,128)(2,1)S(1)} %stack.1.stacked_ref.refs_0_, bf16[512,256]{1,0:T(8,128)(2,1)S(1)} %copy-done, ...), custom_call_target="tpu_custom_call" | custom-call | flops 1610612736 | bytes 1441792 | tf_op jit(solution)/shard_map/rows_calc/pallas_call | solution.py:136
  20.0 4.6 %all-to-all-start = ((f32[16,1,768]{2,1,0:T(1,128)}), f32[16,1,768]{2,1,0:T(1,128)S(1)}, u32[]{:S(2)}, u32[]{:S(2)}) async-start(f32[16,1,768]{2,1,0:T(1,128)} %get-tuple-element.16), calls=%async_computation | async-start | bytes 98304 | tf_op jit(solution)/shard_map/all_to_all | solution.py:325
  24.6 0.1 norm_calc.1.norm_ref
  24.7 1.1 %collective-permute-done.6.refs_2_ = bf16[768,256]{1,0:T(8,128)(2,1)S(1)} collective-permute-done((bf16[768,256]{1,0:T(8,128)(2,1)S(1)}, bf16[768,256]{1,0:T(8,128)(2,1)S(1)}, u32[]{:S(2)}, u32[]{:S(2)}) %collective-permute-start.6) | collective-permute-done | bytes 393248 | tf_op jit(solution)/shard_map/ppermute | solution.py:311
  25.8 2.0 %collective-permute-start.9 = (bf16[192,256]{1,0:T(8,128)(2,1)S(1)}, bf16[192,256]{1,0:T(8,128)(2,1)S(1)}, u32[]{:S(2)}, u32[]{:S(2)}) collective-permute-start(bf16[192,256]{1,0:T(8,128)(2,1)S(1)} %get-tuple-element.21), channel_id=1, source_target_pairs={{0,8},{1,9},{2,10},{3,11},{4,12},{5,13},{6,14},{7,15},{8,0},{9,1},... | collective-permute-start | bytes 294920 | tf_op jit(solution)/shard_map/ppermute | solution.py:311
  27.8 1.5 %collective-permute-start.10 = (bf16[192,256]{1,0:T(8,128)(2,1)S(1)}, bf16[192,256]{1,0:T(8,128)(2,1)S(1)}, u32[]{:S(2)}, u32[]{:S(2)}) collective-permute-start(bf16[192,256]{1,0:T(8,128)(2,1)S(1)} %get-tuple-element.22), channel_id=1, source_target_pairs={{0,12},{1,13},{2,14},{3,15},{4,8},{5,9},{6,10},{7,11},{8,4},{9,5},... | collective-permute-start | bytes 294920 | tf_op jit(solution)/shard_map/ppermute | solution.py:311
  29.3 0.0 collective-permute-start.11
  29.3 2.3 %all-to-all-done.lam_ref = f32[16,1,768]{2,1,0:T(1,128)S(1)} async-done(((f32[16,1,768]{2,1,0:T(1,128)}), f32[16,1,768]{2,1,0:T(1,128)S(1)}, u32[]{:S(2)}, u32[]{:S(2)}) %all-to-all-start) | async-done | bytes 49184 | tf_op jit(solution)/shard_map/all_to_all | solution.py:325
  31.6 1.5 %columns_calc.2 = (f32[512,256]{1,0:T(8,128)S(1)}, f32[512,128]{1,0:T(8,128)S(1)}) custom-call(s32[1]{0:T(128)} %bitcast.place_ref, f32[16,1,768]{2,1,0:T(1,128)S(1)} %all-to-all-done.lam_ref, bf16[512,256]{1,0:T(8,128)(2,1)S(1)} %copy-done, f32[512,128]{1,0:T(8,128)S(1)} %norm_calc.1.norm_ref, bf16[768,256]{1,0:T(8,128)(2,1)S(1)} %stack.1.stacked_ref.refs_0_, ...), custom_call_target="tpu_custom_call" | custom-call | flops 19327352832 | bytes 1703936 | tf_op jit(solution)/shard_map/columns_calc/pallas_call | solution.py:244
  33.2 1.5 %columns_calc.3 = (bf16[512,256]{1,0:T(8,128)(2,1)}, f32[1,512]{1,0:T(1,128)}) custom-call(s32[1]{0:T(128)} %bitcast.place_ref, f32[16,1,768]{2,1,0:T(1,128)S(1)} %all-to-all-done.lam_ref, bf16[512,256]{1,0:T(8,128)(2,1)S(1)} %copy-done, f32[512,128]{1,0:T(8,128)S(1)} %norm_calc.1.norm_ref, bf16[768,256]{1,0:T(8,128)(2,1)S(1)} %collective-permute-done.7.refs_0_, ...), custom_call_target="tpu_custom_call" | custom-call | flops 402653184 | bytes 917504 | tf_op jit(solution)/shard_map/columns_calc/pallas_call | solution.py:244
  34.7 2.1 %collective-permute-done.9.refs_0_ = bf16[192,256]{1,0:T(8,128)(2,1)S(1)} collective-permute-done((bf16[192,256]{1,0:T(8,128)(2,1)S(1)}, bf16[192,256]{1,0:T(8,128)(2,1)S(1)}, u32[]{:S(2)}, u32[]{:S(2)}) %collective-permute-start.9) | collective-permute-done | bytes 98336 | tf_op jit(solution)/shard_map/ppermute | solution.py:311
  36.7 0.9 %collective-permute-done.11.refs_2_ = bf16[192,256]{1,0:T(8,128)(2,1)S(1)} collective-permute-done((bf16[192,256]{1,0:T(8,128)(2,1)S(1)}, bf16[192,256]{1,0:T(8,128)(2,1)S(1)}, u32[]{:S(2)}, u32[]{:S(2)}) %collective-permute-start.11) | collective-permute-done | bytes 98336 | tf_op jit(solution)/shard_map/ppermute | solution.py:311
  37.6 1.0 %combine.1 = (bf16[192,256]{1,0:T(8,128)(2,1)}, f32[1,192]{1,0:T(1,128)}) custom-call(s32[1]{0:T(128)} %bitcast.place_ref, f32[16,1,768]{2,1,0:T(1,128)S(1)} %all-to-all-done.lam_ref, bf16[192,256]{1,0:T(8,128)(2,1)S(1)} %collective-permute-done.9.refs_0_, bf16[192,256]{1,0:T(8,128)(2,1)S(1)} %collective-permute-done.10.refs_1_, ...), custom_call_target="tpu_custom_call" | custom-call | flops 393216 | bytes 393216 | tf_op jit(solution)/shard_map/combine/pallas_call | solution.py:283
  (13 shorter events, 0.1 us)
Async XLA Ops:
  0.6 9.6 %collective-permute-start.4 = (bf16[512,256]{1,0:T(8,128)(2,1)}, bf16[512,256]{1,0:T(8,128)(2,1)S(1)}, u32[]{:S(2)}, u32[]{:S(2)}) collective-permute-start(bf16[512,256]{1,0:T(8,128)(2,1)} %code_ref.5), channel_id=1, source_target_pairs={{0,2},{1,3},{2,0},{3,1},{4,6},{5,7},{6,4},{7,5},{8,10},{9,11},{10,... | collective-permute-start | bytes 786440 | tf_op jit(solution)/shard_map/ppermute | solution.py:311
  3.7 7.7 %collective-permute-start.1 = (bf16[192,256]{1,0:T(8,128)(2,1)}, bf16[192,256]{1,0:T(8,128)(2,1)S(1)}, u32[]{:S(2)}, u32[]{:S(2)}) collective-permute-start(bf16[192,256]{1,0:T(8,128)(2,1)} %x_ref.1), channel_id=1, source_target_pairs={{0,12},{1,13},{2,14},{3,15},{4,8},{5,9},{6,10},{7,11},{8,4},{9,5},... | collective-permute-start | bytes 294920 | tf_op jit(solution)/shard_map/ppermute | solution.py:311
  7.3 8.2 %collective-permute-start = (bf16[192,256]{1,0:T(8,128)(2,1)}, bf16[192,256]{1,0:T(8,128)(2,1)S(1)}, u32[]{:S(2)}, u32[]{:S(2)}) collective-permute-start(bf16[192,256]{1,0:T(8,128)(2,1)} %x_ref.1), channel_id=1, source_target_pairs={{0,8},{1,9},{2,10},{3,11},{4,12},{5,13},{6,14},{7,15},{8,0},{9,1},... | collective-permute-start | bytes 294920 | tf_op jit(solution)/shard_map/ppermute | solution.py:311
  7.3 8.2 %collective-permute-start.2 = (bf16[192,256]{1,0:T(8,128)(2,1)}, bf16[192,256]{1,0:T(8,128)(2,1)S(1)}, u32[]{:S(2)}, u32[]{:S(2)}) collective-permute-start(bf16[192,256]{1,0:T(8,128)(2,1)} %x_ref.1), channel_id=1, source_target_pairs={{0,4},{1,5},{2,6},{3,7},{4,0},{5,1},{6,2},{7,3},{8,12},{9,13},{10,... | collective-permute-start | bytes 294920 | tf_op jit(solution)/shard_map/ppermute | solution.py:311
  8.1 8.0 %collective-permute-start.3 = (bf16[512,256]{1,0:T(8,128)(2,1)}, bf16[512,256]{1,0:T(8,128)(2,1)S(1)}, u32[]{:S(2)}, u32[]{:S(2)}) collective-permute-start(bf16[512,256]{1,0:T(8,128)(2,1)} %code_ref.5), channel_id=1, source_target_pairs={{0,1},{1,0},{2,3},{3,2},{4,5},{5,4},{6,7},{7,6},{8,9},{9,8},{10,11... | collective-permute-start | bytes 786440 | tf_op jit(solution)/shard_map/ppermute | solution.py:311
  8.1 0.9 %copy-start.1 = (bf16[192,256]{1,0:T(8,128)(2,1)S(1)}, bf16[192,256]{1,0:T(8,128)(2,1)}, u32[]{:S(2)}) copy-start(bf16[192,256]{1,0:T(8,128)(2,1)} %x_ref.1) | copy-start | bytes 294916
  10.2 5.9 %collective-permute-start.5 = (bf16[512,256]{1,0:T(8,128)(2,1)S(1)}, bf16[512,256]{1,0:T(8,128)(2,1)S(1)}, u32[]{:S(2)}, u32[]{:S(2)}) collective-permute-start(bf16[512,256]{1,0:T(8,128)(2,1)S(1)} %collective-permute-done.4.refs_2_), channel_id=1, source_target_pairs={{0,1},{1,0},{2,3},{3,2},{4,5},{5,4},{6,7},{7,6},{8,9},{9,8},{10,11... | collective-permute-start | bytes 786440 | tf_op jit(solution)/shard_map/ppermute | solution.py:311
  15.5 1.0 %copy-start = (bf16[512,256]{1,0:T(8,128)(2,1)S(1)}, bf16[512,256]{1,0:T(8,128)(2,1)}, u32[]{:S(2)}) copy-start(bf16[512,256]{1,0:T(8,128)(2,1)} %code_ref.5) | copy-start | bytes 786436
  15.5 10.3 %collective-permute-start.6 = (bf16[768,256]{1,0:T(8,128)(2,1)S(1)}, bf16[768,256]{1,0:T(8,128)(2,1)S(1)}, u32[]{:S(2)}, u32[]{:S(2)}) collective-permute-start(bf16[768,256]{1,0:T(8,128)(2,1)S(1)} %stack.1.stacked_ref.refs_0_), channel_id=1, source_target_pairs={{0,2},{1,3},{2,0},{3,1},{4,6},{5,7},{6,4},{7,5},{8,10},{9,11},{10,... | collective-permute-start | bytes 1179656 | tf_op jit(solution)/shard_map/ppermute | solution.py:311
  16.1 13.2 %collective-permute-start.8 = (bf16[768,256]{1,0:T(8,128)(2,1)S(1)}, bf16[768,256]{1,0:T(8,128)(2,1)S(1)}, u32[]{:S(2)}, u32[]{:S(2)}) collective-permute-start(bf16[768,256]{1,0:T(8,128)(2,1)S(1)} %stack.1.stacked_ref.refs_0_), channel_id=1, source_target_pairs={{0,1},{1,0},{2,3},{3,2},{4,5},{5,4},{6,7},{7,6},{8,9},{9,8},{10,11... | collective-permute-start | bytes 1179656 | tf_op jit(solution)/shard_map/ppermute | solution.py:311
  20.0 11.7 %all-to-all-start = ((f32[16,1,768]{2,1,0:T(1,128)}), f32[16,1,768]{2,1,0:T(1,128)S(1)}, u32[]{:S(2)}, u32[]{:S(2)}) async-start(f32[16,1,768]{2,1,0:T(1,128)} %get-tuple-element.16), calls=%async_computation | async-start | bytes 98304 | tf_op jit(solution)/shard_map/all_to_all | solution.py:325
  25.8 7.4 %collective-permute-start.7 = (bf16[768,256]{1,0:T(8,128)(2,1)S(1)}, bf16[768,256]{1,0:T(8,128)(2,1)S(1)}, u32[]{:S(2)}, u32[]{:S(2)}) collective-permute-start(bf16[768,256]{1,0:T(8,128)(2,1)S(1)} %collective-permute-done.6.refs_2_), channel_id=1, source_target_pairs={{0,1},{1,0},{2,3},{3,2},{4,5},{5,4},{6,7},{7,6},{8,9},{9,8},{10,11... | collective-permute-start | bytes 1179656 | tf_op jit(solution)/shard_map/ppermute | solution.py:311
  25.8 10.9 %collective-permute-start.9 = (bf16[192,256]{1,0:T(8,128)(2,1)S(1)}, bf16[192,256]{1,0:T(8,128)(2,1)S(1)}, u32[]{:S(2)}, u32[]{:S(2)}) collective-permute-start(bf16[192,256]{1,0:T(8,128)(2,1)S(1)} %get-tuple-element.21), channel_id=1, source_target_pairs={{0,8},{1,9},{2,10},{3,11},{4,12},{5,13},{6,14},{7,15},{8,0},{9,1},... | collective-permute-start | bytes 294920 | tf_op jit(solution)/shard_map/ppermute | solution.py:311
  27.8 8.9 %collective-permute-start.10 = (bf16[192,256]{1,0:T(8,128)(2,1)S(1)}, bf16[192,256]{1,0:T(8,128)(2,1)S(1)}, u32[]{:S(2)}, u32[]{:S(2)}) collective-permute-start(bf16[192,256]{1,0:T(8,128)(2,1)S(1)} %get-tuple-element.22), channel_id=1, source_target_pairs={{0,12},{1,13},{2,14},{3,15},{4,8},{5,9},{6,10},{7,11},{8,4},{9,5},... | collective-permute-start | bytes 294920 | tf_op jit(solution)/shard_map/ppermute | solution.py:311
  29.3 8.4 %collective-permute-start.11 = (bf16[192,256]{1,0:T(8,128)(2,1)S(1)}, bf16[192,256]{1,0:T(8,128)(2,1)S(1)}, u32[]{:S(2)}, u32[]{:S(2)}) collective-permute-start(bf16[192,256]{1,0:T(8,128)(2,1)S(1)} %get-tuple-element.23), channel_id=1, source_target_pairs={{0,4},{1,5},{2,6},{3,7},{4,0},{5,1},{6,2},{7,3},{8,12},{9,13},{10,... | collective-permute-start | bytes 294920 | tf_op jit(solution)/shard_map/ppermute | solution.py:311

commit v7 on v6

--- a/solution.py
+++ b/solution.py
@@ -23,15 +23,6 @@
 def norm_column(code, scale):
     c = code.astype(jnp.float32)
     return (0.5 * scale) * jnp.sum(c * c, axis=1, keepdims=True)
-
-
-def tiles(rows, tile, body):
-    count = rows // tile
-    if count <= 4:
-        for t in range(count):
-            body(t * tile, t * tile)
-    else:
-        pl.loop(0, count)(lambda t: body(pl.multiple_of(t * tile, tile), 0))
 
 
 def keep_kernel(x_ref, out_ref):
@@ -96,7 +87,7 @@
         for k in range(inner)
     ]
 
-    def one_tile(start, slot):
+    def first_half(start, slot):
         rows_here = stacked_ref[pl.ds(start, tile), :]
         top = None
         for k in range(inner):
@@ -104,7 +95,9 @@
             scores[slot : slot + tile, k * k_dev : (k + 1) * k_dev] = s
             m = fold_lanes(jnp.maximum, s, lanes)
             top = m if top is None else jnp.maximum(top, m)
-        top = jnp.max(top, axis=1, keepdims=True)
+        return jnp.max(top, axis=1, keepdims=True)
+
+    def second_half(start, slot, top):
         mass = jnp.zeros((tile, lanes), jnp.float32)
         acc = jnp.zeros((tile, width), jnp.float32)
         for k in range(inner):
@@ -120,7 +113,21 @@
         )
         total[pl.ds(start, tile), :] = (acc * (1.0 / mass)).astype(jnp.bfloat16)
 
-    tiles(rows, tile, one_tile)
+    count = rows // tile
+    if count <= 4:
+        top = first_half(0, 0)
+        for t in range(count):
+            here = top
+            if t + 1 < count:
+                top = first_half((t + 1) * tile, (t + 1) * tile)
+            second_half(t * tile, t * tile, here)
+    else:
+
+        @pl.loop(0, count)
+        def one_tile(t):
+            start = pl.multiple_of(t * tile, tile)
+            second_half(start, 0, first_half(start, 0))
+
     for j in range(outer):
         spot = pl.multiple_of((place ^ j) * rows_dev, rows_dev)
         parts[j][...] = total[pl.ds(spot, rows_dev), :]
@@ -220,9 +227,9 @@
     levels = lambda g: read_lse(lam_ref, outer, inner, spoke ^ g)
     add_groups(groups, tile, scale, levels, code_ref, norm_ref, emb, weighted, folded)
     masses = jnp.sum(folded[...], axis=1, keepdims=True)
-    prior = rows_dev / k_dev
+    share = 1.0 / (masses + rows_dev / k_dev)
     shift_ref[...] = (
-        (weighted[...] - masses * code_ref[...].astype(jnp.float32)) / (masses + prior)
+        (weighted[...] - masses * code_ref[...].astype(jnp.float32)) * share
     ).astype(jnp.bfloat16)
     spread = jnp.broadcast_to(masses * (k_dev / rows_dev), folded.shape).T
     occ_ref[...] = spread[:1, :]
@@ -322,7 +329,7 @@
 
     order = (*range(2, outer), 1, 0)
     sent = [swap(parts[j], inner * j) for j in order[:-1]]
-    lam = lax.all_to_all(lam, AXIS, 0, 0)
+    lam = after(lax.all_to_all(lam, AXIS, 0, 0), sent[0])
     norm = norm_calc(codebook, LOG2E * 3.0 / math.sqrt(codebook.shape[1]))
     stacked_yc = swap(stacked_y, 1)
     sums = columns_calc(

time: 38.9 us -> 36.3 us (0.933)
  waiting for transfers between devices: 12.8 us -> 10.2 us
    ppermute x12, waiting for transfers between devices: 10.5 us -> 7.29 us  [swap(): return lax.ppermute(x, AXIS, [(i, i ^ step) for i in range(size)])]
    all_to_all x1, waiting for transfers between devices: 2.35 us -> 2.93 us  [on_device(): lam = after(lax.all_to_all(lam, AXIS, 0, 0), sent[0])]
  transfers between devices with their start and end apart: 13 -> 13, of which waited for: 7 -> 6; matrix products, arithmetic and copies ran while one was open for 0% -> 0% of each run, Pallas kernels for 17% -> 18%
where the time goes in v7:
time: 36.3 us; the launch traced here: 36.1 us
  starting transfers between devices  16.3 us (45%)
  waiting for transfers between devices  10.2 us (28%)
  Pallas kernels  7.62 us (21%)
  local copies, waits for them, and re-layouts  1.25 us (3%)
  between operations  0.68 us (2%)
    ppermute x12, starting transfers between devices, swap(): return lax.ppermute(x, AXIS, [(i, i ^ step) for i in range(size)])  11.8 us
    ppermute x12, waiting for transfers between devices, swap(): return lax.ppermute(x, AXIS, [(i, i ^ step) for i in range(size)])  7.29 us
    all_to_all x1, starting transfers between devices, on_device(): lam = after(lax.all_to_all(lam, AXIS, 0, 0), sent[0])  4.54 us
    pallas_call x1, Pallas kernels, rows_calc(): pl.pallas_call(functools.partial(rows_kernel, outer, inner, tile, LOG2E *...  3.41 us
    pallas_call x2, Pallas kernels, columns_calc(): pl.pallas_call(functools.partial(body, outer, inner, groups, tile, LOG2E...  3.01 us
    all_to_all x1, waiting for transfers between devices, on_device(): lam = after(lax.all_to_all(lam, AXIS, 0, 0), sent[0])  2.93 us
    unnamed x4, local copies, waits for them, and re-layouts  1.25 us
    pallas_call x1, Pallas kernels, combine(): pl.pallas_call(functools.partial(combine_kernel, outer, inner, order), ou...  1.02 us
  transfers between devices with their start and end apart: 13, of which 6 were waited for; matrix products, arithmetic and copies ran while one was open for 0% of the time, Pallas kernels for 18%

profile of v7, /device:TPU:0, one launch (start us, length us, event | category | flops | bytes accessed | tf_op | source)
XLA Modules:
  0.0 36.1 jit_solution(12843750836435204542)
XLA Ops:
  0.6 3.0 %collective-permute-start.4 = (bf16[512,256]{1,0:T(8,128)(2,1)}, bf16[512,256]{1,0:T(8,128)(2,1)S(1)}, u32[]{:S(2)}, u32[]{:S(2)}) collective-permute-start(bf16[512,256]{1,0:T(8,128)(2,1)} %code_ref.5), channel_id=1, source_target_pairs={{0,2},{1,3},{2,0},{3,1},{4,6},{5,7},{6,4},{7,5},{8,10},{9,11},{10,... | collective-permute-start | bytes 786440 | tf_op jit(solution)/shard_map/ppermute | solution.py:318
  3.7 3.6 %collective-permute-start.1 = (bf16[192,256]{1,0:T(8,128)(2,1)}, bf16[192,256]{1,0:T(8,128)(2,1)S(1)}, u32[]{:S(2)}, u32[]{:S(2)}) collective-permute-start(bf16[192,256]{1,0:T(8,128)(2,1)} %x_ref.1), channel_id=1, source_target_pairs={{0,12},{1,13},{2,14},{3,15},{4,8},{5,9},{6,10},{7,11},{8,4},{9,5},... | collective-permute-start | bytes 294920 | tf_op jit(solution)/shard_map/ppermute | solution.py:318
  7.3 0.0 collective-permute-start
  7.3 0.8 %collective-permute-start.2 = (bf16[192,256]{1,0:T(8,128)(2,1)}, bf16[192,256]{1,0:T(8,128)(2,1)S(1)}, u32[]{:S(2)}, u32[]{:S(2)}) collective-permute-start(bf16[192,256]{1,0:T(8,128)(2,1)} %x_ref.1), channel_id=1, source_target_pairs={{0,4},{1,5},{2,6},{3,7},{4,0},{5,1},{6,2},{7,3},{8,12},{9,13},{10,... | collective-permute-start | bytes 294920 | tf_op jit(solution)/shard_map/ppermute | solution.py:318
  8.1 0.0 collective-permute-start.3
  8.1 0.9 %copy-done.1 = bf16[192,256]{1,0:T(8,128)(2,1)S(1)} copy-done((bf16[192,256]{1,0:T(8,128)(2,1)S(1)}, bf16[192,256]{1,0:T(8,128)(2,1)}, u32[]{:S(2)}) %copy-start.1) | copy-done | bytes 98328
  9.0 1.2 %collective-permute-done.4.refs_2_ = bf16[512,256]{1,0:T(8,128)(2,1)S(1)} collective-permute-done((bf16[512,256]{1,0:T(8,128)(2,1)}, bf16[512,256]{1,0:T(8,128)(2,1)S(1)}, u32[]{:S(2)}, u32[]{:S(2)}) %collective-permute-start.4) | collective-permute-done | bytes 262176 | tf_op jit(solution)/shard_map/ppermute | solution.py:318
  10.2 0.0 collective-permute-start.5
  10.2 1.2 %collective-permute-done.1.refs_1_ = bf16[192,256]{1,0:T(8,128)(2,1)S(1)} collective-permute-done((bf16[192,256]{1,0:T(8,128)(2,1)}, bf16[192,256]{1,0:T(8,128)(2,1)S(1)}, u32[]{:S(2)}, u32[]{:S(2)}) %collective-permute-start.1) | collective-permute-done | bytes 98336 | tf_op jit(solution)/shard_map/ppermute | solution.py:318
  11.4 4.1 %collective-permute-done.refs_0_ = bf16[192,256]{1,0:T(8,128)(2,1)S(1)} collective-permute-done((bf16[192,256]{1,0:T(8,128)(2,1)}, bf16[192,256]{1,0:T(8,128)(2,1)S(1)}, u32[]{:S(2)}, u32[]{:S(2)}) %collective-permute-start) | collective-permute-done | bytes 98336 | tf_op jit(solution)/shard_map/ppermute | solution.py:318
  15.5 0.0 collective-permute-done.2.refs_2_
  15.5 0.6 %collective-permute-start.7 = (bf16[768,256]{1,0:T(8,128)(2,1)S(1)}, bf16[768,256]{1,0:T(8,128)(2,1)S(1)}, u32[]{:S(2)}, u32[]{:S(2)}) collective-permute-start(bf16[768,256]{1,0:T(8,128)(2,1)S(1)} %stack.1.stacked_ref.refs_0_), channel_id=1, source_target_pairs={{0,2},{1,3},{2,0},{3,1},{4,6},{5,7},{6,4},{7,5},{8,10},{9,11},{10,... | collective-permute-start | bytes 1179656 | tf_op jit(solution)/shard_map/ppermute | solution.py:318
  16.1 0.3 copy-done
  16.4 3.4 %rows_calc.1 = (f32[16,1,768]{2,1,0:T(1,128)}, bf16[192,256]{1,0:T(8,128)(2,1)S(1)}, bf16[192,256]{1,0:T(8,128)(2,1)S(1)}, bf16[192,256]{1,0:T(8,128)(2,1)S(1)}, bf16[192,256]{1,0:T(8,128)(2,1)S(1)}) custom-call(s32[1]{0:T(128)} %bitcast.place_ref, bf16[768,256]{1,0:T(8,128)(2,1)S(1)} %stack.1.stacked_ref.refs_0_, bf16[512,256]{1,0:T(8,128)(2,1)S(1)} %copy-done, ...), custom_call_target="tpu_custom_call" | custom-call | flops 1610612736 | bytes 1441792 | tf_op jit(solution)/shard_map/rows_calc/pallas_call | solution.py:143
  19.8 0.5 %collective-permute-start.6 = (bf16[192,256]{1,0:T(8,128)(2,1)S(1)}, bf16[192,256]{1,0:T(8,128)(2,1)S(1)}, u32[]{:S(2)}, u32[]{:S(2)}) collective-permute-start(bf16[192,256]{1,0:T(8,128)(2,1)S(1)} %get-tuple-element.18), channel_id=1, source_target_pairs={{0,8},{1,9},{2,10},{3,11},{4,12},{5,13},{6,14},{7,15},{8,0},{9,1},... | collective-permute-start | bytes 294920 | tf_op jit(solution)/shard_map/ppermute | solution.py:318
  20.4 4.5 %all-to-all-start = ((f32[16,1,768]{2,1,0:T(1,128)}), f32[16,1,768]{2,1,0:T(1,128)S(1)}, u32[]{:S(2)}, u32[]{:S(2)}) async-start(f32[16,1,768]{2,1,0:T(1,128)} %get-tuple-element.17), calls=%async_computation | async-start | bytes 98304 | tf_op jit(solution)/shard_map/all_to_all | solution.py:332
  24.9 0.1 norm_calc.1.norm_ref
  25.0 0.7 %collective-permute-done.7.refs_2_ = bf16[768,256]{1,0:T(8,128)(2,1)S(1)} collective-permute-done((bf16[768,256]{1,0:T(8,128)(2,1)S(1)}, bf16[768,256]{1,0:T(8,128)(2,1)S(1)}, u32[]{:S(2)}, u32[]{:S(2)}) %collective-permute-start.7) | collective-permute-done | bytes 393248 | tf_op jit(solution)/shard_map/ppermute | solution.py:318
  25.8 3.2 %collective-permute-start.10 = (bf16[192,256]{1,0:T(8,128)(2,1)S(1)}, bf16[192,256]{1,0:T(8,128)(2,1)S(1)}, u32[]{:S(2)}, u32[]{:S(2)}) collective-permute-start(bf16[192,256]{1,0:T(8,128)(2,1)S(1)} %get-tuple-element.24), channel_id=1, source_target_pairs={{0,12},{1,13},{2,14},{3,15},{4,8},{5,9},{6,10},{7,11},{8,4},{9,5},... | collective-permute-start | bytes 294920 | tf_op jit(solution)/shard_map/ppermute | solution.py:318
  29.0 2.9 %all-to-all-done.lam_ref = f32[16,1,768]{2,1,0:T(1,128)S(1)} async-done(((f32[16,1,768]{2,1,0:T(1,128)}), f32[16,1,768]{2,1,0:T(1,128)S(1)}, u32[]{:S(2)}, u32[]{:S(2)}) %all-to-all-start) | async-done | bytes 49184 | tf_op jit(solution)/shard_map/all_to_all | solution.py:332
  32.0 1.5 %columns_calc.2 = (f32[512,256]{1,0:T(8,128)S(1)}, f32[512,128]{1,0:T(8,128)S(1)}) custom-call(s32[1]{0:T(128)} %bitcast.place_ref, f32[16,1,768]{2,1,0:T(1,128)S(1)} %all-to-all-done.lam_ref, bf16[512,256]{1,0:T(8,128)(2,1)S(1)} %copy-done, f32[512,128]{1,0:T(8,128)S(1)} %norm_calc.1.norm_ref, bf16[768,256]{1,0:T(8,128)(2,1)S(1)} %stack.1.stacked_ref.refs_0_, ...), custom_call_target="tpu_custom_call" | custom-call | flops 19327352832 | bytes 1703936 | tf_op jit(solution)/shard_map/columns_calc/pallas_call | solution.py:251
  33.5 1.5 %columns_calc.3 = (bf16[512,256]{1,0:T(8,128)(2,1)}, f32[1,512]{1,0:T(1,128)}) custom-call(s32[1]{0:T(128)} %bitcast.place_ref, f32[16,1,768]{2,1,0:T(1,128)S(1)} %all-to-all-done.lam_ref, bf16[512,256]{1,0:T(8,128)(2,1)S(1)} %copy-done, f32[512,128]{1,0:T(8,128)S(1)} %norm_calc.1.norm_ref, bf16[768,256]{1,0:T(8,128)(2,1)S(1)} %collective-permute-done.8.refs_0_, ...), custom_call_target="tpu_custom_call" | custom-call | flops 402653184 | bytes 917504 | tf_op jit(solution)/shard_map/columns_calc/pallas_call | solution.py:251
  35.0 0.1 collective-permute-done.11.refs_2_
  35.0 1.0 %combine.1 = (bf16[192,256]{1,0:T(8,128)(2,1)}, f32[1,192]{1,0:T(1,128)}) custom-call(s32[1]{0:T(128)} %bitcast.place_ref, f32[16,1,768]{2,1,0:T(1,128)S(1)} %all-to-all-done.lam_ref, bf16[192,256]{1,0:T(8,128)(2,1)S(1)} %collective-permute-done.6.refs_0_, bf16[192,256]{1,0:T(8,128)(2,1)S(1)} %collective-permute-done.10.refs_1_, ...), custom_call_target="tpu_custom_call" | custom-call | flops 393216 | bytes 393216 | tf_op jit(solution)/shard_map/combine/pallas_call | solution.py:290
  (13 shorter events, 0.1 us)
Async XLA Ops:
  0.6 9.6 %collective-permute-start.4 = (bf16[512,256]{1,0:T(8,128)(2,1)}, bf16[512,256]{1,0:T(8,128)(2,1)S(1)}, u32[]{:S(2)}, u32[]{:S(2)}) collective-permute-start(bf16[512,256]{1,0:T(8,128)(2,1)} %code_ref.5), channel_id=1, source_target_pairs={{0,2},{1,3},{2,0},{3,1},{4,6},{5,7},{6,4},{7,5},{8,10},{9,11},{10,... | collective-permute-start | bytes 786440 | tf_op jit(solution)/shard_map/ppermute | solution.py:318
  3.7 7.7 %collective-permute-start.1 = (bf16[192,256]{1,0:T(8,128)(2,1)}, bf16[192,256]{1,0:T(8,128)(2,1)S(1)}, u32[]{:S(2)}, u32[]{:S(2)}) collective-permute-start(bf16[192,256]{1,0:T(8,128)(2,1)} %x_ref.1), channel_id=1, source_target_pairs={{0,12},{1,13},{2,14},{3,15},{4,8},{5,9},{6,10},{7,11},{8,4},{9,5},... | collective-permute-start | bytes 294920 | tf_op jit(solution)/shard_map/ppermute | solution.py:318
  7.3 8.2 %collective-permute-start = (bf16[192,256]{1,0:T(8,128)(2,1)}, bf16[192,256]{1,0:T(8,128)(2,1)S(1)}, u32[]{:S(2)}, u32[]{:S(2)}) collective-permute-start(bf16[192,256]{1,0:T(8,128)(2,1)} %x_ref.1), channel_id=1, source_target_pairs={{0,8},{1,9},{2,10},{3,11},{4,12},{5,13},{6,14},{7,15},{8,0},{9,1},... | collective-permute-start | bytes 294920 | tf_op jit(solution)/shard_map/ppermute | solution.py:318
  7.3 8.2 %collective-permute-start.2 = (bf16[192,256]{1,0:T(8,128)(2,1)}, bf16[192,256]{1,0:T(8,128)(2,1)S(1)}, u32[]{:S(2)}, u32[]{:S(2)}) collective-permute-start(bf16[192,256]{1,0:T(8,128)(2,1)} %x_ref.1), channel_id=1, source_target_pairs={{0,4},{1,5},{2,6},{3,7},{4,0},{5,1},{6,2},{7,3},{8,12},{9,13},{10,... | collective-permute-start | bytes 294920 | tf_op jit(solution)/shard_map/ppermute | solution.py:318
  8.1 8.0 %collective-permute-start.3 = (bf16[512,256]{1,0:T(8,128)(2,1)}, bf16[512,256]{1,0:T(8,128)(2,1)S(1)}, u32[]{:S(2)}, u32[]{:S(2)}) collective-permute-start(bf16[512,256]{1,0:T(8,128)(2,1)} %code_ref.5), channel_id=1, source_target_pairs={{0,1},{1,0},{2,3},{3,2},{4,5},{5,4},{6,7},{7,6},{8,9},{9,8},{10,11... | collective-permute-start | bytes 786440 | tf_op jit(solution)/shard_map/ppermute | solution.py:318
  8.1 0.9 %copy-start.1 = (bf16[192,256]{1,0:T(8,128)(2,1)S(1)}, bf16[192,256]{1,0:T(8,128)(2,1)}, u32[]{:S(2)}) copy-start(bf16[192,256]{1,0:T(8,128)(2,1)} %x_ref.1) | copy-start | bytes 294916
  10.2 5.9 %collective-permute-start.5 = (bf16[512,256]{1,0:T(8,128)(2,1)S(1)}, bf16[512,256]{1,0:T(8,128)(2,1)S(1)}, u32[]{:S(2)}, u32[]{:S(2)}) collective-permute-start(bf16[512,256]{1,0:T(8,128)(2,1)S(1)} %collective-permute-done.4.refs_2_), channel_id=1, source_target_pairs={{0,1},{1,0},{2,3},{3,2},{4,5},{5,4},{6,7},{7,6},{8,9},{9,8},{10,11... | collective-permute-start | bytes 786440 | tf_op jit(solution)/shard_map/ppermute | solution.py:318
  15.5 1.0 %copy-start = (bf16[512,256]{1,0:T(8,128)(2,1)S(1)}, bf16[512,256]{1,0:T(8,128)(2,1)}, u32[]{:S(2)}) copy-start(bf16[512,256]{1,0:T(8,128)(2,1)} %code_ref.5) | copy-start | bytes 786436
  15.5 10.3 %collective-permute-start.7 = (bf16[768,256]{1,0:T(8,128)(2,1)S(1)}, bf16[768,256]{1,0:T(8,128)(2,1)S(1)}, u32[]{:S(2)}, u32[]{:S(2)}) collective-permute-start(bf16[768,256]{1,0:T(8,128)(2,1)S(1)} %stack.1.stacked_ref.refs_0_), channel_id=1, source_target_pairs={{0,2},{1,3},{2,0},{3,1},{4,6},{5,7},{6,4},{7,5},{8,10},{9,11},{10,... | collective-permute-start | bytes 1179656 | tf_op jit(solution)/shard_map/ppermute | solution.py:318
  16.1 15.9 %collective-permute-start.9 = (bf16[768,256]{1,0:T(8,128)(2,1)S(1)}, bf16[768,256]{1,0:T(8,128)(2,1)S(1)}, u32[]{:S(2)}, u32[]{:S(2)}) collective-permute-start(bf16[768,256]{1,0:T(8,128)(2,1)S(1)} %stack.1.stacked_ref.refs_0_), channel_id=1, source_target_pairs={{0,1},{1,0},{2,3},{3,2},{4,5},{5,4},{6,7},{7,6},{8,9},{9,8},{10,11... | collective-permute-start | bytes 1179656 | tf_op jit(solution)/shard_map/ppermute | solution.py:318
  19.8 12.1 %collective-permute-start.6 = (bf16[192,256]{1,0:T(8,128)(2,1)S(1)}, bf16[192,256]{1,0:T(8,128)(2,1)S(1)}, u32[]{:S(2)}, u32[]{:S(2)}) collective-permute-start(bf16[192,256]{1,0:T(8,128)(2,1)S(1)} %get-tuple-element.18), channel_id=1, source_target_pairs={{0,8},{1,9},{2,10},{3,11},{4,12},{5,13},{6,14},{7,15},{8,0},{9,1},... | collective-permute-start | bytes 294920 | tf_op jit(solution)/shard_map/ppermute | solution.py:318
  20.4 11.6 %all-to-all-start = ((f32[16,1,768]{2,1,0:T(1,128)}), f32[16,1,768]{2,1,0:T(1,128)S(1)}, u32[]{:S(2)}, u32[]{:S(2)}) async-start(f32[16,1,768]{2,1,0:T(1,128)} %get-tuple-element.17), calls=%async_computation | async-start | bytes 98304 | tf_op jit(solution)/shard_map/all_to_all | solution.py:332
  25.8 7.7 %collective-permute-start.8 = (bf16[768,256]{1,0:T(8,128)(2,1)S(1)}, bf16[768,256]{1,0:T(8,128)(2,1)S(1)}, u32[]{:S(2)}, u32[]{:S(2)}) collective-permute-start(bf16[768,256]{1,0:T(8,128)(2,1)S(1)} %collective-permute-done.7.refs_2_), channel_id=1, source_target_pairs={{0,1},{1,0},{2,3},{3,2},{4,5},{5,4},{6,7},{7,6},{8,9},{9,8},{10,11... | collective-permute-start | bytes 1179656 | tf_op jit(solution)/shard_map/ppermute | solution.py:318
  25.8 9.2 %collective-permute-start.10 = (bf16[192,256]{1,0:T(8,128)(2,1)S(1)}, bf16[192,256]{1,0:T(8,128)(2,1)S(1)}, u32[]{:S(2)}, u32[]{:S(2)}) collective-permute-start(bf16[192,256]{1,0:T(8,128)(2,1)S(1)} %get-tuple-element.24), channel_id=1, source_target_pairs={{0,12},{1,13},{2,14},{3,15},{4,8},{5,9},{6,10},{7,11},{8,4},{9,5},... | collective-permute-start | bytes 294920 | tf_op jit(solution)/shard_map/ppermute | solution.py:318
  29.0 6.0 %collective-permute-start.11 = (bf16[192,256]{1,0:T(8,128)(2,1)S(1)}, bf16[192,256]{1,0:T(8,128)(2,1)S(1)}, u32[]{:S(2)}, u32[]{:S(2)}) collective-permute-start(bf16[192,256]{1,0:T(8,128)(2,1)S(1)} %get-tuple-element.25), channel_id=1, source_target_pairs={{0,4},{1,5},{2,6},{3,7},{4,0},{5,1},{6,2},{7,3},{8,12},{9,13},{10,... | collective-permute-start | bytes 294920 | tf_op jit(solution)/shard_map/ppermute | solution.py:318

commit v8 on v7

--- a/solution.py
+++ b/solution.py
@@ -25,21 +25,25 @@
     return (0.5 * scale) * jnp.sum(c * c, axis=1, keepdims=True)
 
 
-def keep_kernel(x_ref, out_ref):
-    out_ref[...] = x_ref[...]
-
-
-def keep(x):
+def keep_kernel(*refs):
+    half = len(refs) // 2
+    for x_ref, out_ref in zip(refs[:half], refs[half:]):
+        out_ref[...] = x_ref[...]
+
+
+def keep(*arrays):
     vmem = pl.BlockSpec(memory_space=pltpu.VMEM)
     return pl.pallas_call(
         keep_kernel,
-        out_shape=jax.ShapeDtypeStruct(x.shape, x.dtype),
-        in_specs=[vmem],
-        out_specs=vmem,
-        compiler_params=pltpu.CompilerParams(vmem_limit_bytes=VMEM_LIMIT),
-        cost_estimate=pl.CostEstimate(flops=0, bytes_accessed=4 * x.size, transcendentals=0),
+        out_shape=[jax.ShapeDtypeStruct(x.shape, x.dtype) for x in arrays],
+        in_specs=[vmem] * len(arrays),
+        out_specs=[vmem] * len(arrays),
+        compiler_params=pltpu.CompilerParams(vmem_limit_bytes=VMEM_LIMIT),
+        cost_estimate=pl.CostEstimate(
+            flops=0, bytes_accessed=4 * sum(x.size for x in arrays), transcendentals=0
+        ),
         name="keep",
-    )(x)
+    )(*arrays)
 
 
 def stack_kernel(inner, steps, place_ref, *refs):
@@ -51,20 +55,19 @@
         out_ref[pl.ds(spot, rows_dev), :] = block[...]
 
 
-def stack(place, blocks, steps, inner, shape, into=()):
+def stack(place, blocks, steps, inner, shape):
     vmem = pl.BlockSpec(memory_space=pltpu.VMEM)
     return pl.pallas_call(
         functools.partial(stack_kernel, inner, steps),
         out_shape=jax.ShapeDtypeStruct(shape, blocks[0].dtype),
-        in_specs=[pl.BlockSpec(memory_space=pltpu.SMEM)] + [vmem] * (len(blocks) + len(into)),
+        in_specs=[pl.BlockSpec(memory_space=pltpu.SMEM)] + [vmem] * len(blocks),
         out_specs=vmem,
-        input_output_aliases={1 + len(blocks): 0} if into else {},
-        compiler_params=pltpu.CompilerParams(vmem_limit_bytes=VMEM_LIMIT),
-        cost_estimate=pl.CostEstimate(
-            flops=0 if into else STACK, bytes_accessed=4 * shape[0] * shape[1], transcendentals=0
+        compiler_params=pltpu.CompilerParams(vmem_limit_bytes=VMEM_LIMIT),
+        cost_estimate=pl.CostEstimate(
+            flops=STACK, bytes_accessed=4 * shape[0] * shape[1], transcendentals=0
         ),
         name="stack",
-    )(place, *blocks, *into)
+    )(place, *blocks)
 
 
 def fold_lanes(op, x, lanes):
@@ -206,7 +209,7 @@
             weighted[...] += jnp.dot(shares, rows_here, preferred_element_type=jnp.float32)
 
 
-def early_kernel(outer, inner, groups, tile, scale, place_ref, lam_ref, code_ref, norm_ref, *refs):
+def early_kernel(outer, inner, groups, tile, scale, order, place_ref, lam_ref, code_ref, norm_ref, *refs):
     emb = refs[: len(groups)]
     weighted, folded = refs[len(groups) :]
     spoke = place_ref[0] % inner
@@ -216,12 +219,14 @@
     add_groups(groups, tile, scale, levels, code_ref, norm_ref, emb, weighted, folded)
 
 
-def late_kernel(outer, inner, groups, tile, scale, place_ref, lam_ref, code_ref, norm_ref, *refs):
-    emb = refs[: len(groups)]
-    weighted_in, folded_in, shift_ref, occ_ref, weighted, folded = refs[len(groups) :]
+def late_kernel(outer, inner, groups, tile, scale, order, place_ref, lam_ref, code_ref, norm_ref, *refs):
+    emb, refs = refs[: len(groups)], refs[len(groups) :]
+    weighted_in, folded_in, parts, refs = refs[0], refs[1], refs[2 : 2 + outer], refs[2 + outer :]
+    shift_ref, occ_ref, soft_ref, own_ref, weighted, folded = refs
     k_dev = code_ref.shape[0]
-    rows_dev = emb[0].shape[0] // outer
-    spoke = place_ref[0] % inner
+    rows_dev, width = parts[0].shape
+    rows = lam_ref.shape[2]
+    place, spoke = place_ref[0] // inner, place_ref[0] % inner
     weighted[...] = weighted_in[...]
     folded[...] = folded_in[...]
     levels = lambda g: read_lse(lam_ref, outer, inner, spoke ^ g)
@@ -234,42 +239,7 @@
     spread = jnp.broadcast_to(masses * (k_dev / rows_dev), folded.shape).T
     occ_ref[...] = spread[:1, :]
 
-
-def columns_calc(place, lam, code, norm, groups, emb, inner, sums=()):
-    k_dev, width = code.shape
-    rows = emb[0].shape[0]
-    outer = lam.shape[0] // inner
-    tile = math.gcd(rows, 768)
-    lanes = norm.shape[1]
-    totals = [((k_dev, width), jnp.float32), ((k_dev, lanes), jnp.float32)]
-    if sums:
-        body, out = late_kernel, [((k_dev, width), jnp.bfloat16), ((1, k_dev), jnp.float32)]
-        scratch = [pltpu.VMEM(*x) for x in totals]
-    else:
-        body, out, scratch = early_kernel, totals, []
-    vmem = pl.BlockSpec(memory_space=pltpu.VMEM)
-    return pl.pallas_call(
-        functools.partial(body, outer, inner, groups, tile, LOG2E * 3.0 / math.sqrt(width)),
-        out_shape=[jax.ShapeDtypeStruct(*x) for x in out],
-        in_specs=[pl.BlockSpec(memory_space=pltpu.SMEM)] + [vmem] * (3 + len(emb) + len(sums)),
-        out_specs=[vmem] * len(out),
-        scratch_shapes=scratch,
-        compiler_params=pltpu.CompilerParams(vmem_limit_bytes=VMEM_LIMIT),
-        cost_estimate=pl.CostEstimate(
-            flops=(4 if sums else EARLY) * len(emb) * rows * k_dev * width,
-            bytes_accessed=2 * (len(emb) * rows + 2 * k_dev) * width,
-            transcendentals=len(emb) * rows * k_dev,
-        ),
-        name="columns_calc",
-    )(place, lam, code, norm, *emb, *sums)
-
-
-def combine_kernel(outer, inner, order, place_ref, lam_ref, *refs):
-    parts, (soft_ref, own_ref) = refs[:outer], refs[outer:]
-    rows_dev, width = parts[0].shape
-    rows = lam_ref.shape[2]
-    place, spoke = place_ref[0] // inner, place_ref[0] % inner
-    mine = read_lse(lam_ref, outer, inner, spoke)
+    mine = levels(0)
     lines = [jnp.exp(lam_ref[(place ^ j) * inner + spoke] - mine) for j in order] + [mine]
     lines += [mine] * (-len(lines) % 8)
     near = pltpu.roll(jnp.concatenate(lines, axis=0), rows - place * rows_dev, 1)
@@ -282,27 +252,43 @@
     own_ref[...] = near[outer : outer + 1, :rows_dev]
 
 
-def combine(place, lam, parts, order):
-    outer = len(parts)
-    inner = lam.shape[0] // outer
-    rows_dev, width = parts[0].shape
+def columns_calc(place, lam, code, norm, groups, emb, inner, sums=(), parts=(), order=()):
+    k_dev, width = code.shape
+    rows = emb[0].shape[0]
+    outer = lam.shape[0] // inner
+    tile = math.gcd(rows, 768)
+    lanes = norm.shape[1]
+    totals = [((k_dev, width), jnp.float32), ((k_dev, lanes), jnp.float32)]
+    if sums:
+        body = late_kernel
+        rows_dev = parts[0].shape[0]
+        out = [
+            ((k_dev, width), jnp.bfloat16),
+            ((1, k_dev), jnp.float32),
+            ((rows_dev, width), jnp.bfloat16),
+            ((1, rows_dev), jnp.float32),
+        ]
+        scratch = [pltpu.VMEM(*x) for x in totals]
+    else:
+        body, out, scratch = early_kernel, totals, []
     vmem = pl.BlockSpec(memory_space=pltpu.VMEM)
     return pl.pallas_call(
-        functools.partial(combine_kernel, outer, inner, order),
-        out_shape=[
-            jax.ShapeDtypeStruct((rows_dev, width), jnp.bfloat16),
-            jax.ShapeDtypeStruct((1, rows_dev), jnp.float32),
-        ],
-        in_specs=[pl.BlockSpec(memory_space=pltpu.SMEM)] + [vmem] * (outer + 1),
-        out_specs=[vmem] * 2,
-        compiler_params=pltpu.CompilerParams(vmem_limit_bytes=VMEM_LIMIT),
-        cost_estimate=pl.CostEstimate(
-            flops=2 * outer * rows_dev * width,
-            bytes_accessed=2 * outer * rows_dev * width,
-            transcendentals=0,
-        ),
-        name="combine",
-    )(place, lam, *parts)
+        functools.partial(
+            body, outer, inner, groups, tile, LOG2E * 3.0 / math.sqrt(width), order
+        ),
+        out_shape=[jax.ShapeDtypeStruct(*x) for x in out],
+        in_specs=[pl.BlockSpec(memory_space=pltpu.SMEM)]
+        + [vmem] * (3 + len(emb) + len(sums) + len(parts)),
+        out_specs=[vmem] * len(out),
+        scratch_shapes=scratch,
+        compiler_params=pltpu.CompilerParams(vmem_limit_bytes=VMEM_LIMIT),
+        cost_estimate=pl.CostEstimate(
+            flops=(4 if sums else EARLY) * len(emb) * rows * k_dev * width,
+            bytes_accessed=2 * (len(emb) * rows + 2 * k_dev) * width,
+            transcendentals=len(emb) * rows * k_dev,
+        ),
+        name="columns_calc",
+    )(place, lam, code, norm, *emb, *sums, *parts)
 
 
 def after(x, y):
@@ -320,25 +306,27 @@
     code_y = swap(codebook, 2)
     code_c = swap(codebook, 1)
     shape = (outer * embeddings.shape[0], embeddings.shape[1])
-    steps = (*range(2, outer), 1, 0)
-    stacked = stack(place, [keep(embeddings) if i == 0 else swap(embeddings, inner * i) for i in steps], steps, inner, shape)
+    order = (*range(2, outer), 1, 0)
+    own_rows, own_code = keep(embeddings, codebook)
+    blocks = [swap(embeddings, inner * j) for j in order[:-1]] + [own_rows]
+    stacked = stack(place, blocks, order, inner, shape)
     stacked_y = swap(stacked, 2)
     stacked_c = swap(stacked, 1)
-    code = [codebook, code_c, code_y, swap(code_y, 1)]
+    code = [own_code, code_c, code_y, swap(code_y, 1)]
     lam, parts = rows_calc(place, stacked, code, outer)
 
-    order = (*range(2, outer), 1, 0)
     sent = [swap(parts[j], inner * j) for j in order[:-1]]
-    lam = after(lax.all_to_all(lam, AXIS, 0, 0), sent[0])
-    norm = norm_calc(codebook, LOG2E * 3.0 / math.sqrt(codebook.shape[1]))
+    lam = lax.all_to_all(lam, AXIS, 0, 0)
+    for part in sent[: outer - 2]:
+        lam = after(lam, part)
+    norm = norm_calc(own_code, LOG2E * 3.0 / math.sqrt(codebook.shape[1]))
     stacked_yc = swap(stacked_y, 1)
     sums = columns_calc(
-        place, lam, codebook, norm, (0, 1, 2), [stacked, stacked_c, stacked_y], inner
+        place, lam, own_code, norm, (0, 1, 2), [stacked, stacked_c, stacked_y], inner
     )
-    shift, occupancy = columns_calc(
-        place, lam, codebook, norm, (3,), [stacked_yc], inner, sums
+    shift, occupancy, soft, own_lse = columns_calc(
+        place, lam, own_code, norm, (3,), [stacked_yc], inner, sums, sent + [parts[0]], order
     )
-    soft, own_lse = combine(place, lam, sent + [after(parts[0], occupancy)], order)
     return shift, occupancy.reshape(-1), soft, own_lse.reshape(-1)
 
 

time: 36.3 us -> 37 us (1.019)
  starting transfers between devices: 16.3 us -> 17.3 us
  Pallas kernels: 7.62 us -> 6.7 us
  local copies, waits for them, and re-layouts: 1.25 us -> 1.84 us
    ppermute x12, waiting for transfers between devices: 7.29 us -> 5.22 us  [swap(): return lax.ppermute(x, AXIS, [(i, i ^ step) for i in range(size)])]
    all_to_all x1, waiting for transfers between devices: 2.93 us -> 4.99 us  [on_device(): lam = lax.all_to_all(lam, AXIS, 0, 0)]
    ppermute x12, starting transfers between devices: 11.8 us -> 13.4 us  [swap(): return lax.ppermute(x, AXIS, [(i, i ^ step) for i in range(size)])]
    pallas_call x2 -> x1, Pallas kernels: 1.03 us -> 0.02 us  [keep(): pl.pallas_call(keep_kernel, out_shape=[jax.ShapeDtypeStruct(x.shape, x.dt...]
    unnamed x4, local copies, waits for them, and re-layouts: 1.25 us -> 1.84 us
    all_to_all x1, starting transfers between devices: 4.54 us -> 3.95 us  [on_device(): lam = lax.all_to_all(lam, AXIS, 0, 0)]
  transfers between devices with their start and end apart: 13 -> 13, of which waited for: 6 -> 4; matrix products, arithmetic and copies ran while one was open for 0% -> 0% of each run, Pallas kernels for 18% -> 14%
where the time goes in v8:
time: 37 us; the launch traced here: 36.8 us
  starting transfers between devices  17.3 us (47%)
  waiting for transfers between devices  10.2 us (28%)
  Pallas kernels  6.7 us (18%)
  local copies, waits for them, and re-layouts  1.84 us (5%)
  between operations  0.7 us (2%)
    ppermute x12, starting transfers between devices, swap(): return lax.ppermute(x, AXIS, [(i, i ^ step) for i in range(size)])  13.4 us
    ppermute x12, waiting for transfers between devices, swap(): return lax.ppermute(x, AXIS, [(i, i ^ step) for i in range(size)])  5.22 us
    all_to_all x1, waiting for transfers between devices, on_device(): lam = lax.all_to_all(lam, AXIS, 0, 0)  4.99 us
    all_to_all x1, starting transfers between devices, on_device(): lam = lax.all_to_all(lam, AXIS, 0, 0)  3.95 us
    pallas_call x1, Pallas kernels, rows_calc(): pl.pallas_call(functools.partial(rows_kernel, outer, inner, tile, LOG2E *...  3.41 us
    pallas_call x2, Pallas kernels, columns_calc(): pl.pallas_call(functools.partial(body, outer, inner, groups, tile, LOG2E...  3.09 us
    unnamed x4, local copies, waits for them, and re-layouts  1.84 us
  transfers between devices with their start and end apart: 13, of which 4 were waited for; matrix products, arithmetic and copies ran while one was open for 0% of the time, Pallas kernels for 14%

profile of v8, /device:TPU:0, one launch (start us, length us, event | category | flops | bytes accessed | tf_op | source)
XLA Modules:
  0.0 36.8 jit_solution(13589963060756914937)
XLA Ops:
  0.6 3.0 %collective-permute-start.4 = (bf16[512,256]{1,0:T(8,128)(2,1)}, bf16[512,256]{1,0:T(8,128)(2,1)S(1)}, u32[]{:S(2)}, u32[]{:S(2)}) collective-permute-start(bf16[512,256]{1,0:T(8,128)(2,1)} %refs_1_.1), channel_id=1, source_target_pairs={{0,2},{1,3},{2,0},{3,1},{4,6},{5,7},{6,4},{7,5},{8,10},{9,11},{10,... | collective-permute-start | bytes 786440 | tf_op jit(solution)/shard_map/ppermute | solution.py:304
  3.7 3.6 %collective-permute-start.1 = (bf16[192,256]{1,0:T(8,128)(2,1)}, bf16[192,256]{1,0:T(8,128)(2,1)S(1)}, u32[]{:S(2)}, u32[]{:S(2)}) collective-permute-start(bf16[192,256]{1,0:T(8,128)(2,1)} %refs_0_.1), channel_id=1, source_target_pairs={{0,12},{1,13},{2,14},{3,15},{4,8},{5,9},{6,10},{7,11},{8,4},{9,5},... | collective-permute-start | bytes 294920 | tf_op jit(solution)/shard_map/ppermute | solution.py:304
  7.3 0.8 %collective-permute-start.2 = (bf16[192,256]{1,0:T(8,128)(2,1)}, bf16[192,256]{1,0:T(8,128)(2,1)S(1)}, u32[]{:S(2)}, u32[]{:S(2)}) collective-permute-start(bf16[192,256]{1,0:T(8,128)(2,1)} %refs_0_.1), channel_id=1, source_target_pairs={{0,4},{1,5},{2,6},{3,7},{4,0},{5,1},{6,2},{7,3},{8,12},{9,13},{10,... | collective-permute-start | bytes 294920 | tf_op jit(solution)/shard_map/ppermute | solution.py:304
  8.1 0.0 collective-permute-start.3
  8.1 0.9 %copy-done = bf16[512,256]{1,0:T(8,128)(2,1)S(1)} copy-done((bf16[512,256]{1,0:T(8,128)(2,1)S(1)}, bf16[512,256]{1,0:T(8,128)(2,1)}, u32[]{:S(2)}) %copy-start) | copy-done | bytes 262168
  9.0 0.9 %copy-done.1 = bf16[192,256]{1,0:T(8,128)(2,1)S(1)} copy-done((bf16[192,256]{1,0:T(8,128)(2,1)S(1)}, bf16[192,256]{1,0:T(8,128)(2,1)}, u32[]{:S(2)}) %copy-start.1) | copy-done | bytes 98328
  9.9 0.2 collective-permute-done.4.refs_2_
  10.2 0.3 collective-permute-start.5
  10.5 0.9 %collective-permute-done.1.refs_1_ = bf16[192,256]{1,0:T(8,128)(2,1)S(1)} collective-permute-done((bf16[192,256]{1,0:T(8,128)(2,1)}, bf16[192,256]{1,0:T(8,128)(2,1)S(1)}, u32[]{:S(2)}, u32[]{:S(2)}) %collective-permute-start.1) | collective-permute-done | bytes 98336 | tf_op jit(solution)/shard_map/ppermute | solution.py:304
  11.4 4.1 %collective-permute-done.refs_0_ = bf16[192,256]{1,0:T(8,128)(2,1)S(1)} collective-permute-done((bf16[192,256]{1,0:T(8,128)(2,1)}, bf16[192,256]{1,0:T(8,128)(2,1)S(1)}, u32[]{:S(2)}, u32[]{:S(2)}) %collective-permute-start) | collective-permute-done | bytes 98336 | tf_op jit(solution)/shard_map/ppermute | solution.py:304
  15.5 0.6 %collective-permute-start.8 = (bf16[768,256]{1,0:T(8,128)(2,1)S(1)}, bf16[768,256]{1,0:T(8,128)(2,1)S(1)}, u32[]{:S(2)}, u32[]{:S(2)}) collective-permute-start(bf16[768,256]{1,0:T(8,128)(2,1)S(1)} %stack.1.stacked_ref.refs_0_), channel_id=1, source_target_pairs={{0,2},{1,3},{2,0},{3,1},{4,6},{5,7},{6,4},{7,5},{8,10},{9,11},{10,... | collective-permute-start | bytes 1179656 | tf_op jit(solution)/shard_map/ppermute | solution.py:304
  16.1 0.0 collective-permute-start.10
  16.1 0.0 collective-permute-done.3.refs_1_
  16.1 0.0 collective-permute-done.5.refs_3_
  16.1 3.4 %rows_calc.1 = (f32[16,1,768]{2,1,0:T(1,128)}, bf16[192,256]{1,0:T(8,128)(2,1)S(1)}, bf16[192,256]{1,0:T(8,128)(2,1)S(1)}, bf16[192,256]{1,0:T(8,128)(2,1)S(1)}, bf16[192,256]{1,0:T(8,128)(2,1)S(1)}) custom-call(s32[1]{0:T(128)} %bitcast.place_ref, bf16[768,256]{1,0:T(8,128)(2,1)S(1)} %stack.1.stacked_ref.refs_0_, ...), custom_call_target="tpu_custom_call" | custom-call | flops 1610612736 | bytes 1441792 | tf_op jit(solution)/shard_map/rows_calc/pallas_call | solution.py:146
  19.5 0.5 %collective-permute-start.6 = (bf16[192,256]{1,0:T(8,128)(2,1)S(1)}, bf16[192,256]{1,0:T(8,128)(2,1)S(1)}, u32[]{:S(2)}, u32[]{:S(2)}) collective-permute-start(bf16[192,256]{1,0:T(8,128)(2,1)S(1)} %get-tuple-element.22), channel_id=1, source_target_pairs={{0,8},{1,9},{2,10},{3,11},{4,12},{5,13},{6,14},{7,15},{8,0},{9,1},... | collective-permute-start | bytes 294920 | tf_op jit(solution)/shard_map/ppermute | solution.py:304
  20.0 2.4 %collective-permute-start.7 = (bf16[192,256]{1,0:T(8,128)(2,1)S(1)}, bf16[192,256]{1,0:T(8,128)(2,1)S(1)}, u32[]{:S(2)}, u32[]{:S(2)}) collective-permute-start(bf16[192,256]{1,0:T(8,128)(2,1)S(1)} %get-tuple-element.24), channel_id=1, source_target_pairs={{0,12},{1,13},{2,14},{3,15},{4,8},{5,9},{6,10},{7,11},{8,4},{9,5},... | collective-permute-start | bytes 294920 | tf_op jit(solution)/shard_map/ppermute | solution.py:304
  22.4 4.0 %all-to-all-start = ((f32[16,1,768]{2,1,0:T(1,128)}), f32[16,1,768]{2,1,0:T(1,128)S(1)}, u32[]{:S(2)}, u32[]{:S(2)}) async-start(f32[16,1,768]{2,1,0:T(1,128)} %get-tuple-element.21), calls=%async_computation | async-start | bytes 98304 | tf_op jit(solution)/shard_map/all_to_all | solution.py:319
  26.3 0.1 norm_calc.1.norm_ref
  26.5 0.5 %collective-permute-start.9 = (bf16[768,256]{1,0:T(8,128)(2,1)S(1)}, bf16[768,256]{1,0:T(8,128)(2,1)S(1)}, u32[]{:S(2)}, u32[]{:S(2)}) collective-permute-start(bf16[768,256]{1,0:T(8,128)(2,1)S(1)} %collective-permute-done.8.refs_2_), channel_id=1, source_target_pairs={{0,1},{1,0},{2,3},{3,2},{4,5},{5,4},{6,7},{7,6},{8,9},{9,8},{10,11... | collective-permute-start | bytes 1179656 | tf_op jit(solution)/shard_map/ppermute | solution.py:304
  27.0 1.7 %collective-permute-start.11 = (bf16[192,256]{1,0:T(8,128)(2,1)S(1)}, bf16[192,256]{1,0:T(8,128)(2,1)S(1)}, u32[]{:S(2)}, u32[]{:S(2)}) collective-permute-start(bf16[192,256]{1,0:T(8,128)(2,1)S(1)} %get-tuple-element.28), channel_id=1, source_target_pairs={{0,4},{1,5},{2,6},{3,7},{4,0},{5,1},{6,2},{7,3},{8,12},{9,13},{10,... | collective-permute-start | bytes 294920 | tf_op jit(solution)/shard_map/ppermute | solution.py:304
  28.7 5.0 %all-to-all-done.lam_ref = f32[16,1,768]{2,1,0:T(1,128)S(1)} async-done(((f32[16,1,768]{2,1,0:T(1,128)}), f32[16,1,768]{2,1,0:T(1,128)S(1)}, u32[]{:S(2)}, u32[]{:S(2)}) %all-to-all-start) | async-done | bytes 49184 | tf_op jit(solution)/shard_map/all_to_all | solution.py:319
  33.7 1.5 %columns_calc.2 = (f32[512,256]{1,0:T(8,128)S(1)}, f32[512,128]{1,0:T(8,128)S(1)}) custom-call(s32[1]{0:T(128)} %bitcast.place_ref, f32[16,1,768]{2,1,0:T(1,128)S(1)} %all-to-all-done.lam_ref, bf16[512,256]{1,0:T(8,128)(2,1)S(1)} %get-tuple-element.20.refs_0_.code_ref, f32[512,128]{1,0:T(8,128)S(1)} %norm_calc.1.norm_ref, ...), custom_call_target="tpu_custom_call" | custom-call | flops 19327352832 | bytes 1703936 | tf_op jit(solution)/shard_map/columns_calc/pallas_call | solution.py:275
  35.2 1.6 %columns_calc.3 = (bf16[512,256]{1,0:T(8,128)(2,1)}, f32[1,512]{1,0:T(1,128)}, bf16[192,256]{1,0:T(8,128)(2,1)}, f32[1,192]{1,0:T(1,128)}) custom-call(s32[1]{0:T(128)} %bitcast.place_ref, f32[16,1,768]{2,1,0:T(1,128)S(1)} %all-to-all-done.lam_ref, bf16[512,256]{1,0:T(8,128)(2,1)S(1)} %get-tuple-element.20.refs_0_.code_ref, ...), custom_call_target="tpu_custom_call" | custom-call | flops 402653184 | bytes 917504 | tf_op jit(solution)/shard_map/columns_calc/pallas_call | solution.py:275
  (12 shorter events, 0.1 us)
Async XLA Ops:
  0.6 9.5 %collective-permute-start.4 = (bf16[512,256]{1,0:T(8,128)(2,1)}, bf16[512,256]{1,0:T(8,128)(2,1)S(1)}, u32[]{:S(2)}, u32[]{:S(2)}) collective-permute-start(bf16[512,256]{1,0:T(8,128)(2,1)} %refs_1_.1), channel_id=1, source_target_pairs={{0,2},{1,3},{2,0},{3,1},{4,6},{5,7},{6,4},{7,5},{8,10},{9,11},{10,... | collective-permute-start | bytes 786440 | tf_op jit(solution)/shard_map/ppermute | solution.py:304
  3.7 7.7 %collective-permute-start.1 = (bf16[192,256]{1,0:T(8,128)(2,1)}, bf16[192,256]{1,0:T(8,128)(2,1)S(1)}, u32[]{:S(2)}, u32[]{:S(2)}) collective-permute-start(bf16[192,256]{1,0:T(8,128)(2,1)} %refs_0_.1), channel_id=1, source_target_pairs={{0,12},{1,13},{2,14},{3,15},{4,8},{5,9},{6,10},{7,11},{8,4},{9,5},... | collective-permute-start | bytes 294920 | tf_op jit(solution)/shard_map/ppermute | solution.py:304
  7.3 8.2 %collective-permute-start = (bf16[192,256]{1,0:T(8,128)(2,1)}, bf16[192,256]{1,0:T(8,128)(2,1)S(1)}, u32[]{:S(2)}, u32[]{:S(2)}) collective-permute-start(bf16[192,256]{1,0:T(8,128)(2,1)} %refs_0_.1), channel_id=1, source_target_pairs={{0,8},{1,9},{2,10},{3,11},{4,12},{5,13},{6,14},{7,15},{8,0},{9,1},... | collective-permute-start | bytes 294920 | tf_op jit(solution)/shard_map/ppermute | solution.py:304
  7.3 8.2 %collective-permute-start.2 = (bf16[192,256]{1,0:T(8,128)(2,1)}, bf16[192,256]{1,0:T(8,128)(2,1)S(1)}, u32[]{:S(2)}, u32[]{:S(2)}) collective-permute-start(bf16[192,256]{1,0:T(8,128)(2,1)} %refs_0_.1), channel_id=1, source_target_pairs={{0,4},{1,5},{2,6},{3,7},{4,0},{5,1},{6,2},{7,3},{8,12},{9,13},{10,... | collective-permute-start | bytes 294920 | tf_op jit(solution)/shard_map/ppermute | solution.py:304
  8.1 8.0 %collective-permute-start.3 = (bf16[512,256]{1,0:T(8,128)(2,1)}, bf16[512,256]{1,0:T(8,128)(2,1)S(1)}, u32[]{:S(2)}, u32[]{:S(2)}) collective-permute-start(bf16[512,256]{1,0:T(8,128)(2,1)} %refs_1_.1), channel_id=1, source_target_pairs={{0,1},{1,0},{2,3},{3,2},{4,5},{5,4},{6,7},{7,6},{8,9},{9,8},{10,11... | collective-permute-start | bytes 786440 | tf_op jit(solution)/shard_map/ppermute | solution.py:304
  8.1 1.0 %copy-start = (bf16[512,256]{1,0:T(8,128)(2,1)S(1)}, bf16[512,256]{1,0:T(8,128)(2,1)}, u32[]{:S(2)}) copy-start(bf16[512,256]{1,0:T(8,128)(2,1)} %refs_1_.1) | copy-start | bytes 786436
  9.0 0.9 %copy-start.1 = (bf16[192,256]{1,0:T(8,128)(2,1)S(1)}, bf16[192,256]{1,0:T(8,128)(2,1)}, u32[]{:S(2)}) copy-start(bf16[192,256]{1,0:T(8,128)(2,1)} %refs_0_.1) | copy-start | bytes 294916
  10.2 5.9 %collective-permute-start.5 = (bf16[512,256]{1,0:T(8,128)(2,1)S(1)}, bf16[512,256]{1,0:T(8,128)(2,1)S(1)}, u32[]{:S(2)}, u32[]{:S(2)}) collective-permute-start(bf16[512,256]{1,0:T(8,128)(2,1)S(1)} %collective-permute-done.4.refs_2_), channel_id=1, source_target_pairs={{0,1},{1,0},{2,3},{3,2},{4,5},{5,4},{6,7},{7,6},{8,9},{9,8},{10,11... | collective-permute-start | bytes 786440 | tf_op jit(solution)/shard_map/ppermute | solution.py:304
  15.5 11.0 %collective-permute-start.8 = (bf16[768,256]{1,0:T(8,128)(2,1)S(1)}, bf16[768,256]{1,0:T(8,128)(2,1)S(1)}, u32[]{:S(2)}, u32[]{:S(2)}) collective-permute-start(bf16[768,256]{1,0:T(8,128)(2,1)S(1)} %stack.1.stacked_ref.refs_0_), channel_id=1, source_target_pairs={{0,2},{1,3},{2,0},{3,1},{4,6},{5,7},{6,4},{7,5},{8,10},{9,11},{10,... | collective-permute-start | bytes 1179656 | tf_op jit(solution)/shard_map/ppermute | solution.py:304
  16.1 17.6 %collective-permute-start.10 = (bf16[768,256]{1,0:T(8,128)(2,1)S(1)}, bf16[768,256]{1,0:T(8,128)(2,1)S(1)}, u32[]{:S(2)}, u32[]{:S(2)}) collective-permute-start(bf16[768,256]{1,0:T(8,128)(2,1)S(1)} %stack.1.stacked_ref.refs_0_), channel_id=1, source_target_pairs={{0,1},{1,0},{2,3},{3,2},{4,5},{5,4},{6,7},{7,6},{8,9},{9,8},{10,11... | collective-permute-start | bytes 1179656 | tf_op jit(solution)/shard_map/ppermute | solution.py:304
  19.5 14.2 %collective-permute-start.6 = (bf16[192,256]{1,0:T(8,128)(2,1)S(1)}, bf16[192,256]{1,0:T(8,128)(2,1)S(1)}, u32[]{:S(2)}, u32[]{:S(2)}) collective-permute-start(bf16[192,256]{1,0:T(8,128)(2,1)S(1)} %get-tuple-element.22), channel_id=1, source_target_pairs={{0,8},{1,9},{2,10},{3,11},{4,12},{5,13},{6,14},{7,15},{8,0},{9,1},... | collective-permute-start | bytes 294920 | tf_op jit(solution)/shard_map/ppermute | solution.py:304
  20.0 13.6 %collective-permute-start.7 = (bf16[192,256]{1,0:T(8,128)(2,1)S(1)}, bf16[192,256]{1,0:T(8,128)(2,1)S(1)}, u32[]{:S(2)}, u32[]{:S(2)}) collective-permute-start(bf16[192,256]{1,0:T(8,128)(2,1)S(1)} %get-tuple-element.24), channel_id=1, source_target_pairs={{0,12},{1,13},{2,14},{3,15},{4,8},{5,9},{6,10},{7,11},{8,4},{9,5},... | collective-permute-start | bytes 294920 | tf_op jit(solution)/shard_map/ppermute | solution.py:304
  22.4 11.3 %all-to-all-start = ((f32[16,1,768]{2,1,0:T(1,128)}), f32[16,1,768]{2,1,0:T(1,128)S(1)}, u32[]{:S(2)}, u32[]{:S(2)}) async-start(f32[16,1,768]{2,1,0:T(1,128)} %get-tuple-element.21), calls=%async_computation | async-start | bytes 98304 | tf_op jit(solution)/shard_map/all_to_all | solution.py:319
  26.5 8.7 %collective-permute-start.9 = (bf16[768,256]{1,0:T(8,128)(2,1)S(1)}, bf16[768,256]{1,0:T(8,128)(2,1)S(1)}, u32[]{:S(2)}, u32[]{:S(2)}) collective-permute-start(bf16[768,256]{1,0:T(8,128)(2,1)S(1)} %collective-permute-done.8.refs_2_), channel_id=1, source_target_pairs={{0,1},{1,0},{2,3},{3,2},{4,5},{5,4},{6,7},{7,6},{8,9},{9,8},{10,11... | collective-permute-start | bytes 1179656 | tf_op jit(solution)/shard_map/ppermute | solution.py:304
  27.0 8.2 %collective-permute-start.11 = (bf16[192,256]{1,0:T(8,128)(2,1)S(1)}, bf16[192,256]{1,0:T(8,128)(2,1)S(1)}, u32[]{:S(2)}, u32[]{:S(2)}) collective-permute-start(bf16[192,256]{1,0:T(8,128)(2,1)S(1)} %get-tuple-element.28), channel_id=1, source_target_pairs={{0,4},{1,5},{2,6},{3,7},{4,0},{5,1},{6,2},{7,3},{8,12},{9,13},{10,... | collective-permute-start | bytes 294920 | tf_op jit(solution)/shard_map/ppermute | solution.py:304

commit v9 on v8

--- a/solution.py
+++ b/solution.py
@@ -75,23 +75,15 @@
     return functools.reduce(op, parts)
 
 
-def rows_kernel(outer, inner, tile, scale, place_ref, stacked_ref, *refs):
-    code = refs[:inner]
-    lam_ref = refs[inner]
-    parts = refs[inner + 1 : inner + 1 + outer]
-    scores, total = refs[inner + 1 + outer :]
-    rows, width = stacked_ref.shape
-    rows_dev = rows // outer
+def rows_tiles(scale, rows_ref, offset, code, norms, scores, total, put):
+    count_rows, width = total.shape
+    lanes = math.gcd(code[0].shape[0], 128)
     k_dev = code[0].shape[0]
-    lanes = math.gcd(k_dev, 128)
-    place = place_ref[0] // inner
-    norms = [
-        jnp.broadcast_to(norm_column(code[k][...], scale), (k_dev, lanes)).T[:1, :]
-        for k in range(inner)
-    ]
+    tile = math.gcd(count_rows, 384)
+    inner = len(code)
 
     def first_half(start, slot):
-        rows_here = stacked_ref[pl.ds(start, tile), :]
+        rows_here = rows_ref[pl.ds(pl.multiple_of(offset + start, tile), tile), :]
         top = None
         for k in range(inner):
             s = scale * nt_dot(rows_here, code[k][...]) - norms[k]
@@ -110,58 +102,118 @@
                 p.astype(jnp.bfloat16), code[k][...], preferred_element_type=jnp.float32
             )
         mass = jnp.sum(mass, axis=1, keepdims=True)
-        lam = jnp.broadcast_to(LN2 * (top + jnp.log2(mass)), (tile, lanes)).T[:1, :]
-        lam_ref[:, :, pl.ds(start, tile)] = jnp.broadcast_to(
-            lam.reshape(1, 1, tile), (lam_ref.shape[0], 1, tile)
-        )
+        put(start, tile, jnp.broadcast_to(LN2 * (top + jnp.log2(mass)), (tile, lanes)).T[:1, :])
         total[pl.ds(start, tile), :] = (acc * (1.0 / mass)).astype(jnp.bfloat16)
 
-    count = rows // tile
-    if count <= 4:
-        top = first_half(0, 0)
-        for t in range(count):
-            here = top
-            if t + 1 < count:
-                top = first_half((t + 1) * tile, (t + 1) * tile)
-            second_half(t * tile, t * tile, here)
+    if count_rows == tile:
+        second_half(0, 0, first_half(0, 0))
     else:
 
-        @pl.loop(0, count)
+        @pl.loop(0, count_rows // tile)
         def one_tile(t):
             start = pl.multiple_of(t * tile, tile)
             second_half(start, 0, first_half(start, 0))
 
-    for j in range(outer):
-        spot = pl.multiple_of((place ^ j) * rows_dev, rows_dev)
+
+def near_kernel(half, inner, scale, place_ref, *refs):
+    blocks, code, refs = refs[:half], refs[half : half + inner], refs[half + inner :]
+    lam_ref, norm_ref, parts, (rows_ref, scores, total) = refs[0], refs[1], refs[2:-3], refs[-3:]
+    rows_dev = blocks[0].shape[0]
+    k_dev = code[0].shape[0]
+    lanes = math.gcd(k_dev, 128)
+    place = place_ref[0] // inner
+
+    def spot(j):
+        return pl.ds(pl.multiple_of(((place ^ j) % half) * rows_dev, rows_dev), rows_dev)
+
+    for j, block in enumerate(blocks):
+        rows_ref[spot(j), :] = block[...]
+    norms = []
+    for k in range(inner):
+        column = norm_column(code[k][...], scale)
+        norms.append(jnp.broadcast_to(column, (k_dev, lanes)).T[:1, :])
+        norm_ref[:, k * k_dev : (k + 1) * k_dev] = norms[k]
+
+    def put(start, tile, lam):
+        lam_ref[:, pl.ds(start, tile)] = lam
+
+    rows_tiles(scale, rows_ref, 0, code, norms, scores, total, put)
+    for j in range(half):
+        parts[j][...] = total[spot(j), :]
+
+
+def far_kernel(half, inner, scale, place_ref, rows_ref, near_ref, norm_ref, *refs):
+    code, refs = refs[:inner], refs[inner:]
+    lam_ref, parts, (scores, total) = refs[0], refs[1:-2], refs[-2:]
+    k_dev = code[0].shape[0]
+    count, rows_dev = lam_ref.shape[0], parts[0].shape[0]
+    span = half * rows_dev
+    place = place_ref[0] // inner
+    side = place // half
+    near, far = side * span, (1 - side) * span
+    norms = [norm_ref[:, k * k_dev : (k + 1) * k_dev] for k in range(inner)]
+    step = math.gcd(span, 128)
+    lam_ref[:, :, pl.ds(pl.multiple_of(near, step), span)] = jnp.broadcast_to(
+        near_ref[...].reshape(1, 1, span), (count, 1, span)
+    )
+
+    def put(start, tile, lam):
+        lam_ref[:, :, pl.ds(pl.multiple_of(far + start, step), tile)] = jnp.broadcast_to(
+            lam.reshape(1, 1, tile), (count, 1, tile)
+        )
+
+    rows_tiles(scale, rows_ref, far, code, norms, scores, total, put)
+    for j in range(half):
+        spot = pl.multiple_of(((place ^ j) % half) * rows_dev, rows_dev)
         parts[j][...] = total[pl.ds(spot, rows_dev), :]
 
 
-def rows_calc(place, stacked, code, outer):
-    inner = len(code)
+def rows_call(body, half, code, shape, out, scratch, operands, name):
+    rows_dev, width = shape
+    span = half * rows_dev
+    entries = len(code) * code[0].shape[0]
+    vmem = pl.BlockSpec(memory_space=pltpu.VMEM)
+    return pl.pallas_call(
+        functools.partial(body, half, len(code), LOG2E * 3.0 / math.sqrt(width)),
+        out_shape=out + [jax.ShapeDtypeStruct(shape, jnp.bfloat16)] * half,
+        in_specs=[pl.BlockSpec(memory_space=pltpu.SMEM)] + [vmem] * (len(operands) - 1),
+        out_specs=[vmem] * (len(out) + half),
+        scratch_shapes=scratch
+        + [
+            pltpu.VMEM((math.gcd(span, 384), entries), jnp.float32),
+            pltpu.VMEM((span, width), jnp.bfloat16),
+        ],
+        compiler_params=pltpu.CompilerParams(vmem_limit_bytes=VMEM_LIMIT),
+        cost_estimate=pl.CostEstimate(
+            flops=4 * span * entries * width,
+            bytes_accessed=2 * (span + entries) * width,
+            transcendentals=span * entries,
+        ),
+        name=name,
+    )(*operands)
+
+
+def near_rows(place, blocks, code):
+    half, shape = len(blocks), blocks[0].shape
+    span = half * shape[0]
+    entries = len(code) * code[0].shape[0]
+    out = [
+        jax.ShapeDtypeStruct((1, span), jnp.float32),
+        jax.ShapeDtypeStruct((1, entries), jnp.float32),
+    ]
+    scratch = [pltpu.VMEM((span, shape[1]), jnp.bfloat16)]
+    operands = [place, *blocks, *code]
+    got = rows_call(near_kernel, half, code, shape, out, scratch, operands, "near_rows")
+    return got[0], got[1], got[2:]
+
+
+def far_rows(place, stacked, near, norms, code, half):
     rows, width = stacked.shape
-    rows_dev = rows // outer
-    entries = inner * code[0].shape[0]
-    tile = math.gcd(rows, 256)
-    vmem = pl.BlockSpec(memory_space=pltpu.VMEM)
-    out = pl.pallas_call(
-        functools.partial(rows_kernel, outer, inner, tile, LOG2E * 3.0 / math.sqrt(width)),
-        out_shape=[jax.ShapeDtypeStruct((outer * inner, 1, rows), jnp.float32)]
-        + [jax.ShapeDtypeStruct((rows_dev, width), jnp.bfloat16)] * outer,
-        in_specs=[pl.BlockSpec(memory_space=pltpu.SMEM)] + [vmem] * (1 + inner),
-        out_specs=[vmem] * (outer + 1),
-        scratch_shapes=[
-            pltpu.VMEM((min(rows, 4 * tile), entries), jnp.float32),
-            pltpu.VMEM((rows, width), jnp.bfloat16),
-        ],
-        compiler_params=pltpu.CompilerParams(vmem_limit_bytes=VMEM_LIMIT),
-        cost_estimate=pl.CostEstimate(
-            flops=4 * rows * entries * width,
-            bytes_accessed=2 * (rows + entries) * width,
-            transcendentals=rows * entries,
-        ),
-        name="rows_calc",
-    )(place, stacked, *code)
-    return out[0], out[1:]
+    shape = (rows // (2 * half), width)
+    out = [jax.ShapeDtypeStruct((2 * half * len(code), 1, rows), jnp.float32)]
+    operands = [place, stacked, near, norms, *code]
+    got = rows_call(far_kernel, half, code, shape, out, [], operands, "far_rows")
+    return got[0], got[1:]
 
 
 def norm_kernel(scale, code_ref, out_ref):
@@ -221,11 +273,10 @@
 
 def late_kernel(outer, inner, groups, tile, scale, order, place_ref, lam_ref, code_ref, norm_ref, *refs):
     emb, refs = refs[: len(groups)], refs[len(groups) :]
-    weighted_in, folded_in, parts, refs = refs[0], refs[1], refs[2 : 2 + outer], refs[2 + outer :]
-    shift_ref, occ_ref, soft_ref, own_ref, weighted, folded = refs
+    weighted_in, folded_in, shift_ref, occ_ref, weight_ref, own_ref, weighted, folded = refs
     k_dev = code_ref.shape[0]
-    rows_dev, width = parts[0].shape
     rows = lam_ref.shape[2]
+    rows_dev = rows // outer
     place, spoke = place_ref[0] // inner, place_ref[0] % inner
     weighted[...] = weighted_in[...]
     folded[...] = folded_in[...]
@@ -244,15 +295,37 @@
     lines += [mine] * (-len(lines) % 8)
     near = pltpu.roll(jnp.concatenate(lines, axis=0), rows - place * rows_dev, 1)
     near = near[:, : min(rows, -(-rows_dev // 128) * 128)]
-    columns = near.T
-    total = jnp.zeros((rows_dev, width), jnp.float32)
+    weight_ref[...] = near.T[:rows_dev, :]
+    own_ref[...] = near[outer : outer + 1, :rows_dev]
+
+
+def soft_kernel(weight_ref, *refs):
+    parts, soft_ref = refs[:-1], refs[-1]
+    total = jnp.zeros(soft_ref.shape, jnp.float32)
     for i, part in enumerate(parts):
-        total = total + columns[:rows_dev, i : i + 1] * part[...].astype(jnp.float32)
+        total = total + weight_ref[:, i : i + 1] * part[...].astype(jnp.float32)
     soft_ref[...] = total.astype(jnp.bfloat16)
-    own_ref[...] = near[outer : outer + 1, :rows_dev]
-
-
-def columns_calc(place, lam, code, norm, groups, emb, inner, sums=(), parts=(), order=()):
+
+
+def soft_calc(weights, parts):
+    vmem = pl.BlockSpec(memory_space=pltpu.VMEM)
+    shape = parts[0].shape
+    return pl.pallas_call(
+        soft_kernel,
+        out_shape=jax.ShapeDtypeStruct(shape, jnp.bfloat16),
+        in_specs=[vmem] * (1 + len(parts)),
+        out_specs=vmem,
+        compiler_params=pltpu.CompilerParams(vmem_limit_bytes=VMEM_LIMIT),
+        cost_estimate=pl.CostEstimate(
+            flops=2 * len(parts) * shape[0] * shape[1],
+            bytes_accessed=2 * (1 + len(parts)) * shape[0] * shape[1],
+            transcendentals=0,
+        ),
+        name="soft_calc",
+    )(weights, *parts)
+
+
+def columns_calc(place, lam, code, norm, groups, emb, inner, sums=(), order=()):
     k_dev, width = code.shape
     rows = emb[0].shape[0]
     outer = lam.shape[0] // inner
@@ -261,11 +334,11 @@
     totals = [((k_dev, width), jnp.float32), ((k_dev, lanes), jnp.float32)]
     if sums:
         body = late_kernel
-        rows_dev = parts[0].shape[0]
+        rows_dev = rows // outer
         out = [
             ((k_dev, width), jnp.bfloat16),
             ((1, k_dev), jnp.float32),
-            ((rows_dev, width), jnp.bfloat16),
+            ((rows_dev, -(-(outer + 1) // 8) * 8), jnp.float32),
             ((1, rows_dev), jnp.float32),
         ]
         scratch = [pltpu.VMEM(*x) for x in totals]
@@ -278,7 +351,7 @@
         ),
         out_shape=[jax.ShapeDtypeStruct(*x) for x in out],
         in_specs=[pl.BlockSpec(memory_space=pltpu.SMEM)]
-        + [vmem] * (3 + len(emb) + len(sums) + len(parts)),
+        + [vmem] * (3 + len(emb) + len(sums)),
         out_specs=[vmem] * len(out),
         scratch_shapes=scratch,
         compiler_params=pltpu.CompilerParams(vmem_limit_bytes=VMEM_LIMIT),
@@ -288,7 +361,7 @@
             transcendentals=len(emb) * rows * k_dev,
         ),
         name="columns_calc",
-    )(place, lam, code, norm, *emb, *sums, *parts)
+    )(place, lam, code, norm, *emb, *sums)
 
 
 def after(x, y):
@@ -306,27 +379,41 @@
     code_y = swap(codebook, 2)
     code_c = swap(codebook, 1)
     shape = (outer * embeddings.shape[0], embeddings.shape[1])
-    order = (*range(2, outer), 1, 0)
+    half = outer // 2
+    order = (*range(half, outer), *range(1, half), 0)
     own_rows, own_code = keep(embeddings, codebook)
-    blocks = [swap(embeddings, inner * j) for j in order[:-1]] + [own_rows]
-    stacked = stack(place, blocks, order, inner, shape)
+    arrived = {0: own_rows}
+    step = outer // 2
+    first = swap(embeddings, inner * step)
+    for j in range(1, half):
+        arrived[j] = swap(embeddings, inner * j)
+    waits = [arrived[j] for j in range(1, half)] + [first]
+    code_y, *waits = lax.optimization_barrier((code_y, *waits))
+    arrived.update({j + 1: w for j, w in enumerate(waits[:-1])})
+    arrived[step] = waits[-1]
+    for j in range(1, half):
+        arrived[step + j] = swap(arrived[step], inner * j)
+    code = [own_code, code_c, code_y, swap(code_y, 1)]
+    near, norms, near_parts = near_rows(place, [arrived[j] for j in range(half)], code)
+    arrived[0] = after(own_rows, near)
+    stacked = stack(place, [arrived[j] for j in order], order, inner, shape)
     stacked_y = swap(stacked, 2)
     stacked_c = swap(stacked, 1)
-    code = [own_code, code_c, code_y, swap(code_y, 1)]
-    lam, parts = rows_calc(place, stacked, code, outer)
+    lam, far_parts = far_rows(place, stacked, near, norms, code, half)
+    parts = [*near_parts, *far_parts]
 
     sent = [swap(parts[j], inner * j) for j in order[:-1]]
     lam = lax.all_to_all(lam, AXIS, 0, 0)
-    for part in sent[: outer - 2]:
-        lam = after(lam, part)
+    lam = after(lam, sent[0])
     norm = norm_calc(own_code, LOG2E * 3.0 / math.sqrt(codebook.shape[1]))
     stacked_yc = swap(stacked_y, 1)
     sums = columns_calc(
         place, lam, own_code, norm, (0, 1, 2), [stacked, stacked_c, stacked_y], inner
     )
-    shift, occupancy, soft, own_lse = columns_calc(
-        place, lam, own_code, norm, (3,), [stacked_yc], inner, sums, sent + [parts[0]], order
+    shift, occupancy, weights, own_lse = columns_calc(
+        place, lam, own_code, norm, (3,), [stacked_yc], inner, sums, order
     )
+    soft = soft_calc(weights, [*sent, parts[0]])
     return shift, occupancy.reshape(-1), soft, own_lse.reshape(-1)
 
 

time: 37 us -> 38.3 us (1.035)
  Pallas kernels: 6.7 us -> 9.26 us
  waiting for transfers between devices: 10.2 us -> 8.57 us
  starting transfers between devices: 17.3 us -> 17.7 us
    pallas_call x1 -> x3, Pallas kernels: 3.41 us -> 6.04 us  [the longest x2 5.22 us: rows_call(): pl.pallas_call(functools.partial(body, half, len(code), LOG2E * 3.0 / mat...]
    all_to_all x1, waiting for transfers between devices: 4.99 us -> 3.15 us  [on_device(): lam = lax.all_to_all(lam, AXIS, 0, 0)]
    ppermute x12, starting transfers between devices: 13.4 us -> 14.1 us  [swap(): return lax.ppermute(x, AXIS, [(i, i ^ step) for i in range(size)])]
  transfers between devices with their start and end apart: 13 -> 13, of which waited for: 4 -> 5; matrix products, arithmetic and copies ran while one was open for 0% -> 0% of each run, Pallas kernels for 14% -> 22%
where the time goes in v9:
time: 38.3 us; the launch traced here: 38.1 us
  starting transfers between devices  17.7 us (46%)
  Pallas kernels  9.26 us (24%)
  waiting for transfers between devices  8.57 us (22%)
  local copies, waits for them, and re-layouts  1.84 us (5%)
  between operations  0.7 us (2%)
    ppermute x12, starting transfers between devices, swap(): return lax.ppermute(x, AXIS, [(i, i ^ step) for i in range(size)])  14.1 us
    ppermute x12, waiting for transfers between devices, swap(): return lax.ppermute(x, AXIS, [(i, i ^ step) for i in range(size)])  5.41 us
    pallas_call x2, Pallas kernels, rows_call(): pl.pallas_call(functools.partial(body, half, len(code), LOG2E * 3.0 / mat...  5.22 us
    all_to_all x1, starting transfers between devices, on_device(): lam = lax.all_to_all(lam, AXIS, 0, 0)  3.6 us
    all_to_all x1, waiting for transfers between devices, on_device(): lam = lax.all_to_all(lam, AXIS, 0, 0)  3.15 us
    pallas_call x2, Pallas kernels, columns_calc(): pl.pallas_call(functools.partial(body, outer, inner, groups, tile, LOG2E...  3.01 us
    unnamed x4, local copies, waits for them, and re-layouts  1.84 us
    pallas_call x1, Pallas kernels, soft_calc(): pl.pallas_call(soft_kernel, out_shape=jax.ShapeDtypeStruct(shape, jnp.bfl...  0.83 us
  transfers between devices with their start and end apart: 13, of which 5 were waited for; matrix products, arithmetic and copies ran while one was open for 0% of the time, Pallas kernels for 22%

profile of v9, /device:TPU:0, one launch (start us, length us, event | category | flops | bytes accessed | tf_op | source)
XLA Modules:
  0.0 38.1 jit_solution(17308132304980591324)
XLA Ops:
  0.6 3.0 %collective-permute-start = (bf16[512,256]{1,0:T(8,128)(2,1)}, bf16[512,256]{1,0:T(8,128)(2,1)S(1)}, u32[]{:S(2)}, u32[]{:S(2)}) collective-permute-start(bf16[512,256]{1,0:T(8,128)(2,1)} %refs_1_.1), channel_id=1, source_target_pairs={{0,2},{1,3},{2,0},{3,1},{4,6},{5,7},{6,4},{7,5},{8,10},{9,11},{10,... | collective-permute-start | bytes 786440 | tf_op jit(solution)/shard_map/ppermute | solution.py:377
  3.7 1.6 %collective-permute-start.1 = (bf16[192,256]{1,0:T(8,128)(2,1)}, bf16[192,256]{1,0:T(8,128)(2,1)S(1)}, u32[]{:S(2)}, u32[]{:S(2)}) collective-permute-start(bf16[192,256]{1,0:T(8,128)(2,1)} %refs_0_.1), channel_id=1, source_target_pairs={{0,4},{1,5},{2,6},{3,7},{4,0},{5,1},{6,2},{7,3},{8,12},{9,13},{10,... | collective-permute-start | bytes 294920 | tf_op jit(solution)/shard_map/ppermute | solution.py:377
  5.2 2.6 %collective-permute-start.2 = (bf16[192,256]{1,0:T(8,128)(2,1)}, bf16[192,256]{1,0:T(8,128)(2,1)S(1)}, u32[]{:S(2)}, u32[]{:S(2)}) collective-permute-start(bf16[192,256]{1,0:T(8,128)(2,1)} %refs_0_.1), channel_id=1, source_target_pairs={{0,8},{1,9},{2,10},{3,11},{4,12},{5,13},{6,14},{7,15},{8,0},{9,1},... | collective-permute-start | bytes 294920 | tf_op jit(solution)/shard_map/ppermute | solution.py:377
  7.8 1.6 %collective-permute-done.1.refs_1_.refs_2_ = bf16[192,256]{1,0:T(8,128)(2,1)S(1)} collective-permute-done((bf16[192,256]{1,0:T(8,128)(2,1)}, bf16[192,256]{1,0:T(8,128)(2,1)S(1)}, u32[]{:S(2)}, u32[]{:S(2)}) %collective-permute-start.1) | collective-permute-done | bytes 98336 | tf_op jit(solution)/shard_map/ppermute | solution.py:377
  9.5 3.0 %collective-permute-done.2.refs_0_ = bf16[192,256]{1,0:T(8,128)(2,1)S(1)} collective-permute-done((bf16[192,256]{1,0:T(8,128)(2,1)}, bf16[192,256]{1,0:T(8,128)(2,1)S(1)}, u32[]{:S(2)}, u32[]{:S(2)}) %collective-permute-start.2) | collective-permute-done | bytes 98336 | tf_op jit(solution)/shard_map/ppermute | solution.py:377
  12.5 0.0 collective-permute-done.refs_4_.refs_2_
  12.5 0.0 collective-permute-start.5
  12.5 0.4 collective-permute-start.3
  12.8 0.9 %copy-done = bf16[512,256]{1,0:T(8,128)(2,1)S(1)} copy-done((bf16[512,256]{1,0:T(8,128)(2,1)S(1)}, bf16[512,256]{1,0:T(8,128)(2,1)}, u32[]{:S(2)}) %copy-start) | copy-done | bytes 262168
  13.8 0.9 %copy-done.1 = bf16[192,256]{1,0:T(8,128)(2,1)S(1)} copy-done((bf16[192,256]{1,0:T(8,128)(2,1)S(1)}, bf16[192,256]{1,0:T(8,128)(2,1)}, u32[]{:S(2)}) %copy-start.1) | copy-done | bytes 98328
  14.7 0.0 collective-permute-done.4.refs_3_.refs_1_
  14.7 2.3 %near_rows.1 = (f32[1,384]{1,0:T(1,128)S(1)}, f32[1,2048]{1,0:T(1,128)S(1)}, bf16[192,256]{1,0:T(8,128)(2,1)S(1)}, bf16[192,256]{1,0:T(8,128)(2,1)S(1)}) custom-call(s32[1]{0:T(128)} %bitcast.place_ref, bf16[192,256]{1,0:T(8,128)(2,1)S(1)} %get-tuple-element.30.refs_0_.refs_3_, bf16[192,256]{1,0:T(8,128)(2,1)S(1)} %collective-permute-done.1.refs_1_.refs_2_, ...), custom_call_target="tpu_custom_call" | custom-call | flops 805306368 | bytes 1245184 | tf_op jit(solution)/shard_map/near_rows/pallas_call | solution.py:176
  17.1 0.6 %collective-permute-done.3.refs_1_ = bf16[192,256]{1,0:T(8,128)(2,1)S(1)} collective-permute-done((bf16[192,256]{1,0:T(8,128)(2,1)S(1)}, bf16[192,256]{1,0:T(8,128)(2,1)S(1)}, u32[]{:S(2)}, u32[]{:S(2)}) %collective-permute-start.3) | collective-permute-done | bytes 98336 | tf_op jit(solution)/shard_map/ppermute | solution.py:377
  17.7 0.6 %collective-permute-start.7 = (bf16[768,256]{1,0:T(8,128)(2,1)S(1)}, bf16[768,256]{1,0:T(8,128)(2,1)S(1)}, u32[]{:S(2)}, u32[]{:S(2)}) collective-permute-start(bf16[768,256]{1,0:T(8,128)(2,1)S(1)} %stack.1.rows_ref.refs_0_), channel_id=1, source_target_pairs={{0,2},{1,3},{2,0},{3,1},{4,6},{5,7},{6,4},{7,5},{8,10},{9,11},{10,... | collective-permute-start | bytes 1179656 | tf_op jit(solution)/shard_map/ppermute | solution.py:377
  18.3 2.9 %far_rows.1 = (f32[16,1,768]{2,1,0:T(1,128)}, bf16[192,256]{1,0:T(8,128)(2,1)S(1)}, bf16[192,256]{1,0:T(8,128)(2,1)S(1)}) custom-call(s32[1]{0:T(128)} %bitcast.place_ref, bf16[768,256]{1,0:T(8,128)(2,1)S(1)} %stack.1.rows_ref.refs_0_, f32[1,384]{1,0:T(1,128)S(1)} %get-tuple-element.29.near_ref, f32[1,2048]{1,0:T(1,128)S(1)} %get-tuple-element.31.norm_ref, ...), custom_call_target="tpu_custom_call" | custom-call | flops 805306368 | bytes 1245184 | tf_op jit(solution)/shard_map/far_rows/pallas_call | solution.py:176
  21.2 2.2 %collective-permute-start.6 = (bf16[192,256]{1,0:T(8,128)(2,1)S(1)}, bf16[192,256]{1,0:T(8,128)(2,1)S(1)}, u32[]{:S(2)}, u32[]{:S(2)}) collective-permute-start(bf16[192,256]{1,0:T(8,128)(2,1)S(1)} %get-tuple-element.33), channel_id=1, source_target_pairs={{0,8},{1,9},{2,10},{3,11},{4,12},{5,13},{6,14},{7,15},{8,0},{9,1},... | collective-permute-start | bytes 294920 | tf_op jit(solution)/shard_map/ppermute | solution.py:377
  23.3 3.6 %all-to-all-start = ((f32[16,1,768]{2,1,0:T(1,128)}), f32[16,1,768]{2,1,0:T(1,128)S(1)}, u32[]{:S(2)}, u32[]{:S(2)}) async-start(f32[16,1,768]{2,1,0:T(1,128)} %get-tuple-element.32), calls=%async_computation | async-start | bytes 98304 | tf_op jit(solution)/shard_map/all_to_all | solution.py:406
  26.9 0.1 norm_calc.1.norm_ref
  27.1 3.8 %collective-permute-start.10 = (bf16[192,256]{1,0:T(8,128)(2,1)S(1)}, bf16[192,256]{1,0:T(8,128)(2,1)S(1)}, u32[]{:S(2)}, u32[]{:S(2)}) collective-permute-start(bf16[192,256]{1,0:T(8,128)(2,1)S(1)} %get-tuple-element.40), channel_id=1, source_target_pairs={{0,12},{1,13},{2,14},{3,15},{4,8},{5,9},{6,10},{7,11},{8,4},{9,5},... | collective-permute-start | bytes 294920 | tf_op jit(solution)/shard_map/ppermute | solution.py:377
  30.9 3.2 %all-to-all-done.lam_ref = f32[16,1,768]{2,1,0:T(1,128)S(1)} async-done(((f32[16,1,768]{2,1,0:T(1,128)}), f32[16,1,768]{2,1,0:T(1,128)S(1)}, u32[]{:S(2)}, u32[]{:S(2)}) %all-to-all-start) | async-done | bytes 49184 | tf_op jit(solution)/shard_map/all_to_all | solution.py:406
  34.1 1.5 %columns_calc.2 = (f32[512,256]{1,0:T(8,128)S(1)}, f32[512,128]{1,0:T(8,128)S(1)}) custom-call(s32[1]{0:T(128)} %bitcast.place_ref, f32[16,1,768]{2,1,0:T(1,128)S(1)} %all-to-all-done.lam_ref, bf16[512,256]{1,0:T(8,128)(2,1)S(1)} %get-tuple-element.27.refs_2_.refs_0_.code_ref, f32[512,128]{1,0:T(8,128)S(1)} %norm_calc.1.norm_ref, ...), custom_call_target="tpu_custom_call" | custom-call | flops 19327352832 | bytes 1703936 | tf_op jit(solution)/shard_map/columns_calc/pallas_call | solution.py:348
  35.6 0.2 collective-permute-done.8.refs_0_
  35.8 1.5 %columns_calc.3 = (bf16[512,256]{1,0:T(8,128)(2,1)}, f32[1,512]{1,0:T(1,128)}, f32[192,8]{1,0:T(8,128)S(1)}, f32[1,192]{1,0:T(1,128)}) custom-call(s32[1]{0:T(128)} %bitcast.place_ref, f32[16,1,768]{2,1,0:T(1,128)S(1)} %all-to-all-done.lam_ref, bf16[512,256]{1,0:T(8,128)(2,1)S(1)} %get-tuple-element.27.refs_2_.refs_0_.code_ref, ...), custom_call_target="tpu_custom_call" | custom-call | flops 402653184 | bytes 917504 | tf_op jit(solution)/shard_map/columns_calc/pallas_call | solution.py:348
  37.3 0.8 %soft_calc.1 = bf16[192,256]{1,0:T(8,128)(2,1)} custom-call(f32[192,8]{1,0:T(8,128)S(1)} %get-tuple-element.39.weight_ref, bf16[192,256]{1,0:T(8,128)(2,1)S(1)} %collective-permute-done.6.refs_0_, bf16[192,256]{1,0:T(8,128)(2,1)S(1)} %collective-permute-done.10.refs_1_, bf16[192,256]{1,0:T(8,128)(2,1)S(1)} %collective-permute-done.11.refs_2_, ...), custom_call_target="tpu_custom_call" | custom-call | flops 393216 | bytes 491520 | tf_op jit(solution)/shard_map/soft_calc/pallas_call | solution.py:313
  (14 shorter events, 0.1 us)
Async XLA Ops:
  0.6 11.8 %collective-permute-start = (bf16[512,256]{1,0:T(8,128)(2,1)}, bf16[512,256]{1,0:T(8,128)(2,1)S(1)}, u32[]{:S(2)}, u32[]{:S(2)}) collective-permute-start(bf16[512,256]{1,0:T(8,128)(2,1)} %refs_1_.1), channel_id=1, source_target_pairs={{0,2},{1,3},{2,0},{3,1},{4,6},{5,7},{6,4},{7,5},{8,10},{9,11},{10,... | collective-permute-start | bytes 786440 | tf_op jit(solution)/shard_map/ppermute | solution.py:377
  3.7 5.8 %collective-permute-start.1 = (bf16[192,256]{1,0:T(8,128)(2,1)}, bf16[192,256]{1,0:T(8,128)(2,1)S(1)}, u32[]{:S(2)}, u32[]{:S(2)}) collective-permute-start(bf16[192,256]{1,0:T(8,128)(2,1)} %refs_0_.1), channel_id=1, source_target_pairs={{0,4},{1,5},{2,6},{3,7},{4,0},{5,1},{6,2},{7,3},{8,12},{9,13},{10,... | collective-permute-start | bytes 294920 | tf_op jit(solution)/shard_map/ppermute | solution.py:377
  5.2 7.2 %collective-permute-start.2 = (bf16[192,256]{1,0:T(8,128)(2,1)}, bf16[192,256]{1,0:T(8,128)(2,1)S(1)}, u32[]{:S(2)}, u32[]{:S(2)}) collective-permute-start(bf16[192,256]{1,0:T(8,128)(2,1)} %refs_0_.1), channel_id=1, source_target_pairs={{0,8},{1,9},{2,10},{3,11},{4,12},{5,13},{6,14},{7,15},{8,0},{9,1},... | collective-permute-start | bytes 294920 | tf_op jit(solution)/shard_map/ppermute | solution.py:377
  7.8 6.9 %collective-permute-start.4 = (bf16[512,256]{1,0:T(8,128)(2,1)}, bf16[512,256]{1,0:T(8,128)(2,1)S(1)}, u32[]{:S(2)}, u32[]{:S(2)}) collective-permute-start(bf16[512,256]{1,0:T(8,128)(2,1)} %refs_1_.1), channel_id=1, source_target_pairs={{0,1},{1,0},{2,3},{3,2},{4,5},{5,4},{6,7},{7,6},{8,9},{9,8},{10,11... | collective-permute-start | bytes 786440 | tf_op jit(solution)/shard_map/ppermute | solution.py:377
  12.5 2.3 %collective-permute-start.5 = (bf16[512,256]{1,0:T(8,128)(2,1)S(1)}, bf16[512,256]{1,0:T(8,128)(2,1)S(1)}, u32[]{:S(2)}, u32[]{:S(2)}) collective-permute-start(bf16[512,256]{1,0:T(8,128)(2,1)S(1)} %collective-permute-done.refs_4_.refs_2_), channel_id=1, source_target_pairs={{0,1},{1,0},{2,3},{3,2},{4,5},{5,4},{6,7},{7,6},{8,9},{9,8},{10,11... | collective-permute-start | bytes 786440 | tf_op jit(solution)/shard_map/ppermute | solution.py:377
  12.5 5.2 %collective-permute-start.3 = (bf16[192,256]{1,0:T(8,128)(2,1)S(1)}, bf16[192,256]{1,0:T(8,128)(2,1)S(1)}, u32[]{:S(2)}, u32[]{:S(2)}) collective-permute-start(bf16[192,256]{1,0:T(8,128)(2,1)S(1)} %collective-permute-done.2.refs_0_), channel_id=1, source_target_pairs={{0,4},{1,5},{2,6},{3,7},{4,0},{5,1},{6,2},{7,3},{8,12},{9,13},{10,... | collective-permute-start | bytes 294920 | tf_op jit(solution)/shard_map/ppermute | solution.py:377
  12.8 0.9 %copy-start = (bf16[512,256]{1,0:T(8,128)(2,1)S(1)}, bf16[512,256]{1,0:T(8,128)(2,1)}, u32[]{:S(2)}) copy-start(bf16[512,256]{1,0:T(8,128)(2,1)} %refs_1_.1) | copy-start | bytes 786436
  13.8 0.9 %copy-start.1 = (bf16[192,256]{1,0:T(8,128)(2,1)S(1)}, bf16[192,256]{1,0:T(8,128)(2,1)}, u32[]{:S(2)}) copy-start(bf16[192,256]{1,0:T(8,128)(2,1)} %refs_0_.1) | copy-start | bytes 294916
  17.7 16.3 %collective-permute-start.7 = (bf16[768,256]{1,0:T(8,128)(2,1)S(1)}, bf16[768,256]{1,0:T(8,128)(2,1)S(1)}, u32[]{:S(2)}, u32[]{:S(2)}) collective-permute-start(bf16[768,256]{1,0:T(8,128)(2,1)S(1)} %stack.1.rows_ref.refs_0_), channel_id=1, source_target_pairs={{0,2},{1,3},{2,0},{3,1},{4,6},{5,7},{6,4},{7,5},{8,10},{9,11},{10,... | collective-permute-start | bytes 1179656 | tf_op jit(solution)/shard_map/ppermute | solution.py:377
  18.3 15.8 %collective-permute-start.9 = (bf16[768,256]{1,0:T(8,128)(2,1)S(1)}, bf16[768,256]{1,0:T(8,128)(2,1)S(1)}, u32[]{:S(2)}, u32[]{:S(2)}) collective-permute-start(bf16[768,256]{1,0:T(8,128)(2,1)S(1)} %stack.1.rows_ref.refs_0_), channel_id=1, source_target_pairs={{0,1},{1,0},{2,3},{3,2},{4,5},{5,4},{6,7},{7,6},{8,9},{9,8},{10,11... | collective-permute-start | bytes 1179656 | tf_op jit(solution)/shard_map/ppermute | solution.py:377
  21.2 12.9 %collective-permute-start.6 = (bf16[192,256]{1,0:T(8,128)(2,1)S(1)}, bf16[192,256]{1,0:T(8,128)(2,1)S(1)}, u32[]{:S(2)}, u32[]{:S(2)}) collective-permute-start(bf16[192,256]{1,0:T(8,128)(2,1)S(1)} %get-tuple-element.33), channel_id=1, source_target_pairs={{0,8},{1,9},{2,10},{3,11},{4,12},{5,13},{6,14},{7,15},{8,0},{9,1},... | collective-permute-start | bytes 294920 | tf_op jit(solution)/shard_map/ppermute | solution.py:377
  23.3 10.7 %all-to-all-start = ((f32[16,1,768]{2,1,0:T(1,128)}), f32[16,1,768]{2,1,0:T(1,128)S(1)}, u32[]{:S(2)}, u32[]{:S(2)}) async-start(f32[16,1,768]{2,1,0:T(1,128)} %get-tuple-element.32), calls=%async_computation | async-start | bytes 98304 | tf_op jit(solution)/shard_map/all_to_all | solution.py:406
  27.1 10.2 %collective-permute-start.10 = (bf16[192,256]{1,0:T(8,128)(2,1)S(1)}, bf16[192,256]{1,0:T(8,128)(2,1)S(1)}, u32[]{:S(2)}, u32[]{:S(2)}) collective-permute-start(bf16[192,256]{1,0:T(8,128)(2,1)S(1)} %get-tuple-element.40), channel_id=1, source_target_pairs={{0,12},{1,13},{2,14},{3,15},{4,8},{5,9},{6,10},{7,11},{8,4},{9,5},... | collective-permute-start | bytes 294920 | tf_op jit(solution)/shard_map/ppermute | solution.py:377
  30.9 6.4 %collective-permute-start.11 = (bf16[192,256]{1,0:T(8,128)(2,1)S(1)}, bf16[192,256]{1,0:T(8,128)(2,1)S(1)}, u32[]{:S(2)}, u32[]{:S(2)}) collective-permute-start(bf16[192,256]{1,0:T(8,128)(2,1)S(1)} %get-tuple-element.41), channel_id=1, source_target_pairs={{0,4},{1,5},{2,6},{3,7},{4,0},{5,1},{6,2},{7,3},{8,12},{9,13},{10,... | collective-permute-start | bytes 294920 | tf_op jit(solution)/shard_map/ppermute | solution.py:377
  34.0 1.7 %collective-permute-start.8 = (bf16[768,256]{1,0:T(8,128)(2,1)S(1)}, bf16[768,256]{1,0:T(8,128)(2,1)S(1)}, u32[]{:S(2)}, u32[]{:S(2)}) collective-permute-start(bf16[768,256]{1,0:T(8,128)(2,1)S(1)} %collective-permute-done.7.refs_2_), channel_id=1, source_target_pairs={{0,1},{1,0},{2,3},{3,2},{4,5},{5,4},{6,7},{7,6},{8,9},{9,8},{10,11... | collective-permute-start | bytes 1179656 | tf_op jit(solution)/shard_map/ppermute | solution.py:377

commit v10 on v8

--- a/solution.py
+++ b/solution.py
@@ -221,11 +221,10 @@
 
 def late_kernel(outer, inner, groups, tile, scale, order, place_ref, lam_ref, code_ref, norm_ref, *refs):
     emb, refs = refs[: len(groups)], refs[len(groups) :]
-    weighted_in, folded_in, parts, refs = refs[0], refs[1], refs[2 : 2 + outer], refs[2 + outer :]
-    shift_ref, occ_ref, soft_ref, own_ref, weighted, folded = refs
+    weighted_in, folded_in, shift_ref, occ_ref, weight_ref, own_ref, weighted, folded = refs
     k_dev = code_ref.shape[0]
-    rows_dev, width = parts[0].shape
     rows = lam_ref.shape[2]
+    rows_dev = rows // outer
     place, spoke = place_ref[0] // inner, place_ref[0] % inner
     weighted[...] = weighted_in[...]
     folded[...] = folded_in[...]
@@ -244,15 +243,37 @@
     lines += [mine] * (-len(lines) % 8)
     near = pltpu.roll(jnp.concatenate(lines, axis=0), rows - place * rows_dev, 1)
     near = near[:, : min(rows, -(-rows_dev // 128) * 128)]
-    columns = near.T
-    total = jnp.zeros((rows_dev, width), jnp.float32)
+    weight_ref[...] = near.T[:rows_dev, :]
+    own_ref[...] = near[outer : outer + 1, :rows_dev]
+
+
+def soft_kernel(weight_ref, *refs):
+    parts, soft_ref = refs[:-1], refs[-1]
+    total = jnp.zeros(soft_ref.shape, jnp.float32)
     for i, part in enumerate(parts):
-        total = total + columns[:rows_dev, i : i + 1] * part[...].astype(jnp.float32)
+        total = total + weight_ref[:, i : i + 1] * part[...].astype(jnp.float32)
     soft_ref[...] = total.astype(jnp.bfloat16)
-    own_ref[...] = near[outer : outer + 1, :rows_dev]
-
-
-def columns_calc(place, lam, code, norm, groups, emb, inner, sums=(), parts=(), order=()):
+
+
+def soft_calc(weights, parts):
+    vmem = pl.BlockSpec(memory_space=pltpu.VMEM)
+    shape = parts[0].shape
+    return pl.pallas_call(
+        soft_kernel,
+        out_shape=jax.ShapeDtypeStruct(shape, jnp.bfloat16),
+        in_specs=[vmem] * (1 + len(parts)),
+        out_specs=vmem,
+        compiler_params=pltpu.CompilerParams(vmem_limit_bytes=VMEM_LIMIT),
+        cost_estimate=pl.CostEstimate(
+            flops=2 * len(parts) * shape[0] * shape[1],
+            bytes_accessed=2 * (1 + len(parts)) * shape[0] * shape[1],
+            transcendentals=0,
+        ),
+        name="soft_calc",
+    )(weights, *parts)
+
+
+def columns_calc(place, lam, code, norm, groups, emb, inner, sums=(), order=()):
     k_dev, width = code.shape
     rows = emb[0].shape[0]
     outer = lam.shape[0] // inner
@@ -261,11 +282,11 @@
     totals = [((k_dev, width), jnp.float32), ((k_dev, lanes), jnp.float32)]
     if sums:
         body = late_kernel
-        rows_dev = parts[0].shape[0]
+        rows_dev = rows // outer
         out = [
             ((k_dev, width), jnp.bfloat16),
             ((1, k_dev), jnp.float32),
-            ((rows_dev, width), jnp.bfloat16),
+            ((rows_dev, -(-(outer + 1) // 8) * 8), jnp.float32),
             ((1, rows_dev), jnp.float32),
         ]
         scratch = [pltpu.VMEM(*x) for x in totals]
@@ -278,7 +299,7 @@
         ),
         out_shape=[jax.ShapeDtypeStruct(*x) for x in out],
         in_specs=[pl.BlockSpec(memory_space=pltpu.SMEM)]
-        + [vmem] * (3 + len(emb) + len(sums) + len(parts)),
+        + [vmem] * (3 + len(emb) + len(sums)),
         out_specs=[vmem] * len(out),
         scratch_shapes=scratch,
         compiler_params=pltpu.CompilerParams(vmem_limit_bytes=VMEM_LIMIT),
@@ -288,7 +309,7 @@
             transcendentals=len(emb) * rows * k_dev,
         ),
         name="columns_calc",
-    )(place, lam, code, norm, *emb, *sums, *parts)
+    )(place, lam, code, norm, *emb, *sums)
 
 
 def after(x, y):
@@ -317,16 +338,16 @@
 
     sent = [swap(parts[j], inner * j) for j in order[:-1]]
     lam = lax.all_to_all(lam, AXIS, 0, 0)
-    for part in sent[: outer - 2]:
-        lam = after(lam, part)
+    lam = after(lam, sent[0])
     norm = norm_calc(own_code, LOG2E * 3.0 / math.sqrt(codebook.shape[1]))
     stacked_yc = swap(stacked_y, 1)
     sums = columns_calc(
         place, lam, own_code, norm, (0, 1, 2), [stacked, stacked_c, stacked_y], inner
     )
-    shift, occupancy, soft, own_lse = columns_calc(
-        place, lam, own_code, norm, (3,), [stacked_yc], inner, sums, sent + [parts[0]], order
+    shift, occupancy, weights, own_lse = columns_calc(
+        place, lam, own_code, norm, (3,), [stacked_yc], inner, sums, order
     )
+    soft = soft_calc(weights, [*sent, parts[0]])
     return shift, occupancy.reshape(-1), soft, own_lse.reshape(-1)
 
 

time: 37 us -> 36.1 us (0.976)
  waiting for transfers between devices: 10.2 us -> 8.96 us
  Pallas kernels: 6.7 us -> 7.44 us
  starting transfers between devices: 17.3 us -> 16.9 us
    all_to_all x1, waiting for transfers between devices: 4.99 us -> 2.93 us  [on_device(): lam = lax.all_to_all(lam, AXIS, 0, 0)]
    ppermute x12, starting transfers between devices: 13.4 us -> 12.1 us  [swap(): return lax.ppermute(x, AXIS, [(i, i ^ step) for i in range(size)])]
    all_to_all x1, starting transfers between devices: 3.95 us -> 4.85 us  [on_device(): lam = lax.all_to_all(lam, AXIS, 0, 0)]
    pallas_call x0 -> x1, Pallas kernels: none -> 0.83 us  [soft_calc(): pl.pallas_call(soft_kernel, out_shape=jax.ShapeDtypeStruct(shape, jnp.bfl...]
    ppermute x12, waiting for transfers between devices: 5.22 us -> 6.03 us  [swap(): return lax.ppermute(x, AXIS, [(i, i ^ step) for i in range(size)])]
  transfers between devices with their start and end apart: 13 -> 13, of which waited for: 4 -> 6; matrix products, arithmetic and copies ran while one was open for 0% -> 0% of each run, Pallas kernels for 14% -> 18%
where the time goes in v10:
time: 36.1 us; the launch traced here: 35.8 us
  starting transfers between devices  16.9 us (47%)
  waiting for transfers between devices  8.96 us (25%)
  Pallas kernels  7.44 us (21%)
  local copies, waits for them, and re-layouts  1.84 us (5%)
  between operations  0.69 us (2%)
    ppermute x12, starting transfers between devices, swap(): return lax.ppermute(x, AXIS, [(i, i ^ step) for i in range(size)])  12.1 us
    ppermute x12, waiting for transfers between devices, swap(): return lax.ppermute(x, AXIS, [(i, i ^ step) for i in range(size)])  6.03 us
    all_to_all x1, starting transfers between devices, on_device(): lam = lax.all_to_all(lam, AXIS, 0, 0)  4.85 us
    pallas_call x1, Pallas kernels, rows_calc(): pl.pallas_call(functools.partial(rows_kernel, outer, inner, tile, LOG2E *...  3.41 us
    pallas_call x2, Pallas kernels, columns_calc(): pl.pallas_call(functools.partial(body, outer, inner, groups, tile, LOG2E...  3.01 us
    all_to_all x1, waiting for transfers between devices, on_device(): lam = lax.all_to_all(lam, AXIS, 0, 0)  2.93 us
    unnamed x4, local copies, waits for them, and re-layouts  1.84 us
    pallas_call x1, Pallas kernels, soft_calc(): pl.pallas_call(soft_kernel, out_shape=jax.ShapeDtypeStruct(shape, jnp.bfl...  0.83 us
  transfers between devices with their start and end apart: 13, of which 6 were waited for; matrix products, arithmetic and copies ran while one was open for 0% of the time, Pallas kernels for 18%

profile of v10, /device:TPU:0, one launch (start us, length us, event | category | flops | bytes accessed | tf_op | source)
XLA Modules:
  0.0 35.8 jit_solution(1039995593429162809)
XLA Ops:
  0.6 3.0 %collective-permute-start.4 = (bf16[512,256]{1,0:T(8,128)(2,1)}, bf16[512,256]{1,0:T(8,128)(2,1)S(1)}, u32[]{:S(2)}, u32[]{:S(2)}) collective-permute-start(bf16[512,256]{1,0:T(8,128)(2,1)} %refs_1_.1), channel_id=1, source_target_pairs={{0,2},{1,3},{2,0},{3,1},{4,6},{5,7},{6,4},{7,5},{8,10},{9,11},{10,... | collective-permute-start | bytes 786440 | tf_op jit(solution)/shard_map/ppermute | solution.py:325
  3.7 3.6 %collective-permute-start.1 = (bf16[192,256]{1,0:T(8,128)(2,1)}, bf16[192,256]{1,0:T(8,128)(2,1)S(1)}, u32[]{:S(2)}, u32[]{:S(2)}) collective-permute-start(bf16[192,256]{1,0:T(8,128)(2,1)} %refs_0_.1), channel_id=1, source_target_pairs={{0,12},{1,13},{2,14},{3,15},{4,8},{5,9},{6,10},{7,11},{8,4},{9,5},... | collective-permute-start | bytes 294920 | tf_op jit(solution)/shard_map/ppermute | solution.py:325
  7.3 0.0 collective-permute-start
  7.3 0.8 %collective-permute-start.2 = (bf16[192,256]{1,0:T(8,128)(2,1)}, bf16[192,256]{1,0:T(8,128)(2,1)S(1)}, u32[]{:S(2)}, u32[]{:S(2)}) collective-permute-start(bf16[192,256]{1,0:T(8,128)(2,1)} %refs_0_.1), channel_id=1, source_target_pairs={{0,4},{1,5},{2,6},{3,7},{4,0},{5,1},{6,2},{7,3},{8,12},{9,13},{10,... | collective-permute-start | bytes 294920 | tf_op jit(solution)/shard_map/ppermute | solution.py:325
  8.1 0.9 %copy-done = bf16[512,256]{1,0:T(8,128)(2,1)S(1)} copy-done((bf16[512,256]{1,0:T(8,128)(2,1)S(1)}, bf16[512,256]{1,0:T(8,128)(2,1)}, u32[]{:S(2)}) %copy-start) | copy-done | bytes 262168
  9.0 0.9 %copy-done.1 = bf16[192,256]{1,0:T(8,128)(2,1)S(1)} copy-done((bf16[192,256]{1,0:T(8,128)(2,1)S(1)}, bf16[192,256]{1,0:T(8,128)(2,1)}, u32[]{:S(2)}) %copy-start.1) | copy-done | bytes 98328
  9.9 0.2 collective-permute-done.4.refs_2_
  10.2 0.3 collective-permute-start.5
  10.5 0.9 %collective-permute-done.1.refs_1_ = bf16[192,256]{1,0:T(8,128)(2,1)S(1)} collective-permute-done((bf16[192,256]{1,0:T(8,128)(2,1)}, bf16[192,256]{1,0:T(8,128)(2,1)S(1)}, u32[]{:S(2)}, u32[]{:S(2)}) %collective-permute-start.1) | collective-permute-done | bytes 98336 | tf_op jit(solution)/shard_map/ppermute | solution.py:325
  11.4 4.1 %collective-permute-done.refs_0_ = bf16[192,256]{1,0:T(8,128)(2,1)S(1)} collective-permute-done((bf16[192,256]{1,0:T(8,128)(2,1)}, bf16[192,256]{1,0:T(8,128)(2,1)S(1)}, u32[]{:S(2)}, u32[]{:S(2)}) %collective-permute-start) | collective-permute-done | bytes 98336 | tf_op jit(solution)/shard_map/ppermute | solution.py:325
  15.5 0.6 %collective-permute-start.7 = (bf16[768,256]{1,0:T(8,128)(2,1)S(1)}, bf16[768,256]{1,0:T(8,128)(2,1)S(1)}, u32[]{:S(2)}, u32[]{:S(2)}) collective-permute-start(bf16[768,256]{1,0:T(8,128)(2,1)S(1)} %stack.1.stacked_ref.refs_0_), channel_id=1, source_target_pairs={{0,2},{1,3},{2,0},{3,1},{4,6},{5,7},{6,4},{7,5},{8,10},{9,11},{10,... | collective-permute-start | bytes 1179656 | tf_op jit(solution)/shard_map/ppermute | solution.py:325
  16.1 0.0 collective-permute-start.9
  16.1 3.4 %rows_calc.1 = (f32[16,1,768]{2,1,0:T(1,128)}, bf16[192,256]{1,0:T(8,128)(2,1)S(1)}, bf16[192,256]{1,0:T(8,128)(2,1)S(1)}, bf16[192,256]{1,0:T(8,128)(2,1)S(1)}, bf16[192,256]{1,0:T(8,128)(2,1)S(1)}) custom-call(s32[1]{0:T(128)} %bitcast.place_ref, bf16[768,256]{1,0:T(8,128)(2,1)S(1)} %stack.1.stacked_ref.refs_0_, ...), custom_call_target="tpu_custom_call" | custom-call | flops 1610612736 | bytes 1441792 | tf_op jit(solution)/shard_map/rows_calc/pallas_call | solution.py:146
  19.5 0.5 %collective-permute-start.6 = (bf16[192,256]{1,0:T(8,128)(2,1)S(1)}, bf16[192,256]{1,0:T(8,128)(2,1)S(1)}, u32[]{:S(2)}, u32[]{:S(2)}) collective-permute-start(bf16[192,256]{1,0:T(8,128)(2,1)S(1)} %get-tuple-element.21), channel_id=1, source_target_pairs={{0,8},{1,9},{2,10},{3,11},{4,12},{5,13},{6,14},{7,15},{8,0},{9,1},... | collective-permute-start | bytes 294920 | tf_op jit(solution)/shard_map/ppermute | solution.py:325
  20.0 4.8 %all-to-all-start = ((f32[16,1,768]{2,1,0:T(1,128)}), f32[16,1,768]{2,1,0:T(1,128)S(1)}, u32[]{:S(2)}, u32[]{:S(2)}) async-start(f32[16,1,768]{2,1,0:T(1,128)} %get-tuple-element.20), calls=%async_computation | async-start | bytes 98304 | tf_op jit(solution)/shard_map/all_to_all | solution.py:340
  24.9 0.1 norm_calc.1.norm_ref
  25.0 0.8 %collective-permute-done.7.refs_2_ = bf16[768,256]{1,0:T(8,128)(2,1)S(1)} collective-permute-done((bf16[768,256]{1,0:T(8,128)(2,1)S(1)}, bf16[768,256]{1,0:T(8,128)(2,1)S(1)}, u32[]{:S(2)}, u32[]{:S(2)}) %collective-permute-start.7) | collective-permute-done | bytes 393248 | tf_op jit(solution)/shard_map/ppermute | solution.py:325
  25.8 3.2 %collective-permute-start.10 = (bf16[192,256]{1,0:T(8,128)(2,1)S(1)}, bf16[192,256]{1,0:T(8,128)(2,1)S(1)}, u32[]{:S(2)}, u32[]{:S(2)}) collective-permute-start(bf16[192,256]{1,0:T(8,128)(2,1)S(1)} %get-tuple-element.28), channel_id=1, source_target_pairs={{0,12},{1,13},{2,14},{3,15},{4,8},{5,9},{6,10},{7,11},{8,4},{9,5},... | collective-permute-start | bytes 294920 | tf_op jit(solution)/shard_map/ppermute | solution.py:325
  29.0 0.0 collective-permute-start.11
  29.0 2.9 %all-to-all-done.lam_ref = f32[16,1,768]{2,1,0:T(1,128)S(1)} async-done(((f32[16,1,768]{2,1,0:T(1,128)}), f32[16,1,768]{2,1,0:T(1,128)S(1)}, u32[]{:S(2)}, u32[]{:S(2)}) %all-to-all-start) | async-done | bytes 49184 | tf_op jit(solution)/shard_map/all_to_all | solution.py:340
  31.9 1.5 %columns_calc.2 = (f32[512,256]{1,0:T(8,128)S(1)}, f32[512,128]{1,0:T(8,128)S(1)}) custom-call(s32[1]{0:T(128)} %bitcast.place_ref, f32[16,1,768]{2,1,0:T(1,128)S(1)} %all-to-all-done.lam_ref, bf16[512,256]{1,0:T(8,128)(2,1)S(1)} %get-tuple-element.19.refs_0_.code_ref, f32[512,128]{1,0:T(8,128)S(1)} %norm_calc.1.norm_ref, ...), custom_call_target="tpu_custom_call" | custom-call | flops 19327352832 | bytes 1703936 | tf_op jit(solution)/shard_map/columns_calc/pallas_call | solution.py:296
  33.5 1.5 %columns_calc.3 = (bf16[512,256]{1,0:T(8,128)(2,1)}, f32[1,512]{1,0:T(1,128)}, f32[192,8]{1,0:T(8,128)S(1)}, f32[1,192]{1,0:T(1,128)}) custom-call(s32[1]{0:T(128)} %bitcast.place_ref, f32[16,1,768]{2,1,0:T(1,128)S(1)} %all-to-all-done.lam_ref, bf16[512,256]{1,0:T(8,128)(2,1)S(1)} %get-tuple-element.19.refs_0_.code_ref, f32[512,128]{1,0:T(8,128)S(1)} %norm_calc.1.norm_ref, ...), custom_call_target="tpu_custom_call" | custom-call | flops 402653184 | bytes 917504 | tf_op jit(solution)/shard_map/columns_calc/pallas_call | solution.py:296
  35.0 0.1 collective-permute-done.11.refs_2_
  35.0 0.8 %soft_calc.1 = bf16[192,256]{1,0:T(8,128)(2,1)} custom-call(f32[192,8]{1,0:T(8,128)S(1)} %get-tuple-element.27.weight_ref, bf16[192,256]{1,0:T(8,128)(2,1)S(1)} %collective-permute-done.6.refs_0_, bf16[192,256]{1,0:T(8,128)(2,1)S(1)} %collective-permute-done.10.refs_1_, bf16[192,256]{1,0:T(8,128)(2,1)S(1)} %collective-permute-done.11.refs_2_, ...), custom_call_target="tpu_custom_call" | custom-call | flops 393216 | bytes 491520 | tf_op jit(solution)/shard_map/soft_calc/pallas_call | solution.py:261
  (13 shorter events, 0.1 us)
Async XLA Ops:
  0.6 9.5 %collective-permute-start.4 = (bf16[512,256]{1,0:T(8,128)(2,1)}, bf16[512,256]{1,0:T(8,128)(2,1)S(1)}, u32[]{:S(2)}, u32[]{:S(2)}) collective-permute-start(bf16[512,256]{1,0:T(8,128)(2,1)} %refs_1_.1), channel_id=1, source_target_pairs={{0,2},{1,3},{2,0},{3,1},{4,6},{5,7},{6,4},{7,5},{8,10},{9,11},{10,... | collective-permute-start | bytes 786440 | tf_op jit(solution)/shard_map/ppermute | solution.py:325
  3.7 7.7 %collective-permute-start.1 = (bf16[192,256]{1,0:T(8,128)(2,1)}, bf16[192,256]{1,0:T(8,128)(2,1)S(1)}, u32[]{:S(2)}, u32[]{:S(2)}) collective-permute-start(bf16[192,256]{1,0:T(8,128)(2,1)} %refs_0_.1), channel_id=1, source_target_pairs={{0,12},{1,13},{2,14},{3,15},{4,8},{5,9},{6,10},{7,11},{8,4},{9,5},... | collective-permute-start | bytes 294920 | tf_op jit(solution)/shard_map/ppermute | solution.py:325
  7.3 8.2 %collective-permute-start = (bf16[192,256]{1,0:T(8,128)(2,1)}, bf16[192,256]{1,0:T(8,128)(2,1)S(1)}, u32[]{:S(2)}, u32[]{:S(2)}) collective-permute-start(bf16[192,256]{1,0:T(8,128)(2,1)} %refs_0_.1), channel_id=1, source_target_pairs={{0,8},{1,9},{2,10},{3,11},{4,12},{5,13},{6,14},{7,15},{8,0},{9,1},... | collective-permute-start | bytes 294920 | tf_op jit(solution)/shard_map/ppermute | solution.py:325
  7.3 8.2 %collective-permute-start.2 = (bf16[192,256]{1,0:T(8,128)(2,1)}, bf16[192,256]{1,0:T(8,128)(2,1)S(1)}, u32[]{:S(2)}, u32[]{:S(2)}) collective-permute-start(bf16[192,256]{1,0:T(8,128)(2,1)} %refs_0_.1), channel_id=1, source_target_pairs={{0,4},{1,5},{2,6},{3,7},{4,0},{5,1},{6,2},{7,3},{8,12},{9,13},{10,... | collective-permute-start | bytes 294920 | tf_op jit(solution)/shard_map/ppermute | solution.py:325
  8.1 8.0 %collective-permute-start.3 = (bf16[512,256]{1,0:T(8,128)(2,1)}, bf16[512,256]{1,0:T(8,128)(2,1)S(1)}, u32[]{:S(2)}, u32[]{:S(2)}) collective-permute-start(bf16[512,256]{1,0:T(8,128)(2,1)} %refs_1_.1), channel_id=1, source_target_pairs={{0,1},{1,0},{2,3},{3,2},{4,5},{5,4},{6,7},{7,6},{8,9},{9,8},{10,11... | collective-permute-start | bytes 786440 | tf_op jit(solution)/shard_map/ppermute | solution.py:325
  8.1 1.0 %copy-start = (bf16[512,256]{1,0:T(8,128)(2,1)S(1)}, bf16[512,256]{1,0:T(8,128)(2,1)}, u32[]{:S(2)}) copy-start(bf16[512,256]{1,0:T(8,128)(2,1)} %refs_1_.1) | copy-start | bytes 786436
  9.0 0.9 %copy-start.1 = (bf16[192,256]{1,0:T(8,128)(2,1)S(1)}, bf16[192,256]{1,0:T(8,128)(2,1)}, u32[]{:S(2)}) copy-start(bf16[192,256]{1,0:T(8,128)(2,1)} %refs_0_.1) | copy-start | bytes 294916
  10.2 5.9 %collective-permute-start.5 = (bf16[512,256]{1,0:T(8,128)(2,1)S(1)}, bf16[512,256]{1,0:T(8,128)(2,1)S(1)}, u32[]{:S(2)}, u32[]{:S(2)}) collective-permute-start(bf16[512,256]{1,0:T(8,128)(2,1)S(1)} %collective-permute-done.4.refs_2_), channel_id=1, source_target_pairs={{0,1},{1,0},{2,3},{3,2},{4,5},{5,4},{6,7},{7,6},{8,9},{9,8},{10,11... | collective-permute-start | bytes 786440 | tf_op jit(solution)/shard_map/ppermute | solution.py:325
  15.5 10.3 %collective-permute-start.7 = (bf16[768,256]{1,0:T(8,128)(2,1)S(1)}, bf16[768,256]{1,0:T(8,128)(2,1)S(1)}, u32[]{:S(2)}, u32[]{:S(2)}) collective-permute-start(bf16[768,256]{1,0:T(8,128)(2,1)S(1)} %stack.1.stacked_ref.refs_0_), channel_id=1, source_target_pairs={{0,2},{1,3},{2,0},{3,1},{4,6},{5,7},{6,4},{7,5},{8,10},{9,11},{10,... | collective-permute-start | bytes 1179656 | tf_op jit(solution)/shard_map/ppermute | solution.py:325
  16.1 15.9 %collective-permute-start.9 = (bf16[768,256]{1,0:T(8,128)(2,1)S(1)}, bf16[768,256]{1,0:T(8,128)(2,1)S(1)}, u32[]{:S(2)}, u32[]{:S(2)}) collective-permute-start(bf16[768,256]{1,0:T(8,128)(2,1)S(1)} %stack.1.stacked_ref.refs_0_), channel_id=1, source_target_pairs={{0,1},{1,0},{2,3},{3,2},{4,5},{5,4},{6,7},{7,6},{8,9},{9,8},{10,11... | collective-permute-start | bytes 1179656 | tf_op jit(solution)/shard_map/ppermute | solution.py:325
  19.5 12.4 %collective-permute-start.6 = (bf16[192,256]{1,0:T(8,128)(2,1)S(1)}, bf16[192,256]{1,0:T(8,128)(2,1)S(1)}, u32[]{:S(2)}, u32[]{:S(2)}) collective-permute-start(bf16[192,256]{1,0:T(8,128)(2,1)S(1)} %get-tuple-element.21), channel_id=1, source_target_pairs={{0,8},{1,9},{2,10},{3,11},{4,12},{5,13},{6,14},{7,15},{8,0},{9,1},... | collective-permute-start | bytes 294920 | tf_op jit(solution)/shard_map/ppermute | solution.py:325
  20.0 11.9 %all-to-all-start = ((f32[16,1,768]{2,1,0:T(1,128)}), f32[16,1,768]{2,1,0:T(1,128)S(1)}, u32[]{:S(2)}, u32[]{:S(2)}) async-start(f32[16,1,768]{2,1,0:T(1,128)} %get-tuple-element.20), calls=%async_computation | async-start | bytes 98304 | tf_op jit(solution)/shard_map/all_to_all | solution.py:340
  25.8 7.7 %collective-permute-start.8 = (bf16[768,256]{1,0:T(8,128)(2,1)S(1)}, bf16[768,256]{1,0:T(8,128)(2,1)S(1)}, u32[]{:S(2)}, u32[]{:S(2)}) collective-permute-start(bf16[768,256]{1,0:T(8,128)(2,1)S(1)} %collective-permute-done.7.refs_2_), channel_id=1, source_target_pairs={{0,1},{1,0},{2,3},{3,2},{4,5},{5,4},{6,7},{7,6},{8,9},{9,8},{10,11... | collective-permute-start | bytes 1179656 | tf_op jit(solution)/shard_map/ppermute | solution.py:325
  25.8 9.2 %collective-permute-start.10 = (bf16[192,256]{1,0:T(8,128)(2,1)S(1)}, bf16[192,256]{1,0:T(8,128)(2,1)S(1)}, u32[]{:S(2)}, u32[]{:S(2)}) collective-permute-start(bf16[192,256]{1,0:T(8,128)(2,1)S(1)} %get-tuple-element.28), channel_id=1, source_target_pairs={{0,12},{1,13},{2,14},{3,15},{4,8},{5,9},{6,10},{7,11},{8,4},{9,5},... | collective-permute-start | bytes 294920 | tf_op jit(solution)/shard_map/ppermute | solution.py:325
  29.0 6.0 %collective-permute-start.11 = (bf16[192,256]{1,0:T(8,128)(2,1)S(1)}, bf16[192,256]{1,0:T(8,128)(2,1)S(1)}, u32[]{:S(2)}, u32[]{:S(2)}) collective-permute-start(bf16[192,256]{1,0:T(8,128)(2,1)S(1)} %get-tuple-element.29), channel_id=1, source_target_pairs={{0,4},{1,5},{2,6},{3,7},{4,0},{5,1},{6,2},{7,3},{8,12},{9,13},{10,... | collective-permute-start | bytes 294920 | tf_op jit(solution)/shard_map/ppermute | solution.py:325

commit v11 on v10

--- a/solution.py
+++ b/solution.py
@@ -327,10 +327,11 @@
     code_y = swap(codebook, 2)
     code_c = swap(codebook, 1)
     shape = (outer * embeddings.shape[0], embeddings.shape[1])
-    order = (*range(2, outer), 1, 0)
+    order = (outer // 2, *(j for j in range(1, outer) if j != outer // 2), 0)
     own_rows, own_code = keep(embeddings, codebook)
-    blocks = [swap(embeddings, inner * j) for j in order[:-1]] + [own_rows]
-    stacked = stack(place, blocks, order, inner, shape)
+    first = (*range(2, outer), 1, 0)
+    blocks = [swap(embeddings, inner * j) for j in first[:-1]] + [own_rows]
+    stacked = stack(place, blocks, first, inner, shape)
     stacked_y = swap(stacked, 2)
     stacked_c = swap(stacked, 1)
     code = [own_code, code_c, code_y, swap(code_y, 1)]

time: 36.1 us -> 36 us (level)
  waiting for transfers between devices: 8.96 us -> 8.34 us
  starting transfers between devices: 16.9 us -> 17.5 us
    all_to_all x1, waiting for transfers between devices: 2.93 us -> 2.37 us  [on_device(): lam = lax.all_to_all(lam, AXIS, 0, 0)]
    ppermute x12, starting transfers between devices: 12.1 us -> 12.6 us  [swap(): return lax.ppermute(x, AXIS, [(i, i ^ step) for i in range(size)])]
  transfers between devices with their start and end apart: 13 -> 13, of which waited for: 6 -> 5; matrix products, arithmetic and copies ran while one was open for 0% -> 0% of each run, Pallas kernels for 18% -> 18%
where the time goes in v11:
time: 36 us; the launch traced here: 35.8 us
  starting transfers between devices  17.5 us (49%)
  waiting for transfers between devices  8.34 us (23%)
  Pallas kernels  7.44 us (21%)
  local copies, waits for them, and re-layouts  1.84 us (5%)
  between operations  0.69 us (2%)
    ppermute x12, starting transfers between devices, swap(): return lax.ppermute(x, AXIS, [(i, i ^ step) for i in range(size)])  12.6 us
    ppermute x12, waiting for transfers between devices, swap(): return lax.ppermute(x, AXIS, [(i, i ^ step) for i in range(size)])  5.98 us
    all_to_all x1, starting transfers between devices, on_device(): lam = lax.all_to_all(lam, AXIS, 0, 0)  4.85 us
    pallas_call x1, Pallas kernels, rows_calc(): pl.pallas_call(functools.partial(rows_kernel, outer, inner, tile, LOG2E *...  3.41 us
    pallas_call x2, Pallas kernels, columns_calc(): pl.pallas_call(functools.partial(body, outer, inner, groups, tile, LOG2E...  3.01 us
    all_to_all x1, waiting for transfers between devices, on_device(): lam = lax.all_to_all(lam, AXIS, 0, 0)  2.37 us
    unnamed x4, local copies, waits for them, and re-layouts  1.84 us
    pallas_call x1, Pallas kernels, soft_calc(): pl.pallas_call(soft_kernel, out_shape=jax.ShapeDtypeStruct(shape, jnp.bfl...  0.83 us
  transfers between devices with their start and end apart: 13, of which 5 were waited for; matrix products, arithmetic and copies ran while one was open for 0% of the time, Pallas kernels for 18%

profile of v11, /device:TPU:0, one launch (start us, length us, event | category | flops | bytes accessed | tf_op | source)
XLA Modules:
  0.0 35.8 jit_solution(8971460315499379030)
XLA Ops:
  0.6 3.0 %collective-permute-start.4 = (bf16[512,256]{1,0:T(8,128)(2,1)}, bf16[512,256]{1,0:T(8,128)(2,1)S(1)}, u32[]{:S(2)}, u32[]{:S(2)}) collective-permute-start(bf16[512,256]{1,0:T(8,128)(2,1)} %refs_1_.1), channel_id=1, source_target_pairs={{0,2},{1,3},{2,0},{3,1},{4,6},{5,7},{6,4},{7,5},{8,10},{9,11},{10,... | collective-permute-start | bytes 786440 | tf_op jit(solution)/shard_map/ppermute | solution.py:325
  3.7 3.6 %collective-permute-start.1 = (bf16[192,256]{1,0:T(8,128)(2,1)}, bf16[192,256]{1,0:T(8,128)(2,1)S(1)}, u32[]{:S(2)}, u32[]{:S(2)}) collective-permute-start(bf16[192,256]{1,0:T(8,128)(2,1)} %refs_0_.1), channel_id=1, source_target_pairs={{0,12},{1,13},{2,14},{3,15},{4,8},{5,9},{6,10},{7,11},{8,4},{9,5},... | collective-permute-start | bytes 294920 | tf_op jit(solution)/shard_map/ppermute | solution.py:325
  7.3 0.8 %collective-permute-start.2 = (bf16[192,256]{1,0:T(8,128)(2,1)}, bf16[192,256]{1,0:T(8,128)(2,1)S(1)}, u32[]{:S(2)}, u32[]{:S(2)}) collective-permute-start(bf16[192,256]{1,0:T(8,128)(2,1)} %refs_0_.1), channel_id=1, source_target_pairs={{0,4},{1,5},{2,6},{3,7},{4,0},{5,1},{6,2},{7,3},{8,12},{9,13},{10,... | collective-permute-start | bytes 294920 | tf_op jit(solution)/shard_map/ppermute | solution.py:325
  8.1 0.9 %copy-done = bf16[512,256]{1,0:T(8,128)(2,1)S(1)} copy-done((bf16[512,256]{1,0:T(8,128)(2,1)S(1)}, bf16[512,256]{1,0:T(8,128)(2,1)}, u32[]{:S(2)}) %copy-start) | copy-done | bytes 262168
  9.0 0.9 %copy-done.1 = bf16[192,256]{1,0:T(8,128)(2,1)S(1)} copy-done((bf16[192,256]{1,0:T(8,128)(2,1)S(1)}, bf16[192,256]{1,0:T(8,128)(2,1)}, u32[]{:S(2)}) %copy-start.1) | copy-done | bytes 98328
  9.9 0.2 collective-permute-done.4.refs_2_
  10.2 0.3 collective-permute-start.5
  10.5 0.9 %collective-permute-done.1.refs_1_ = bf16[192,256]{1,0:T(8,128)(2,1)S(1)} collective-permute-done((bf16[192,256]{1,0:T(8,128)(2,1)}, bf16[192,256]{1,0:T(8,128)(2,1)S(1)}, u32[]{:S(2)}, u32[]{:S(2)}) %collective-permute-start.1) | collective-permute-done | bytes 98336 | tf_op jit(solution)/shard_map/ppermute | solution.py:325
  11.4 4.1 %collective-permute-done.refs_0_ = bf16[192,256]{1,0:T(8,128)(2,1)S(1)} collective-permute-done((bf16[192,256]{1,0:T(8,128)(2,1)}, bf16[192,256]{1,0:T(8,128)(2,1)S(1)}, u32[]{:S(2)}, u32[]{:S(2)}) %collective-permute-start) | collective-permute-done | bytes 98336 | tf_op jit(solution)/shard_map/ppermute | solution.py:325
  15.5 0.0 collective-permute-done.2.refs_2_
  15.5 0.6 %collective-permute-start.7 = (bf16[768,256]{1,0:T(8,128)(2,1)S(1)}, bf16[768,256]{1,0:T(8,128)(2,1)S(1)}, u32[]{:S(2)}, u32[]{:S(2)}) collective-permute-start(bf16[768,256]{1,0:T(8,128)(2,1)S(1)} %stack.1.stacked_ref.refs_0_), channel_id=1, source_target_pairs={{0,2},{1,3},{2,0},{3,1},{4,6},{5,7},{6,4},{7,5},{8,10},{9,11},{10,... | collective-permute-start | bytes 1179656 | tf_op jit(solution)/shard_map/ppermute | solution.py:325
  16.1 0.0 collective-permute-start.9
  16.1 3.4 %rows_calc.1 = (f32[16,1,768]{2,1,0:T(1,128)}, bf16[192,256]{1,0:T(8,128)(2,1)S(1)}, bf16[192,256]{1,0:T(8,128)(2,1)S(1)}, bf16[192,256]{1,0:T(8,128)(2,1)S(1)}, bf16[192,256]{1,0:T(8,128)(2,1)S(1)}) custom-call(s32[1]{0:T(128)} %bitcast.place_ref, bf16[768,256]{1,0:T(8,128)(2,1)S(1)} %stack.1.stacked_ref.refs_0_, ...), custom_call_target="tpu_custom_call" | custom-call | flops 1610612736 | bytes 1441792 | tf_op jit(solution)/shard_map/rows_calc/pallas_call | solution.py:146
  19.5 0.5 %collective-permute-start.6 = (bf16[192,256]{1,0:T(8,128)(2,1)S(1)}, bf16[192,256]{1,0:T(8,128)(2,1)S(1)}, u32[]{:S(2)}, u32[]{:S(2)}) collective-permute-start(bf16[192,256]{1,0:T(8,128)(2,1)S(1)} %get-tuple-element.21), channel_id=1, source_target_pairs={{0,8},{1,9},{2,10},{3,11},{4,12},{5,13},{6,14},{7,15},{8,0},{9,1},... | collective-permute-start | bytes 294920 | tf_op jit(solution)/shard_map/ppermute | solution.py:325
  20.0 4.8 %all-to-all-start = ((f32[16,1,768]{2,1,0:T(1,128)}), f32[16,1,768]{2,1,0:T(1,128)S(1)}, u32[]{:S(2)}, u32[]{:S(2)}) async-start(f32[16,1,768]{2,1,0:T(1,128)} %get-tuple-element.20), calls=%async_computation | async-start | bytes 98304 | tf_op jit(solution)/shard_map/all_to_all | solution.py:341
  24.9 0.1 norm_calc.1.norm_ref
  25.0 0.8 %collective-permute-done.7.refs_2_ = bf16[768,256]{1,0:T(8,128)(2,1)S(1)} collective-permute-done((bf16[768,256]{1,0:T(8,128)(2,1)S(1)}, bf16[768,256]{1,0:T(8,128)(2,1)S(1)}, u32[]{:S(2)}, u32[]{:S(2)}) %collective-permute-start.7) | collective-permute-done | bytes 393248 | tf_op jit(solution)/shard_map/ppermute | solution.py:325
  25.8 1.4 %collective-permute-start.10 = (bf16[192,256]{1,0:T(8,128)(2,1)S(1)}, bf16[192,256]{1,0:T(8,128)(2,1)S(1)}, u32[]{:S(2)}, u32[]{:S(2)}) collective-permute-start(bf16[192,256]{1,0:T(8,128)(2,1)S(1)} %get-tuple-element.28), channel_id=1, source_target_pairs={{0,4},{1,5},{2,6},{3,7},{4,0},{5,1},{6,2},{7,3},{8,12},{9,13},{10,... | collective-permute-start | bytes 294920 | tf_op jit(solution)/shard_map/ppermute | solution.py:325
  27.2 2.4 %collective-permute-start.11 = (bf16[192,256]{1,0:T(8,128)(2,1)S(1)}, bf16[192,256]{1,0:T(8,128)(2,1)S(1)}, u32[]{:S(2)}, u32[]{:S(2)}) collective-permute-start(bf16[192,256]{1,0:T(8,128)(2,1)S(1)} %get-tuple-element.29), channel_id=1, source_target_pairs={{0,12},{1,13},{2,14},{3,15},{4,8},{5,9},{6,10},{7,11},{8,4},{9,5},... | collective-permute-start | bytes 294920 | tf_op jit(solution)/shard_map/ppermute | solution.py:325
  29.6 2.4 %all-to-all-done.lam_ref = f32[16,1,768]{2,1,0:T(1,128)S(1)} async-done(((f32[16,1,768]{2,1,0:T(1,128)}), f32[16,1,768]{2,1,0:T(1,128)S(1)}, u32[]{:S(2)}, u32[]{:S(2)}) %all-to-all-start) | async-done | bytes 49184 | tf_op jit(solution)/shard_map/all_to_all | solution.py:341
  31.9 1.5 %columns_calc.2 = (f32[512,256]{1,0:T(8,128)S(1)}, f32[512,128]{1,0:T(8,128)S(1)}) custom-call(s32[1]{0:T(128)} %bitcast.place_ref, f32[16,1,768]{2,1,0:T(1,128)S(1)} %all-to-all-done.lam_ref, bf16[512,256]{1,0:T(8,128)(2,1)S(1)} %get-tuple-element.19.refs_0_.code_ref, f32[512,128]{1,0:T(8,128)S(1)} %norm_calc.1.norm_ref, ...), custom_call_target="tpu_custom_call" | custom-call | flops 19327352832 | bytes 1703936 | tf_op jit(solution)/shard_map/columns_calc/pallas_call | solution.py:296
  33.5 1.5 %columns_calc.3 = (bf16[512,256]{1,0:T(8,128)(2,1)}, f32[1,512]{1,0:T(1,128)}, f32[192,8]{1,0:T(8,128)S(1)}, f32[1,192]{1,0:T(1,128)}) custom-call(s32[1]{0:T(128)} %bitcast.place_ref, f32[16,1,768]{2,1,0:T(1,128)S(1)} %all-to-all-done.lam_ref, bf16[512,256]{1,0:T(8,128)(2,1)S(1)} %get-tuple-element.19.refs_0_.code_ref, f32[512,128]{1,0:T(8,128)S(1)} %norm_calc.1.norm_ref, ...), custom_call_target="tpu_custom_call" | custom-call | flops 402653184 | bytes 917504 | tf_op jit(solution)/shard_map/columns_calc/pallas_call | solution.py:296
  35.0 0.0 collective-permute-done.11.refs_2_
  35.0 0.8 %soft_calc.1 = bf16[192,256]{1,0:T(8,128)(2,1)} custom-call(f32[192,8]{1,0:T(8,128)S(1)} %get-tuple-element.27.weight_ref, bf16[192,256]{1,0:T(8,128)(2,1)S(1)} %collective-permute-done.6.refs_0_, bf16[192,256]{1,0:T(8,128)(2,1)S(1)} %collective-permute-done.10.refs_1_, bf16[192,256]{1,0:T(8,128)(2,1)S(1)} %collective-permute-done.11.refs_2_, ...), custom_call_target="tpu_custom_call" | custom-call | flops 393216 | bytes 491520 | tf_op jit(solution)/shard_map/soft_calc/pallas_call | solution.py:261
  (13 shorter events, 0.1 us)
Async XLA Ops:
  0.6 9.5 %collective-permute-start.4 = (bf16[512,256]{1,0:T(8,128)(2,1)}, bf16[512,256]{1,0:T(8,128)(2,1)S(1)}, u32[]{:S(2)}, u32[]{:S(2)}) collective-permute-start(bf16[512,256]{1,0:T(8,128)(2,1)} %refs_1_.1), channel_id=1, source_target_pairs={{0,2},{1,3},{2,0},{3,1},{4,6},{5,7},{6,4},{7,5},{8,10},{9,11},{10,... | collective-permute-start | bytes 786440 | tf_op jit(solution)/shard_map/ppermute | solution.py:325
  3.7 7.7 %collective-permute-start.1 = (bf16[192,256]{1,0:T(8,128)(2,1)}, bf16[192,256]{1,0:T(8,128)(2,1)S(1)}, u32[]{:S(2)}, u32[]{:S(2)}) collective-permute-start(bf16[192,256]{1,0:T(8,128)(2,1)} %refs_0_.1), channel_id=1, source_target_pairs={{0,12},{1,13},{2,14},{3,15},{4,8},{5,9},{6,10},{7,11},{8,4},{9,5},... | collective-permute-start | bytes 294920 | tf_op jit(solution)/shard_map/ppermute | solution.py:325
  7.3 8.2 %collective-permute-start = (bf16[192,256]{1,0:T(8,128)(2,1)}, bf16[192,256]{1,0:T(8,128)(2,1)S(1)}, u32[]{:S(2)}, u32[]{:S(2)}) collective-permute-start(bf16[192,256]{1,0:T(8,128)(2,1)} %refs_0_.1), channel_id=1, source_target_pairs={{0,8},{1,9},{2,10},{3,11},{4,12},{5,13},{6,14},{7,15},{8,0},{9,1},... | collective-permute-start | bytes 294920 | tf_op jit(solution)/shard_map/ppermute | solution.py:325
  7.3 8.2 %collective-permute-start.2 = (bf16[192,256]{1,0:T(8,128)(2,1)}, bf16[192,256]{1,0:T(8,128)(2,1)S(1)}, u32[]{:S(2)}, u32[]{:S(2)}) collective-permute-start(bf16[192,256]{1,0:T(8,128)(2,1)} %refs_0_.1), channel_id=1, source_target_pairs={{0,4},{1,5},{2,6},{3,7},{4,0},{5,1},{6,2},{7,3},{8,12},{9,13},{10,... | collective-permute-start | bytes 294920 | tf_op jit(solution)/shard_map/ppermute | solution.py:325
  8.1 8.0 %collective-permute-start.3 = (bf16[512,256]{1,0:T(8,128)(2,1)}, bf16[512,256]{1,0:T(8,128)(2,1)S(1)}, u32[]{:S(2)}, u32[]{:S(2)}) collective-permute-start(bf16[512,256]{1,0:T(8,128)(2,1)} %refs_1_.1), channel_id=1, source_target_pairs={{0,1},{1,0},{2,3},{3,2},{4,5},{5,4},{6,7},{7,6},{8,9},{9,8},{10,11... | collective-permute-start | bytes 786440 | tf_op jit(solution)/shard_map/ppermute | solution.py:325
  8.1 1.0 %copy-start = (bf16[512,256]{1,0:T(8,128)(2,1)S(1)}, bf16[512,256]{1,0:T(8,128)(2,1)}, u32[]{:S(2)}) copy-start(bf16[512,256]{1,0:T(8,128)(2,1)} %refs_1_.1) | copy-start | bytes 786436
  9.0 0.9 %copy-start.1 = (bf16[192,256]{1,0:T(8,128)(2,1)S(1)}, bf16[192,256]{1,0:T(8,128)(2,1)}, u32[]{:S(2)}) copy-start(bf16[192,256]{1,0:T(8,128)(2,1)} %refs_0_.1) | copy-start | bytes 294916
  10.2 5.9 %collective-permute-start.5 = (bf16[512,256]{1,0:T(8,128)(2,1)S(1)}, bf16[512,256]{1,0:T(8,128)(2,1)S(1)}, u32[]{:S(2)}, u32[]{:S(2)}) collective-permute-start(bf16[512,256]{1,0:T(8,128)(2,1)S(1)} %collective-permute-done.4.refs_2_), channel_id=1, source_target_pairs={{0,1},{1,0},{2,3},{3,2},{4,5},{5,4},{6,7},{7,6},{8,9},{9,8},{10,11... | collective-permute-start | bytes 786440 | tf_op jit(solution)/shard_map/ppermute | solution.py:325
  15.5 10.3 %collective-permute-start.7 = (bf16[768,256]{1,0:T(8,128)(2,1)S(1)}, bf16[768,256]{1,0:T(8,128)(2,1)S(1)}, u32[]{:S(2)}, u32[]{:S(2)}) collective-permute-start(bf16[768,256]{1,0:T(8,128)(2,1)S(1)} %stack.1.stacked_ref.refs_0_), channel_id=1, source_target_pairs={{0,2},{1,3},{2,0},{3,1},{4,6},{5,7},{6,4},{7,5},{8,10},{9,11},{10,... | collective-permute-start | bytes 1179656 | tf_op jit(solution)/shard_map/ppermute | solution.py:325
  16.1 15.9 %collective-permute-start.9 = (bf16[768,256]{1,0:T(8,128)(2,1)S(1)}, bf16[768,256]{1,0:T(8,128)(2,1)S(1)}, u32[]{:S(2)}, u32[]{:S(2)}) collective-permute-start(bf16[768,256]{1,0:T(8,128)(2,1)S(1)} %stack.1.stacked_ref.refs_0_), channel_id=1, source_target_pairs={{0,1},{1,0},{2,3},{3,2},{4,5},{5,4},{6,7},{7,6},{8,9},{9,8},{10,11... | collective-permute-start | bytes 1179656 | tf_op jit(solution)/shard_map/ppermute | solution.py:325
  19.5 12.4 %collective-permute-start.6 = (bf16[192,256]{1,0:T(8,128)(2,1)S(1)}, bf16[192,256]{1,0:T(8,128)(2,1)S(1)}, u32[]{:S(2)}, u32[]{:S(2)}) collective-permute-start(bf16[192,256]{1,0:T(8,128)(2,1)S(1)} %get-tuple-element.21), channel_id=1, source_target_pairs={{0,8},{1,9},{2,10},{3,11},{4,12},{5,13},{6,14},{7,15},{8,0},{9,1},... | collective-permute-start | bytes 294920 | tf_op jit(solution)/shard_map/ppermute | solution.py:325
  20.0 11.9 %all-to-all-start = ((f32[16,1,768]{2,1,0:T(1,128)}), f32[16,1,768]{2,1,0:T(1,128)S(1)}, u32[]{:S(2)}, u32[]{:S(2)}) async-start(f32[16,1,768]{2,1,0:T(1,128)} %get-tuple-element.20), calls=%async_computation | async-start | bytes 98304 | tf_op jit(solution)/shard_map/all_to_all | solution.py:341
  25.8 7.7 %collective-permute-start.8 = (bf16[768,256]{1,0:T(8,128)(2,1)S(1)}, bf16[768,256]{1,0:T(8,128)(2,1)S(1)}, u32[]{:S(2)}, u32[]{:S(2)}) collective-permute-start(bf16[768,256]{1,0:T(8,128)(2,1)S(1)} %collective-permute-done.7.refs_2_), channel_id=1, source_target_pairs={{0,1},{1,0},{2,3},{3,2},{4,5},{5,4},{6,7},{7,6},{8,9},{9,8},{10,11... | collective-permute-start | bytes 1179656 | tf_op jit(solution)/shard_map/ppermute | solution.py:325
  25.8 9.2 %collective-permute-start.10 = (bf16[192,256]{1,0:T(8,128)(2,1)S(1)}, bf16[192,256]{1,0:T(8,128)(2,1)S(1)}, u32[]{:S(2)}, u32[]{:S(2)}) collective-permute-start(bf16[192,256]{1,0:T(8,128)(2,1)S(1)} %get-tuple-element.28), channel_id=1, source_target_pairs={{0,4},{1,5},{2,6},{3,7},{4,0},{5,1},{6,2},{7,3},{8,12},{9,13},{10,... | collective-permute-start | bytes 294920 | tf_op jit(solution)/shard_map/ppermute | solution.py:325
  27.2 7.8 %collective-permute-start.11 = (bf16[192,256]{1,0:T(8,128)(2,1)S(1)}, bf16[192,256]{1,0:T(8,128)(2,1)S(1)}, u32[]{:S(2)}, u32[]{:S(2)}) collective-permute-start(bf16[192,256]{1,0:T(8,128)(2,1)S(1)} %get-tuple-element.29), channel_id=1, source_target_pairs={{0,12},{1,13},{2,14},{3,15},{4,8},{5,9},{6,10},{7,11},{8,4},{9,5},... | collective-permute-start | bytes 294920 | tf_op jit(solution)/shard_map/ppermute | solution.py:325

commit v12 on v11

--- a/solution.py
+++ b/solution.py
@@ -241,7 +241,7 @@
     mine = levels(0)
     lines = [jnp.exp(lam_ref[(place ^ j) * inner + spoke] - mine) for j in order] + [mine]
     lines += [mine] * (-len(lines) % 8)
-    near = pltpu.roll(jnp.concatenate(lines, axis=0), rows - place * rows_dev, 1)
+    near = pltpu.roll(jnp.concatenate(lines, axis=0), (outer - place) % outer * rows_dev, 1)
     near = near[:, : min(rows, -(-rows_dev // 128) * 128)]
     weight_ref[...] = near.T[:rows_dev, :]
     own_ref[...] = near[outer : outer + 1, :rows_dev]

time: 36 us -> 36 us (level)
  no operation moved by 1% of the time
where the time goes in v12:
time: 36 us; the launch traced here: 35.8 us
  starting transfers between devices  17.5 us (49%)
  waiting for transfers between devices  8.34 us (23%)
  Pallas kernels  7.44 us (21%)
  local copies, waits for them, and re-layouts  1.84 us (5%)
  between operations  0.69 us (2%)
    ppermute x12, starting transfers between devices, swap(): return lax.ppermute(x, AXIS, [(i, i ^ step) for i in range(size)])  12.6 us
    ppermute x12, waiting for transfers between devices, swap(): return lax.ppermute(x, AXIS, [(i, i ^ step) for i in range(size)])  5.98 us
    all_to_all x1, starting transfers between devices, on_device(): lam = lax.all_to_all(lam, AXIS, 0, 0)  4.85 us
    pallas_call x1, Pallas kernels, rows_calc(): pl.pallas_call(functools.partial(rows_kernel, outer, inner, tile, LOG2E *...  3.41 us
    pallas_call x2, Pallas kernels, columns_calc(): pl.pallas_call(functools.partial(body, outer, inner, groups, tile, LOG2E...  3.01 us
    all_to_all x1, waiting for transfers between devices, on_device(): lam = lax.all_to_all(lam, AXIS, 0, 0)  2.37 us
    unnamed x4, local copies, waits for them, and re-layouts  1.84 us
    pallas_call x1, Pallas kernels, soft_calc(): pl.pallas_call(soft_kernel, out_shape=jax.ShapeDtypeStruct(shape, jnp.bfl...  0.83 us
  transfers between devices with their start and end apart: 13, of which 5 were waited for; matrix products, arithmetic and copies ran while one was open for 0% of the time, Pallas kernels for 18%

profile of v12, /device:TPU:0, one launch (start us, length us, event | category | flops | bytes accessed | tf_op | source)
XLA Modules:
  0.0 35.8 jit_solution(17229861820355206828)
XLA Ops:
  0.6 3.0 %collective-permute-start.4 = (bf16[512,256]{1,0:T(8,128)(2,1)}, bf16[512,256]{1,0:T(8,128)(2,1)S(1)}, u32[]{:S(2)}, u32[]{:S(2)}) collective-permute-start(bf16[512,256]{1,0:T(8,128)(2,1)} %refs_1_.1), channel_id=1, source_target_pairs={{0,2},{1,3},{2,0},{3,1},{4,6},{5,7},{6,4},{7,5},{8,10},{9,11},{10,... | collective-permute-start | bytes 786440 | tf_op jit(solution)/shard_map/ppermute | solution.py:325
  3.7 3.6 %collective-permute-start.1 = (bf16[192,256]{1,0:T(8,128)(2,1)}, bf16[192,256]{1,0:T(8,128)(2,1)S(1)}, u32[]{:S(2)}, u32[]{:S(2)}) collective-permute-start(bf16[192,256]{1,0:T(8,128)(2,1)} %refs_0_.1), channel_id=1, source_target_pairs={{0,12},{1,13},{2,14},{3,15},{4,8},{5,9},{6,10},{7,11},{8,4},{9,5},... | collective-permute-start | bytes 294920 | tf_op jit(solution)/shard_map/ppermute | solution.py:325
  7.3 0.8 %collective-permute-start.2 = (bf16[192,256]{1,0:T(8,128)(2,1)}, bf16[192,256]{1,0:T(8,128)(2,1)S(1)}, u32[]{:S(2)}, u32[]{:S(2)}) collective-permute-start(bf16[192,256]{1,0:T(8,128)(2,1)} %refs_0_.1), channel_id=1, source_target_pairs={{0,4},{1,5},{2,6},{3,7},{4,0},{5,1},{6,2},{7,3},{8,12},{9,13},{10,... | collective-permute-start | bytes 294920 | tf_op jit(solution)/shard_map/ppermute | solution.py:325
  8.1 0.9 %copy-done = bf16[512,256]{1,0:T(8,128)(2,1)S(1)} copy-done((bf16[512,256]{1,0:T(8,128)(2,1)S(1)}, bf16[512,256]{1,0:T(8,128)(2,1)}, u32[]{:S(2)}) %copy-start) | copy-done | bytes 262168
  9.0 0.9 %copy-done.1 = bf16[192,256]{1,0:T(8,128)(2,1)S(1)} copy-done((bf16[192,256]{1,0:T(8,128)(2,1)S(1)}, bf16[192,256]{1,0:T(8,128)(2,1)}, u32[]{:S(2)}) %copy-start.1) | copy-done | bytes 98328
  9.9 0.2 collective-permute-done.4.refs_2_
  10.2 0.3 collective-permute-start.5
  10.5 0.9 %collective-permute-done.1.refs_1_ = bf16[192,256]{1,0:T(8,128)(2,1)S(1)} collective-permute-done((bf16[192,256]{1,0:T(8,128)(2,1)}, bf16[192,256]{1,0:T(8,128)(2,1)S(1)}, u32[]{:S(2)}, u32[]{:S(2)}) %collective-permute-start.1) | collective-permute-done | bytes 98336 | tf_op jit(solution)/shard_map/ppermute | solution.py:325
  11.4 4.1 %collective-permute-done.refs_0_ = bf16[192,256]{1,0:T(8,128)(2,1)S(1)} collective-permute-done((bf16[192,256]{1,0:T(8,128)(2,1)}, bf16[192,256]{1,0:T(8,128)(2,1)S(1)}, u32[]{:S(2)}, u32[]{:S(2)}) %collective-permute-start) | collective-permute-done | bytes 98336 | tf_op jit(solution)/shard_map/ppermute | solution.py:325
  15.5 0.0 collective-permute-done.2.refs_2_
  15.5 0.6 %collective-permute-start.7 = (bf16[768,256]{1,0:T(8,128)(2,1)S(1)}, bf16[768,256]{1,0:T(8,128)(2,1)S(1)}, u32[]{:S(2)}, u32[]{:S(2)}) collective-permute-start(bf16[768,256]{1,0:T(8,128)(2,1)S(1)} %stack.1.stacked_ref.refs_0_), channel_id=1, source_target_pairs={{0,2},{1,3},{2,0},{3,1},{4,6},{5,7},{6,4},{7,5},{8,10},{9,11},{10,... | collective-permute-start | bytes 1179656 | tf_op jit(solution)/shard_map/ppermute | solution.py:325
  16.1 0.0 collective-permute-start.9
  16.1 3.4 %rows_calc.1 = (f32[16,1,768]{2,1,0:T(1,128)}, bf16[192,256]{1,0:T(8,128)(2,1)S(1)}, bf16[192,256]{1,0:T(8,128)(2,1)S(1)}, bf16[192,256]{1,0:T(8,128)(2,1)S(1)}, bf16[192,256]{1,0:T(8,128)(2,1)S(1)}) custom-call(s32[1]{0:T(128)} %bitcast.place_ref, bf16[768,256]{1,0:T(8,128)(2,1)S(1)} %stack.1.stacked_ref.refs_0_, ...), custom_call_target="tpu_custom_call" | custom-call | flops 1610612736 | bytes 1441792 | tf_op jit(solution)/shard_map/rows_calc/pallas_call | solution.py:146
  19.5 0.5 %collective-permute-start.6 = (bf16[192,256]{1,0:T(8,128)(2,1)S(1)}, bf16[192,256]{1,0:T(8,128)(2,1)S(1)}, u32[]{:S(2)}, u32[]{:S(2)}) collective-permute-start(bf16[192,256]{1,0:T(8,128)(2,1)S(1)} %get-tuple-element.21), channel_id=1, source_target_pairs={{0,8},{1,9},{2,10},{3,11},{4,12},{5,13},{6,14},{7,15},{8,0},{9,1},... | collective-permute-start | bytes 294920 | tf_op jit(solution)/shard_map/ppermute | solution.py:325
  20.0 4.8 %all-to-all-start = ((f32[16,1,768]{2,1,0:T(1,128)}), f32[16,1,768]{2,1,0:T(1,128)S(1)}, u32[]{:S(2)}, u32[]{:S(2)}) async-start(f32[16,1,768]{2,1,0:T(1,128)} %get-tuple-element.20), calls=%async_computation | async-start | bytes 98304 | tf_op jit(solution)/shard_map/all_to_all | solution.py:341
  24.9 0.1 norm_calc.1.norm_ref
  25.0 0.8 %collective-permute-done.7.refs_2_ = bf16[768,256]{1,0:T(8,128)(2,1)S(1)} collective-permute-done((bf16[768,256]{1,0:T(8,128)(2,1)S(1)}, bf16[768,256]{1,0:T(8,128)(2,1)S(1)}, u32[]{:S(2)}, u32[]{:S(2)}) %collective-permute-start.7) | collective-permute-done | bytes 393248 | tf_op jit(solution)/shard_map/ppermute | solution.py:325
  25.8 1.4 %collective-permute-start.10 = (bf16[192,256]{1,0:T(8,128)(2,1)S(1)}, bf16[192,256]{1,0:T(8,128)(2,1)S(1)}, u32[]{:S(2)}, u32[]{:S(2)}) collective-permute-start(bf16[192,256]{1,0:T(8,128)(2,1)S(1)} %get-tuple-element.28), channel_id=1, source_target_pairs={{0,4},{1,5},{2,6},{3,7},{4,0},{5,1},{6,2},{7,3},{8,12},{9,13},{10,... | collective-permute-start | bytes 294920 | tf_op jit(solution)/shard_map/ppermute | solution.py:325
  27.2 2.4 %collective-permute-start.11 = (bf16[192,256]{1,0:T(8,128)(2,1)S(1)}, bf16[192,256]{1,0:T(8,128)(2,1)S(1)}, u32[]{:S(2)}, u32[]{:S(2)}) collective-permute-start(bf16[192,256]{1,0:T(8,128)(2,1)S(1)} %get-tuple-element.29), channel_id=1, source_target_pairs={{0,12},{1,13},{2,14},{3,15},{4,8},{5,9},{6,10},{7,11},{8,4},{9,5},... | collective-permute-start | bytes 294920 | tf_op jit(solution)/shard_map/ppermute | solution.py:325
  29.6 2.4 %all-to-all-done.lam_ref = f32[16,1,768]{2,1,0:T(1,128)S(1)} async-done(((f32[16,1,768]{2,1,0:T(1,128)}), f32[16,1,768]{2,1,0:T(1,128)S(1)}, u32[]{:S(2)}, u32[]{:S(2)}) %all-to-all-start) | async-done | bytes 49184 | tf_op jit(solution)/shard_map/all_to_all | solution.py:341
  31.9 1.5 %columns_calc.2 = (f32[512,256]{1,0:T(8,128)S(1)}, f32[512,128]{1,0:T(8,128)S(1)}) custom-call(s32[1]{0:T(128)} %bitcast.place_ref, f32[16,1,768]{2,1,0:T(1,128)S(1)} %all-to-all-done.lam_ref, bf16[512,256]{1,0:T(8,128)(2,1)S(1)} %get-tuple-element.19.refs_0_.code_ref, f32[512,128]{1,0:T(8,128)S(1)} %norm_calc.1.norm_ref, ...), custom_call_target="tpu_custom_call" | custom-call | flops 19327352832 | bytes 1703936 | tf_op jit(solution)/shard_map/columns_calc/pallas_call | solution.py:296
  33.5 1.5 %columns_calc.3 = (bf16[512,256]{1,0:T(8,128)(2,1)}, f32[1,512]{1,0:T(1,128)}, f32[192,8]{1,0:T(8,128)S(1)}, f32[1,192]{1,0:T(1,128)}) custom-call(s32[1]{0:T(128)} %bitcast.place_ref, f32[16,1,768]{2,1,0:T(1,128)S(1)} %all-to-all-done.lam_ref, bf16[512,256]{1,0:T(8,128)(2,1)S(1)} %get-tuple-element.19.refs_0_.code_ref, f32[512,128]{1,0:T(8,128)S(1)} %norm_calc.1.norm_ref, ...), custom_call_target="tpu_custom_call" | custom-call | flops 402653184 | bytes 917504 | tf_op jit(solution)/shard_map/columns_calc/pallas_call | solution.py:296
  35.0 0.0 collective-permute-done.11.refs_2_
  35.0 0.8 %soft_calc.1 = bf16[192,256]{1,0:T(8,128)(2,1)} custom-call(f32[192,8]{1,0:T(8,128)S(1)} %get-tuple-element.27.weight_ref, bf16[192,256]{1,0:T(8,128)(2,1)S(1)} %collective-permute-done.6.refs_0_, bf16[192,256]{1,0:T(8,128)(2,1)S(1)} %collective-permute-done.10.refs_1_, bf16[192,256]{1,0:T(8,128)(2,1)S(1)} %collective-permute-done.11.refs_2_, ...), custom_call_target="tpu_custom_call" | custom-call | flops 393216 | bytes 491520 | tf_op jit(solution)/shard_map/soft_calc/pallas_call | solution.py:261
  (13 shorter events, 0.1 us)
Async XLA Ops:
  0.6 9.5 %collective-permute-start.4 = (bf16[512,256]{1,0:T(8,128)(2,1)}, bf16[512,256]{1,0:T(8,128)(2,1)S(1)}, u32[]{:S(2)}, u32[]{:S(2)}) collective-permute-start(bf16[512,256]{1,0:T(8,128)(2,1)} %refs_1_.1), channel_id=1, source_target_pairs={{0,2},{1,3},{2,0},{3,1},{4,6},{5,7},{6,4},{7,5},{8,10},{9,11},{10,... | collective-permute-start | bytes 786440 | tf_op jit(solution)/shard_map/ppermute | solution.py:325
  3.7 7.7 %collective-permute-start.1 = (bf16[192,256]{1,0:T(8,128)(2,1)}, bf16[192,256]{1,0:T(8,128)(2,1)S(1)}, u32[]{:S(2)}, u32[]{:S(2)}) collective-permute-start(bf16[192,256]{1,0:T(8,128)(2,1)} %refs_0_.1), channel_id=1, source_target_pairs={{0,12},{1,13},{2,14},{3,15},{4,8},{5,9},{6,10},{7,11},{8,4},{9,5},... | collective-permute-start | bytes 294920 | tf_op jit(solution)/shard_map/ppermute | solution.py:325
  7.3 8.2 %collective-permute-start = (bf16[192,256]{1,0:T(8,128)(2,1)}, bf16[192,256]{1,0:T(8,128)(2,1)S(1)}, u32[]{:S(2)}, u32[]{:S(2)}) collective-permute-start(bf16[192,256]{1,0:T(8,128)(2,1)} %refs_0_.1), channel_id=1, source_target_pairs={{0,8},{1,9},{2,10},{3,11},{4,12},{5,13},{6,14},{7,15},{8,0},{9,1},... | collective-permute-start | bytes 294920 | tf_op jit(solution)/shard_map/ppermute | solution.py:325
  7.3 8.2 %collective-permute-start.2 = (bf16[192,256]{1,0:T(8,128)(2,1)}, bf16[192,256]{1,0:T(8,128)(2,1)S(1)}, u32[]{:S(2)}, u32[]{:S(2)}) collective-permute-start(bf16[192,256]{1,0:T(8,128)(2,1)} %refs_0_.1), channel_id=1, source_target_pairs={{0,4},{1,5},{2,6},{3,7},{4,0},{5,1},{6,2},{7,3},{8,12},{9,13},{10,... | collective-permute-start | bytes 294920 | tf_op jit(solution)/shard_map/ppermute | solution.py:325
  8.1 8.0 %collective-permute-start.3 = (bf16[512,256]{1,0:T(8,128)(2,1)}, bf16[512,256]{1,0:T(8,128)(2,1)S(1)}, u32[]{:S(2)}, u32[]{:S(2)}) collective-permute-start(bf16[512,256]{1,0:T(8,128)(2,1)} %refs_1_.1), channel_id=1, source_target_pairs={{0,1},{1,0},{2,3},{3,2},{4,5},{5,4},{6,7},{7,6},{8,9},{9,8},{10,11... | collective-permute-start | bytes 786440 | tf_op jit(solution)/shard_map/ppermute | solution.py:325
  8.1 1.0 %copy-start = (bf16[512,256]{1,0:T(8,128)(2,1)S(1)}, bf16[512,256]{1,0:T(8,128)(2,1)}, u32[]{:S(2)}) copy-start(bf16[512,256]{1,0:T(8,128)(2,1)} %refs_1_.1) | copy-start | bytes 786436
  9.0 0.9 %copy-start.1 = (bf16[192,256]{1,0:T(8,128)(2,1)S(1)}, bf16[192,256]{1,0:T(8,128)(2,1)}, u32[]{:S(2)}) copy-start(bf16[192,256]{1,0:T(8,128)(2,1)} %refs_0_.1) | copy-start | bytes 294916
  10.2 5.9 %collective-permute-start.5 = (bf16[512,256]{1,0:T(8,128)(2,1)S(1)}, bf16[512,256]{1,0:T(8,128)(2,1)S(1)}, u32[]{:S(2)}, u32[]{:S(2)}) collective-permute-start(bf16[512,256]{1,0:T(8,128)(2,1)S(1)} %collective-permute-done.4.refs_2_), channel_id=1, source_target_pairs={{0,1},{1,0},{2,3},{3,2},{4,5},{5,4},{6,7},{7,6},{8,9},{9,8},{10,11... | collective-permute-start | bytes 786440 | tf_op jit(solution)/shard_map/ppermute | solution.py:325
  15.5 10.3 %collective-permute-start.7 = (bf16[768,256]{1,0:T(8,128)(2,1)S(1)}, bf16[768,256]{1,0:T(8,128)(2,1)S(1)}, u32[]{:S(2)}, u32[]{:S(2)}) collective-permute-start(bf16[768,256]{1,0:T(8,128)(2,1)S(1)} %stack.1.stacked_ref.refs_0_), channel_id=1, source_target_pairs={{0,2},{1,3},{2,0},{3,1},{4,6},{5,7},{6,4},{7,5},{8,10},{9,11},{10,... | collective-permute-start | bytes 1179656 | tf_op jit(solution)/shard_map/ppermute | solution.py:325
  16.1 15.9 %collective-permute-start.9 = (bf16[768,256]{1,0:T(8,128)(2,1)S(1)}, bf16[768,256]{1,0:T(8,128)(2,1)S(1)}, u32[]{:S(2)}, u32[]{:S(2)}) collective-permute-start(bf16[768,256]{1,0:T(8,128)(2,1)S(1)} %stack.1.stacked_ref.refs_0_), channel_id=1, source_target_pairs={{0,1},{1,0},{2,3},{3,2},{4,5},{5,4},{6,7},{7,6},{8,9},{9,8},{10,11... | collective-permute-start | bytes 1179656 | tf_op jit(solution)/shard_map/ppermute | solution.py:325
  19.5 12.4 %collective-permute-start.6 = (bf16[192,256]{1,0:T(8,128)(2,1)S(1)}, bf16[192,256]{1,0:T(8,128)(2,1)S(1)}, u32[]{:S(2)}, u32[]{:S(2)}) collective-permute-start(bf16[192,256]{1,0:T(8,128)(2,1)S(1)} %get-tuple-element.21), channel_id=1, source_target_pairs={{0,8},{1,9},{2,10},{3,11},{4,12},{5,13},{6,14},{7,15},{8,0},{9,1},... | collective-permute-start | bytes 294920 | tf_op jit(solution)/shard_map/ppermute | solution.py:325
  20.0 11.9 %all-to-all-start = ((f32[16,1,768]{2,1,0:T(1,128)}), f32[16,1,768]{2,1,0:T(1,128)S(1)}, u32[]{:S(2)}, u32[]{:S(2)}) async-start(f32[16,1,768]{2,1,0:T(1,128)} %get-tuple-element.20), calls=%async_computation | async-start | bytes 98304 | tf_op jit(solution)/shard_map/all_to_all | solution.py:341
  25.8 7.7 %collective-permute-start.8 = (bf16[768,256]{1,0:T(8,128)(2,1)S(1)}, bf16[768,256]{1,0:T(8,128)(2,1)S(1)}, u32[]{:S(2)}, u32[]{:S(2)}) collective-permute-start(bf16[768,256]{1,0:T(8,128)(2,1)S(1)} %collective-permute-done.7.refs_2_), channel_id=1, source_target_pairs={{0,1},{1,0},{2,3},{3,2},{4,5},{5,4},{6,7},{7,6},{8,9},{9,8},{10,11... | collective-permute-start | bytes 1179656 | tf_op jit(solution)/shard_map/ppermute | solution.py:325
  25.8 9.2 %collective-permute-start.10 = (bf16[192,256]{1,0:T(8,128)(2,1)S(1)}, bf16[192,256]{1,0:T(8,128)(2,1)S(1)}, u32[]{:S(2)}, u32[]{:S(2)}) collective-permute-start(bf16[192,256]{1,0:T(8,128)(2,1)S(1)} %get-tuple-element.28), channel_id=1, source_target_pairs={{0,4},{1,5},{2,6},{3,7},{4,0},{5,1},{6,2},{7,3},{8,12},{9,13},{10,... | collective-permute-start | bytes 294920 | tf_op jit(solution)/shard_map/ppermute | solution.py:325
  27.2 7.8 %collective-permute-start.11 = (bf16[192,256]{1,0:T(8,128)(2,1)S(1)}, bf16[192,256]{1,0:T(8,128)(2,1)S(1)}, u32[]{:S(2)}, u32[]{:S(2)}) collective-permute-start(bf16[192,256]{1,0:T(8,128)(2,1)S(1)} %get-tuple-element.29), channel_id=1, source_target_pairs={{0,12},{1,13},{2,14},{3,15},{4,8},{5,9},{6,10},{7,11},{8,4},{9,5},... | collective-permute-start | bytes 294920 | tf_op jit(solution)/shard_map/ppermute | solution.py:325

commit v13 on v12

--- a/solution.py
+++ b/solution.py
@@ -191,7 +191,9 @@
     return top + jnp.log(sum(jnp.exp(x - top) for x in each))
 
 
-def add_groups(groups, tile, scale, levels, code_ref, norm_ref, emb, weighted, folded):
+def add_groups(
+    groups, tile, scale, levels, code_ref, norm_ref, emb, weighted, folded, before=None
+):
     lanes = folded.shape[1]
     code = code_ref[...]
     norm = jnp.concatenate([norm_ref[...]] * (tile // lanes), axis=1)
@@ -202,19 +204,18 @@
             s = scale * nt_dot(code, rows_here) - norm
             shares = jnp.exp2(s - level[:, start : start + tile]).astype(jnp.bfloat16)
             wide = shares.astype(jnp.float32)
-            part = folded[...]
-            for i in range(tile // lanes):
-                part = part + wide[:, i * lanes : (i + 1) * lanes]
-            folded[...] = part
-            weighted[...] += jnp.dot(shares, rows_here, preferred_element_type=jnp.float32)
+            part = fold_lanes(jnp.add, wide, lanes)
+            product = jnp.dot(shares, rows_here, preferred_element_type=jnp.float32)
+            if before is not None:
+                product, part = product + before[0][...], part + before[1][...]
+            weighted[...], folded[...] = product, part
+            before = weighted, folded
 
 
 def early_kernel(outer, inner, groups, tile, scale, order, place_ref, lam_ref, code_ref, norm_ref, *refs):
     emb = refs[: len(groups)]
     weighted, folded = refs[len(groups) :]
     spoke = place_ref[0] % inner
-    weighted[...] = jnp.zeros_like(weighted)
-    folded[...] = jnp.zeros_like(folded)
     levels = lambda g: read_lse(lam_ref, outer, inner, spoke ^ g)
     add_groups(groups, tile, scale, levels, code_ref, norm_ref, emb, weighted, folded)
 
@@ -226,10 +227,9 @@
     rows = lam_ref.shape[2]
     rows_dev = rows // outer
     place, spoke = place_ref[0] // inner, place_ref[0] % inner
-    weighted[...] = weighted_in[...]
-    folded[...] = folded_in[...]
     levels = lambda g: read_lse(lam_ref, outer, inner, spoke ^ g)
-    add_groups(groups, tile, scale, levels, code_ref, norm_ref, emb, weighted, folded)
+    before = weighted_in, folded_in
+    add_groups(groups, tile, scale, levels, code_ref, norm_ref, emb, weighted, folded, before)
     masses = jnp.sum(folded[...], axis=1, keepdims=True)
     share = 1.0 / (masses + rows_dev / k_dev)
     shift_ref[...] = (

time: 36 us -> 36 us (level)
  no operation moved by 1% of the time
where the time goes in v13:
time: 36 us; the launch traced here: 35.8 us
  starting transfers between devices  17.5 us (49%)
  waiting for transfers between devices  8.34 us (23%)
  Pallas kernels  7.45 us (21%)
  local copies, waits for them, and re-layouts  1.84 us (5%)
  between operations  0.69 us (2%)
    ppermute x12, starting transfers between devices, swap(): return lax.ppermute(x, AXIS, [(i, i ^ step) for i in range(size)])  12.6 us
    ppermute x12, waiting for transfers between devices, swap(): return lax.ppermute(x, AXIS, [(i, i ^ step) for i in range(size)])  5.97 us
    all_to_all x1, starting transfers between devices, on_device(): lam = lax.all_to_all(lam, AXIS, 0, 0)  4.85 us
    pallas_call x1, Pallas kernels, rows_calc(): pl.pallas_call(functools.partial(rows_kernel, outer, inner, tile, LOG2E *...  3.41 us
    pallas_call x2, Pallas kernels, columns_calc(): pl.pallas_call(functools.partial(body, outer, inner, groups, tile, LOG2E...  3.01 us
    all_to_all x1, waiting for transfers between devices, on_device(): lam = lax.all_to_all(lam, AXIS, 0, 0)  2.37 us
    unnamed x4, local copies, waits for them, and re-layouts  1.84 us
    pallas_call x1, Pallas kernels, soft_calc(): pl.pallas_call(soft_kernel, out_shape=jax.ShapeDtypeStruct(shape, jnp.bfl...  0.83 us
  transfers between devices with their start and end apart: 13, of which 5 were waited for; matrix products, arithmetic and copies ran while one was open for 0% of the time, Pallas kernels for 18%

profile of v13, /device:TPU:0, one launch (start us, length us, event | category | flops | bytes accessed | tf_op | source)
XLA Modules:
  0.0 35.8 jit_solution(575038921198502878)
XLA Ops:
  0.6 3.0 %collective-permute-start.4 = (bf16[512,256]{1,0:T(8,128)(2,1)}, bf16[512,256]{1,0:T(8,128)(2,1)S(1)}, u32[]{:S(2)}, u32[]{:S(2)}) collective-permute-start(bf16[512,256]{1,0:T(8,128)(2,1)} %refs_1_.1), channel_id=1, source_target_pairs={{0,2},{1,3},{2,0},{3,1},{4,6},{5,7},{6,4},{7,5},{8,10},{9,11},{10,... | collective-permute-start | bytes 786440 | tf_op jit(solution)/shard_map/ppermute | solution.py:325
  3.7 3.6 %collective-permute-start.1 = (bf16[192,256]{1,0:T(8,128)(2,1)}, bf16[192,256]{1,0:T(8,128)(2,1)S(1)}, u32[]{:S(2)}, u32[]{:S(2)}) collective-permute-start(bf16[192,256]{1,0:T(8,128)(2,1)} %refs_0_.1), channel_id=1, source_target_pairs={{0,12},{1,13},{2,14},{3,15},{4,8},{5,9},{6,10},{7,11},{8,4},{9,5},... | collective-permute-start | bytes 294920 | tf_op jit(solution)/shard_map/ppermute | solution.py:325
  7.3 0.8 %collective-permute-start.2 = (bf16[192,256]{1,0:T(8,128)(2,1)}, bf16[192,256]{1,0:T(8,128)(2,1)S(1)}, u32[]{:S(2)}, u32[]{:S(2)}) collective-permute-start(bf16[192,256]{1,0:T(8,128)(2,1)} %refs_0_.1), channel_id=1, source_target_pairs={{0,4},{1,5},{2,6},{3,7},{4,0},{5,1},{6,2},{7,3},{8,12},{9,13},{10,... | collective-permute-start | bytes 294920 | tf_op jit(solution)/shard_map/ppermute | solution.py:325
  8.1 0.9 %copy-done = bf16[512,256]{1,0:T(8,128)(2,1)S(1)} copy-done((bf16[512,256]{1,0:T(8,128)(2,1)S(1)}, bf16[512,256]{1,0:T(8,128)(2,1)}, u32[]{:S(2)}) %copy-start) | copy-done | bytes 262168
  9.0 0.9 %copy-done.1 = bf16[192,256]{1,0:T(8,128)(2,1)S(1)} copy-done((bf16[192,256]{1,0:T(8,128)(2,1)S(1)}, bf16[192,256]{1,0:T(8,128)(2,1)}, u32[]{:S(2)}) %copy-start.1) | copy-done | bytes 98328
  9.9 0.2 collective-permute-done.4.refs_2_
  10.2 0.3 collective-permute-start.5
  10.5 0.9 %collective-permute-done.1.refs_1_ = bf16[192,256]{1,0:T(8,128)(2,1)S(1)} collective-permute-done((bf16[192,256]{1,0:T(8,128)(2,1)}, bf16[192,256]{1,0:T(8,128)(2,1)S(1)}, u32[]{:S(2)}, u32[]{:S(2)}) %collective-permute-start.1) | collective-permute-done | bytes 98336 | tf_op jit(solution)/shard_map/ppermute | solution.py:325
  11.4 4.1 %collective-permute-done.refs_0_ = bf16[192,256]{1,0:T(8,128)(2,1)S(1)} collective-permute-done((bf16[192,256]{1,0:T(8,128)(2,1)}, bf16[192,256]{1,0:T(8,128)(2,1)S(1)}, u32[]{:S(2)}, u32[]{:S(2)}) %collective-permute-start) | collective-permute-done | bytes 98336 | tf_op jit(solution)/shard_map/ppermute | solution.py:325
  15.5 0.6 %collective-permute-start.7 = (bf16[768,256]{1,0:T(8,128)(2,1)S(1)}, bf16[768,256]{1,0:T(8,128)(2,1)S(1)}, u32[]{:S(2)}, u32[]{:S(2)}) collective-permute-start(bf16[768,256]{1,0:T(8,128)(2,1)S(1)} %stack.1.stacked_ref.refs_0_), channel_id=1, source_target_pairs={{0,2},{1,3},{2,0},{3,1},{4,6},{5,7},{6,4},{7,5},{8,10},{9,11},{10,... | collective-permute-start | bytes 1179656 | tf_op jit(solution)/shard_map/ppermute | solution.py:325
  16.1 0.0 collective-permute-start.9
  16.1 3.4 %rows_calc.1 = (f32[16,1,768]{2,1,0:T(1,128)}, bf16[192,256]{1,0:T(8,128)(2,1)S(1)}, bf16[192,256]{1,0:T(8,128)(2,1)S(1)}, bf16[192,256]{1,0:T(8,128)(2,1)S(1)}, bf16[192,256]{1,0:T(8,128)(2,1)S(1)}) custom-call(s32[1]{0:T(128)} %bitcast.place_ref, bf16[768,256]{1,0:T(8,128)(2,1)S(1)} %stack.1.stacked_ref.refs_0_, ...), custom_call_target="tpu_custom_call" | custom-call | flops 1610612736 | bytes 1441792 | tf_op jit(solution)/shard_map/rows_calc/pallas_call | solution.py:146
  19.5 0.5 %collective-permute-start.6 = (bf16[192,256]{1,0:T(8,128)(2,1)S(1)}, bf16[192,256]{1,0:T(8,128)(2,1)S(1)}, u32[]{:S(2)}, u32[]{:S(2)}) collective-permute-start(bf16[192,256]{1,0:T(8,128)(2,1)S(1)} %get-tuple-element.21), channel_id=1, source_target_pairs={{0,8},{1,9},{2,10},{3,11},{4,12},{5,13},{6,14},{7,15},{8,0},{9,1},... | collective-permute-start | bytes 294920 | tf_op jit(solution)/shard_map/ppermute | solution.py:325
  20.0 4.8 %all-to-all-start = ((f32[16,1,768]{2,1,0:T(1,128)}), f32[16,1,768]{2,1,0:T(1,128)S(1)}, u32[]{:S(2)}, u32[]{:S(2)}) async-start(f32[16,1,768]{2,1,0:T(1,128)} %get-tuple-element.20), calls=%async_computation | async-start | bytes 98304 | tf_op jit(solution)/shard_map/all_to_all | solution.py:341
  24.9 0.1 norm_calc.1.norm_ref
  25.0 0.8 %collective-permute-done.7.refs_2_ = bf16[768,256]{1,0:T(8,128)(2,1)S(1)} collective-permute-done((bf16[768,256]{1,0:T(8,128)(2,1)S(1)}, bf16[768,256]{1,0:T(8,128)(2,1)S(1)}, u32[]{:S(2)}, u32[]{:S(2)}) %collective-permute-start.7) | collective-permute-done | bytes 393248 | tf_op jit(solution)/shard_map/ppermute | solution.py:325
  25.8 1.4 %collective-permute-start.10 = (bf16[192,256]{1,0:T(8,128)(2,1)S(1)}, bf16[192,256]{1,0:T(8,128)(2,1)S(1)}, u32[]{:S(2)}, u32[]{:S(2)}) collective-permute-start(bf16[192,256]{1,0:T(8,128)(2,1)S(1)} %get-tuple-element.28), channel_id=1, source_target_pairs={{0,4},{1,5},{2,6},{3,7},{4,0},{5,1},{6,2},{7,3},{8,12},{9,13},{10,... | collective-permute-start | bytes 294920 | tf_op jit(solution)/shard_map/ppermute | solution.py:325
  27.2 2.4 %collective-permute-start.11 = (bf16[192,256]{1,0:T(8,128)(2,1)S(1)}, bf16[192,256]{1,0:T(8,128)(2,1)S(1)}, u32[]{:S(2)}, u32[]{:S(2)}) collective-permute-start(bf16[192,256]{1,0:T(8,128)(2,1)S(1)} %get-tuple-element.29), channel_id=1, source_target_pairs={{0,12},{1,13},{2,14},{3,15},{4,8},{5,9},{6,10},{7,11},{8,4},{9,5},... | collective-permute-start | bytes 294920 | tf_op jit(solution)/shard_map/ppermute | solution.py:325
  29.6 2.4 %all-to-all-done.lam_ref = f32[16,1,768]{2,1,0:T(1,128)S(1)} async-done(((f32[16,1,768]{2,1,0:T(1,128)}), f32[16,1,768]{2,1,0:T(1,128)S(1)}, u32[]{:S(2)}, u32[]{:S(2)}) %all-to-all-start) | async-done | bytes 49184 | tf_op jit(solution)/shard_map/all_to_all | solution.py:341
  31.9 0.0 collective-permute-done.6.refs_0_
  31.9 0.0 collective-permute-done.9.refs_1_
  31.9 1.5 %columns_calc.2 = (f32[512,256]{1,0:T(8,128)S(1)}, f32[512,128]{1,0:T(8,128)S(1)}) custom-call(s32[1]{0:T(128)} %bitcast.place_ref, f32[16,1,768]{2,1,0:T(1,128)S(1)} %all-to-all-done.lam_ref, bf16[512,256]{1,0:T(8,128)(2,1)S(1)} %get-tuple-element.19.refs_0_.code_ref, f32[512,128]{1,0:T(8,128)S(1)} %norm_calc.1.norm_ref, ...), custom_call_target="tpu_custom_call" | custom-call | flops 19327352832 | bytes 1703936 | tf_op jit(solution)/shard_map/columns_calc/pallas_call | solution.py:296
  33.5 1.5 %columns_calc.3 = (bf16[512,256]{1,0:T(8,128)(2,1)}, f32[1,512]{1,0:T(1,128)}, f32[192,8]{1,0:T(8,128)S(1)}, f32[1,192]{1,0:T(1,128)}) custom-call(s32[1]{0:T(128)} %bitcast.place_ref, f32[16,1,768]{2,1,0:T(1,128)S(1)} %all-to-all-done.lam_ref, bf16[512,256]{1,0:T(8,128)(2,1)S(1)} %get-tuple-element.19.refs_0_.code_ref, f32[512,128]{1,0:T(8,128)S(1)} %norm_calc.1.norm_ref, ...), custom_call_target="tpu_custom_call" | custom-call | flops 402653184 | bytes 917504 | tf_op jit(solution)/shard_map/columns_calc/pallas_call | solution.py:296
  35.0 0.8 %soft_calc.1 = bf16[192,256]{1,0:T(8,128)(2,1)} custom-call(f32[192,8]{1,0:T(8,128)S(1)} %get-tuple-element.27.weight_ref, bf16[192,256]{1,0:T(8,128)(2,1)S(1)} %collective-permute-done.6.refs_0_, bf16[192,256]{1,0:T(8,128)(2,1)S(1)} %collective-permute-done.10.refs_1_, bf16[192,256]{1,0:T(8,128)(2,1)S(1)} %collective-permute-done.11.refs_2_, ...), custom_call_target="tpu_custom_call" | custom-call | flops 393216 | bytes 491520 | tf_op jit(solution)/shard_map/soft_calc/pallas_call | solution.py:261
  (13 shorter events, 0.1 us)
Async XLA Ops:
  0.6 9.5 %collective-permute-start.4 = (bf16[512,256]{1,0:T(8,128)(2,1)}, bf16[512,256]{1,0:T(8,128)(2,1)S(1)}, u32[]{:S(2)}, u32[]{:S(2)}) collective-permute-start(bf16[512,256]{1,0:T(8,128)(2,1)} %refs_1_.1), channel_id=1, source_target_pairs={{0,2},{1,3},{2,0},{3,1},{4,6},{5,7},{6,4},{7,5},{8,10},{9,11},{10,... | collective-permute-start | bytes 786440 | tf_op jit(solution)/shard_map/ppermute | solution.py:325
  3.7 7.7 %collective-permute-start.1 = (bf16[192,256]{1,0:T(8,128)(2,1)}, bf16[192,256]{1,0:T(8,128)(2,1)S(1)}, u32[]{:S(2)}, u32[]{:S(2)}) collective-permute-start(bf16[192,256]{1,0:T(8,128)(2,1)} %refs_0_.1), channel_id=1, source_target_pairs={{0,12},{1,13},{2,14},{3,15},{4,8},{5,9},{6,10},{7,11},{8,4},{9,5},... | collective-permute-start | bytes 294920 | tf_op jit(solution)/shard_map/ppermute | solution.py:325
  7.3 8.2 %collective-permute-start = (bf16[192,256]{1,0:T(8,128)(2,1)}, bf16[192,256]{1,0:T(8,128)(2,1)S(1)}, u32[]{:S(2)}, u32[]{:S(2)}) collective-permute-start(bf16[192,256]{1,0:T(8,128)(2,1)} %refs_0_.1), channel_id=1, source_target_pairs={{0,8},{1,9},{2,10},{3,11},{4,12},{5,13},{6,14},{7,15},{8,0},{9,1},... | collective-permute-start | bytes 294920 | tf_op jit(solution)/shard_map/ppermute | solution.py:325
  7.3 8.2 %collective-permute-start.2 = (bf16[192,256]{1,0:T(8,128)(2,1)}, bf16[192,256]{1,0:T(8,128)(2,1)S(1)}, u32[]{:S(2)}, u32[]{:S(2)}) collective-permute-start(bf16[192,256]{1,0:T(8,128)(2,1)} %refs_0_.1), channel_id=1, source_target_pairs={{0,4},{1,5},{2,6},{3,7},{4,0},{5,1},{6,2},{7,3},{8,12},{9,13},{10,... | collective-permute-start | bytes 294920 | tf_op jit(solution)/shard_map/ppermute | solution.py:325
  8.1 8.0 %collective-permute-start.3 = (bf16[512,256]{1,0:T(8,128)(2,1)}, bf16[512,256]{1,0:T(8,128)(2,1)S(1)}, u32[]{:S(2)}, u32[]{:S(2)}) collective-permute-start(bf16[512,256]{1,0:T(8,128)(2,1)} %refs_1_.1), channel_id=1, source_target_pairs={{0,1},{1,0},{2,3},{3,2},{4,5},{5,4},{6,7},{7,6},{8,9},{9,8},{10,11... | collective-permute-start | bytes 786440 | tf_op jit(solution)/shard_map/ppermute | solution.py:325
  8.1 1.0 %copy-start = (bf16[512,256]{1,0:T(8,128)(2,1)S(1)}, bf16[512,256]{1,0:T(8,128)(2,1)}, u32[]{:S(2)}) copy-start(bf16[512,256]{1,0:T(8,128)(2,1)} %refs_1_.1) | copy-start | bytes 786436
  9.0 0.9 %copy-start.1 = (bf16[192,256]{1,0:T(8,128)(2,1)S(1)}, bf16[192,256]{1,0:T(8,128)(2,1)}, u32[]{:S(2)}) copy-start(bf16[192,256]{1,0:T(8,128)(2,1)} %refs_0_.1) | copy-start | bytes 294916
  10.2 5.9 %collective-permute-start.5 = (bf16[512,256]{1,0:T(8,128)(2,1)S(1)}, bf16[512,256]{1,0:T(8,128)(2,1)S(1)}, u32[]{:S(2)}, u32[]{:S(2)}) collective-permute-start(bf16[512,256]{1,0:T(8,128)(2,1)S(1)} %collective-permute-done.4.refs_2_), channel_id=1, source_target_pairs={{0,1},{1,0},{2,3},{3,2},{4,5},{5,4},{6,7},{7,6},{8,9},{9,8},{10,11... | collective-permute-start | bytes 786440 | tf_op jit(solution)/shard_map/ppermute | solution.py:325
  15.5 10.3 %collective-permute-start.7 = (bf16[768,256]{1,0:T(8,128)(2,1)S(1)}, bf16[768,256]{1,0:T(8,128)(2,1)S(1)}, u32[]{:S(2)}, u32[]{:S(2)}) collective-permute-start(bf16[768,256]{1,0:T(8,128)(2,1)S(1)} %stack.1.stacked_ref.refs_0_), channel_id=1, source_target_pairs={{0,2},{1,3},{2,0},{3,1},{4,6},{5,7},{6,4},{7,5},{8,10},{9,11},{10,... | collective-permute-start | bytes 1179656 | tf_op jit(solution)/shard_map/ppermute | solution.py:325
  16.1 15.9 %collective-permute-start.9 = (bf16[768,256]{1,0:T(8,128)(2,1)S(1)}, bf16[768,256]{1,0:T(8,128)(2,1)S(1)}, u32[]{:S(2)}, u32[]{:S(2)}) collective-permute-start(bf16[768,256]{1,0:T(8,128)(2,1)S(1)} %stack.1.stacked_ref.refs_0_), channel_id=1, source_target_pairs={{0,1},{1,0},{2,3},{3,2},{4,5},{5,4},{6,7},{7,6},{8,9},{9,8},{10,11... | collective-permute-start | bytes 1179656 | tf_op jit(solution)/shard_map/ppermute | solution.py:325
  19.5 12.4 %collective-permute-start.6 = (bf16[192,256]{1,0:T(8,128)(2,1)S(1)}, bf16[192,256]{1,0:T(8,128)(2,1)S(1)}, u32[]{:S(2)}, u32[]{:S(2)}) collective-permute-start(bf16[192,256]{1,0:T(8,128)(2,1)S(1)} %get-tuple-element.21), channel_id=1, source_target_pairs={{0,8},{1,9},{2,10},{3,11},{4,12},{5,13},{6,14},{7,15},{8,0},{9,1},... | collective-permute-start | bytes 294920 | tf_op jit(solution)/shard_map/ppermute | solution.py:325
  20.0 11.9 %all-to-all-start = ((f32[16,1,768]{2,1,0:T(1,128)}), f32[16,1,768]{2,1,0:T(1,128)S(1)}, u32[]{:S(2)}, u32[]{:S(2)}) async-start(f32[16,1,768]{2,1,0:T(1,128)} %get-tuple-element.20), calls=%async_computation | async-start | bytes 98304 | tf_op jit(solution)/shard_map/all_to_all | solution.py:341
  25.8 7.7 %collective-permute-start.8 = (bf16[768,256]{1,0:T(8,128)(2,1)S(1)}, bf16[768,256]{1,0:T(8,128)(2,1)S(1)}, u32[]{:S(2)}, u32[]{:S(2)}) collective-permute-start(bf16[768,256]{1,0:T(8,128)(2,1)S(1)} %collective-permute-done.7.refs_2_), channel_id=1, source_target_pairs={{0,1},{1,0},{2,3},{3,2},{4,5},{5,4},{6,7},{7,6},{8,9},{9,8},{10,11... | collective-permute-start | bytes 1179656 | tf_op jit(solution)/shard_map/ppermute | solution.py:325
  25.8 9.2 %collective-permute-start.10 = (bf16[192,256]{1,0:T(8,128)(2,1)S(1)}, bf16[192,256]{1,0:T(8,128)(2,1)S(1)}, u32[]{:S(2)}, u32[]{:S(2)}) collective-permute-start(bf16[192,256]{1,0:T(8,128)(2,1)S(1)} %get-tuple-element.28), channel_id=1, source_target_pairs={{0,4},{1,5},{2,6},{3,7},{4,0},{5,1},{6,2},{7,3},{8,12},{9,13},{10,... | collective-permute-start | bytes 294920 | tf_op jit(solution)/shard_map/ppermute | solution.py:325
  27.2 7.8 %collective-permute-start.11 = (bf16[192,256]{1,0:T(8,128)(2,1)S(1)}, bf16[192,256]{1,0:T(8,128)(2,1)S(1)}, u32[]{:S(2)}, u32[]{:S(2)}) collective-permute-start(bf16[192,256]{1,0:T(8,128)(2,1)S(1)} %get-tuple-element.29), channel_id=1, source_target_pairs={{0,12},{1,13},{2,14},{3,15},{4,8},{5,9},{6,10},{7,11},{8,4},{9,5},... | collective-permute-start | bytes 294920 | tf_op jit(solution)/shard_map/ppermute | solution.py:325

commit v14 on v13

--- a/solution.py
+++ b/solution.py
@@ -118,12 +118,9 @@
 
     count = rows // tile
     if count <= 4:
-        top = first_half(0, 0)
+        tops = [first_half(t * tile, t * tile) for t in range(count)]
         for t in range(count):
-            here = top
-            if t + 1 < count:
-                top = first_half((t + 1) * tile, (t + 1) * tile)
-            second_half(t * tile, t * tile, here)
+            second_half(t * tile, t * tile, tops[t])
     else:
 
         @pl.loop(0, count)

time: 36 us -> 36 us (level)
  no operation moved by 1% of the time
where the time goes in v14:
time: 36 us; the launch traced here: 35.8 us
  starting transfers between devices  17.5 us (49%)
  waiting for transfers between devices  8.35 us (23%)
  Pallas kernels  7.43 us (21%)
  local copies, waits for them, and re-layouts  1.84 us (5%)
  between operations  0.69 us (2%)
    ppermute x12, starting transfers between devices, swap(): return lax.ppermute(x, AXIS, [(i, i ^ step) for i in range(size)])  12.6 us
    ppermute x12, waiting for transfers between devices, swap(): return lax.ppermute(x, AXIS, [(i, i ^ step) for i in range(size)])  5.99 us
    all_to_all x1, starting transfers between devices, on_device(): lam = lax.all_to_all(lam, AXIS, 0, 0)  4.85 us
    pallas_call x1, Pallas kernels, rows_calc(): pl.pallas_call(functools.partial(rows_kernel, outer, inner, tile, LOG2E *...  3.4 us
    pallas_call x2, Pallas kernels, columns_calc(): pl.pallas_call(functools.partial(body, outer, inner, groups, tile, LOG2E...  3.01 us
    all_to_all x1, waiting for transfers between devices, on_device(): lam = lax.all_to_all(lam, AXIS, 0, 0)  2.37 us
    unnamed x4, local copies, waits for them, and re-layouts  1.84 us
    pallas_call x1, Pallas kernels, soft_calc(): pl.pallas_call(soft_kernel, out_shape=jax.ShapeDtypeStruct(shape, jnp.bfl...  0.83 us
  transfers between devices with their start and end apart: 13, of which 5 were waited for; matrix products, arithmetic and copies ran while one was open for 0% of the time, Pallas kernels for 18%

profile of v14, /device:TPU:0, one launch (start us, length us, event | category | flops | bytes accessed | tf_op | source)
XLA Modules:
  0.0 35.8 jit_solution(7397110995763129479)
XLA Ops:
  0.6 3.0 %collective-permute-start.4 = (bf16[512,256]{1,0:T(8,128)(2,1)}, bf16[512,256]{1,0:T(8,128)(2,1)S(1)}, u32[]{:S(2)}, u32[]{:S(2)}) collective-permute-start(bf16[512,256]{1,0:T(8,128)(2,1)} %refs_1_.1), channel_id=1, source_target_pairs={{0,2},{1,3},{2,0},{3,1},{4,6},{5,7},{6,4},{7,5},{8,10},{9,11},{10,... | collective-permute-start | bytes 786440 | tf_op jit(solution)/shard_map/ppermute | solution.py:322
  3.7 3.6 %collective-permute-start.1 = (bf16[192,256]{1,0:T(8,128)(2,1)}, bf16[192,256]{1,0:T(8,128)(2,1)S(1)}, u32[]{:S(2)}, u32[]{:S(2)}) collective-permute-start(bf16[192,256]{1,0:T(8,128)(2,1)} %refs_0_.1), channel_id=1, source_target_pairs={{0,12},{1,13},{2,14},{3,15},{4,8},{5,9},{6,10},{7,11},{8,4},{9,5},... | collective-permute-start | bytes 294920 | tf_op jit(solution)/shard_map/ppermute | solution.py:322
  7.3 0.0 collective-permute-start
  7.3 0.8 %collective-permute-start.2 = (bf16[192,256]{1,0:T(8,128)(2,1)}, bf16[192,256]{1,0:T(8,128)(2,1)S(1)}, u32[]{:S(2)}, u32[]{:S(2)}) collective-permute-start(bf16[192,256]{1,0:T(8,128)(2,1)} %refs_0_.1), channel_id=1, source_target_pairs={{0,4},{1,5},{2,6},{3,7},{4,0},{5,1},{6,2},{7,3},{8,12},{9,13},{10,... | collective-permute-start | bytes 294920 | tf_op jit(solution)/shard_map/ppermute | solution.py:322
  8.1 0.0 collective-permute-start.3
  8.1 0.9 %copy-done = bf16[512,256]{1,0:T(8,128)(2,1)S(1)} copy-done((bf16[512,256]{1,0:T(8,128)(2,1)S(1)}, bf16[512,256]{1,0:T(8,128)(2,1)}, u32[]{:S(2)}) %copy-start) | copy-done | bytes 262168
  9.0 0.9 %copy-done.1 = bf16[192,256]{1,0:T(8,128)(2,1)S(1)} copy-done((bf16[192,256]{1,0:T(8,128)(2,1)S(1)}, bf16[192,256]{1,0:T(8,128)(2,1)}, u32[]{:S(2)}) %copy-start.1) | copy-done | bytes 98328
  9.9 0.2 collective-permute-done.4.refs_2_
  10.2 0.3 collective-permute-start.5
  10.5 0.9 %collective-permute-done.1.refs_1_ = bf16[192,256]{1,0:T(8,128)(2,1)S(1)} collective-permute-done((bf16[192,256]{1,0:T(8,128)(2,1)}, bf16[192,256]{1,0:T(8,128)(2,1)S(1)}, u32[]{:S(2)}, u32[]{:S(2)}) %collective-permute-start.1) | collective-permute-done | bytes 98336 | tf_op jit(solution)/shard_map/ppermute | solution.py:322
  11.4 4.1 %collective-permute-done.refs_0_ = bf16[192,256]{1,0:T(8,128)(2,1)S(1)} collective-permute-done((bf16[192,256]{1,0:T(8,128)(2,1)}, bf16[192,256]{1,0:T(8,128)(2,1)S(1)}, u32[]{:S(2)}, u32[]{:S(2)}) %collective-permute-start) | collective-permute-done | bytes 98336 | tf_op jit(solution)/shard_map/ppermute | solution.py:322
  15.5 0.6 %collective-permute-start.7 = (bf16[768,256]{1,0:T(8,128)(2,1)S(1)}, bf16[768,256]{1,0:T(8,128)(2,1)S(1)}, u32[]{:S(2)}, u32[]{:S(2)}) collective-permute-start(bf16[768,256]{1,0:T(8,128)(2,1)S(1)} %stack.1.stacked_ref.refs_0_), channel_id=1, source_target_pairs={{0,2},{1,3},{2,0},{3,1},{4,6},{5,7},{6,4},{7,5},{8,10},{9,11},{10,... | collective-permute-start | bytes 1179656 | tf_op jit(solution)/shard_map/ppermute | solution.py:322
  16.1 3.4 %rows_calc.1 = (f32[16,1,768]{2,1,0:T(1,128)}, bf16[192,256]{1,0:T(8,128)(2,1)S(1)}, bf16[192,256]{1,0:T(8,128)(2,1)S(1)}, bf16[192,256]{1,0:T(8,128)(2,1)S(1)}, bf16[192,256]{1,0:T(8,128)(2,1)S(1)}) custom-call(s32[1]{0:T(128)} %bitcast.place_ref, bf16[768,256]{1,0:T(8,128)(2,1)S(1)} %stack.1.stacked_ref.refs_0_, ...), custom_call_target="tpu_custom_call" | custom-call | flops 1610612736 | bytes 1441792 | tf_op jit(solution)/shard_map/rows_calc/pallas_call | solution.py:143
  19.5 0.5 %collective-permute-start.6 = (bf16[192,256]{1,0:T(8,128)(2,1)S(1)}, bf16[192,256]{1,0:T(8,128)(2,1)S(1)}, u32[]{:S(2)}, u32[]{:S(2)}) collective-permute-start(bf16[192,256]{1,0:T(8,128)(2,1)S(1)} %get-tuple-element.21), channel_id=1, source_target_pairs={{0,8},{1,9},{2,10},{3,11},{4,12},{5,13},{6,14},{7,15},{8,0},{9,1},... | collective-permute-start | bytes 294920 | tf_op jit(solution)/shard_map/ppermute | solution.py:322
  20.0 4.9 %all-to-all-start = ((f32[16,1,768]{2,1,0:T(1,128)}), f32[16,1,768]{2,1,0:T(1,128)S(1)}, u32[]{:S(2)}, u32[]{:S(2)}) async-start(f32[16,1,768]{2,1,0:T(1,128)} %get-tuple-element.20), calls=%async_computation | async-start | bytes 98304 | tf_op jit(solution)/shard_map/all_to_all | solution.py:338
  24.9 0.1 norm_calc.1.norm_ref
  25.0 0.8 %collective-permute-done.7.refs_2_ = bf16[768,256]{1,0:T(8,128)(2,1)S(1)} collective-permute-done((bf16[768,256]{1,0:T(8,128)(2,1)S(1)}, bf16[768,256]{1,0:T(8,128)(2,1)S(1)}, u32[]{:S(2)}, u32[]{:S(2)}) %collective-permute-start.7) | collective-permute-done | bytes 393248 | tf_op jit(solution)/shard_map/ppermute | solution.py:322
  25.8 1.4 %collective-permute-start.10 = (bf16[192,256]{1,0:T(8,128)(2,1)S(1)}, bf16[192,256]{1,0:T(8,128)(2,1)S(1)}, u32[]{:S(2)}, u32[]{:S(2)}) collective-permute-start(bf16[192,256]{1,0:T(8,128)(2,1)S(1)} %get-tuple-element.28), channel_id=1, source_target_pairs={{0,4},{1,5},{2,6},{3,7},{4,0},{5,1},{6,2},{7,3},{8,12},{9,13},{10,... | collective-permute-start | bytes 294920 | tf_op jit(solution)/shard_map/ppermute | solution.py:322
  27.2 2.4 %collective-permute-start.11 = (bf16[192,256]{1,0:T(8,128)(2,1)S(1)}, bf16[192,256]{1,0:T(8,128)(2,1)S(1)}, u32[]{:S(2)}, u32[]{:S(2)}) collective-permute-start(bf16[192,256]{1,0:T(8,128)(2,1)S(1)} %get-tuple-element.29), channel_id=1, source_target_pairs={{0,12},{1,13},{2,14},{3,15},{4,8},{5,9},{6,10},{7,11},{8,4},{9,5},... | collective-permute-start | bytes 294920 | tf_op jit(solution)/shard_map/ppermute | solution.py:322
  29.5 2.4 %all-to-all-done.lam_ref = f32[16,1,768]{2,1,0:T(1,128)S(1)} async-done(((f32[16,1,768]{2,1,0:T(1,128)}), f32[16,1,768]{2,1,0:T(1,128)S(1)}, u32[]{:S(2)}, u32[]{:S(2)}) %all-to-all-start) | async-done | bytes 49184 | tf_op jit(solution)/shard_map/all_to_all | solution.py:338
  31.9 1.5 %columns_calc.2 = (f32[512,256]{1,0:T(8,128)S(1)}, f32[512,128]{1,0:T(8,128)S(1)}) custom-call(s32[1]{0:T(128)} %bitcast.place_ref, f32[16,1,768]{2,1,0:T(1,128)S(1)} %all-to-all-done.lam_ref, bf16[512,256]{1,0:T(8,128)(2,1)S(1)} %get-tuple-element.19.refs_0_.code_ref, f32[512,128]{1,0:T(8,128)S(1)} %norm_calc.1.norm_ref, ...), custom_call_target="tpu_custom_call" | custom-call | flops 19327352832 | bytes 1703936 | tf_op jit(solution)/shard_map/columns_calc/pallas_call | solution.py:293
  33.5 1.5 %columns_calc.3 = (bf16[512,256]{1,0:T(8,128)(2,1)}, f32[1,512]{1,0:T(1,128)}, f32[192,8]{1,0:T(8,128)S(1)}, f32[1,192]{1,0:T(1,128)}) custom-call(s32[1]{0:T(128)} %bitcast.place_ref, f32[16,1,768]{2,1,0:T(1,128)S(1)} %all-to-all-done.lam_ref, bf16[512,256]{1,0:T(8,128)(2,1)S(1)} %get-tuple-element.19.refs_0_.code_ref, f32[512,128]{1,0:T(8,128)S(1)} %norm_calc.1.norm_ref, ...), custom_call_target="tpu_custom_call" | custom-call | flops 402653184 | bytes 917504 | tf_op jit(solution)/shard_map/columns_calc/pallas_call | solution.py:293
  34.9 0.0 collective-permute-done.11.refs_2_
  35.0 0.8 %soft_calc.1 = bf16[192,256]{1,0:T(8,128)(2,1)} custom-call(f32[192,8]{1,0:T(8,128)S(1)} %get-tuple-element.27.weight_ref, bf16[192,256]{1,0:T(8,128)(2,1)S(1)} %collective-permute-done.6.refs_0_, bf16[192,256]{1,0:T(8,128)(2,1)S(1)} %collective-permute-done.10.refs_1_, bf16[192,256]{1,0:T(8,128)(2,1)S(1)} %collective-permute-done.11.refs_2_, ...), custom_call_target="tpu_custom_call" | custom-call | flops 393216 | bytes 491520 | tf_op jit(solution)/shard_map/soft_calc/pallas_call | solution.py:258
  (13 shorter events, 0.1 us)
Async XLA Ops:
  0.6 9.5 %collective-permute-start.4 = (bf16[512,256]{1,0:T(8,128)(2,1)}, bf16[512,256]{1,0:T(8,128)(2,1)S(1)}, u32[]{:S(2)}, u32[]{:S(2)}) collective-permute-start(bf16[512,256]{1,0:T(8,128)(2,1)} %refs_1_.1), channel_id=1, source_target_pairs={{0,2},{1,3},{2,0},{3,1},{4,6},{5,7},{6,4},{7,5},{8,10},{9,11},{10,... | collective-permute-start | bytes 786440 | tf_op jit(solution)/shard_map/ppermute | solution.py:322
  3.7 7.7 %collective-permute-start.1 = (bf16[192,256]{1,0:T(8,128)(2,1)}, bf16[192,256]{1,0:T(8,128)(2,1)S(1)}, u32[]{:S(2)}, u32[]{:S(2)}) collective-permute-start(bf16[192,256]{1,0:T(8,128)(2,1)} %refs_0_.1), channel_id=1, source_target_pairs={{0,12},{1,13},{2,14},{3,15},{4,8},{5,9},{6,10},{7,11},{8,4},{9,5},... | collective-permute-start | bytes 294920 | tf_op jit(solution)/shard_map/ppermute | solution.py:322
  7.3 8.2 %collective-permute-start = (bf16[192,256]{1,0:T(8,128)(2,1)}, bf16[192,256]{1,0:T(8,128)(2,1)S(1)}, u32[]{:S(2)}, u32[]{:S(2)}) collective-permute-start(bf16[192,256]{1,0:T(8,128)(2,1)} %refs_0_.1), channel_id=1, source_target_pairs={{0,8},{1,9},{2,10},{3,11},{4,12},{5,13},{6,14},{7,15},{8,0},{9,1},... | collective-permute-start | bytes 294920 | tf_op jit(solution)/shard_map/ppermute | solution.py:322
  7.3 8.2 %collective-permute-start.2 = (bf16[192,256]{1,0:T(8,128)(2,1)}, bf16[192,256]{1,0:T(8,128)(2,1)S(1)}, u32[]{:S(2)}, u32[]{:S(2)}) collective-permute-start(bf16[192,256]{1,0:T(8,128)(2,1)} %refs_0_.1), channel_id=1, source_target_pairs={{0,4},{1,5},{2,6},{3,7},{4,0},{5,1},{6,2},{7,3},{8,12},{9,13},{10,... | collective-permute-start | bytes 294920 | tf_op jit(solution)/shard_map/ppermute | solution.py:322
  8.1 8.0 %collective-permute-start.3 = (bf16[512,256]{1,0:T(8,128)(2,1)}, bf16[512,256]{1,0:T(8,128)(2,1)S(1)}, u32[]{:S(2)}, u32[]{:S(2)}) collective-permute-start(bf16[512,256]{1,0:T(8,128)(2,1)} %refs_1_.1), channel_id=1, source_target_pairs={{0,1},{1,0},{2,3},{3,2},{4,5},{5,4},{6,7},{7,6},{8,9},{9,8},{10,11... | collective-permute-start | bytes 786440 | tf_op jit(solution)/shard_map/ppermute | solution.py:322
  8.1 1.0 %copy-start = (bf16[512,256]{1,0:T(8,128)(2,1)S(1)}, bf16[512,256]{1,0:T(8,128)(2,1)}, u32[]{:S(2)}) copy-start(bf16[512,256]{1,0:T(8,128)(2,1)} %refs_1_.1) | copy-start | bytes 786436
  9.0 0.9 %copy-start.1 = (bf16[192,256]{1,0:T(8,128)(2,1)S(1)}, bf16[192,256]{1,0:T(8,128)(2,1)}, u32[]{:S(2)}) copy-start(bf16[192,256]{1,0:T(8,128)(2,1)} %refs_0_.1) | copy-start | bytes 294916
  10.2 5.9 %collective-permute-start.5 = (bf16[512,256]{1,0:T(8,128)(2,1)S(1)}, bf16[512,256]{1,0:T(8,128)(2,1)S(1)}, u32[]{:S(2)}, u32[]{:S(2)}) collective-permute-start(bf16[512,256]{1,0:T(8,128)(2,1)S(1)} %collective-permute-done.4.refs_2_), channel_id=1, source_target_pairs={{0,1},{1,0},{2,3},{3,2},{4,5},{5,4},{6,7},{7,6},{8,9},{9,8},{10,11... | collective-permute-start | bytes 786440 | tf_op jit(solution)/shard_map/ppermute | solution.py:322
  15.5 10.3 %collective-permute-start.7 = (bf16[768,256]{1,0:T(8,128)(2,1)S(1)}, bf16[768,256]{1,0:T(8,128)(2,1)S(1)}, u32[]{:S(2)}, u32[]{:S(2)}) collective-permute-start(bf16[768,256]{1,0:T(8,128)(2,1)S(1)} %stack.1.stacked_ref.refs_0_), channel_id=1, source_target_pairs={{0,2},{1,3},{2,0},{3,1},{4,6},{5,7},{6,4},{7,5},{8,10},{9,11},{10,... | collective-permute-start | bytes 1179656 | tf_op jit(solution)/shard_map/ppermute | solution.py:322
  16.1 15.8 %collective-permute-start.9 = (bf16[768,256]{1,0:T(8,128)(2,1)S(1)}, bf16[768,256]{1,0:T(8,128)(2,1)S(1)}, u32[]{:S(2)}, u32[]{:S(2)}) collective-permute-start(bf16[768,256]{1,0:T(8,128)(2,1)S(1)} %stack.1.stacked_ref.refs_0_), channel_id=1, source_target_pairs={{0,1},{1,0},{2,3},{3,2},{4,5},{5,4},{6,7},{7,6},{8,9},{9,8},{10,11... | collective-permute-start | bytes 1179656 | tf_op jit(solution)/shard_map/ppermute | solution.py:322
  19.5 12.4 %collective-permute-start.6 = (bf16[192,256]{1,0:T(8,128)(2,1)S(1)}, bf16[192,256]{1,0:T(8,128)(2,1)S(1)}, u32[]{:S(2)}, u32[]{:S(2)}) collective-permute-start(bf16[192,256]{1,0:T(8,128)(2,1)S(1)} %get-tuple-element.21), channel_id=1, source_target_pairs={{0,8},{1,9},{2,10},{3,11},{4,12},{5,13},{6,14},{7,15},{8,0},{9,1},... | collective-permute-start | bytes 294920 | tf_op jit(solution)/shard_map/ppermute | solution.py:322
  20.0 11.9 %all-to-all-start = ((f32[16,1,768]{2,1,0:T(1,128)}), f32[16,1,768]{2,1,0:T(1,128)S(1)}, u32[]{:S(2)}, u32[]{:S(2)}) async-start(f32[16,1,768]{2,1,0:T(1,128)} %get-tuple-element.20), calls=%async_computation | async-start | bytes 98304 | tf_op jit(solution)/shard_map/all_to_all | solution.py:338
  25.8 7.7 %collective-permute-start.8 = (bf16[768,256]{1,0:T(8,128)(2,1)S(1)}, bf16[768,256]{1,0:T(8,128)(2,1)S(1)}, u32[]{:S(2)}, u32[]{:S(2)}) collective-permute-start(bf16[768,256]{1,0:T(8,128)(2,1)S(1)} %collective-permute-done.7.refs_2_), channel_id=1, source_target_pairs={{0,1},{1,0},{2,3},{3,2},{4,5},{5,4},{6,7},{7,6},{8,9},{9,8},{10,11... | collective-permute-start | bytes 1179656 | tf_op jit(solution)/shard_map/ppermute | solution.py:322
  25.8 9.2 %collective-permute-start.10 = (bf16[192,256]{1,0:T(8,128)(2,1)S(1)}, bf16[192,256]{1,0:T(8,128)(2,1)S(1)}, u32[]{:S(2)}, u32[]{:S(2)}) collective-permute-start(bf16[192,256]{1,0:T(8,128)(2,1)S(1)} %get-tuple-element.28), channel_id=1, source_target_pairs={{0,4},{1,5},{2,6},{3,7},{4,0},{5,1},{6,2},{7,3},{8,12},{9,13},{10,... | collective-permute-start | bytes 294920 | tf_op jit(solution)/shard_map/ppermute | solution.py:322
  27.2 7.8 %collective-permute-start.11 = (bf16[192,256]{1,0:T(8,128)(2,1)S(1)}, bf16[192,256]{1,0:T(8,128)(2,1)S(1)}, u32[]{:S(2)}, u32[]{:S(2)}) collective-permute-start(bf16[192,256]{1,0:T(8,128)(2,1)S(1)} %get-tuple-element.29), channel_id=1, source_target_pairs={{0,12},{1,13},{2,14},{3,15},{4,8},{5,9},{6,10},{7,11},{8,4},{9,5},... | collective-permute-start | bytes 294920 | tf_op jit(solution)/shard_map/ppermute | solution.py:322
